TPU v7x, 32 devices: a whole 2x2x4 slice. The times are simulated.
32 devices in a mesh: seq: 4 (over y, core), fsdp: 8 (over z, x).
Axes of the slice: x: 2, y: 2, z: 4, core: 2. Of those that a mesh axis runs over, the one named last changes fastest.
Arguments:
- latents: bfloat16 [8, 1536, 1536], P('fsdp', 'seq'), may hold values from -48 to 48
- qkv_weight: bfloat16 [1536, 768], P('fsdp'), may hold values from -1 to 1
- out_weight: bfloat16 [256, 1536], P('fsdp'), may hold values from -0.375 to 0.375
- tile_mask: int32 [4, 4], replicated, may hold values from 0 to 1, as said below
- tile_counts: int32 [4], replicated, may hold values from 64 to 384, as said below
Outputs:
- layer_out: bfloat16 [8, 1536, 1536], P('fsdp', 'seq')
Inputs may be any that keep to these rules, and one draw needn't show every extreme that they name: `tile_mask`: tiles are numbered frame first, then 2 along the height, then 2 along the width. Row q marks a box of whole tiles that contains tile q, of at most 4 tiles; row 0 marks exactly 4. `tile_counts`: the real tokens of a tile fill its first slots. Only tiles on the last frame index may be partial; a partial tile holds k * 64 tokens for some k of 1 to 6, the first tile of the last frame index is full, and the last tile is partial with k of 1 to 5.
All inputs are finite; a program needn't handle non-finite values.
Results may differ from a plain program's by a relative error of at most 0.0074.
Values may be sent and summed in bfloat16 or wider, within the bound.
No kernel may reach another device: no remote copies, remote signals or barrier semaphores. Data moves between devices by JAX's collectives and lax.ppermute only.
A program may use at most 64 MiB of HBM per device.

v0:
```python
import jax
import jax.numpy as jnp
from jax import lax
from jax.sharding import PartitionSpec as P

E = 64
TILE = 384
WINDOW = 4


def attend(queries, keys, values, tile_mask, tile_counts):
    tile_total = tile_mask.shape[0]
    score_scale = float(E) ** (-0.5)
    token_live = jnp.arange(TILE, dtype=jnp.int32)[None, :] < tile_counts[:, None]
    query_tiles = queries.reshape(tile_total, TILE, E)
    key_tiles_all = keys.reshape(tile_total, TILE, E)
    value_tiles_all = values.reshape(tile_total, TILE, E)
    tile_numbers = jnp.arange(tile_total, dtype=jnp.int32)

    def one_tile(tile_index):
        mask_row = tile_mask[tile_index]
        tile_order = jnp.argsort((1 - mask_row) * tile_total + tile_numbers)
        key_tiles = tile_order[:WINDOW]
        slot_live = jnp.arange(WINDOW, dtype=jnp.int32) < jnp.sum(mask_row)
        keys_sel = key_tiles_all[key_tiles].reshape(WINDOW * TILE, E)
        values_sel = value_tiles_all[key_tiles].reshape(WINDOW * TILE, E)
        allowed = (token_live[key_tiles] & slot_live[:, None]).reshape(WINDOW * TILE)[None, :]
        scores = (
            lax.dot_general(
                query_tiles[tile_index],
                keys_sel,
                (((1,), (1,)), ((), ())),
                preferred_element_type=jnp.float32,
            )
            * score_scale
        )
        masked = jnp.where(allowed, scores, -1e30)
        row_max = jnp.max(masked, axis=1, keepdims=True)
        numerators = jnp.where(allowed, jnp.exp(masked - row_max), 0.0)
        denominator = jnp.sum(numerators, axis=1, keepdims=True)
        softmax_top = numerators.astype(jnp.bfloat16)
        summed = jnp.dot(softmax_top, values_sel, preferred_element_type=jnp.float32) / denominator
        return jnp.where(token_live[tile_index][:, None], summed, 0.0).astype(jnp.bfloat16)

    return lax.map(one_tile, tile_numbers).reshape(tile_total * TILE, E)


def local(latents, qkv_weight, out_weight, tile_mask, tile_counts):
    seq_count = lax.axis_size("seq")
    local_rows = latents[0]
    row_count = local_rows.shape[0]
    column_count = qkv_weight.shape[1]
    head_columns = column_count // 3
    device_columns = head_columns // seq_count
    full_qkv = lax.all_gather(qkv_weight, "fsdp", axis=0, tiled=True)
    projected = jnp.dot(local_rows, full_qkv, preferred_element_type=jnp.float32)
    projected = projected.astype(jnp.bfloat16).reshape(row_count, 3, seq_count, device_columns)
    by_heads = lax.all_to_all(projected, "seq", split_axis=2, concat_axis=0, tiled=True)
    head_outputs = attend(
        by_heads[:, 0, 0, 0:E],
        by_heads[:, 1, 0, 0:E],
        by_heads[:, 2, 0, 0:E],
        tile_mask,
        tile_counts,
    )
    attended = head_outputs.reshape(seq_count, row_count, device_columns)
    by_tokens = lax.all_to_all(attended, "seq", split_axis=0, concat_axis=2, tiled=True)[0]
    full_out = lax.all_gather(out_weight, "fsdp", axis=0, tiled=True)
    layer_out = jnp.dot(by_tokens, full_out, preferred_element_type=jnp.float32)
    return layer_out.astype(jnp.bfloat16)[None]


def solution(mesh):
    return jax.shard_map(
        local,
        mesh=mesh,
        in_specs=(P("fsdp", "seq", None), P("fsdp", None), P("fsdp", None), P(), P()),
        out_specs=P("fsdp", "seq", None),
        check_vma=False,
    )
```

profile of v0, /device:TPU:0, one launch (start us, length us, event | category | flops | bytes accessed | tf_op | source)
XLA Modules:
  0.0 196.7 jit_solution(5970017230775210502)
XLA Ops:
  6.5 0.7 all-gather.2.cloned.1.call-update
  7.3 57.1 %all-gather.2.cloned.1.call-done = bf16[1536,768]{1,0:T(8,128)(2,1)} async-done(((bf16[192,768]{1,0:T(8,128)(2,1)}), bf16[1536,768]{1,0:T(8,128)(2,1)}) %all-gather.2.cloned.1.call-update) | async-done | bytes 2359312 | tf_op jit(solution)/shard_map/all_gather | solution.py:55
  64.4 2.7 %convolution_convert_fusion.1 = bf16[384,768]{1,0:T(8,128)(2,1)S(1)} fusion(bf16[1536,768]{1,0:T(8,128)(2,1)} %all-gather.2.cloned.1.call-done, bf16[1,384,1536]{2,1,0:T(8,128)(2,1)S(1)} %copy-done), kind=kOutput, calls=%fused_computation.31 | convolution fusion | flops 906264576 | bytes 4128768 | tf_op jit(solution)/shard_map/dot_general | solution.py:56
  67.1 0.3 copy.11
  67.4 0.9 copy.12
  68.3 3.5 %all-to-all-start = ((bf16[384,3,4,64]{0,3,1,2:T(8,128)(2,1)}), bf16[384,3,4,64]{0,3,1,2:T(8,128)(2,1)S(1)}, u32[]{:S(2)}, u32[]{:S(2)}) async-start(bf16[384,3,4,64]{0,3,1,2:T(8,128)(2,1)} %copy.12), calls=%async_computation | async-start | bytes 1179648 | tf_op jit(solution)/shard_map/all_to_all | solution.py:58
  71.8 0.1 iota_compare_fusion.1
  71.9 9.4 %all-to-all-done = bf16[384,3,4,64]{0,3,1,2:T(8,128)(2,1)S(1)} async-done(((bf16[384,3,4,64]{0,3,1,2:T(8,128)(2,1)}), bf16[384,3,4,64]{0,3,1,2:T(8,128)(2,1)S(1)}, u32[]{:S(2)}, u32[]{:S(2)}) %all-to-all-start) | async-done | bytes 589856 | tf_op jit(solution)/shard_map/all_to_all | solution.py:58
  81.4 0.9 copy.17
  82.3 0.9 copy.18
  83.3 0.9 copy.19
  84.2 0.6 iota.18
  84.8 67.9 %while.11 = (s32[]{:T(128)}, bf16[4,384,64]{1,2,0:T(8,128)(2,1)}, s32[4]{0:T(128)}, pred[4,384]{1,0:T(4,128)(4,1)S(1)}, s32[4,4]{1,0:T(4,128)}, /*index=5*/bf16[...) while((s32[]{:T(128)}, bf16[4,384,64]{1,2,0:T(8,128)(2,1)}, ...), condition=%wide.region_5.6_spmd.clone, body=%wide.region_0.5_spmd.clone.sunk | while | flops 156378912 | bytes 8826411 | solution.py:45
  84.8 1.3 dynamic_slice.38
  87.9 0.7 bitcast_add_fusion.2
  88.6 0.8 sort.19
  89.4 0.6 gather_fusion.2
  90.0 1.3 fusion.47
  91.3 0.6 iota_compare_fusion.3
  92.0 0.1 broadcast_and_fusion.2
  92.1 2.3 %gather_fusion.1 = bf16[4,384,64]{2,1,0:T(8,128)(2,1)} fusion(bf16[4,384,64]{2,1,0:T(8,128)(2,1)} %get-tuple-element.193, s32[1024]{0:T(1024)S(1)} %pad_clamp_fusion.2), kind=kCustom, calls=%fused_computation.1.clone.1 | custom fusion | bytes 393232 | tf_op jit(solution)/shard_map/while/body/eval_jaxpr/gather | solution.py:25
  94.4 1.6 fusion.48
  96.0 1.1 fusion.49
  97.2 2.3 %gather_fusion = bf16[4,384,64]{2,1,0:T(8,128)(2,1)} fusion(bf16[4,384,64]{2,1,0:T(8,128)(2,1)} %get-tuple-element.194, s32[1024]{0:T(1024)S(1)} %pad_clamp_fusion.2), kind=kCustom, calls=%fused_computation.2.clone.1 | custom fusion | bytes 393232 | tf_op jit(solution)/shard_map/while/body/eval_jaxpr/gather | solution.py:26
  99.5 2.2 %fusion.50 = bf16[4,384,64]{1,2,0:T(8,128)(2,1)} fusion(bf16[4,384,64]{1,2,0:T(8,128)(2,1)} %get-tuple-element.177, s32[]{:T(128)} %get-tuple-element.176, bf16[1536,64]{1,0:T(8,128)(2,1)} %bitcast.56, f32[384,1536]{1,0:T(8,128)S(1)} %get-tuple-element.163, f32[384]{0:T(512)S(1)} %get-tuple-element.164, pred[1536]{0:T(1024)(128)(4,1)S(1)} %and.25, ...), kind=kOutput, calls=%fused_computation.16.clone.1 | convolution fusion | flops 77340672 | bytes 2807680 | tf_op jit(solution)/shard_map/while/body/eval_jaxpr/dot_general | solution.py:42
  101.7 1.3 dynamic_slice.38
  104.9 0.7 bitcast_add_fusion.2
  105.6 0.8 sort.19
  106.4 0.6 gather_fusion.2
  107.0 1.3 fusion.47
  108.3 0.6 iota_compare_fusion.3
  109.0 0.1 broadcast_and_fusion.2
  109.1 2.3 %gather_fusion.1 = bf16[4,384,64]{2,1,0:T(8,128)(2,1)} fusion(bf16[4,384,64]{2,1,0:T(8,128)(2,1)} %get-tuple-element.193, s32[1024]{0:T(1024)S(1)} %pad_clamp_fusion.2), kind=kCustom, calls=%fused_computation.1.clone.1 | custom fusion | bytes 393232 | tf_op jit(solution)/shard_map/while/body/eval_jaxpr/gather | solution.py:25
  111.4 1.6 fusion.48
  113.0 1.1 fusion.49
  114.1 2.3 %gather_fusion = bf16[4,384,64]{2,1,0:T(8,128)(2,1)} fusion(bf16[4,384,64]{2,1,0:T(8,128)(2,1)} %get-tuple-element.194, s32[1024]{0:T(1024)S(1)} %pad_clamp_fusion.2), kind=kCustom, calls=%fused_computation.2.clone.1 | custom fusion | bytes 393232 | tf_op jit(solution)/shard_map/while/body/eval_jaxpr/gather | solution.py:26
  116.5 2.2 %fusion.50 = bf16[4,384,64]{1,2,0:T(8,128)(2,1)} fusion(bf16[4,384,64]{1,2,0:T(8,128)(2,1)} %get-tuple-element.177, s32[]{:T(128)} %get-tuple-element.176, bf16[1536,64]{1,0:T(8,128)(2,1)} %bitcast.56, f32[384,1536]{1,0:T(8,128)S(1)} %get-tuple-element.163, f32[384]{0:T(512)S(1)} %get-tuple-element.164, pred[1536]{0:T(1024)(128)(4,1)S(1)} %and.25, ...), kind=kOutput, calls=%fused_computation.16.clone.1 | convolution fusion | flops 77340672 | bytes 2807680 | tf_op jit(solution)/shard_map/while/body/eval_jaxpr/dot_general | solution.py:42
  118.7 1.3 dynamic_slice.38
  121.9 0.7 bitcast_add_fusion.2
  122.6 0.8 sort.19
  123.4 0.6 gather_fusion.2
  124.0 1.3 fusion.47
  125.3 0.6 iota_compare_fusion.3
  126.0 0.1 broadcast_and_fusion.2
  126.1 2.3 %gather_fusion.1 = bf16[4,384,64]{2,1,0:T(8,128)(2,1)} fusion(bf16[4,384,64]{2,1,0:T(8,128)(2,1)} %get-tuple-element.193, s32[1024]{0:T(1024)S(1)} %pad_clamp_fusion.2), kind=kCustom, calls=%fused_computation.1.clone.1 | custom fusion | bytes 393232 | tf_op jit(solution)/shard_map/while/body/eval_jaxpr/gather | solution.py:25
  128.4 1.6 fusion.48
  130.0 1.1 fusion.49
  131.1 2.3 %gather_fusion = bf16[4,384,64]{2,1,0:T(8,128)(2,1)} fusion(bf16[4,384,64]{2,1,0:T(8,128)(2,1)} %get-tuple-element.194, s32[1024]{0:T(1024)S(1)} %pad_clamp_fusion.2), kind=kCustom, calls=%fused_computation.2.clone.1 | custom fusion | bytes 393232 | tf_op jit(solution)/shard_map/while/body/eval_jaxpr/gather | solution.py:26
  133.5 2.2 %fusion.50 = bf16[4,384,64]{1,2,0:T(8,128)(2,1)} fusion(bf16[4,384,64]{1,2,0:T(8,128)(2,1)} %get-tuple-element.177, s32[]{:T(128)} %get-tuple-element.176, bf16[1536,64]{1,0:T(8,128)(2,1)} %bitcast.56, f32[384,1536]{1,0:T(8,128)S(1)} %get-tuple-element.163, f32[384]{0:T(512)S(1)} %get-tuple-element.164, pred[1536]{0:T(1024)(128)(4,1)S(1)} %and.25, ...), kind=kOutput, calls=%fused_computation.16.clone.1 | convolution fusion | flops 77340672 | bytes 2807680 | tf_op jit(solution)/shard_map/while/body/eval_jaxpr/dot_general | solution.py:42
  135.7 1.3 dynamic_slice.38
  138.9 0.7 bitcast_add_fusion.2
  139.6 0.8 sort.19
  140.4 0.6 gather_fusion.2
  141.0 1.3 fusion.47
  142.3 0.6 iota_compare_fusion.3
  143.0 0.1 broadcast_and_fusion.2
  143.0 2.3 %gather_fusion.1 = bf16[4,384,64]{2,1,0:T(8,128)(2,1)} fusion(bf16[4,384,64]{2,1,0:T(8,128)(2,1)} %get-tuple-element.193, s32[1024]{0:T(1024)S(1)} %pad_clamp_fusion.2), kind=kCustom, calls=%fused_computation.1.clone.1 | custom fusion | bytes 393232 | tf_op jit(solution)/shard_map/while/body/eval_jaxpr/gather | solution.py:25
  145.4 1.6 fusion.48
  147.0 1.1 fusion.49
  148.1 2.3 %gather_fusion = bf16[4,384,64]{2,1,0:T(8,128)(2,1)} fusion(bf16[4,384,64]{2,1,0:T(8,128)(2,1)} %get-tuple-element.194, s32[1024]{0:T(1024)S(1)} %pad_clamp_fusion.2), kind=kCustom, calls=%fused_computation.2.clone.1 | custom fusion | bytes 393232 | tf_op jit(solution)/shard_map/while/body/eval_jaxpr/gather | solution.py:26
  150.5 2.2 %fusion.50 = bf16[4,384,64]{1,2,0:T(8,128)(2,1)} fusion(bf16[4,384,64]{1,2,0:T(8,128)(2,1)} %get-tuple-element.177, s32[]{:T(128)} %get-tuple-element.176, bf16[1536,64]{1,0:T(8,128)(2,1)} %bitcast.56, f32[384,1536]{1,0:T(8,128)S(1)} %get-tuple-element.163, f32[384]{0:T(512)S(1)} %get-tuple-element.164, pred[1536]{0:T(1024)(128)(4,1)S(1)} %and.25, ...), kind=kOutput, calls=%fused_computation.16.clone.1 | convolution fusion | flops 77340672 | bytes 2807680 | tf_op jit(solution)/shard_map/while/body/eval_jaxpr/dot_general | solution.py:42
  152.7 3.4 %all-to-all-start.1 = ((bf16[4,384,64]{1,2,0:T(8,128)(2,1)}), bf16[4,384,64]{1,2,0:T(8,128)(2,1)S(1)}, u32[]{:S(2)}, u32[]{:S(2)}) async-start(bf16[4,384,64]{1,2,0:T(8,128)(2,1)} %get-tuple-element.51), calls=%async_computation.1 | async-start | bytes 393216 | tf_op jit(solution)/shard_map/all_to_all | solution.py:67
  156.1 32.3 %all_gather.7 = bf16[256,1536]{1,0:T(8,128)(2,1)S(1)} all-gather(bf16[32,1536]{1,0:T(8,128)(2,1)} %param.9), channel_id=1, replica_groups=mesh['seq'=4,'fsdp'=8] {'fsdp'}, dimensions={0}, use_global_device_ids=true | all-gather | bytes 884736 | tf_op jit(solution)/shard_map/all_gather | solution.py:68
  188.3 1.5 fusion.28
  (29 shorter events, 0.4 us)
Async XLA Ops:
  6.5 57.8 %copy-start = (bf16[1,384,1536]{2,1,0:T(8,128)(2,1)S(1)}, bf16[1,384,1536]{2,1,0:T(8,128)(2,1)}, u32[]{:S(2)}) copy-start(bf16[1,384,1536]{2,1,0:T(8,128)(2,1)} %param.7) | copy-start | bytes 3538948
  6.5 57.8 %all-gather.2.cloned.1.call-start = ((), (), s32[]{:S(2)}) async-start(), calls=%async_computation.2 | async-start | bytes 2654208 | tf_op jit(solution)/shard_map/all_gather | solution.py:55
  67.1 4.7 %copy-start.1 = (s32[4]{0:T(128)S(1)}, s32[4]{0:T(128)}, u32[]{:S(2)}) copy-start(s32[4]{0:T(128)} %param.11) | copy-start | bytes 52
  68.3 13.0 %all-to-all-start = ((bf16[384,3,4,64]{0,3,1,2:T(8,128)(2,1)}), bf16[384,3,4,64]{0,3,1,2:T(8,128)(2,1)S(1)}, u32[]{:S(2)}, u32[]{:S(2)}) async-start(bf16[384,3,4,64]{0,3,1,2:T(8,128)(2,1)} %copy.12), calls=%async_computation | async-start | bytes 1179648 | tf_op jit(solution)/shard_map/all_to_all | solution.py:58
  152.7 35.6 %all-to-all-start.1 = ((bf16[4,384,64]{1,2,0:T(8,128)(2,1)}), bf16[4,384,64]{1,2,0:T(8,128)(2,1)S(1)}, u32[]{:S(2)}, u32[]{:S(2)}) async-start(bf16[4,384,64]{1,2,0:T(8,128)(2,1)} %get-tuple-element.51), calls=%async_computation.1 | async-start | bytes 393216 | tf_op jit(solution)/shard_map/all_to_all | solution.py:67
Sparse Core Ops, SparseCore 0:
  9.5 54.7 all-gather.1
where the time goes:
time: 198 us; the launch traced here: 197 us
  waiting for transfers between devices  67.2 us (34%)
  blocking collectives  32.3 us (16%)
  local copies, waits for them, and re-layouts  30.9 us (16%)
  matrix products  19.6 us (10%)
  other arithmetic  18.7 us (9%)
  between operations  13.5 us (7%)
  loops' own time  7.68 us (4%)
  starting transfers between devices  6.84 us (3%)
    all_gather x1, waiting for transfers between devices, local(): full_qkv = lax.all_gather(qkv_weight, 'fsdp', axis=0, tiled=True)  57.1 us
    all_gather x1, blocking collectives, local(): full_out = lax.all_gather(out_weight, 'fsdp', axis=0, tiled=True)  32.3 us
    all_to_all x1, waiting for transfers between devices, local(): lax.all_to_all(projected, 'seq', split_axis=2, concat_axis=0, tiled=True)  9.42 us
    gather x4, local copies, waits for them, and re-layouts, one_tile(): keys_sel = key_tiles_all[key_tiles].reshape(WINDOW * TILE, E)  9.34 us
    gather x4, local copies, waits for them, and re-layouts, one_tile(): values_sel = value_tiles_all[key_tiles].reshape(WINDOW * TILE, E)  9.34 us
    dot_general x4, matrix products, one_tile(): jnp.dot(softmax_top, values_sel, preferred_element_type=jnp.float32)  8.88 us
    another operation x1, loops' own time, attend(): return lax.map(one_tile, tile_numbers).reshape(tile_total * TILE, E)  7.68 us
    dot_general x4, matrix products, one_tile(): lax.dot_general(query_tiles[tile_index], keys_sel, (((1,), (1,)), ((), ()...  6.5 us
  transfers between devices with their start and end apart: 3, of which 2 were waited for; matrix products, arithmetic and copies ran while one was open for 0% of the time, Pallas kernels for 0%

commit v1 on v0

v1 whole, which is shorter than its diff:
```python
import jax
import jax.numpy as jnp
from jax import lax
from jax.experimental import pallas as pl
from jax.experimental.pallas import tpu as pltpu
from jax.sharding import PartitionSpec as P

E = 64
TILE = 384
LANES = 128
CORES = 2
NEG = -1e30

VMEM = pl.BlockSpec(memory_space=pltpu.VMEM)
SMEM = pl.BlockSpec(memory_space=pltpu.SMEM)


def grid_of(fsdp_count):
    x_count = 1
    while (2 * x_count) ** 2 <= fsdp_count and fsdp_count % (2 * x_count) == 0:
        x_count *= 2
    return fsdp_count // x_count, x_count


def z_rotation(z_count, x_count, step):
    return [(z * x_count + x, (z + step) % z_count * x_count + x) for z in range(z_count) for x in range(x_count)]


def x_rotation(z_count, x_count, step):
    return [(z * x_count + x, z * x_count + (x + step) % x_count) for z in range(z_count) for x in range(x_count)]


def core_swap(seq_count):
    return [(s, s ^ 1) for s in range(seq_count)]


def y_rotation(seq_count, step):
    return [(s, (s + CORES * step) % seq_count) for s in range(seq_count)]


def call(kernel, out_shape, in_specs, out_specs, scratch_shapes=(), name=None):
    return pl.pallas_call(
        kernel,
        out_shape=out_shape,
        in_specs=in_specs,
        out_specs=out_specs,
        scratch_shapes=scratch_shapes,
        name=name,
    )


def halves(qkv_weight, out_weight, core):
    rows, columns = qkv_weight.shape
    head_columns = columns // 3
    own_columns = head_columns // CORES
    out_rows, width = out_weight.shape
    own_width = width // CORES

    def kernel(core_ref, qkv_ref, out_ref, qkv_half_ref, out_half_ref):
        which = core_ref[0]
        for part in range(3):
            start = pl.multiple_of(part * head_columns + which * own_columns, LANES)
            qkv_half_ref[:, part * own_columns : (part + 1) * own_columns] = qkv_ref[:, pl.ds(start, own_columns)]
        out_half_ref[...] = out_ref[:, pl.ds(pl.multiple_of(which * own_width, LANES), own_width)]

    return call(
        kernel,
        (
            jax.ShapeDtypeStruct((rows, 3 * own_columns), qkv_weight.dtype),
            jax.ShapeDtypeStruct((out_rows, own_width), out_weight.dtype),
        ),
        [SMEM, VMEM, VMEM],
        (VMEM, VMEM),
        name="halves",
    )(core, qkv_weight, out_weight)


def project(positions, core, blocks, latents_own, latents_other):
    count = len(blocks)
    rows, columns = blocks[0].shape
    depth = count * rows
    own_columns = columns // 3
    row_count = latents_own.shape[0]
    dtype = latents_own.dtype

    def kernel(position_ref, core_ref, *refs):
        block_refs = refs[:count]
        own_ref, other_ref, queries_own_ref, queries_other_ref, key_value_ref, weight_ref = refs[count:]
        for block, block_ref in enumerate(block_refs):
            start = pl.multiple_of(position_ref[block] * rows, 16)
            weight_ref[pl.ds(start, rows), :] = block_ref[...]
        which = core_ref[0]
        weight = weight_ref[...]
        for latents_ref, queries_ref, place in ((own_ref, queries_own_ref, which), (other_ref, queries_other_ref, 1 - which)):
            projected = jnp.dot(latents_ref[...], weight, preferred_element_type=jnp.float32).astype(dtype)
            queries_ref[...] = projected[:, :own_columns]
            key_value_ref[pl.ds(pl.multiple_of(place * row_count, 16), row_count), :] = projected[:, own_columns:]

    return call(
        kernel,
        (
            jax.ShapeDtypeStruct((row_count, own_columns), dtype),
            jax.ShapeDtypeStruct((row_count, own_columns), dtype),
            jax.ShapeDtypeStruct((CORES * row_count, 2 * own_columns), dtype),
        ),
        [SMEM, SMEM] + [VMEM] * (count + 2),
        (VMEM, VMEM, VMEM),
        [pltpu.VMEM((depth, columns), dtype)],
        name="project",
    )(positions, core, *blocks, latents_own, latents_other)


def attend(place, tile_mask, tile_counts, queries_own, queries_other, key_values):
    chips = len(key_values)
    row_count, own_columns = queries_own.shape
    dtype = queries_own.dtype
    per_group = LANES // E
    scale = float(E) ** -0.5
    rows = row_count // 2

    def kernel(place_ref, mask_ref, count_ref, own_ref, other_ref, *refs):
        key_value_refs = refs[:chips]
        attended_own_ref, attended_other_ref = refs[chips:]
        chip = place_ref[0]
        which = place_ref[1]
        slot = lax.broadcasted_iota(jnp.int32, (1, row_count), 1)
        lane = lax.broadcasted_iota(jnp.int32, (1, LANES), 1)
        for queries_ref, attended_ref, member in ((own_ref, attended_own_ref, which), (other_ref, attended_other_ref, 1 - which)):
            tile = CORES * chip + member
            biases = []
            for step in range(chips):
                key_chip = lax.rem(chip + chips - step, chips)
                for key_member in range(CORES):
                    key_tile = CORES * key_chip + key_member
                    live = jnp.where(mask_ref[tile, key_tile] > 0, count_ref[key_tile], 0)
                    biases.append(jnp.where(slot < live, 0.0, NEG))
            bias = jnp.concatenate(biases, axis=1)
            for group in range(own_columns // LANES):
                columns = slice(group * LANES, (group + 1) * LANES)
                value_columns = slice(own_columns + group * LANES, own_columns + (group + 1) * LANES)
                keys = jnp.concatenate([ref[:, columns] for ref in key_value_refs], axis=0)
                values = jnp.concatenate([ref[:, value_columns] for ref in key_value_refs], axis=0)
                for start in range(0, row_count, rows):
                    queries = queries_ref[start : start + rows, columns] * jnp.asarray(scale, dtype)
                    position = start + lax.broadcasted_iota(jnp.int32, (rows, 1), 0)
                    attended = jnp.zeros((rows, LANES), jnp.float32)
                    for head in range(per_group):
                        inside = (lane >= head * E) & (lane < (head + 1) * E)
                        head_queries = jnp.where(inside, queries, jnp.zeros_like(queries))
                        scores = lax.dot_general(
                            head_queries, keys, (((1,), (1,)), ((), ())), preferred_element_type=jnp.float32
                        )
                        scores = scores + bias
                        numerators = jnp.exp(scores - jnp.max(scores, axis=1, keepdims=True))
                        denominator = jnp.sum(numerators, axis=1, keepdims=True)
                        summed = jnp.dot(numerators.astype(dtype), values, preferred_element_type=jnp.float32)
                        factor = jnp.where(position < count_ref[tile], 1.0 / denominator, 0.0)
                        attended = jnp.where(inside, summed * factor, attended)
                    attended_ref[start : start + rows, columns] = attended.astype(dtype)

    shape = jax.ShapeDtypeStruct((row_count, own_columns), dtype)
    return call(
        kernel,
        (shape, shape),
        [SMEM, SMEM, SMEM] + [VMEM] * (2 + chips),
        (VMEM, VMEM),
        name="attend",
    )(place, tile_mask, tile_counts, queries_own, queries_other, *key_values)


def stack_rows(positions, blocks):
    count = len(blocks)
    rows, columns = blocks[0].shape

    def kernel(position_ref, *refs):
        stacked_ref = refs[count]
        for block in range(count):
            start = pl.multiple_of(position_ref[block] * rows, 16)
            stacked_ref[pl.ds(start, rows), :] = refs[block][...]

    return call(
        kernel,
        jax.ShapeDtypeStruct((count * rows, columns), blocks[0].dtype),
        [SMEM] + [VMEM] * count,
        VMEM,
        name="stack_rows",
    )(positions, *blocks)


def project_out(core, attended_own, attended_partner, out_own, out_partner):
    row_count, own_columns = attended_own.shape
    width = out_own.shape[1]
    dtype = attended_own.dtype

    def kernel(core_ref, own_ref, partner_ref, out_own_ref, out_partner_ref, result_ref):
        which = core_ref[0]
        own_rows = pl.ds(pl.multiple_of(which * own_columns, 16), own_columns)
        partner_rows = pl.ds(pl.multiple_of((1 - which) * own_columns, 16), own_columns)
        for weight_ref, side in ((out_own_ref, which), (out_partner_ref, 1 - which)):
            total = jnp.dot(own_ref[...], weight_ref[own_rows, :], preferred_element_type=jnp.float32)
            total += jnp.dot(partner_ref[...], weight_ref[partner_rows, :], preferred_element_type=jnp.float32)
            result_ref[:, pl.ds(pl.multiple_of(side * width, LANES), width)] = total.astype(dtype)

    return call(
        kernel,
        jax.ShapeDtypeStruct((row_count, CORES * width), dtype),
        [SMEM] + [VMEM] * 4,
        VMEM,
        name="project_out",
    )(core, attended_own, attended_partner, out_own, out_partner)


def local(latents, qkv_weight, out_weight, tile_mask, tile_counts):
    seq_count = lax.axis_size("seq")
    fsdp_count = lax.axis_size("fsdp")
    z_count, x_count = grid_of(fsdp_count)
    chips = seq_count // CORES
    seq_index = lax.axis_index("seq")
    fsdp_index = lax.axis_index("fsdp")
    chip = seq_index // CORES
    core = (seq_index % CORES)[None]
    z_index = fsdp_index // x_count
    x_index = fsdp_index % x_count
    latents_own = latents[0]

    qkv_half, out_half = halves(qkv_weight, out_weight, core)
    latents_other = lax.ppermute(latents_own, "seq", core_swap(seq_count))

    shifts = [(0, 0)]
    blocks = [qkv_half]
    for x_step in range(1, x_count):
        shifts.append((0, x_step))
        blocks.append(lax.ppermute(qkv_half, "fsdp", x_rotation(z_count, x_count, x_step)))
    for z_step in range(1, z_count):
        came = lax.ppermute(qkv_half, "fsdp", z_rotation(z_count, x_count, z_step))
        shifts.append((z_step, 0))
        blocks.append(came)
        for x_step in range(1, x_count):
            shifts.append((z_step, x_step))
            blocks.append(lax.ppermute(came, "fsdp", x_rotation(z_count, x_count, x_step)))
    positions = jnp.stack(
        [(z_index + z_count - dz) % z_count * x_count + (x_index + x_count - dx) % x_count for dz, dx in shifts]
    )
    queries_own, queries_other, key_value = project(positions, core, blocks, latents_own, latents_other)

    key_values = [key_value] + [
        lax.ppermute(key_value, "seq", y_rotation(seq_count, step)) for step in range(1, chips)
    ]
    out_half, _ = lax.optimization_barrier((out_half, key_value))
    layer = [out_half] + [
        lax.ppermute(out_half, "fsdp", x_rotation(z_count, x_count, step)) for step in range(1, x_count)
    ]
    out_positions = jnp.stack([(x_index + x_count - step) % x_count for step in range(x_count)])
    layer = stack_rows(out_positions, layer)
    layers = [layer] + [
        lax.ppermute(layer, "fsdp", z_rotation(z_count, x_count, step)) for step in range(1, z_count)
    ]
    layer_positions = jnp.stack([(z_index + z_count - step) % z_count for step in range(z_count)])
    out_own = stack_rows(layer_positions, layers)
    out_partner = lax.ppermute(out_own, "seq", core_swap(seq_count))

    place = jnp.stack([chip, seq_index % CORES])
    attended_own, attended_other = attend(place, tile_mask, tile_counts, queries_own, queries_other, key_values)
    attended_partner = lax.ppermute(attended_other, "seq", core_swap(seq_count))
    return project_out(core, attended_own, attended_partner, out_own, out_partner)[None]


def solution(mesh):
    return jax.shard_map(
        local,
        mesh=mesh,
        in_specs=(P("fsdp", "seq", None), P("fsdp", None), P("fsdp", None), P(), P()),
        out_specs=P("fsdp", "seq", None),
        check_vma=False,
    )
```

time: 198 us -> 66.1 us (0.33)
  waiting for transfers between devices: 67.2 us -> 22.9 us
  blocking collectives: 32.3 us -> 0 us
  local copies, waits for them, and re-layouts: 30.9 us -> 5.69 us
  matrix products: 19.6 us -> 0 us
  Pallas kernels: 0 us -> 18.8 us
  other arithmetic: 18.7 us -> 1.78 us
  between operations: 13.5 us -> 0.09 us
  starting transfers between devices: 6.84 us -> 16.6 us
  loops' own time: 7.68 us -> 0 us
    all_gather x1 -> x0, waiting for transfers between devices: 57.1 us -> none  [local(): full_qkv = lax.all_gather(qkv_weight, 'fsdp', axis=0, tiled=True)]
    all_gather x1 -> x0, blocking collectives: 32.3 us -> none  [local(): full_out = lax.all_gather(out_weight, 'fsdp', axis=0, tiled=True)]
    ppermute x0 -> x15, waiting for transfers between devices: none -> 22.9 us  [the longest x3 9.41 us: local(): came = lax.ppermute(qkv_half, 'fsdp', z_rotation(z_count, x_count, z_step))]
    gather x12 -> x0, local copies, waits for them, and re-layouts: 21 us -> none  [the longest x4 9.34 us: one_tile(): keys_sel = key_tiles_all[key_tiles].reshape(WINDOW * TILE, E)]
    dot_general x10 -> x0, matrix products: 19.6 us -> none  [the longest x4 8.88 us: one_tile(): jnp.dot(softmax_top, values_sel, preferred_element_type=jnp.float32)]
    pallas_call x0 -> x6, Pallas kernels: none -> 18.8 us  [the longest x1 6.35 us: attend(): call(kernel, (shape, shape), [SMEM, SMEM, SMEM] + [VMEM] * (2 + chips), (...]
    ppermute x0 -> x15, starting transfers between devices: none -> 16.6 us  [the longest x3 5.61 us: local(): came = lax.ppermute(qkv_half, 'fsdp', z_rotation(z_count, x_count, z_step))]
    reduce_sum x8 -> x0, other arithmetic: 9.84 us -> none  [the longest x4 5.4 us: one_tile(): slot_live = jnp.arange(WINDOW, dtype=jnp.int32) < jnp.sum(mask_row)]
  transfers between devices with their start and end apart: 3 -> 15, of which waited for: 2 -> 8; matrix products, arithmetic and copies ran while one was open for 0% -> 4% of each run, Pallas kernels for 0% -> 17%
where the time goes in v1:
time: 66.1 us; the launch traced here: 65.8 us
  waiting for transfers between devices  22.9 us (35%)
  Pallas kernels  18.8 us (28%)
  starting transfers between devices  16.6 us (25%)
  local copies, waits for them, and re-layouts  5.69 us (9%)
  other arithmetic  1.78 us (3%)
    ppermute x3, waiting for transfers between devices, local(): came = lax.ppermute(qkv_half, 'fsdp', z_rotation(z_count, x_count, z_step))  9.41 us
    pallas_call x1, Pallas kernels, attend(): call(kernel, (shape, shape), [SMEM, SMEM, SMEM] + [VMEM] * (2 + chips), (...  6.35 us
    ppermute x3, waiting for transfers between devices, local(): lax.ppermute(layer, 'fsdp', z_rotation(z_count, x_count, step))  6.1 us
    ppermute x3, waiting for transfers between devices, local(): lax.ppermute(came, 'fsdp', x_rotation(z_count, x_count, x_step))  5.69 us
    ppermute x3, starting transfers between devices, local(): came = lax.ppermute(qkv_half, 'fsdp', z_rotation(z_count, x_count, z_step))  5.61 us
    unnamed x32, local copies, waits for them, and re-layouts  5.03 us
    pallas_call x1, Pallas kernels, project(): call(kernel, (jax.ShapeDtypeStruct((row_count, own_columns), dtype), jax....  4.41 us
    ppermute x3, starting transfers between devices, local(): lax.ppermute(came, 'fsdp', x_rotation(z_count, x_count, x_step))  3.52 us
  transfers between devices with their start and end apart: 15, of which 8 were waited for; matrix products, arithmetic and copies ran while one was open for 4% of the time, Pallas kernels for 17%

profile of v1, /device:TPU:0, one launch (start us, length us, event | category | flops | bytes accessed | tf_op | source)
XLA Modules:
  0.0 65.8 jit_solution(4611855716804422527)
XLA Ops:
  0.0 0.5 collective-permute-start.7
  0.5 1.7 %halves.1 = (bf16[192,384]{1,0:T(8,128)(2,1)}, bf16[32,768]{1,0:T(8,128)(2,1)}) custom-call(s32[1]{0:T(128)} %bitcast.core_ref, bf16[192,768]{1,0:T(8,128)(2,1)} %qkv_ref.1, bf16[32,1536]{1,0:T(8,128)(2,1)} %out_ref.1), custom_call_target="tpu_custom_call" | custom-call | tf_op jit(solution)/shard_map/halves/pallas_call | solution.py:66
  2.2 4.6 %collective-permute-start.5 = (bf16[192,384]{1,0:T(8,128)(2,1)}, bf16[192,384]{1,0:T(8,128)(2,1)S(1)}, u32[]{:S(2)}, u32[]{:S(2)}) collective-permute-start(bf16[192,384]{1,0:T(8,128)(2,1)} %get-tuple-element.13.refs_0_), channel_id=1, source_target_pairs={{0,6},{1,7},{2,0},{3,1},{4,2},{5,3},{6,4},{7,5},{8,14},{9,15},{10,... | collective-permute-start | bytes 442376 | tf_op jit(solution)/shard_map/ppermute | solution.py:235
  6.8 0.0 collective-permute-start.3
  6.8 1.0 %collective-permute-start.1 = (bf16[192,384]{1,0:T(8,128)(2,1)}, bf16[192,384]{1,0:T(8,128)(2,1)S(1)}, u32[]{:S(2)}, u32[]{:S(2)}) collective-permute-start(bf16[192,384]{1,0:T(8,128)(2,1)} %get-tuple-element.13.refs_0_), channel_id=1, source_target_pairs={{0,2},{1,3},{2,4},{3,5},{4,6},{5,7},{6,0},{7,1},{8,10},{9,11},{10,... | collective-permute-start | bytes 442376 | tf_op jit(solution)/shard_map/ppermute | solution.py:235
  7.8 1.5 %collective-permute-start = (bf16[192,384]{1,0:T(8,128)(2,1)}, bf16[192,384]{1,0:T(8,128)(2,1)S(1)}, u32[]{:S(2)}, u32[]{:S(2)}) collective-permute-start(bf16[192,384]{1,0:T(8,128)(2,1)} %get-tuple-element.13.refs_0_), channel_id=1, source_target_pairs={{0,1},{1,0},{2,3},{3,2},{4,5},{5,4},{6,7},{7,6},{8,9},{9,8},{10,11... | collective-permute-start | bytes 442376 | tf_op jit(solution)/shard_map/ppermute | solution.py:233
  9.3 2.1 %collective-permute-done.5.refs_6_ = bf16[192,384]{1,0:T(8,128)(2,1)S(1)} collective-permute-done((bf16[192,384]{1,0:T(8,128)(2,1)}, bf16[192,384]{1,0:T(8,128)(2,1)S(1)}, u32[]{:S(2)}, u32[]{:S(2)}) %collective-permute-start.5) | collective-permute-done | bytes 147488 | tf_op jit(solution)/shard_map/ppermute | solution.py:235
  11.3 0.0 copy-start.3
  11.3 1.5 %collective-permute-start.6 = (bf16[192,384]{1,0:T(8,128)(2,1)S(1)}, bf16[192,384]{1,0:T(8,128)(2,1)S(1)}, u32[]{:S(2)}, u32[]{:S(2)}) collective-permute-start(bf16[192,384]{1,0:T(8,128)(2,1)S(1)} %collective-permute-done.5.refs_6_), channel_id=1, source_target_pairs={{0,1},{1,0},{2,3},{3,2},{4,5},{5,4},{6,7},{7,6},{8,9},{9,8},{10,11... | collective-permute-start | bytes 442376 | tf_op jit(solution)/shard_map/ppermute | solution.py:240
  12.8 7.3 %collective-permute-done.3.refs_4_ = bf16[192,384]{1,0:T(8,128)(2,1)S(1)} collective-permute-done((bf16[192,384]{1,0:T(8,128)(2,1)}, bf16[192,384]{1,0:T(8,128)(2,1)S(1)}, u32[]{:S(2)}, u32[]{:S(2)}) %collective-permute-start.3) | collective-permute-done | bytes 147488 | tf_op jit(solution)/shard_map/ppermute | solution.py:235
  20.2 0.0 copy-start.4
  20.2 1.5 %collective-permute-start.4 = (bf16[192,384]{1,0:T(8,128)(2,1)S(1)}, bf16[192,384]{1,0:T(8,128)(2,1)S(1)}, u32[]{:S(2)}, u32[]{:S(2)}) collective-permute-start(bf16[192,384]{1,0:T(8,128)(2,1)S(1)} %collective-permute-done.3.refs_4_), channel_id=1, source_target_pairs={{0,1},{1,0},{2,3},{3,2},{4,5},{5,4},{6,7},{7,6},{8,9},{9,8},{10,11... | collective-permute-start | bytes 442376 | tf_op jit(solution)/shard_map/ppermute | solution.py:240
  21.7 0.0 collective-permute-done.1.refs_2_
  21.7 0.0 copy-start.5
  21.7 0.5 collective-permute-start.2
  22.2 0.7 stack.68.position_ref
  22.9 0.0 copy-start.14
  22.9 0.0 collective-permute-done.refs_1_
  22.9 0.0 copy-start.6
  22.9 0.0 collective-permute-done.6.refs_7_
  22.9 0.0 copy-start.7
  22.9 4.1 %collective-permute-done.4.refs_5_ = bf16[192,384]{1,0:T(8,128)(2,1)S(1)} collective-permute-done((bf16[192,384]{1,0:T(8,128)(2,1)S(1)}, bf16[192,384]{1,0:T(8,128)(2,1)S(1)}, u32[]{:S(2)}, u32[]{:S(2)}) %collective-permute-start.4) | collective-permute-done | bytes 147488 | tf_op jit(solution)/shard_map/ppermute | solution.py:240
  27.0 0.0 copy-start.8
  27.0 1.6 %collective-permute-done.2.refs_3_ = bf16[192,384]{1,0:T(8,128)(2,1)S(1)} collective-permute-done((bf16[192,384]{1,0:T(8,128)(2,1)S(1)}, bf16[192,384]{1,0:T(8,128)(2,1)S(1)}, u32[]{:S(2)}, u32[]{:S(2)}) %collective-permute-start.2) | collective-permute-done | bytes 147488 | tf_op jit(solution)/shard_map/ppermute | solution.py:240
  28.6 0.0 copy-start.9
  28.6 0.0 collective-permute-done.7.refs_9_
  28.6 0.0 copy-done.3
  28.6 0.0 copy-done.4
  28.6 0.0 copy-done.5
  28.6 0.0 copy-done.6
  28.6 0.0 copy-done.7
  28.6 0.0 copy-done.8
  28.6 0.6 copy-done.9
  29.2 1.0 %copy-done = bf16[384,1536]{1,0:T(8,128)(2,1)} copy-done((bf16[384,1536]{1,0:T(8,128)(2,1)}, bf16[384,1536]{1,0:T(8,128)(2,1)S(1)}, u32[]{:S(2)}) %copy-start) | copy-done | bytes 1179672
  30.2 4.4 %project.1 = (bf16[384,128]{1,0:T(8,128)(2,1)}, bf16[384,128]{1,0:T(8,128)(2,1)}, bf16[768,256]{1,0:T(8,128)(2,1)}) custom-call(s32[8]{0:T(128)} %stack.68.position_ref, s32[1]{0:T(128)} %bitcast.core_ref, bf16[192,384]{1,0:T(8,128)(2,1)} %get-tuple-element.13.refs_0_, bf16[192,384]{1,0:T(8,128)(2,1)} %copy-done.6, bf16[192,384]{1,0:T(8,128)(2,1)} %copy-done.5, ...), custom_call_target="tpu_custom_call" | custom-call | tf_op jit(solution)/shard_map/project/pallas_call | solution.py:99
  34.6 0.0 copy-done.14
  34.7 1.5 %collective-permute-start.10 = (bf16[32,768]{1,0:T(8,128)(2,1)S(1)}, bf16[32,768]{1,0:T(8,128)(2,1)S(1)}, u32[]{:S(2)}, u32[]{:S(2)}) collective-permute-start(bf16[32,768]{1,0:T(8,128)(2,1)S(1)} %copy-done.14), channel_id=1, source_target_pairs={{0,1},{1,0},{2,3},{3,2},{4,5},{5,4},{6,7},{7,6},{8,9},{9,8},{10,11... | collective-permute-start | bytes 147464 | tf_op jit(solution)/shard_map/ppermute | solution.py:251
  36.1 0.6 pad_add_fusion.2.position_ref
  36.7 1.5 %collective-permute-start.8 = (bf16[768,256]{1,0:T(8,128)(2,1)}, bf16[768,256]{1,0:T(8,128)(2,1)S(1)}, u32[]{:S(2)}, u32[]{:S(2)}) collective-permute-start(bf16[768,256]{1,0:T(8,128)(2,1)} %get-tuple-element.16.refs_0_), channel_id=1, source_target_pairs={{0,16},{8,24},{16,0},{24,8},{1,17},{9,25},{17,1},{25,9},{2,18},{10... | collective-permute-start | bytes 1179656 | tf_op jit(solution)/shard_map/ppermute | solution.py:247
  38.2 0.5 collective-permute-done.10.refs_1_
  38.7 0.6 copy-done.15
  39.4 1.5 %stack_rows.2.refs_0_ = bf16[64,768]{1,0:T(8,128)(2,1)} custom-call(s32[2]{0:T(128)} %pad_add_fusion.2.position_ref, bf16[32,768]{1,0:T(8,128)(2,1)} %get-tuple-element.20.refs_0_, bf16[32,768]{1,0:T(8,128)(2,1)} %copy-done.15), custom_call_target="tpu_custom_call" | custom-call | tf_op jit(solution)/shard_map/stack_rows/pallas_call | solution.py:181
  40.8 0.4 collective-permute-start.13
  41.3 0.0 collective-permute-start.12
  41.3 1.6 %collective-permute-start.11 = (bf16[64,768]{1,0:T(8,128)(2,1)}, bf16[64,768]{1,0:T(8,128)(2,1)S(1)}, u32[]{:S(2)}, u32[]{:S(2)}) collective-permute-start(bf16[64,768]{1,0:T(8,128)(2,1)} %stack_rows.2.refs_0_), channel_id=1, source_target_pairs={{0,2},{1,3},{2,4},{3,5},{4,6},{5,7},{6,0},{7,1},{8,10},{9,11},{10,... | collective-permute-start | bytes 294920 | tf_op jit(solution)/shard_map/ppermute | solution.py:256
  42.9 0.6 pad_add_fusion.1.position_ref
  43.5 4.0 %collective-permute-done.13.refs_3_ = bf16[64,768]{1,0:T(8,128)(2,1)S(1)} collective-permute-done((bf16[64,768]{1,0:T(8,128)(2,1)}, bf16[64,768]{1,0:T(8,128)(2,1)S(1)}, u32[]{:S(2)}, u32[]{:S(2)}) %collective-permute-start.13) | collective-permute-done | bytes 98336 | tf_op jit(solution)/shard_map/ppermute | solution.py:256
  47.4 2.1 %collective-permute-done.12.refs_2_ = bf16[64,768]{1,0:T(8,128)(2,1)S(1)} collective-permute-done((bf16[64,768]{1,0:T(8,128)(2,1)}, bf16[64,768]{1,0:T(8,128)(2,1)S(1)}, u32[]{:S(2)}, u32[]{:S(2)}) %collective-permute-start.12) | collective-permute-done | bytes 98336 | tf_op jit(solution)/shard_map/ppermute | solution.py:256
  49.6 0.0 collective-permute-done.11.refs_1_
  49.6 0.0 copy-done.11
  49.6 0.6 copy-done.12
  50.2 0.6 copy-done.13
  50.9 1.8 %stack_rows.3.out_own_ref = bf16[256,768]{1,0:T(8,128)(2,1)} custom-call(s32[4]{0:T(128)} %pad_add_fusion.1.position_ref, bf16[64,768]{1,0:T(8,128)(2,1)} %stack_rows.2.refs_0_, bf16[64,768]{1,0:T(8,128)(2,1)} %copy-done.13, bf16[64,768]{1,0:T(8,128)(2,1)} %copy-done.12, bf16[64,768]{1,0:T(8,128)(2,1)} %copy-done.11), custom_call_target="tpu_custom_call" | custom-call | tf_op jit(solution)/shard_map/stack_rows/pallas_call | solution.py:181
  52.7 0.0 collective-permute-start.14
  52.7 0.6 pad_add_fusion.place_ref
  53.3 0.0 collective-permute-done.8.refs_1_
  53.3 0.7 %copy-done.2 = bf16[768,256]{1,0:T(8,128)(2,1)} copy-done((bf16[768,256]{1,0:T(8,128)(2,1)}, bf16[768,256]{1,0:T(8,128)(2,1)S(1)}, u32[]{:S(2)}) %copy-start.2) | copy-done | bytes 393240
  54.1 6.3 %attend.1 = (bf16[384,128]{1,0:T(8,128)(2,1)}, bf16[384,128]{1,0:T(8,128)(2,1)}) custom-call(s32[2]{0:T(128)} %pad_add_fusion.place_ref, s32[4,4]{1,0:T(4,128)} %mask_ref.1, s32[4]{0:T(128)} %count_ref.1, bf16[384,128]{1,0:T(8,128)(2,1)} %get-tuple-element.14.own_ref, bf16[384,128]{1,0:T(8,128)(2,1)} %get-tuple-element.15.other_ref, ...), custom_call_target="tpu_custom_call" | custom-call | tf_op jit(solution)/shard_map/attend/pallas_call | solution.py:162
  60.4 0.5 collective-permute-start.9
  60.9 1.2 %collective-permute-done.9.partner_ref = bf16[384,128]{1,0:T(8,128)(2,1)S(1)} collective-permute-done((bf16[384,128]{1,0:T(8,128)(2,1)}, bf16[384,128]{1,0:T(8,128)(2,1)S(1)}, u32[]{:S(2)}, u32[]{:S(2)}) %collective-permute-start.9) | collective-permute-done | bytes 98336 | tf_op jit(solution)/shard_map/ppermute | solution.py:264
  62.1 0.0 collective-permute-done.14.out_partner_ref
  62.1 0.6 copy-done.10
  62.7 0.1 copy-done.1
  62.8 3.0 %project_out.1 = bf16[384,1536]{1,0:T(8,128)(2,1)} custom-call(s32[1]{0:T(128)} %bitcast.core_ref, bf16[384,128]{1,0:T(8,128)(2,1)} %get-tuple-element.17.own_ref, bf16[384,128]{1,0:T(8,128)(2,1)} %copy-done.10, bf16[256,768]{1,0:T(8,128)(2,1)} %stack_rows.3.out_own_ref, bf16[256,768]{1,0:T(8,128)(2,1)} %copy-done.1), custom_call_target="tpu_custom_call" | custom-call | tf_op jit(solution)/shard_map/project_out/pallas_call | solution.py:204
  (8 shorter events, 0.0 us)
Async XLA Ops:
  0.0 28.6 %collective-permute-start.7 = (bf16[384,1536]{1,0:T(8,128)(2,1)}, bf16[384,1536]{1,0:T(8,128)(2,1)S(1)}, u32[]{:S(2)}, u32[]{:S(2)}) collective-permute-start(bf16[384,1536]{1,0:T(8,128)(2,1)} %bitcast.18), channel_id=1, source_target_pairs={{0,8},{8,0},{16,24},{24,16},{1,9},{9,1},{17,25},{25,17},{2,10},{10... | collective-permute-start | bytes 3538952 | tf_op jit(solution)/shard_map/ppermute | solution.py:227
  2.2 9.2 %collective-permute-start.5 = (bf16[192,384]{1,0:T(8,128)(2,1)}, bf16[192,384]{1,0:T(8,128)(2,1)S(1)}, u32[]{:S(2)}, u32[]{:S(2)}) collective-permute-start(bf16[192,384]{1,0:T(8,128)(2,1)} %get-tuple-element.13.refs_0_), channel_id=1, source_target_pairs={{0,6},{1,7},{2,0},{3,1},{4,2},{5,3},{6,4},{7,5},{8,14},{9,15},{10,... | collective-permute-start | bytes 442376 | tf_op jit(solution)/shard_map/ppermute | solution.py:235
  6.8 13.4 %collective-permute-start.3 = (bf16[192,384]{1,0:T(8,128)(2,1)}, bf16[192,384]{1,0:T(8,128)(2,1)S(1)}, u32[]{:S(2)}, u32[]{:S(2)}) collective-permute-start(bf16[192,384]{1,0:T(8,128)(2,1)} %get-tuple-element.13.refs_0_), channel_id=1, source_target_pairs={{0,4},{1,5},{2,6},{3,7},{4,0},{5,1},{6,2},{7,3},{8,12},{9,13},{10,... | collective-permute-start | bytes 442376 | tf_op jit(solution)/shard_map/ppermute | solution.py:235
  6.8 14.9 %collective-permute-start.1 = (bf16[192,384]{1,0:T(8,128)(2,1)}, bf16[192,384]{1,0:T(8,128)(2,1)S(1)}, u32[]{:S(2)}, u32[]{:S(2)}) collective-permute-start(bf16[192,384]{1,0:T(8,128)(2,1)} %get-tuple-element.13.refs_0_), channel_id=1, source_target_pairs={{0,2},{1,3},{2,4},{3,5},{4,6},{5,7},{6,0},{7,1},{8,10},{9,11},{10,... | collective-permute-start | bytes 442376 | tf_op jit(solution)/shard_map/ppermute | solution.py:235
  7.8 15.1 %collective-permute-start = (bf16[192,384]{1,0:T(8,128)(2,1)}, bf16[192,384]{1,0:T(8,128)(2,1)S(1)}, u32[]{:S(2)}, u32[]{:S(2)}) collective-permute-start(bf16[192,384]{1,0:T(8,128)(2,1)} %get-tuple-element.13.refs_0_), channel_id=1, source_target_pairs={{0,1},{1,0},{2,3},{3,2},{4,5},{5,4},{6,7},{7,6},{8,9},{9,8},{10,11... | collective-permute-start | bytes 442376 | tf_op jit(solution)/shard_map/ppermute | solution.py:233
  11.3 17.3 %copy-start.3 = (bf16[192,384]{1,0:T(8,128)(2,1)}, bf16[192,384]{1,0:T(8,128)(2,1)S(1)}, u32[]{:S(2)}) copy-start(bf16[192,384]{1,0:T(8,128)(2,1)S(1)} %collective-permute-done.5.refs_6_) | copy-start | bytes 442372
  11.3 11.5 %collective-permute-start.6 = (bf16[192,384]{1,0:T(8,128)(2,1)S(1)}, bf16[192,384]{1,0:T(8,128)(2,1)S(1)}, u32[]{:S(2)}, u32[]{:S(2)}) collective-permute-start(bf16[192,384]{1,0:T(8,128)(2,1)S(1)} %collective-permute-done.5.refs_6_), channel_id=1, source_target_pairs={{0,1},{1,0},{2,3},{3,2},{4,5},{5,4},{6,7},{7,6},{8,9},{9,8},{10,11... | collective-permute-start | bytes 442376 | tf_op jit(solution)/shard_map/ppermute | solution.py:240
  20.2 8.4 %copy-start.4 = (bf16[192,384]{1,0:T(8,128)(2,1)}, bf16[192,384]{1,0:T(8,128)(2,1)S(1)}, u32[]{:S(2)}) copy-start(bf16[192,384]{1,0:T(8,128)(2,1)S(1)} %collective-permute-done.3.refs_4_) | copy-start | bytes 442372
  20.2 6.8 %collective-permute-start.4 = (bf16[192,384]{1,0:T(8,128)(2,1)S(1)}, bf16[192,384]{1,0:T(8,128)(2,1)S(1)}, u32[]{:S(2)}, u32[]{:S(2)}) collective-permute-start(bf16[192,384]{1,0:T(8,128)(2,1)S(1)} %collective-permute-done.3.refs_4_), channel_id=1, source_target_pairs={{0,1},{1,0},{2,3},{3,2},{4,5},{5,4},{6,7},{7,6},{8,9},{9,8},{10,11... | collective-permute-start | bytes 442376 | tf_op jit(solution)/shard_map/ppermute | solution.py:240
  21.7 6.9 %copy-start.5 = (bf16[192,384]{1,0:T(8,128)(2,1)}, bf16[192,384]{1,0:T(8,128)(2,1)S(1)}, u32[]{:S(2)}) copy-start(bf16[192,384]{1,0:T(8,128)(2,1)S(1)} %collective-permute-done.1.refs_2_) | copy-start | bytes 442372
  21.7 6.9 %collective-permute-start.2 = (bf16[192,384]{1,0:T(8,128)(2,1)S(1)}, bf16[192,384]{1,0:T(8,128)(2,1)S(1)}, u32[]{:S(2)}, u32[]{:S(2)}) collective-permute-start(bf16[192,384]{1,0:T(8,128)(2,1)S(1)} %collective-permute-done.1.refs_2_), channel_id=1, source_target_pairs={{0,1},{1,0},{2,3},{3,2},{4,5},{5,4},{6,7},{7,6},{8,9},{9,8},{10,11... | collective-permute-start | bytes 442376 | tf_op jit(solution)/shard_map/ppermute | solution.py:240
  22.9 11.8 %copy-start.14 = (bf16[32,768]{1,0:T(8,128)(2,1)S(1)}, bf16[32,768]{1,0:T(8,128)(2,1)}, u32[]{:S(2)}) copy-start(bf16[32,768]{1,0:T(8,128)(2,1)} %get-tuple-element.20.refs_0_) | copy-start | bytes 147460
  22.9 5.7 %copy-start.6 = (bf16[192,384]{1,0:T(8,128)(2,1)}, bf16[192,384]{1,0:T(8,128)(2,1)S(1)}, u32[]{:S(2)}) copy-start(bf16[192,384]{1,0:T(8,128)(2,1)S(1)} %collective-permute-done.refs_1_) | copy-start | bytes 442372
  22.9 5.7 %copy-start.7 = (bf16[192,384]{1,0:T(8,128)(2,1)}, bf16[192,384]{1,0:T(8,128)(2,1)S(1)}, u32[]{:S(2)}) copy-start(bf16[192,384]{1,0:T(8,128)(2,1)S(1)} %collective-permute-done.6.refs_7_) | copy-start | bytes 442372
  27.0 1.7 %copy-start.8 = (bf16[192,384]{1,0:T(8,128)(2,1)}, bf16[192,384]{1,0:T(8,128)(2,1)S(1)}, u32[]{:S(2)}) copy-start(bf16[192,384]{1,0:T(8,128)(2,1)S(1)} %collective-permute-done.4.refs_5_) | copy-start | bytes 442372
  28.6 0.7 copy-start.9
  29.2 1.0 %copy-start = (bf16[384,1536]{1,0:T(8,128)(2,1)}, bf16[384,1536]{1,0:T(8,128)(2,1)S(1)}, u32[]{:S(2)}) copy-start(bf16[384,1536]{1,0:T(8,128)(2,1)S(1)} %collective-permute-done.7.refs_9_) | copy-start | bytes 3538948
  34.7 4.1 %collective-permute-start.10 = (bf16[32,768]{1,0:T(8,128)(2,1)S(1)}, bf16[32,768]{1,0:T(8,128)(2,1)S(1)}, u32[]{:S(2)}, u32[]{:S(2)}) collective-permute-start(bf16[32,768]{1,0:T(8,128)(2,1)S(1)} %copy-done.14), channel_id=1, source_target_pairs={{0,1},{1,0},{2,3},{3,2},{4,5},{5,4},{6,7},{7,6},{8,9},{9,8},{10,11... | collective-permute-start | bytes 147464 | tf_op jit(solution)/shard_map/ppermute | solution.py:251
  36.7 16.6 %collective-permute-start.8 = (bf16[768,256]{1,0:T(8,128)(2,1)}, bf16[768,256]{1,0:T(8,128)(2,1)S(1)}, u32[]{:S(2)}, u32[]{:S(2)}) collective-permute-start(bf16[768,256]{1,0:T(8,128)(2,1)} %get-tuple-element.16.refs_0_), channel_id=1, source_target_pairs={{0,16},{8,24},{16,0},{24,8},{1,17},{9,25},{17,1},{25,9},{2,18},{10... | collective-permute-start | bytes 1179656 | tf_op jit(solution)/shard_map/ppermute | solution.py:247
  38.7 0.6 copy-start.15
  40.8 6.6 %collective-permute-start.13 = (bf16[64,768]{1,0:T(8,128)(2,1)}, bf16[64,768]{1,0:T(8,128)(2,1)S(1)}, u32[]{:S(2)}, u32[]{:S(2)}) collective-permute-start(bf16[64,768]{1,0:T(8,128)(2,1)} %stack_rows.2.refs_0_), channel_id=1, source_target_pairs={{0,6},{1,7},{2,0},{3,1},{4,2},{5,3},{6,4},{7,5},{8,14},{9,15},{10,... | collective-permute-start | bytes 294920 | tf_op jit(solution)/shard_map/ppermute | solution.py:256
  41.3 8.3 %collective-permute-start.12 = (bf16[64,768]{1,0:T(8,128)(2,1)}, bf16[64,768]{1,0:T(8,128)(2,1)S(1)}, u32[]{:S(2)}, u32[]{:S(2)}) collective-permute-start(bf16[64,768]{1,0:T(8,128)(2,1)} %stack_rows.2.refs_0_), channel_id=1, source_target_pairs={{0,4},{1,5},{2,6},{3,7},{4,0},{5,1},{6,2},{7,3},{8,12},{9,13},{10,... | collective-permute-start | bytes 294920 | tf_op jit(solution)/shard_map/ppermute | solution.py:256
  41.3 8.3 %collective-permute-start.11 = (bf16[64,768]{1,0:T(8,128)(2,1)}, bf16[64,768]{1,0:T(8,128)(2,1)S(1)}, u32[]{:S(2)}, u32[]{:S(2)}) collective-permute-start(bf16[64,768]{1,0:T(8,128)(2,1)} %stack_rows.2.refs_0_), channel_id=1, source_target_pairs={{0,2},{1,3},{2,4},{3,5},{4,6},{5,7},{6,0},{7,1},{8,10},{9,11},{10,... | collective-permute-start | bytes 294920 | tf_op jit(solution)/shard_map/ppermute | solution.py:256
  47.4 2.2 %copy-start.11 = (bf16[64,768]{1,0:T(8,128)(2,1)}, bf16[64,768]{1,0:T(8,128)(2,1)S(1)}, u32[]{:S(2)}) copy-start(bf16[64,768]{1,0:T(8,128)(2,1)S(1)} %collective-permute-done.13.refs_3_) | copy-start | bytes 294916
  49.6 0.6 copy-start.12
  50.2 0.6 copy-start.13
  52.7 9.4 %collective-permute-start.14 = (bf16[256,768]{1,0:T(8,128)(2,1)}, bf16[256,768]{1,0:T(8,128)(2,1)S(1)}, u32[]{:S(2)}, u32[]{:S(2)}) collective-permute-start(bf16[256,768]{1,0:T(8,128)(2,1)} %stack_rows.3.out_own_ref), channel_id=1, source_target_pairs={{0,8},{8,0},{16,24},{24,16},{1,9},{9,1},{17,25},{25,17},{2,10},{10... | collective-permute-start | bytes 1179656 | tf_op jit(solution)/shard_map/ppermute | solution.py:260
  53.3 0.7 %copy-start.2 = (bf16[768,256]{1,0:T(8,128)(2,1)}, bf16[768,256]{1,0:T(8,128)(2,1)S(1)}, u32[]{:S(2)}) copy-start(bf16[768,256]{1,0:T(8,128)(2,1)S(1)} %collective-permute-done.8.refs_1_) | copy-start | bytes 1179652
  60.4 1.7 %collective-permute-start.9 = (bf16[384,128]{1,0:T(8,128)(2,1)}, bf16[384,128]{1,0:T(8,128)(2,1)S(1)}, u32[]{:S(2)}, u32[]{:S(2)}) collective-permute-start(bf16[384,128]{1,0:T(8,128)(2,1)} %get-tuple-element.18), channel_id=1, source_target_pairs={{0,8},{8,0},{16,24},{24,16},{1,9},{9,1},{17,25},{25,17},{2,10},{10... | collective-permute-start | bytes 294920 | tf_op jit(solution)/shard_map/ppermute | solution.py:264
  62.1 0.6 copy-start.10
  62.1 0.8 %copy-start.1 = (bf16[256,768]{1,0:T(8,128)(2,1)}, bf16[256,768]{1,0:T(8,128)(2,1)S(1)}, u32[]{:S(2)}) copy-start(bf16[256,768]{1,0:T(8,128)(2,1)S(1)} %collective-permute-done.14.out_partner_ref) | copy-start | bytes 1179652

commit v2 on v0

v2 whole, which is shorter than its diff:
```python
import jax
import jax.numpy as jnp
from jax import lax
from jax.experimental import pallas as pl
from jax.experimental.pallas import tpu as pltpu
from jax.sharding import PartitionSpec as P

E = 64
LANES = 128
CORES = 2
NEG = -1e30
COST1 = 4_000_000_000
COST = 1_000_000_000

VMEM = pl.BlockSpec(memory_space=pltpu.VMEM)
SMEM = pl.BlockSpec(memory_space=pltpu.SMEM)
HBM = pl.BlockSpec(memory_space=pltpu.HBM)


def grid_of(fsdp_count):
    x_count = 1
    while (2 * x_count) ** 2 <= fsdp_count and fsdp_count % (2 * x_count) == 0:
        x_count *= 2
    return fsdp_count // x_count, x_count


def rotation(z_count, x_count, z_step, x_step):
    return [
        (z * x_count + x, (z + z_step) % z_count * x_count + (x + x_step) % x_count)
        for z in range(z_count)
        for x in range(x_count)
    ]


def core_swap(array, seq_count):
    return lax.ppermute(array, "seq", [(s, s ^ 1) for s in range(seq_count)])


def y_rotation(array, seq_count, step):
    return lax.ppermute(array, "seq", [(s, (s + CORES * step) % seq_count) for s in range(seq_count)])


def call(kernel, name, in_specs, out_shapes, out_specs=None, scratch_shapes=(), cost=0):
    out_specs = [VMEM] * len(out_shapes) if out_specs is None else out_specs
    shapes = [
        pltpu.VMEM(shape.shape, shape.dtype) if spec is VMEM else shape for shape, spec in zip(out_shapes, out_specs)
    ]
    inner = pl.pallas_call(
        kernel,
        out_shape=shapes,
        in_specs=in_specs,
        out_specs=out_specs,
        scratch_shapes=scratch_shapes,
        cost_estimate=pl.CostEstimate(flops=cost, bytes_accessed=0, transcendentals=0) if cost else None,
        compiler_params=pltpu.CompilerParams(vmem_limit_bytes=24 << 20),
        name=name,
    )

    def run(*args):
        return inner(
            *[
                arg if spec is SMEM else pltpu.with_memory_space_constraint(arg, spec.memory_space)
                for arg, spec in zip(args, in_specs)
            ]
        )

    return run


def shaped(shape, dtype):
    return jax.ShapeDtypeStruct(shape, dtype)


def halves(qkv_weight, out_weight):
    rows, columns = qkv_weight.shape
    head_columns = columns // 3
    own = head_columns // CORES
    out_rows, width = out_weight.shape
    side = width // CORES

    def kernel(qkv_ref, out_ref, qkv_half_ref, out_half_ref, sems):
        core = lax.rem(lax.axis_index("seq"), CORES)
        copies = []
        for part in range(3):
            start = pl.multiple_of(part * head_columns + core * own, LANES)
            copies.append(
                pltpu.make_async_copy(
                    qkv_ref.at[:, pl.ds(start, own)], qkv_half_ref.at[:, part * own : (part + 1) * own], sems.at[part]
                )
            )
        start = pl.multiple_of(core * side, LANES)
        copies.append(pltpu.make_async_copy(out_ref.at[:, pl.ds(start, side)], out_half_ref, sems.at[3]))
        for copy in copies:
            copy.start()
        for copy in copies:
            copy.wait()

    return call(
        kernel,
        "halves",
        [HBM, HBM],
        [shaped((rows, 3 * own), qkv_weight.dtype), shaped((out_rows, side), out_weight.dtype)],
        scratch_shapes=[pltpu.SemaphoreType.DMA((4,))],
    )(qkv_weight, out_weight)


def side_by_side(blocks, x_count):
    rows, columns = blocks[0].shape

    def kernel(*refs):
        x_index = lax.rem(lax.axis_index("fsdp"), x_count)
        for step in range(x_count):
            place = lax.rem(x_index + x_count - step, x_count)
            refs[x_count][pl.ds(pl.multiple_of(place * rows, 16), rows), :] = refs[step][...]

    return call(kernel, "side_by_side", [VMEM] * x_count, [shaped((x_count * rows, columns), blocks[0].dtype)])(
        *blocks
    )[0]


def lane_pick(per_head):
    lane = lax.broadcasted_iota(jnp.int32, (1, LANES), 1)
    picked = per_head[0]
    for head in range(1, len(per_head)):
        picked = jnp.where(lane >= head * E, per_head[head], picked)
    return jnp.broadcast_to(picked, (picked.shape[0], LANES))


def attend_part(queries, keys, values, bias):
    lane = lax.broadcasted_iota(jnp.int32, (1, LANES), 1)
    maxima, sums, outs = [], [], []
    for head in range(LANES // E):
        inside = (lane >= head * E) & (lane < (head + 1) * E)
        head_queries = jnp.where(inside, queries, jnp.zeros_like(queries))
        scores = lax.dot_general(head_queries, keys, (((1,), (1,)), ((), ())), preferred_element_type=jnp.float32)
        scores = scores + bias
        row_max = jnp.max(scores, axis=1, keepdims=True)
        numerators = jnp.exp(scores - row_max)
        maxima.append(row_max)
        sums.append(jnp.sum(numerators, axis=1, keepdims=True))
        outs.append(jnp.dot(numerators.astype(values.dtype), values, preferred_element_type=jnp.float32))
    return lane_pick(maxima), lane_pick(sums), lane_pick(outs)


def merge(old, new):
    top = jnp.maximum(old[0], new[0])
    keep = jnp.exp(old[0] - top)
    add = jnp.exp(new[0] - top)
    return top, old[1] * keep + new[1] * add, old[2] * keep + new[2] * add


def key_bias(mask_ref, count_ref, tile, key_tile, slots):
    slot = lax.broadcasted_iota(jnp.int32, (1, slots), 1)
    live = jnp.where(mask_ref[tile, key_tile] > 0, count_ref[key_tile], 0)
    return jnp.where(slot < live, 0.0, NEG)


def row_chunks(row_count):
    rows = row_count // 2 if row_count % 32 == 0 else row_count
    return [(start, rows) for start in range(0, row_count, rows)]


def first_part(z_count, x_count, shifts, blocks, latents_own, latents_other, tile_mask, tile_counts):
    count = len(blocks)
    rows, columns = blocks[0].shape
    depth = count * rows
    own = columns // 3
    row_count = latents_own.shape[0]
    dtype = latents_own.dtype
    scale = float(E) ** -0.5

    def kernel(mask_ref, count_ref, own_ref, other_ref, *refs):
        block_refs = refs[:count]
        queries_ref, weight_ref, state_ref, full_ref, latents_ref, key_value_ref, sem = refs[count:]
        fetch = pltpu.make_async_copy(own_ref, latents_ref, sem)
        fetch.start()
        seq_index = lax.axis_index("seq")
        fsdp_index = lax.axis_index("fsdp")
        z_index = fsdp_index // x_count
        x_index = lax.rem(fsdp_index, x_count)
        for (dz, dx), block_ref in zip(shifts, block_refs):
            place = lax.rem(z_index + z_count - dz, z_count) * x_count + lax.rem(x_index + x_count - dx, x_count)
            full_ref[pl.ds(pl.multiple_of(place * rows, 16), rows), :] = block_ref[...]
        weight_ref[...] = full_ref[:, own:]
        for member, from_ref in ((1, other_ref), (0, latents_ref)):
            if member == 0:
                fetch.wait()
            projected = jnp.dot(from_ref[...], full_ref[...], preferred_element_type=jnp.float32).astype(dtype)
            queries_ref[member] = projected[:, :own] * jnp.asarray(scale, dtype)
            key_value_ref[member * row_count : (member + 1) * row_count, :] = projected[:, own:]
        core = lax.rem(seq_index, CORES)
        chip_tile = seq_index - core
        tiles = [chip_tile + core, chip_tile + 1 - core]
        for member in range(CORES):
            bias = jnp.concatenate(
                [key_bias(mask_ref, count_ref, tiles[member], key_tile, row_count) for key_tile in tiles], axis=1
            )
            for group in range(own // LANES):
                lanes = slice(group * LANES, (group + 1) * LANES)
                value_lanes = slice(own + group * LANES, own + (group + 1) * LANES)
                for start, size in row_chunks(row_count):
                    parts = attend_part(
                        queries_ref[member, start : start + size, lanes],
                        key_value_ref[:, lanes],
                        key_value_ref[:, value_lanes],
                        bias,
                    )
                    for which, part in enumerate(parts):
                        state_ref[member, which, start : start + size, lanes] = part

    return call(
        kernel,
        "first_part",
        [SMEM, SMEM, HBM] + [VMEM] * (count + 1),
        [
            shaped((CORES, row_count, own), dtype),
            shaped((depth, 2 * own), dtype),
            shaped((CORES, 3, row_count, own), jnp.float32),
        ],
        scratch_shapes=[
            pltpu.VMEM((depth, columns), dtype),
            pltpu.VMEM((row_count, latents_own.shape[1]), dtype),
            pltpu.VMEM((CORES * row_count, 2 * own), dtype),
            pltpu.SemaphoreType.DMA(()),
        ],
        cost=COST1,
    )(tile_mask, tile_counts, latents_own, latents_other, *blocks)


def next_part(seq_count, y_step, swapped, last, weight, latents, queries, state, tile_mask, tile_counts, layers=()):
    columns = weight.shape[1]
    z_count = len(layers)
    own = columns // 2
    row_count = latents.shape[0]
    dtype = latents.dtype

    def kernel(mask_ref, count_ref, weight_ref, latents_ref, queries_ref, old_ref, *refs):
        layer_refs, refs = refs[:z_count], refs[z_count:]
        out_refs, key_value_ref = refs[:-1], refs[-1]
        if layers:
            rows = layers[0].shape[0]
            z_index = lax.axis_index("fsdp") // (lax.axis_size("fsdp") // z_count)
            for step in range(z_count):
                place = lax.rem(z_index + z_count - step, z_count)
                out_refs[-1][pl.ds(pl.multiple_of(place * rows, 16), rows), :] = layer_refs[step][...]
        seq_index = lax.axis_index("seq")
        core = lax.rem(seq_index, CORES)
        key_place = lax.rem(seq_index + seq_count - CORES * y_step, seq_count)
        key_tile = key_place + 1 - 2 * core if swapped else key_place
        chip_tile = seq_index - core
        tiles = [chip_tile + core, chip_tile + 1 - core]
        key_value_ref[...] = jnp.dot(
            latents_ref[...], weight_ref[...], preferred_element_type=jnp.float32
        ).astype(dtype)
        for member in range(CORES):
            bias = key_bias(mask_ref, count_ref, tiles[member], key_tile, row_count)
            for group in range(own // LANES):
                lanes = slice(group * LANES, (group + 1) * LANES)
                value_lanes = slice(own + group * LANES, own + (group + 1) * LANES)
                for start, size in row_chunks(row_count):
                    chunk = slice(start, start + size)
                    parts = attend_part(
                        queries_ref[member, chunk, lanes], key_value_ref[:, lanes], key_value_ref[:, value_lanes], bias
                    )
                    parts = merge([old_ref[member, which, chunk, lanes] for which in range(3)], parts)
                    if last:
                        position = start + lax.broadcasted_iota(jnp.int32, (size, 1), 0)
                        attended = jnp.where(position < count_ref[tiles[member]], parts[2] / parts[1], 0.0)
                        out_refs[member][chunk, lanes] = attended.astype(dtype)
                    else:
                        for which, part in enumerate(parts):
                            out_refs[0][member, which, chunk, lanes] = part

    if last:
        out_shapes = [shaped((row_count, own), dtype)] * 2
    else:
        out_shapes = [shaped(state.shape, state.dtype)]
    if layers:
        out_shapes.append(shaped((z_count * layers[0].shape[0], layers[0].shape[1]), layers[0].dtype))
    return call(
        kernel,
        "last_part" if last else "next_part",
        [SMEM, SMEM] + [VMEM] * (4 + z_count),
        out_shapes,
        scratch_shapes=[pltpu.VMEM((row_count, columns), dtype)],
        cost=COST,
    )(tile_mask, tile_counts, weight, latents, queries, state, *layers)


def project_out(attended_own, attended_partner, out_own, out_partner):
    row_count, own = attended_own.shape
    side = out_own.shape[1]
    dtype = attended_own.dtype

    def kernel(own_ref, partner_ref, out_own_ref, out_partner_ref, result_ref, staged_ref, sems):
        core = lax.rem(lax.axis_index("seq"), CORES)
        own_rows = pl.ds(pl.multiple_of(core * own, 16), own)
        partner_rows = pl.ds(pl.multiple_of((1 - core) * own, 16), own)
        copies = []
        for half, weight_ref in enumerate((out_own_ref, out_partner_ref)):
            total = jnp.dot(own_ref[...], weight_ref[own_rows, :], preferred_element_type=jnp.float32)
            total += jnp.dot(partner_ref[...], weight_ref[partner_rows, :], preferred_element_type=jnp.float32)
            staged_ref[half] = total.astype(dtype)
            start = pl.multiple_of((core if half == 0 else 1 - core) * side, LANES)
            copies.append(
                pltpu.make_async_copy(staged_ref.at[half], result_ref.at[:, pl.ds(start, side)], sems.at[half])
            )
            copies[-1].start()
        for copy in copies:
            copy.wait()

    return call(
        kernel,
        "project_out",
        [VMEM] * 4,
        [shaped((row_count, CORES * side), dtype)],
        [HBM],
        scratch_shapes=[pltpu.VMEM((CORES, row_count, side), dtype), pltpu.SemaphoreType.DMA((CORES,))],
    )(attended_own, attended_partner, out_own, out_partner)[0]


def local(latents, qkv_weight, out_weight, tile_mask, tile_counts):
    seq_count = lax.axis_size("seq")
    fsdp_count = lax.axis_size("fsdp")
    z_count, x_count = grid_of(fsdp_count)
    chips = seq_count // CORES
    latents_own = latents[0]

    along_y = [y_rotation(latents_own, seq_count, step) for step in range(1, chips)]
    latents_other = core_swap(latents_own, seq_count)
    qkv_half, out_half = halves(qkv_weight, out_weight)

    shifts, blocks = [(0, 0)], [qkv_half]
    for z_step in reversed(range(z_count)):
        came = qkv_half
        if z_step:
            came = lax.ppermute(qkv_half, "fsdp", rotation(z_count, x_count, z_step, 0))
            shifts.append((z_step, 0))
            blocks.append(came)
        for x_step in range(1, x_count):
            shifts.append((z_step, x_step))
            if z_step == 1:
                blocks.append(lax.ppermute(qkv_half, "fsdp", rotation(z_count, x_count, z_step, x_step)))
            else:
                blocks.append(lax.ppermute(came, "fsdp", rotation(z_count, x_count, 0, x_step)))

    layer = side_by_side(
        [out_half]
        + [lax.ppermute(out_half, "fsdp", rotation(z_count, x_count, 0, x_step)) for x_step in range(1, x_count)],
        x_count,
    )
    blocks[0], layer = lax.optimization_barrier((blocks[0], layer))
    layers = [layer] + [
        lax.ppermute(layer, "fsdp", rotation(z_count, x_count, z_step, 0)) for z_step in range(1, z_count)
    ]

    queries, weight, state = first_part(
        z_count, x_count, shifts, blocks, latents_own, latents_other, tile_mask, tile_counts
    )
    parts = [(step, swapped) for step in range(1, chips) for swapped in (False, True)]
    for step, swapped in parts:
        if not swapped:
            came, state = lax.optimization_barrier((along_y[step - 1], state))
        else:
            came = core_swap(came, seq_count)
        last = (step, swapped) == parts[-1]
        result = next_part(
            seq_count,
            step,
            swapped,
            last,
            weight,
            came,
            queries,
            state,
            tile_mask,
            tile_counts,
            layers if (step, swapped) == parts[0] else (),
        )
        if (step, swapped) == parts[0]:
            *result, out_own = result
        if last:
            attended_own, attended_other = result
        else:
            state = result[0]
    out_partner = core_swap(out_own, seq_count)
    attended_partner = core_swap(attended_other, seq_count)
    return project_out(attended_own, attended_partner, out_own, out_partner)[None]


def solution(mesh):
    return jax.shard_map(
        local,
        mesh=mesh,
        in_specs=(P("fsdp", "seq", None), P("fsdp", None), P("fsdp", None), P(), P()),
        out_specs=P("fsdp", "seq", None),
        check_vma=False,
    )
```

time: 198 us -> 65.6 us (0.33)
  waiting for transfers between devices: 67.2 us -> 31.3 us
  blocking collectives: 32.3 us -> 0 us
  local copies, waits for them, and re-layouts: 30.9 us -> 1.34 us
  matrix products: 19.6 us -> 0 us
  other arithmetic: 18.7 us -> 0 us
  Pallas kernels: 0 us -> 16.2 us
  between operations: 13.5 us -> 0.09 us
  starting transfers between devices: 6.84 us -> 16.5 us
  loops' own time: 7.68 us -> 0 us
    all_gather x1 -> x0, waiting for transfers between devices: 57.1 us -> none  [local(): full_qkv = lax.all_gather(qkv_weight, 'fsdp', axis=0, tiled=True)]
    all_gather x1 -> x0, blocking collectives: 32.3 us -> none  [local(): full_out = lax.all_gather(out_weight, 'fsdp', axis=0, tiled=True)]
    ppermute x0 -> x16, waiting for transfers between devices: none -> 31.3 us  [the longest x3 11.9 us: local(): came = lax.ppermute(qkv_half, 'fsdp', rotation(z_count, x_count, z_step, 0))]
    gather x12 -> x0, local copies, waits for them, and re-layouts: 21 us -> none  [the longest x4 9.34 us: one_tile(): keys_sel = key_tiles_all[key_tiles].reshape(WINDOW * TILE, E)]
    dot_general x10 -> x0, matrix products: 19.6 us -> none  [the longest x4 8.88 us: one_tile(): jnp.dot(softmax_top, values_sel, preferred_element_type=jnp.float32)]
    ppermute x0 -> x16, starting transfers between devices: none -> 16.5 us  [the longest x3 3.87 us: local(): lax.ppermute(layer, 'fsdp', rotation(z_count, x_count, z_step, 0))]
    pallas_call x0 -> x6, Pallas kernels: none -> 16.2 us  [run(): inner(*[arg if spec is SMEM else pltpu.with_memory_space_constraint(arg,...]
    reduce_sum x8 -> x0, other arithmetic: 9.84 us -> none  [the longest x4 5.4 us: one_tile(): slot_live = jnp.arange(WINDOW, dtype=jnp.int32) < jnp.sum(mask_row)]
  transfers between devices with their start and end apart: 3 -> 16, of which waited for: 2 -> 9; matrix products, arithmetic and copies ran while one was open for 0% -> 0% of each run, Pallas kernels for 0% -> 22%
where the time goes in v2:
time: 65.6 us; the launch traced here: 65.4 us
  waiting for transfers between devices  31.3 us (48%)
  starting transfers between devices  16.5 us (25%)
  Pallas kernels  16.2 us (25%)
  local copies, waits for them, and re-layouts  1.34 us (2%)
    pallas_call x6, Pallas kernels, run(): inner(*[arg if spec is SMEM else pltpu.with_memory_space_constraint(arg,...  16.2 us
    ppermute x3, waiting for transfers between devices, local(): came = lax.ppermute(qkv_half, 'fsdp', rotation(z_count, x_count, z_step, 0))  11.9 us
    ppermute x3, waiting for transfers between devices, local(): lax.ppermute(came, 'fsdp', rotation(z_count, x_count, 0, x_step))  8.8 us
    ppermute x3, waiting for transfers between devices, local(): lax.ppermute(layer, 'fsdp', rotation(z_count, x_count, z_step, 0))  6.99 us
    ppermute x3, starting transfers between devices, local(): lax.ppermute(layer, 'fsdp', rotation(z_count, x_count, z_step, 0))  3.87 us
    ppermute x3, starting transfers between devices, local(): came = lax.ppermute(qkv_half, 'fsdp', rotation(z_count, x_count, z_step, 0))  3.66 us
    ppermute x3, starting transfers between devices, local(): lax.ppermute(came, 'fsdp', rotation(z_count, x_count, 0, x_step))  3.04 us
    ppermute x1, waiting for transfers between devices, local(): lax.ppermute(out_half, 'fsdp', rotation(z_count, x_count, 0, x_step))  2.6 us
  transfers between devices with their start and end apart: 16, of which 9 were waited for; matrix products, arithmetic and copies ran while one was open for 0% of the time, Pallas kernels for 22%

profile of v2, /device:TPU:0, one launch (start us, length us, event | category | flops | bytes accessed | tf_op | source)
XLA Modules:
  0.0 65.4 jit_solution(810855517744155346)
XLA Ops:
  0.0 0.5 collective-permute-start
  0.5 2.5 %collective-permute-start.9 = (bf16[384,1536]{1,0:T(8,128)(2,1)}, bf16[384,1536]{1,0:T(8,128)(2,1)S(1)}, u32[]{:S(2)}, u32[]{:S(2)}) collective-permute-start(bf16[384,1536]{1,0:T(8,128)(2,1)} %bitcast.3), channel_id=1, source_target_pairs={{0,16},{8,24},{16,0},{24,8},{1,17},{9,25},{17,1},{25,9},{2,18},{10... | collective-permute-start | bytes 3538952 | tf_op jit(solution)/shard_map/ppermute | solution.py:40
  3.0 0.9 %halves.1 = (bf16[192,384]{1,0:T(8,128)(2,1)S(1)}, bf16[32,768]{1,0:T(8,128)(2,1)S(1)}) custom-call(bf16[192,768]{1,0:T(8,128)(2,1)} %qkv_ref.1, bf16[32,1536]{1,0:T(8,128)(2,1)} %out_ref.1), custom_call_target="tpu_custom_call" | custom-call | tf_op jit(solution)/shard_map/halves/pallas_call | solution.py:60
  3.9 3.7 %collective-permute-start.2 = (bf16[192,384]{1,0:T(8,128)(2,1)S(1)}, bf16[192,384]{1,0:T(8,128)(2,1)S(1)}, u32[]{:S(2)}, u32[]{:S(2)}) collective-permute-start(bf16[192,384]{1,0:T(8,128)(2,1)S(1)} %get-tuple-element.20.refs_0_), channel_id=1, source_target_pairs={{0,6},{1,7},{2,0},{3,1},{4,2},{5,3},{6,4},{7,5},{8,14},{9,15},{10,... | collective-permute-start | bytes 442376 | tf_op jit(solution)/shard_map/ppermute | solution.py:337
  7.5 1.5 %collective-permute-start.1 = (bf16[32,768]{1,0:T(8,128)(2,1)S(1)}, bf16[32,768]{1,0:T(8,128)(2,1)S(1)}, u32[]{:S(2)}, u32[]{:S(2)}) collective-permute-start(bf16[32,768]{1,0:T(8,128)(2,1)S(1)} %get-tuple-element.19.refs_0_), channel_id=1, source_target_pairs={{0,1},{1,0},{2,3},{3,2},{4,5},{5,4},{6,7},{7,6},{8,9},{9,8},{10,11... | collective-permute-start | bytes 147464 | tf_op jit(solution)/shard_map/ppermute | solution.py:349
  9.0 0.0 collective-permute-start.4
  9.0 2.6 %collective-permute-done.1.refs_1_ = bf16[32,768]{1,0:T(8,128)(2,1)S(1)} collective-permute-done((bf16[32,768]{1,0:T(8,128)(2,1)S(1)}, bf16[32,768]{1,0:T(8,128)(2,1)S(1)}, u32[]{:S(2)}, u32[]{:S(2)}) %collective-permute-start.1) | collective-permute-done | bytes 49184 | tf_op jit(solution)/shard_map/ppermute | solution.py:349
  11.6 0.0 collective-permute-start.6
  11.6 0.2 collective-permute-done.2.refs_1_
  11.8 0.8 %collective-permute-start.7 = (bf16[192,384]{1,0:T(8,128)(2,1)S(1)}, bf16[192,384]{1,0:T(8,128)(2,1)S(1)}, u32[]{:S(2)}, u32[]{:S(2)}) collective-permute-start(bf16[192,384]{1,0:T(8,128)(2,1)S(1)} %get-tuple-element.20.refs_0_), channel_id=1, source_target_pairs={{0,3},{1,2},{2,5},{3,4},{4,7},{5,6},{6,1},{7,0},{8,11},{9,10},{10,... | collective-permute-start | bytes 442376 | tf_op jit(solution)/shard_map/ppermute | solution.py:343
  12.6 11.8 %collective-permute-done.4.refs_3_ = bf16[192,384]{1,0:T(8,128)(2,1)S(1)} collective-permute-done((bf16[192,384]{1,0:T(8,128)(2,1)S(1)}, bf16[192,384]{1,0:T(8,128)(2,1)S(1)}, u32[]{:S(2)}, u32[]{:S(2)}) %collective-permute-start.4) | collective-permute-done | bytes 147488 | tf_op jit(solution)/shard_map/ppermute | solution.py:337
  24.4 1.0 %collective-permute-start.8 = (bf16[192,384]{1,0:T(8,128)(2,1)S(1)}, bf16[192,384]{1,0:T(8,128)(2,1)S(1)}, u32[]{:S(2)}, u32[]{:S(2)}) collective-permute-start(bf16[192,384]{1,0:T(8,128)(2,1)S(1)} %get-tuple-element.20.refs_0_), channel_id=1, source_target_pairs={{0,1},{1,0},{2,3},{3,2},{4,5},{5,4},{6,7},{7,6},{8,9},{9,8},{10,11... | collective-permute-start | bytes 442376 | tf_op jit(solution)/shard_map/ppermute | solution.py:345
  25.4 0.0 collective-permute-done.6.refs_5_
  25.4 1.0 %collective-permute-start.3 = (bf16[192,384]{1,0:T(8,128)(2,1)S(1)}, bf16[192,384]{1,0:T(8,128)(2,1)S(1)}, u32[]{:S(2)}, u32[]{:S(2)}) collective-permute-start(bf16[192,384]{1,0:T(8,128)(2,1)S(1)} %collective-permute-done.2.refs_1_), channel_id=1, source_target_pairs={{0,1},{1,0},{2,3},{3,2},{4,5},{5,4},{6,7},{7,6},{8,9},{9,8},{10,11... | collective-permute-start | bytes 442376 | tf_op jit(solution)/shard_map/ppermute | solution.py:345
  26.4 0.0 collective-permute-done.7.refs_6_
  26.4 1.0 %collective-permute-start.5 = (bf16[192,384]{1,0:T(8,128)(2,1)S(1)}, bf16[192,384]{1,0:T(8,128)(2,1)S(1)}, u32[]{:S(2)}, u32[]{:S(2)}) collective-permute-start(bf16[192,384]{1,0:T(8,128)(2,1)S(1)} %collective-permute-done.4.refs_3_), channel_id=1, source_target_pairs={{0,1},{1,0},{2,3},{3,2},{4,5},{5,4},{6,7},{7,6},{8,9},{9,8},{10,11... | collective-permute-start | bytes 442376 | tf_op jit(solution)/shard_map/ppermute | solution.py:345
  27.4 3.7 %collective-permute-done.8.refs_7_ = bf16[192,384]{1,0:T(8,128)(2,1)S(1)} collective-permute-done((bf16[192,384]{1,0:T(8,128)(2,1)S(1)}, bf16[192,384]{1,0:T(8,128)(2,1)S(1)}, u32[]{:S(2)}, u32[]{:S(2)}) %collective-permute-start.8) | collective-permute-done | bytes 147488 | tf_op jit(solution)/shard_map/ppermute | solution.py:345
  31.1 3.2 %collective-permute-done.3.refs_2_ = bf16[192,384]{1,0:T(8,128)(2,1)S(1)} collective-permute-done((bf16[192,384]{1,0:T(8,128)(2,1)S(1)}, bf16[192,384]{1,0:T(8,128)(2,1)S(1)}, u32[]{:S(2)}, u32[]{:S(2)}) %collective-permute-start.3) | collective-permute-done | bytes 147488 | tf_op jit(solution)/shard_map/ppermute | solution.py:345
  34.3 2.0 %collective-permute-done.5.refs_4_ = bf16[192,384]{1,0:T(8,128)(2,1)S(1)} collective-permute-done((bf16[192,384]{1,0:T(8,128)(2,1)S(1)}, bf16[192,384]{1,0:T(8,128)(2,1)S(1)}, u32[]{:S(2)}, u32[]{:S(2)}) %collective-permute-start.5) | collective-permute-done | bytes 147488 | tf_op jit(solution)/shard_map/ppermute | solution.py:345
  36.2 0.0 collective-permute-done.other_ref
  36.2 0.0 copy-start
  36.2 0.7 %copy-done = s32[4,4]{1,0:T(4,128)S(1)} copy-done((s32[4,4]{1,0:T(4,128)S(1)}, s32[4,4]{1,0:T(4,128)}, u32[]{:S(2)}) %copy-start) | copy-done | bytes 88
  36.9 0.0 copy-start.1
  36.9 0.7 copy-done.1
  37.6 5.7 %first_part.1 = (bf16[2,384,128]{2,1,0:T(8,128)(2,1)S(1)}, bf16[1536,256]{1,0:T(8,128)(2,1)S(1)}, f32[2,3,384,128]{3,2,1,0:T(8,128)S(1)}) custom-call(s32[4,4]{1,0:T(4,128)S(1)} %copy-done, s32[4]{0:T(128)S(1)} %copy-done.1, bf16[384,1536]{1,0:T(8,128)(2,1)} %bitcast.4, bf16[384,1536]{1,0:T(8,128)(2,1)S(1)} %collective-permute-done.other_ref, ...), custom_call_target="tpu_custom_call" | custom-call | flops 4000000000 | tf_op jit(solution)/shard_map/first_part/pallas_call | solution.py:60
  43.3 0.0 collective-permute-done.9.latents_ref
  43.3 0.1 collective-permute-start.10
  43.4 0.1 collective-permute-start.11
  43.5 0.9 %collective-permute-start.12 = (bf16[64,768]{1,0:T(8,128)(2,1)S(1)}, bf16[64,768]{1,0:T(8,128)(2,1)S(1)}, u32[]{:S(2)}, u32[]{:S(2)}) collective-permute-start(bf16[64,768]{1,0:T(8,128)(2,1)S(1)} %side_by_side.1.refs_0_), channel_id=1, source_target_pairs={{0,4},{1,5},{2,6},{3,7},{4,0},{5,1},{6,2},{7,3},{8,12},{9,13},{10,... | collective-permute-start | bytes 294920 | tf_op jit(solution)/shard_map/ppermute | solution.py:354
  44.4 2.9 %collective-permute-start.13 = (bf16[64,768]{1,0:T(8,128)(2,1)S(1)}, bf16[64,768]{1,0:T(8,128)(2,1)S(1)}, u32[]{:S(2)}, u32[]{:S(2)}) collective-permute-start(bf16[64,768]{1,0:T(8,128)(2,1)S(1)} %side_by_side.1.refs_0_), channel_id=1, source_target_pairs={{0,6},{1,7},{2,0},{3,1},{4,2},{5,3},{6,4},{7,5},{8,14},{9,15},{10,... | collective-permute-start | bytes 294920 | tf_op jit(solution)/shard_map/ppermute | solution.py:354
  47.3 3.7 %collective-permute-done.11.refs_1_ = bf16[64,768]{1,0:T(8,128)(2,1)S(1)} collective-permute-done((bf16[64,768]{1,0:T(8,128)(2,1)S(1)}, bf16[64,768]{1,0:T(8,128)(2,1)S(1)}, u32[]{:S(2)}, u32[]{:S(2)}) %collective-permute-start.11) | collective-permute-done | bytes 98336 | tf_op jit(solution)/shard_map/ppermute | solution.py:354
  50.9 3.3 %collective-permute-done.12.refs_2_ = bf16[64,768]{1,0:T(8,128)(2,1)S(1)} collective-permute-done((bf16[64,768]{1,0:T(8,128)(2,1)S(1)}, bf16[64,768]{1,0:T(8,128)(2,1)S(1)}, u32[]{:S(2)}, u32[]{:S(2)}) %collective-permute-start.12) | collective-permute-done | bytes 98336 | tf_op jit(solution)/shard_map/ppermute | solution.py:354
  54.3 0.0 collective-permute-done.13.refs_3_
  54.3 3.9 %next_part.1 = (f32[2,3,384,128]{3,2,1,0:T(8,128)S(1)}, bf16[256,768]{1,0:T(8,128)(2,1)S(1)}) custom-call(s32[4,4]{1,0:T(4,128)S(1)} %copy-done, s32[4]{0:T(128)S(1)} %copy-done.1, bf16[1536,256]{1,0:T(8,128)(2,1)S(1)} %get-tuple-element.21.weight_ref, bf16[384,1536]{1,0:T(8,128)(2,1)S(1)} %collective-permute-done.9.latents_ref, ...), custom_call_target="tpu_custom_call" | custom-call | flops 1000000000 | tf_op jit(solution)/shard_map/next_part/pallas_call | solution.py:60
  58.2 0.1 collective-permute-start.15
  58.3 0.0 collective-permute-done.10.latents_ref
  58.3 4.0 %last_part.1 = (bf16[384,128]{1,0:T(8,128)(2,1)S(1)}, bf16[384,128]{1,0:T(8,128)(2,1)S(1)}) custom-call(s32[4,4]{1,0:T(4,128)S(1)} %copy-done, s32[4]{0:T(128)S(1)} %copy-done.1, bf16[1536,256]{1,0:T(8,128)(2,1)S(1)} %get-tuple-element.21.weight_ref, bf16[384,1536]{1,0:T(8,128)(2,1)S(1)} %collective-permute-done.10.latents_ref, ...), custom_call_target="tpu_custom_call" | custom-call | flops 1000000000 | tf_op jit(solution)/shard_map/last_part/pallas_call | solution.py:60
  62.3 0.6 collective-permute-start.14
  62.8 0.0 collective-permute-done.15.out_partner_ref
  62.8 0.9 %collective-permute-done.14.partner_ref = bf16[384,128]{1,0:T(8,128)(2,1)S(1)} collective-permute-done((bf16[384,128]{1,0:T(8,128)(2,1)S(1)}, bf16[384,128]{1,0:T(8,128)(2,1)S(1)}, u32[]{:S(2)}, u32[]{:S(2)}) %collective-permute-start.14) | collective-permute-done | bytes 98336 | tf_op jit(solution)/shard_map/ppermute | solution.py:36
  63.8 1.6 %project_out.1 = bf16[384,1536]{1,0:T(8,128)(2,1)} custom-call(bf16[384,128]{1,0:T(8,128)(2,1)S(1)} %get-tuple-element.28.own_ref, bf16[384,128]{1,0:T(8,128)(2,1)S(1)} %collective-permute-done.14.partner_ref, bf16[256,768]{1,0:T(8,128)(2,1)S(1)} %get-tuple-element.30.out_own_ref, bf16[256,768]{1,0:T(8,128)(2,1)S(1)} %collective-permute-done.15.out_partner_ref), custom_call_target="tpu_custom_call" | custom-call | tf_op jit(solution)/shard_map/project_out/pallas_call | solution.py:60
  (1 shorter events, 0.0 us)
Async XLA Ops:
  0.0 36.2 %collective-permute-start = (bf16[384,1536]{1,0:T(8,128)(2,1)}, bf16[384,1536]{1,0:T(8,128)(2,1)S(1)}, u32[]{:S(2)}, u32[]{:S(2)}) collective-permute-start(bf16[384,1536]{1,0:T(8,128)(2,1)} %bitcast.2), channel_id=1, source_target_pairs={{0,8},{8,0},{16,24},{24,16},{1,9},{9,1},{17,25},{25,17},{2,10},{10... | collective-permute-start | bytes 3538952 | tf_op jit(solution)/shard_map/ppermute | solution.py:36
  0.5 42.8 %collective-permute-start.9 = (bf16[384,1536]{1,0:T(8,128)(2,1)}, bf16[384,1536]{1,0:T(8,128)(2,1)S(1)}, u32[]{:S(2)}, u32[]{:S(2)}) collective-permute-start(bf16[384,1536]{1,0:T(8,128)(2,1)} %bitcast.3), channel_id=1, source_target_pairs={{0,16},{8,24},{16,0},{24,8},{1,17},{9,25},{17,1},{25,9},{2,18},{10... | collective-permute-start | bytes 3538952 | tf_op jit(solution)/shard_map/ppermute | solution.py:40
  3.9 7.9 %collective-permute-start.2 = (bf16[192,384]{1,0:T(8,128)(2,1)S(1)}, bf16[192,384]{1,0:T(8,128)(2,1)S(1)}, u32[]{:S(2)}, u32[]{:S(2)}) collective-permute-start(bf16[192,384]{1,0:T(8,128)(2,1)S(1)} %get-tuple-element.20.refs_0_), channel_id=1, source_target_pairs={{0,6},{1,7},{2,0},{3,1},{4,2},{5,3},{6,4},{7,5},{8,14},{9,15},{10,... | collective-permute-start | bytes 442376 | tf_op jit(solution)/shard_map/ppermute | solution.py:337
  7.5 4.1 %collective-permute-start.1 = (bf16[32,768]{1,0:T(8,128)(2,1)S(1)}, bf16[32,768]{1,0:T(8,128)(2,1)S(1)}, u32[]{:S(2)}, u32[]{:S(2)}) collective-permute-start(bf16[32,768]{1,0:T(8,128)(2,1)S(1)} %get-tuple-element.19.refs_0_), channel_id=1, source_target_pairs={{0,1},{1,0},{2,3},{3,2},{4,5},{5,4},{6,7},{7,6},{8,9},{9,8},{10,11... | collective-permute-start | bytes 147464 | tf_op jit(solution)/shard_map/ppermute | solution.py:349
  9.0 15.3 %collective-permute-start.4 = (bf16[192,384]{1,0:T(8,128)(2,1)S(1)}, bf16[192,384]{1,0:T(8,128)(2,1)S(1)}, u32[]{:S(2)}, u32[]{:S(2)}) collective-permute-start(bf16[192,384]{1,0:T(8,128)(2,1)S(1)} %get-tuple-element.20.refs_0_), channel_id=1, source_target_pairs={{0,4},{1,5},{2,6},{3,7},{4,0},{5,1},{6,2},{7,3},{8,12},{9,13},{10,... | collective-permute-start | bytes 442376 | tf_op jit(solution)/shard_map/ppermute | solution.py:337
  11.6 13.7 %collective-permute-start.6 = (bf16[192,384]{1,0:T(8,128)(2,1)S(1)}, bf16[192,384]{1,0:T(8,128)(2,1)S(1)}, u32[]{:S(2)}, u32[]{:S(2)}) collective-permute-start(bf16[192,384]{1,0:T(8,128)(2,1)S(1)} %get-tuple-element.20.refs_0_), channel_id=1, source_target_pairs={{0,2},{1,3},{2,4},{3,5},{4,6},{5,7},{6,0},{7,1},{8,10},{9,11},{10,... | collective-permute-start | bytes 442376 | tf_op jit(solution)/shard_map/ppermute | solution.py:337
  11.8 14.6 %collective-permute-start.7 = (bf16[192,384]{1,0:T(8,128)(2,1)S(1)}, bf16[192,384]{1,0:T(8,128)(2,1)S(1)}, u32[]{:S(2)}, u32[]{:S(2)}) collective-permute-start(bf16[192,384]{1,0:T(8,128)(2,1)S(1)} %get-tuple-element.20.refs_0_), channel_id=1, source_target_pairs={{0,3},{1,2},{2,5},{3,4},{4,7},{5,6},{6,1},{7,0},{8,11},{9,10},{10,... | collective-permute-start | bytes 442376 | tf_op jit(solution)/shard_map/ppermute | solution.py:343
  24.4 6.7 %collective-permute-start.8 = (bf16[192,384]{1,0:T(8,128)(2,1)S(1)}, bf16[192,384]{1,0:T(8,128)(2,1)S(1)}, u32[]{:S(2)}, u32[]{:S(2)}) collective-permute-start(bf16[192,384]{1,0:T(8,128)(2,1)S(1)} %get-tuple-element.20.refs_0_), channel_id=1, source_target_pairs={{0,1},{1,0},{2,3},{3,2},{4,5},{5,4},{6,7},{7,6},{8,9},{9,8},{10,11... | collective-permute-start | bytes 442376 | tf_op jit(solution)/shard_map/ppermute | solution.py:345
  25.4 8.9 %collective-permute-start.3 = (bf16[192,384]{1,0:T(8,128)(2,1)S(1)}, bf16[192,384]{1,0:T(8,128)(2,1)S(1)}, u32[]{:S(2)}, u32[]{:S(2)}) collective-permute-start(bf16[192,384]{1,0:T(8,128)(2,1)S(1)} %collective-permute-done.2.refs_1_), channel_id=1, source_target_pairs={{0,1},{1,0},{2,3},{3,2},{4,5},{5,4},{6,7},{7,6},{8,9},{9,8},{10,11... | collective-permute-start | bytes 442376 | tf_op jit(solution)/shard_map/ppermute | solution.py:345
  26.4 9.8 %collective-permute-start.5 = (bf16[192,384]{1,0:T(8,128)(2,1)S(1)}, bf16[192,384]{1,0:T(8,128)(2,1)S(1)}, u32[]{:S(2)}, u32[]{:S(2)}) collective-permute-start(bf16[192,384]{1,0:T(8,128)(2,1)S(1)} %collective-permute-done.4.refs_3_), channel_id=1, source_target_pairs={{0,1},{1,0},{2,3},{3,2},{4,5},{5,4},{6,7},{7,6},{8,9},{9,8},{10,11... | collective-permute-start | bytes 442376 | tf_op jit(solution)/shard_map/ppermute | solution.py:345
  36.2 0.7 %copy-start = (s32[4,4]{1,0:T(4,128)S(1)}, s32[4,4]{1,0:T(4,128)}, u32[]{:S(2)}) copy-start(s32[4,4]{1,0:T(4,128)} %mask_ref.5) | copy-start | bytes 196
  36.9 0.7 %copy-start.1 = (s32[4]{0:T(128)S(1)}, s32[4]{0:T(128)}, u32[]{:S(2)}) copy-start(s32[4]{0:T(128)} %count_ref.5) | copy-start | bytes 52
  43.3 15.0 %collective-permute-start.10 = (bf16[384,1536]{1,0:T(8,128)(2,1)S(1)}, bf16[384,1536]{1,0:T(8,128)(2,1)S(1)}, u32[]{:S(2)}, u32[]{:S(2)}) collective-permute-start(bf16[384,1536]{1,0:T(8,128)(2,1)S(1)} %collective-permute-done.9.latents_ref), channel_id=1, source_target_pairs={{0,8},{8,0},{16,24},{24,16},{1,9},{9,1},{17,25},{25,17},{2,10},{10... | collective-permute-start | bytes 3538952 | tf_op jit(solution)/shard_map/ppermute | solution.py:36
  43.4 7.5 %collective-permute-start.11 = (bf16[64,768]{1,0:T(8,128)(2,1)S(1)}, bf16[64,768]{1,0:T(8,128)(2,1)S(1)}, u32[]{:S(2)}, u32[]{:S(2)}) collective-permute-start(bf16[64,768]{1,0:T(8,128)(2,1)S(1)} %side_by_side.1.refs_0_), channel_id=1, source_target_pairs={{0,2},{1,3},{2,4},{3,5},{4,6},{5,7},{6,0},{7,1},{8,10},{9,11},{10,... | collective-permute-start | bytes 294920 | tf_op jit(solution)/shard_map/ppermute | solution.py:354
  43.5 10.8 %collective-permute-start.12 = (bf16[64,768]{1,0:T(8,128)(2,1)S(1)}, bf16[64,768]{1,0:T(8,128)(2,1)S(1)}, u32[]{:S(2)}, u32[]{:S(2)}) collective-permute-start(bf16[64,768]{1,0:T(8,128)(2,1)S(1)} %side_by_side.1.refs_0_), channel_id=1, source_target_pairs={{0,4},{1,5},{2,6},{3,7},{4,0},{5,1},{6,2},{7,3},{8,12},{9,13},{10,... | collective-permute-start | bytes 294920 | tf_op jit(solution)/shard_map/ppermute | solution.py:354
  44.4 9.9 %collective-permute-start.13 = (bf16[64,768]{1,0:T(8,128)(2,1)S(1)}, bf16[64,768]{1,0:T(8,128)(2,1)S(1)}, u32[]{:S(2)}, u32[]{:S(2)}) collective-permute-start(bf16[64,768]{1,0:T(8,128)(2,1)S(1)} %side_by_side.1.refs_0_), channel_id=1, source_target_pairs={{0,6},{1,7},{2,0},{3,1},{4,2},{5,3},{6,4},{7,5},{8,14},{9,15},{10,... | collective-permute-start | bytes 294920 | tf_op jit(solution)/shard_map/ppermute | solution.py:354
  58.2 4.6 %collective-permute-start.15 = (bf16[256,768]{1,0:T(8,128)(2,1)S(1)}, bf16[256,768]{1,0:T(8,128)(2,1)S(1)}, u32[]{:S(2)}, u32[]{:S(2)}) collective-permute-start(bf16[256,768]{1,0:T(8,128)(2,1)S(1)} %get-tuple-element.30.out_own_ref), channel_id=1, source_target_pairs={{0,8},{8,0},{16,24},{24,16},{1,9},{9,1},{17,25},{25,17},{2,10},{10... | collective-permute-start | bytes 1179656 | tf_op jit(solution)/shard_map/ppermute | solution.py:36
  62.3 1.5 %collective-permute-start.14 = (bf16[384,128]{1,0:T(8,128)(2,1)S(1)}, bf16[384,128]{1,0:T(8,128)(2,1)S(1)}, u32[]{:S(2)}, u32[]{:S(2)}) collective-permute-start(bf16[384,128]{1,0:T(8,128)(2,1)S(1)} %get-tuple-element.29), channel_id=1, source_target_pairs={{0,8},{8,0},{16,24},{24,16},{1,9},{9,1},{17,25},{25,17},{2,10},{10... | collective-permute-start | bytes 294920 | tf_op jit(solution)/shard_map/ppermute | solution.py:36

commit v3 on v2

--- a/solution.py
+++ b/solution.py
@@ -9,7 +9,7 @@
 LANES = 128
 CORES = 2
 NEG = -1e30
-COST1 = 4_000_000_000
+COST1 = 1_000_000_000
 COST = 1_000_000_000
 
 VMEM = pl.BlockSpec(memory_space=pltpu.VMEM)
@@ -59,7 +59,7 @@
     def run(*args):
         return inner(
             *[
-                arg if spec is SMEM else pltpu.with_memory_space_constraint(arg, spec.memory_space)
+                pltpu.with_memory_space_constraint(arg, pltpu.HBM if spec is SMEM else spec.memory_space)
                 for arg, spec in zip(args, in_specs)
             ]
         )
@@ -69,6 +69,11 @@
 
 def shaped(shape, dtype):
     return jax.ShapeDtypeStruct(shape, dtype)
+
+
+def strips(width, columns):
+    strip = min(width, columns)
+    return [(start, strip) for start in range(0, width, strip)]
 
 
 def halves(qkv_weight, out_weight):
@@ -77,43 +82,56 @@
     own = head_columns // CORES
     out_rows, width = out_weight.shape
     side = width // CORES
-
-    def kernel(qkv_ref, out_ref, qkv_half_ref, out_half_ref, sems):
+    pieces = strips(side, 3 * own)
+
+    def kernel(qkv_ref, out_ref, half_ref, packed_ref, sems):
         core = lax.rem(lax.axis_index("seq"), CORES)
         copies = []
+
+        def copy(source, target):
+            copies.append(pltpu.make_async_copy(source, target, sems.at[len(copies)]))
+            copies[-1].start()
+
         for part in range(3):
-            start = pl.multiple_of(part * head_columns + core * own, LANES)
-            copies.append(
-                pltpu.make_async_copy(
-                    qkv_ref.at[:, pl.ds(start, own)], qkv_half_ref.at[:, part * own : (part + 1) * own], sems.at[part]
-                )
+            source = qkv_ref.at[:, pl.ds(pl.multiple_of(part * head_columns + core * own, LANES), own)]
+            lanes = slice(part * own, (part + 1) * own)
+            copy(source, half_ref.at[:, lanes])
+            copy(source, packed_ref.at[:rows, lanes])
+        for piece, (start, strip) in enumerate(pieces):
+            first = rows + piece * out_rows
+            copy(
+                out_ref.at[:, pl.ds(pl.multiple_of(core * side + start, LANES), strip)],
+                packed_ref.at[first : first + out_rows, :strip],
             )
-        start = pl.multiple_of(core * side, LANES)
-        copies.append(pltpu.make_async_copy(out_ref.at[:, pl.ds(start, side)], out_half_ref, sems.at[3]))
-        for copy in copies:
-            copy.start()
-        for copy in copies:
-            copy.wait()
+        for each in copies:
+            each.wait()
 
     return call(
         kernel,
         "halves",
         [HBM, HBM],
-        [shaped((rows, 3 * own), qkv_weight.dtype), shaped((out_rows, side), out_weight.dtype)],
-        scratch_shapes=[pltpu.SemaphoreType.DMA((4,))],
+        [
+            shaped((rows, 3 * own), qkv_weight.dtype),
+            shaped((rows + len(pieces) * out_rows, 3 * own), qkv_weight.dtype),
+        ],
+        scratch_shapes=[pltpu.SemaphoreType.DMA((6 + len(pieces),))],
     )(qkv_weight, out_weight)
 
 
-def side_by_side(blocks, x_count):
-    rows, columns = blocks[0].shape
+def side_by_side(blocks, x_count, rows, out_rows, side):
+    pieces = strips(side, blocks[0].shape[1])
 
     def kernel(*refs):
         x_index = lax.rem(lax.axis_index("fsdp"), x_count)
         for step in range(x_count):
             place = lax.rem(x_index + x_count - step, x_count)
-            refs[x_count][pl.ds(pl.multiple_of(place * rows, 16), rows), :] = refs[step][...]
-
-    return call(kernel, "side_by_side", [VMEM] * x_count, [shaped((x_count * rows, columns), blocks[0].dtype)])(
+            for piece, (start, strip) in enumerate(pieces):
+                first = rows + piece * out_rows
+                refs[x_count][pl.ds(pl.multiple_of(place * out_rows, 16), out_rows), start : start + strip] = refs[step][
+                    first : first + out_rows, :strip
+                ]
+
+    return call(kernel, "side_by_side", [VMEM] * x_count, [shaped((x_count * out_rows, side), blocks[0].dtype)])(
         *blocks
     )[0]
 
@@ -162,7 +180,8 @@
 
 def first_part(z_count, x_count, shifts, blocks, latents_own, latents_other, tile_mask, tile_counts):
     count = len(blocks)
-    rows, columns = blocks[0].shape
+    rows = latents_own.shape[1] // count
+    columns = blocks[0].shape[1]
     depth = count * rows
     own = columns // 3
     row_count = latents_own.shape[0]
@@ -180,7 +199,7 @@
         x_index = lax.rem(fsdp_index, x_count)
         for (dz, dx), block_ref in zip(shifts, block_refs):
             place = lax.rem(z_index + z_count - dz, z_count) * x_count + lax.rem(x_index + x_count - dx, x_count)
-            full_ref[pl.ds(pl.multiple_of(place * rows, 16), rows), :] = block_ref[...]
+            full_ref[pl.ds(pl.multiple_of(place * rows, 16), rows), :] = block_ref[:rows, :]
         weight_ref[...] = full_ref[:, own:]
         for member, from_ref in ((1, other_ref), (0, latents_ref)):
             if member == 0:
@@ -227,14 +246,14 @@
     )(tile_mask, tile_counts, latents_own, latents_other, *blocks)
 
 
-def next_part(seq_count, y_step, swapped, last, weight, latents, queries, state, tile_mask, tile_counts, layers=()):
+def next_part(seq_count, y_step, last, weight, latents, queries, state, tile_mask, tile_counts, layers=()):
     columns = weight.shape[1]
     z_count = len(layers)
     own = columns // 2
-    row_count = latents.shape[0]
-    dtype = latents.dtype
-
-    def kernel(mask_ref, count_ref, weight_ref, latents_ref, queries_ref, old_ref, *refs):
+    row_count = latents[0].shape[0]
+    dtype = latents[0].dtype
+
+    def kernel(mask_ref, count_ref, weight_ref, near_ref, far_ref, queries_ref, old_ref, *refs):
         layer_refs, refs = refs[:z_count], refs[z_count:]
         out_refs, key_value_ref = refs[:-1], refs[-1]
         if layers:
@@ -246,14 +265,20 @@
         seq_index = lax.axis_index("seq")
         core = lax.rem(seq_index, CORES)
         key_place = lax.rem(seq_index + seq_count - CORES * y_step, seq_count)
-        key_tile = key_place + 1 - 2 * core if swapped else key_place
         chip_tile = seq_index - core
         tiles = [chip_tile + core, chip_tile + 1 - core]
-        key_value_ref[...] = jnp.dot(
-            latents_ref[...], weight_ref[...], preferred_element_type=jnp.float32
-        ).astype(dtype)
+        for part, latents_ref in enumerate((near_ref, far_ref)):
+            key_value_ref[part * row_count : (part + 1) * row_count, :] = jnp.dot(
+                latents_ref[...], weight_ref[...], preferred_element_type=jnp.float32
+            ).astype(dtype)
         for member in range(CORES):
-            bias = key_bias(mask_ref, count_ref, tiles[member], key_tile, row_count)
+            bias = jnp.concatenate(
+                [
+                    key_bias(mask_ref, count_ref, tiles[member], key_tile, row_count)
+                    for key_tile in (key_place, key_place + 1 - 2 * core)
+                ],
+                axis=1,
+            )
             for group in range(own // LANES):
                 lanes = slice(group * LANES, (group + 1) * LANES)
                 value_lanes = slice(own + group * LANES, own + (group + 1) * LANES)
@@ -280,11 +305,11 @@
     return call(
         kernel,
         "last_part" if last else "next_part",
-        [SMEM, SMEM] + [VMEM] * (4 + z_count),
+        [SMEM, SMEM] + [VMEM] * (5 + z_count),
         out_shapes,
-        scratch_shapes=[pltpu.VMEM((row_count, columns), dtype)],
+        scratch_shapes=[pltpu.VMEM((CORES * row_count, columns), dtype)],
         cost=COST,
-    )(tile_mask, tile_counts, weight, latents, queries, state, *layers)
+    )(tile_mask, tile_counts, weight, *latents, queries, state, *layers)
 
 
 def project_out(attended_own, attended_partner, out_own, out_partner):
@@ -319,6 +344,10 @@
     )(attended_own, attended_partner, out_own, out_partner)[0]
 
 
+def after(array, *others):
+    return lax.optimization_barrier((array, *others))[0]
+
+
 def local(latents, qkv_weight, out_weight, tile_mask, tile_counts):
     seq_count = lax.axis_size("seq")
     fsdp_count = lax.axis_size("fsdp")
@@ -326,58 +355,51 @@
     chips = seq_count // CORES
     latents_own = latents[0]
 
+    def hop(array, z_step, x_step):
+        return lax.ppermute(array, "fsdp", rotation(z_count, x_count, z_step, x_step))
+
     along_y = [y_rotation(latents_own, seq_count, step) for step in range(1, chips)]
-    latents_other = core_swap(latents_own, seq_count)
-    qkv_half, out_half = halves(qkv_weight, out_weight)
-
-    shifts, blocks = [(0, 0)], [qkv_half]
-    for z_step in reversed(range(z_count)):
-        came = qkv_half
-        if z_step:
-            came = lax.ppermute(qkv_half, "fsdp", rotation(z_count, x_count, z_step, 0))
-            shifts.append((z_step, 0))
-            blocks.append(came)
-        for x_step in range(1, x_count):
-            shifts.append((z_step, x_step))
-            if z_step == 1:
-                blocks.append(lax.ppermute(qkv_half, "fsdp", rotation(z_count, x_count, z_step, x_step)))
-            else:
-                blocks.append(lax.ppermute(came, "fsdp", rotation(z_count, x_count, 0, x_step)))
-
-    layer = side_by_side(
-        [out_half]
-        + [lax.ppermute(out_half, "fsdp", rotation(z_count, x_count, 0, x_step)) for x_step in range(1, x_count)],
-        x_count,
+    half, packed = halves(qkv_weight, out_weight)
+
+    came = {(0, 0): half}
+    for x_step in range(1, x_count):
+        came[0, x_step] = hop(packed, 0, x_step)
+    order = [step for step in range(2, z_count)] + [1]
+    for z_step in order:
+        came[z_step, 0] = hop(half, z_step, 0)
+    beside = [came[0, x_step] for x_step in range(1, x_count)]
+    for x_step in range(1, x_count):
+        came[1, x_step] = hop(after(half, *beside), 1, x_step)
+        for z_step in order[:-1]:
+            came[z_step, x_step] = hop(came[z_step, 0], 0, x_step)
+    latents_other = core_swap(after(latents_own, came[order[0], x_count - 1]), seq_count)
+
+    layer = side_by_side([packed] + beside, x_count, half.shape[0], out_weight.shape[0], out_weight.shape[1] // CORES)
+    layer = after(layer, *[came[z_step, 0] for z_step in order])
+    layers = [layer] + [hop(layer, z_step, 0) for z_step in range(1, z_count)]
+
+    arrived = list(came.values())[1:]
+    came[0, 0] = after(half, *along_y)
+    queries, weight, state = first_part(
+        z_count, x_count, list(came), list(came.values()), latents_own, latents_other, tile_mask, tile_counts
     )
-    blocks[0], layer = lax.optimization_barrier((blocks[0], layer))
-    layers = [layer] + [
-        lax.ppermute(layer, "fsdp", rotation(z_count, x_count, z_step, 0)) for z_step in range(1, z_count)
-    ]
-
-    queries, weight, state = first_part(
-        z_count, x_count, shifts, blocks, latents_own, latents_other, tile_mask, tile_counts
-    )
-    parts = [(step, swapped) for step in range(1, chips) for swapped in (False, True)]
-    for step, swapped in parts:
-        if not swapped:
-            came, state = lax.optimization_barrier((along_y[step - 1], state))
-        else:
-            came = core_swap(came, seq_count)
-        last = (step, swapped) == parts[-1]
+    for step in range(1, chips):
+        near = along_y[step - 1]
+        far = core_swap(after(near, *arrived), seq_count)
+        last = step == chips - 1
         result = next_part(
             seq_count,
             step,
-            swapped,
             last,
             weight,
-            came,
+            (near, far),
             queries,
             state,
             tile_mask,
             tile_counts,
-            layers if (step, swapped) == parts[0] else (),
+            layers if step == 1 else (),
         )
-        if (step, swapped) == parts[0]:
+        if step == 1:
             *result, out_own = result
         if last:
             attended_own, attended_other = result

time: 65.6 us -> 49.8 us (0.76)
  waiting for transfers between devices: 31.3 us -> 15.4 us
  starting transfers between devices: 16.5 us -> 20.4 us
  Pallas kernels: 16.2 us -> 13.6 us
  local copies, waits for them, and re-layouts: 1.34 us -> 0 us
    ppermute x11 -> x10, waiting for transfers between devices: 30.3 us -> 13.3 us  [hop(): lax.ppermute(array, 'fsdp', rotation(z_count, x_count, z_step, x_step))]
    ppermute x11 -> x10, starting transfers between devices: 12.8 us -> 16.9 us  [hop(): lax.ppermute(array, 'fsdp', rotation(z_count, x_count, z_step, x_step))]
    pallas_call x6 -> x5, Pallas kernels: 16.2 us -> 13.6 us  [run(): inner(*[pltpu.with_memory_space_constraint(arg, pltpu.HBM if spec is SMEM...]
    unnamed x4 -> x0, local copies, waits for them, and re-layouts: 1.34 us -> none
    ppermute x1, waiting for transfers between devices: 0.01 us -> 0.71 us  [y_rotation(): lax.ppermute(array, 'seq', [(s, (s + CORES * step) % seq_count) for s in...]
  transfers between devices with their start and end apart: 16 -> 15, of which waited for: 9 -> 5; matrix products, arithmetic and copies ran while one was open for 0% -> 0% of each run, Pallas kernels for 22% -> 15%
where the time goes in v3:
time: 49.8 us; the launch traced here: 49.5 us
  starting transfers between devices  20.4 us (41%)
  waiting for transfers between devices  15.4 us (31%)
  Pallas kernels  13.6 us (27%)
    ppermute x10, starting transfers between devices, hop(): lax.ppermute(array, 'fsdp', rotation(z_count, x_count, z_step, x_step))  16.9 us
    pallas_call x5, Pallas kernels, run(): inner(*[pltpu.with_memory_space_constraint(arg, pltpu.HBM if spec is SMEM...  13.6 us
    ppermute x10, waiting for transfers between devices, hop(): lax.ppermute(array, 'fsdp', rotation(z_count, x_count, z_step, x_step))  13.3 us
    ppermute x1, starting transfers between devices, y_rotation(): lax.ppermute(array, 'seq', [(s, (s + CORES * step) % seq_count) for s in...  2.97 us
    ppermute x4, waiting for transfers between devices, core_swap(): return lax.ppermute(array, 'seq', [(s, s ^ 1) for s in range(seq_count)])  1.36 us
  transfers between devices with their start and end apart: 15, of which 5 were waited for; matrix products, arithmetic and copies ran while one was open for 0% of the time, Pallas kernels for 15%

profile of v3, /device:TPU:0, one launch (start us, length us, event | category | flops | bytes accessed | tf_op | source)
XLA Modules:
  0.0 49.5 jit_solution(4248878347295993488)
XLA Ops:
  0.0 3.0 %collective-permute-start.3 = (bf16[384,1536]{1,0:T(8,128)(2,1)}, bf16[384,1536]{1,0:T(8,128)(2,1)S(1)}, u32[]{:S(2)}, u32[]{:S(2)}) collective-permute-start(bf16[384,1536]{1,0:T(8,128)(2,1)} %bitcast.2), channel_id=1, source_target_pairs={{0,16},{8,24},{16,0},{24,8},{1,17},{9,25},{17,1},{25,9},{2,18},{10... | collective-permute-start | bytes 3538952 | tf_op jit(solution)/shard_map/ppermute | solution.py:40
  3.0 1.0 %halves.1 = (bf16[192,384]{1,0:T(8,128)(2,1)S(1)}, bf16[256,384]{1,0:T(8,128)(2,1)S(1)}) custom-call(bf16[192,768]{1,0:T(8,128)(2,1)} %qkv_ref.1, bf16[32,1536]{1,0:T(8,128)(2,1)} %out_ref.1), custom_call_target="tpu_custom_call" | custom-call | tf_op jit(solution)/shard_map/halves/pallas_call | solution.py:60
  4.0 2.7 %collective-permute-start = (bf16[192,384]{1,0:T(8,128)(2,1)S(1)}, bf16[192,384]{1,0:T(8,128)(2,1)S(1)}, u32[]{:S(2)}, u32[]{:S(2)}) collective-permute-start(bf16[192,384]{1,0:T(8,128)(2,1)S(1)} %get-tuple-element.22.refs_0_), channel_id=1, source_target_pairs={{0,4},{1,5},{2,6},{3,7},{4,0},{5,1},{6,2},{7,3},{8,12},{9,13},{10,... | collective-permute-start | bytes 442376 | tf_op jit(solution)/shard_map/ppermute | solution.py:359
  6.6 1.5 %collective-permute-start.4 = (bf16[256,384]{1,0:T(8,128)(2,1)S(1)}, bf16[256,384]{1,0:T(8,128)(2,1)S(1)}, u32[]{:S(2)}, u32[]{:S(2)}) collective-permute-start(bf16[256,384]{1,0:T(8,128)(2,1)S(1)} %get-tuple-element.21.refs_0_), channel_id=1, source_target_pairs={{0,1},{1,0},{2,3},{3,2},{4,5},{5,4},{6,7},{7,6},{8,9},{9,8},{10,11... | collective-permute-start | bytes 589832 | tf_op jit(solution)/shard_map/ppermute | solution.py:359
  8.1 1.3 %collective-permute-start.5 = (bf16[192,384]{1,0:T(8,128)(2,1)S(1)}, bf16[192,384]{1,0:T(8,128)(2,1)S(1)}, u32[]{:S(2)}, u32[]{:S(2)}) collective-permute-start(bf16[192,384]{1,0:T(8,128)(2,1)S(1)} %get-tuple-element.22.refs_0_), channel_id=1, source_target_pairs={{0,6},{1,7},{2,0},{3,1},{4,2},{5,3},{6,4},{7,5},{8,14},{9,15},{10,... | collective-permute-start | bytes 442376 | tf_op jit(solution)/shard_map/ppermute | solution.py:359
  9.5 5.1 %collective-permute-done.refs_2_ = bf16[192,384]{1,0:T(8,128)(2,1)S(1)} collective-permute-done((bf16[192,384]{1,0:T(8,128)(2,1)S(1)}, bf16[192,384]{1,0:T(8,128)(2,1)S(1)}, u32[]{:S(2)}, u32[]{:S(2)}) %collective-permute-start) | collective-permute-done | bytes 147488 | tf_op jit(solution)/shard_map/ppermute | solution.py:359
  14.6 1.5 %collective-permute-start.1 = (bf16[192,384]{1,0:T(8,128)(2,1)S(1)}, bf16[192,384]{1,0:T(8,128)(2,1)S(1)}, u32[]{:S(2)}, u32[]{:S(2)}) collective-permute-start(bf16[192,384]{1,0:T(8,128)(2,1)S(1)} %collective-permute-done.refs_2_), channel_id=1, source_target_pairs={{0,1},{1,0},{2,3},{3,2},{4,5},{5,4},{6,7},{7,6},{8,9},{9,8},{10,11... | collective-permute-start | bytes 442376 | tf_op jit(solution)/shard_map/ppermute | solution.py:359
  16.1 2.7 %collective-permute-start.6 = (bf16[192,384]{1,0:T(8,128)(2,1)S(1)}, bf16[192,384]{1,0:T(8,128)(2,1)S(1)}, u32[]{:S(2)}, u32[]{:S(2)}) collective-permute-start(bf16[192,384]{1,0:T(8,128)(2,1)S(1)} %get-tuple-element.22.refs_0_), channel_id=1, source_target_pairs={{0,2},{1,3},{2,4},{3,5},{4,6},{5,7},{6,0},{7,1},{8,10},{9,11},{10,... | collective-permute-start | bytes 442376 | tf_op jit(solution)/shard_map/ppermute | solution.py:359
  18.7 0.0 collective-permute-done.5.refs_3_
  18.7 0.5 %collective-permute-start.8 = (bf16[192,384]{1,0:T(8,128)(2,1)S(1)}, bf16[192,384]{1,0:T(8,128)(2,1)S(1)}, u32[]{:S(2)}, u32[]{:S(2)}) collective-permute-start(bf16[192,384]{1,0:T(8,128)(2,1)S(1)} %collective-permute-done.5.refs_3_), channel_id=1, source_target_pairs={{0,1},{1,0},{2,3},{3,2},{4,5},{5,4},{6,7},{7,6},{8,9},{9,8},{10,11... | collective-permute-start | bytes 442376 | tf_op jit(solution)/shard_map/ppermute | solution.py:359
  19.3 0.0 collective-permute-done.4.refs_1_
  19.3 0.9 %collective-permute-start.7 = (bf16[192,384]{1,0:T(8,128)(2,1)S(1)}, bf16[192,384]{1,0:T(8,128)(2,1)S(1)}, u32[]{:S(2)}, u32[]{:S(2)}) collective-permute-start(bf16[192,384]{1,0:T(8,128)(2,1)S(1)} %get-tuple-element.22.refs_0_), channel_id=1, source_target_pairs={{0,3},{1,2},{2,5},{3,4},{4,7},{5,6},{6,1},{7,0},{8,11},{9,10},{10,... | collective-permute-start | bytes 442376 | tf_op jit(solution)/shard_map/ppermute | solution.py:359
  20.2 0.0 collective-permute-done.1.refs_6_
  20.2 0.0 collective-permute-start.2
  20.2 6.0 %collective-permute-done.6.refs_4_ = bf16[192,384]{1,0:T(8,128)(2,1)S(1)} collective-permute-done((bf16[192,384]{1,0:T(8,128)(2,1)S(1)}, bf16[192,384]{1,0:T(8,128)(2,1)S(1)}, u32[]{:S(2)}, u32[]{:S(2)}) %collective-permute-start.6) | collective-permute-done | bytes 147488 | tf_op jit(solution)/shard_map/ppermute | solution.py:359
  26.2 0.0 collective-permute-done.8.refs_7_
  26.2 2.2 %collective-permute-done.7.refs_5_ = bf16[192,384]{1,0:T(8,128)(2,1)S(1)} collective-permute-done((bf16[192,384]{1,0:T(8,128)(2,1)S(1)}, bf16[192,384]{1,0:T(8,128)(2,1)S(1)}, u32[]{:S(2)}, u32[]{:S(2)}) %collective-permute-start.7) | collective-permute-done | bytes 147488 | tf_op jit(solution)/shard_map/ppermute | solution.py:359
  28.4 0.7 %collective-permute-done.3.near_ref = bf16[384,1536]{1,0:T(8,128)(2,1)S(1)} collective-permute-done((bf16[384,1536]{1,0:T(8,128)(2,1)}, bf16[384,1536]{1,0:T(8,128)(2,1)S(1)}, u32[]{:S(2)}, u32[]{:S(2)}) %collective-permute-start.3) | collective-permute-done | bytes 1179680 | tf_op jit(solution)/shard_map/ppermute | solution.py:40
  29.1 0.0 collective-permute-start.9
  29.2 1.9 %collective-permute-start.10 = (bf16[64,768]{1,0:T(8,128)(2,1)S(1)}, bf16[64,768]{1,0:T(8,128)(2,1)S(1)}, u32[]{:S(2)}, u32[]{:S(2)}) collective-permute-start(bf16[64,768]{1,0:T(8,128)(2,1)S(1)} %side_by_side.1.refs_0_), channel_id=1, source_target_pairs={{0,2},{1,3},{2,4},{3,5},{4,6},{5,7},{6,0},{7,1},{8,10},{9,11},{10,... | collective-permute-start | bytes 294920 | tf_op jit(solution)/shard_map/ppermute | solution.py:359
  31.0 2.6 %collective-permute-start.11 = (bf16[64,768]{1,0:T(8,128)(2,1)S(1)}, bf16[64,768]{1,0:T(8,128)(2,1)S(1)}, u32[]{:S(2)}, u32[]{:S(2)}) collective-permute-start(bf16[64,768]{1,0:T(8,128)(2,1)S(1)} %side_by_side.1.refs_0_), channel_id=1, source_target_pairs={{0,4},{1,5},{2,6},{3,7},{4,0},{5,1},{6,2},{7,3},{8,12},{9,13},{10,... | collective-permute-start | bytes 294920 | tf_op jit(solution)/shard_map/ppermute | solution.py:359
  33.6 1.3 %collective-permute-start.12 = (bf16[64,768]{1,0:T(8,128)(2,1)S(1)}, bf16[64,768]{1,0:T(8,128)(2,1)S(1)}, u32[]{:S(2)}, u32[]{:S(2)}) collective-permute-start(bf16[64,768]{1,0:T(8,128)(2,1)S(1)} %side_by_side.1.refs_0_), channel_id=1, source_target_pairs={{0,6},{1,7},{2,0},{3,1},{4,2},{5,3},{6,4},{7,5},{8,14},{9,15},{10,... | collective-permute-start | bytes 294920 | tf_op jit(solution)/shard_map/ppermute | solution.py:359
  35.0 0.0 collective-permute-done.2.other_ref
  35.0 6.4 %first_part.1 = (bf16[2,384,128]{2,1,0:T(8,128)(2,1)S(1)}, bf16[1536,256]{1,0:T(8,128)(2,1)S(1)}, f32[2,3,384,128]{3,2,1,0:T(8,128)S(1)}) custom-call(s32[4,4]{1,0:T(4,128)} %mask_ref.3, s32[4]{0:T(128)} %count_ref.3, bf16[384,1536]{1,0:T(8,128)(2,1)} %bitcast.4, bf16[384,1536]{1,0:T(8,128)(2,1)S(1)} %collective-permute-done.2.other_ref, ...), custom_call_target="tpu_custom_call" | custom-call | flops 1000000000 | tf_op jit(solution)/shard_map/first_part/pallas_call | solution.py:60
  41.4 0.0 collective-permute-done.10.refs_1_
  41.4 0.0 collective-permute-done.11.refs_2_
  41.4 0.0 collective-permute-done.12.refs_3_
  41.5 0.0 collective-permute-done.9.far_ref
  41.5 4.5 %last_part.1 = (bf16[384,128]{1,0:T(8,128)(2,1)S(1)}, bf16[384,128]{1,0:T(8,128)(2,1)S(1)}, bf16[256,768]{1,0:T(8,128)(2,1)S(1)}) custom-call(s32[4,4]{1,0:T(4,128)} %mask_ref.3, s32[4]{0:T(128)} %count_ref.3, bf16[1536,256]{1,0:T(8,128)(2,1)S(1)} %get-tuple-element.23.weight_ref, bf16[384,1536]{1,0:T(8,128)(2,1)S(1)} %collective-permute-done.3.near_ref, ...), custom_call_target="tpu_custom_call" | custom-call | flops 1000000000 | tf_op jit(solution)/shard_map/last_part/pallas_call | solution.py:60
  46.0 0.1 collective-permute-start.14
  46.1 0.5 %collective-permute-start.13 = (bf16[384,128]{1,0:T(8,128)(2,1)S(1)}, bf16[384,128]{1,0:T(8,128)(2,1)S(1)}, u32[]{:S(2)}, u32[]{:S(2)}) collective-permute-start(bf16[384,128]{1,0:T(8,128)(2,1)S(1)} %get-tuple-element.29), channel_id=1, source_target_pairs={{0,8},{8,0},{16,24},{24,16},{1,9},{9,1},{17,25},{25,17},{2,10},{10... | collective-permute-start | bytes 294920 | tf_op jit(solution)/shard_map/ppermute | solution.py:36
  46.6 1.4 %collective-permute-done.13.partner_ref = bf16[384,128]{1,0:T(8,128)(2,1)S(1)} collective-permute-done((bf16[384,128]{1,0:T(8,128)(2,1)S(1)}, bf16[384,128]{1,0:T(8,128)(2,1)S(1)}, u32[]{:S(2)}, u32[]{:S(2)}) %collective-permute-start.13) | collective-permute-done | bytes 98336 | tf_op jit(solution)/shard_map/ppermute | solution.py:36
  47.9 0.0 collective-permute-done.14.out_partner_ref
  47.9 1.6 %project_out.1 = bf16[384,1536]{1,0:T(8,128)(2,1)} custom-call(bf16[384,128]{1,0:T(8,128)(2,1)S(1)} %get-tuple-element.28.own_ref, bf16[384,128]{1,0:T(8,128)(2,1)S(1)} %collective-permute-done.13.partner_ref, bf16[256,768]{1,0:T(8,128)(2,1)S(1)} %get-tuple-element.30.out_own_ref, bf16[256,768]{1,0:T(8,128)(2,1)S(1)} %collective-permute-done.14.out_partner_ref), custom_call_target="tpu_custom_call" | custom-call | tf_op jit(solution)/shard_map/project_out/pallas_call | solution.py:60
  (1 shorter events, 0.0 us)
Async XLA Ops:
  0.0 29.1 %collective-permute-start.3 = (bf16[384,1536]{1,0:T(8,128)(2,1)}, bf16[384,1536]{1,0:T(8,128)(2,1)S(1)}, u32[]{:S(2)}, u32[]{:S(2)}) collective-permute-start(bf16[384,1536]{1,0:T(8,128)(2,1)} %bitcast.2), channel_id=1, source_target_pairs={{0,16},{8,24},{16,0},{24,8},{1,17},{9,25},{17,1},{25,9},{2,18},{10... | collective-permute-start | bytes 3538952 | tf_op jit(solution)/shard_map/ppermute | solution.py:40
  4.0 10.6 %collective-permute-start = (bf16[192,384]{1,0:T(8,128)(2,1)S(1)}, bf16[192,384]{1,0:T(8,128)(2,1)S(1)}, u32[]{:S(2)}, u32[]{:S(2)}) collective-permute-start(bf16[192,384]{1,0:T(8,128)(2,1)S(1)} %get-tuple-element.22.refs_0_), channel_id=1, source_target_pairs={{0,4},{1,5},{2,6},{3,7},{4,0},{5,1},{6,2},{7,3},{8,12},{9,13},{10,... | collective-permute-start | bytes 442376 | tf_op jit(solution)/shard_map/ppermute | solution.py:359
  6.6 12.7 %collective-permute-start.4 = (bf16[256,384]{1,0:T(8,128)(2,1)S(1)}, bf16[256,384]{1,0:T(8,128)(2,1)S(1)}, u32[]{:S(2)}, u32[]{:S(2)}) collective-permute-start(bf16[256,384]{1,0:T(8,128)(2,1)S(1)} %get-tuple-element.21.refs_0_), channel_id=1, source_target_pairs={{0,1},{1,0},{2,3},{3,2},{4,5},{5,4},{6,7},{7,6},{8,9},{9,8},{10,11... | collective-permute-start | bytes 589832 | tf_op jit(solution)/shard_map/ppermute | solution.py:359
  8.1 10.6 %collective-permute-start.5 = (bf16[192,384]{1,0:T(8,128)(2,1)S(1)}, bf16[192,384]{1,0:T(8,128)(2,1)S(1)}, u32[]{:S(2)}, u32[]{:S(2)}) collective-permute-start(bf16[192,384]{1,0:T(8,128)(2,1)S(1)} %get-tuple-element.22.refs_0_), channel_id=1, source_target_pairs={{0,6},{1,7},{2,0},{3,1},{4,2},{5,3},{6,4},{7,5},{8,14},{9,15},{10,... | collective-permute-start | bytes 442376 | tf_op jit(solution)/shard_map/ppermute | solution.py:359
  14.6 5.6 %collective-permute-start.1 = (bf16[192,384]{1,0:T(8,128)(2,1)S(1)}, bf16[192,384]{1,0:T(8,128)(2,1)S(1)}, u32[]{:S(2)}, u32[]{:S(2)}) collective-permute-start(bf16[192,384]{1,0:T(8,128)(2,1)S(1)} %collective-permute-done.refs_2_), channel_id=1, source_target_pairs={{0,1},{1,0},{2,3},{3,2},{4,5},{5,4},{6,7},{7,6},{8,9},{9,8},{10,11... | collective-permute-start | bytes 442376 | tf_op jit(solution)/shard_map/ppermute | solution.py:359
  16.1 10.2 %collective-permute-start.6 = (bf16[192,384]{1,0:T(8,128)(2,1)S(1)}, bf16[192,384]{1,0:T(8,128)(2,1)S(1)}, u32[]{:S(2)}, u32[]{:S(2)}) collective-permute-start(bf16[192,384]{1,0:T(8,128)(2,1)S(1)} %get-tuple-element.22.refs_0_), channel_id=1, source_target_pairs={{0,2},{1,3},{2,4},{3,5},{4,6},{5,7},{6,0},{7,1},{8,10},{9,11},{10,... | collective-permute-start | bytes 442376 | tf_op jit(solution)/shard_map/ppermute | solution.py:359
  18.7 7.5 %collective-permute-start.8 = (bf16[192,384]{1,0:T(8,128)(2,1)S(1)}, bf16[192,384]{1,0:T(8,128)(2,1)S(1)}, u32[]{:S(2)}, u32[]{:S(2)}) collective-permute-start(bf16[192,384]{1,0:T(8,128)(2,1)S(1)} %collective-permute-done.5.refs_3_), channel_id=1, source_target_pairs={{0,1},{1,0},{2,3},{3,2},{4,5},{5,4},{6,7},{7,6},{8,9},{9,8},{10,11... | collective-permute-start | bytes 442376 | tf_op jit(solution)/shard_map/ppermute | solution.py:359
  19.3 9.2 %collective-permute-start.7 = (bf16[192,384]{1,0:T(8,128)(2,1)S(1)}, bf16[192,384]{1,0:T(8,128)(2,1)S(1)}, u32[]{:S(2)}, u32[]{:S(2)}) collective-permute-start(bf16[192,384]{1,0:T(8,128)(2,1)S(1)} %get-tuple-element.22.refs_0_), channel_id=1, source_target_pairs={{0,3},{1,2},{2,5},{3,4},{4,7},{5,6},{6,1},{7,0},{8,11},{9,10},{10,... | collective-permute-start | bytes 442376 | tf_op jit(solution)/shard_map/ppermute | solution.py:359
  20.2 14.8 %collective-permute-start.2 = (bf16[384,1536]{1,0:T(8,128)(2,1)}, bf16[384,1536]{1,0:T(8,128)(2,1)S(1)}, u32[]{:S(2)}, u32[]{:S(2)}) collective-permute-start(bf16[384,1536]{1,0:T(8,128)(2,1)} %bitcast.3), channel_id=1, source_target_pairs={{0,8},{8,0},{16,24},{24,16},{1,9},{9,1},{17,25},{25,17},{2,10},{10... | collective-permute-start | bytes 3538952 | tf_op jit(solution)/shard_map/ppermute | solution.py:36
  29.1 12.3 %collective-permute-start.9 = (bf16[384,1536]{1,0:T(8,128)(2,1)S(1)}, bf16[384,1536]{1,0:T(8,128)(2,1)S(1)}, u32[]{:S(2)}, u32[]{:S(2)}) collective-permute-start(bf16[384,1536]{1,0:T(8,128)(2,1)S(1)} %collective-permute-done.3.near_ref), channel_id=1, source_target_pairs={{0,8},{8,0},{16,24},{24,16},{1,9},{9,1},{17,25},{25,17},{2,10},{10... | collective-permute-start | bytes 3538952 | tf_op jit(solution)/shard_map/ppermute | solution.py:36
  29.2 12.3 %collective-permute-start.10 = (bf16[64,768]{1,0:T(8,128)(2,1)S(1)}, bf16[64,768]{1,0:T(8,128)(2,1)S(1)}, u32[]{:S(2)}, u32[]{:S(2)}) collective-permute-start(bf16[64,768]{1,0:T(8,128)(2,1)S(1)} %side_by_side.1.refs_0_), channel_id=1, source_target_pairs={{0,2},{1,3},{2,4},{3,5},{4,6},{5,7},{6,0},{7,1},{8,10},{9,11},{10,... | collective-permute-start | bytes 294920 | tf_op jit(solution)/shard_map/ppermute | solution.py:359
  31.0 10.4 %collective-permute-start.11 = (bf16[64,768]{1,0:T(8,128)(2,1)S(1)}, bf16[64,768]{1,0:T(8,128)(2,1)S(1)}, u32[]{:S(2)}, u32[]{:S(2)}) collective-permute-start(bf16[64,768]{1,0:T(8,128)(2,1)S(1)} %side_by_side.1.refs_0_), channel_id=1, source_target_pairs={{0,4},{1,5},{2,6},{3,7},{4,0},{5,1},{6,2},{7,3},{8,12},{9,13},{10,... | collective-permute-start | bytes 294920 | tf_op jit(solution)/shard_map/ppermute | solution.py:359
  33.6 7.8 %collective-permute-start.12 = (bf16[64,768]{1,0:T(8,128)(2,1)S(1)}, bf16[64,768]{1,0:T(8,128)(2,1)S(1)}, u32[]{:S(2)}, u32[]{:S(2)}) collective-permute-start(bf16[64,768]{1,0:T(8,128)(2,1)S(1)} %side_by_side.1.refs_0_), channel_id=1, source_target_pairs={{0,6},{1,7},{2,0},{3,1},{4,2},{5,3},{6,4},{7,5},{8,14},{9,15},{10,... | collective-permute-start | bytes 294920 | tf_op jit(solution)/shard_map/ppermute | solution.py:359
  46.0 1.9 %collective-permute-start.14 = (bf16[256,768]{1,0:T(8,128)(2,1)S(1)}, bf16[256,768]{1,0:T(8,128)(2,1)S(1)}, u32[]{:S(2)}, u32[]{:S(2)}) collective-permute-start(bf16[256,768]{1,0:T(8,128)(2,1)S(1)} %get-tuple-element.30.out_own_ref), channel_id=1, source_target_pairs={{0,8},{8,0},{16,24},{24,16},{1,9},{9,1},{17,25},{25,17},{2,10},{10... | collective-permute-start | bytes 1179656 | tf_op jit(solution)/shard_map/ppermute | solution.py:36
  46.1 1.9 %collective-permute-start.13 = (bf16[384,128]{1,0:T(8,128)(2,1)S(1)}, bf16[384,128]{1,0:T(8,128)(2,1)S(1)}, u32[]{:S(2)}, u32[]{:S(2)}) collective-permute-start(bf16[384,128]{1,0:T(8,128)(2,1)S(1)} %get-tuple-element.29), channel_id=1, source_target_pairs={{0,8},{8,0},{16,24},{24,16},{1,9},{9,1},{17,25},{25,17},{2,10},{10... | collective-permute-start | bytes 294920 | tf_op jit(solution)/shard_map/ppermute | solution.py:36

commit v4 on v3

v4 whole, which is shorter than its diff:
```python
import jax
import jax.numpy as jnp
from jax import lax
from jax.experimental import pallas as pl
from jax.experimental.pallas import tpu as pltpu
from jax.sharding import PartitionSpec as P

E = 64
LANES = 128
CORES = 2
NEG = -1e30
ROWS = 192
COST1 = 1_000_000_000
COST = 1_000_000_000

VMEM = pl.BlockSpec(memory_space=pltpu.VMEM)
SMEM = pl.BlockSpec(memory_space=pltpu.SMEM)
HBM = pl.BlockSpec(memory_space=pltpu.HBM)


def grid_of(fsdp_count):
    x_count = 1
    while (2 * x_count) ** 2 <= fsdp_count and fsdp_count % (2 * x_count) == 0:
        x_count *= 2
    return fsdp_count // x_count, x_count


def rotation(z_count, x_count, z_step, x_step):
    return [
        (z * x_count + x, (z + z_step) % z_count * x_count + (x + x_step) % x_count)
        for z in range(z_count)
        for x in range(x_count)
    ]


def core_swap(array, seq_count):
    return lax.ppermute(array, "seq", [(s, s ^ 1) for s in range(seq_count)])


def y_rotation(array, seq_count, step):
    return lax.ppermute(array, "seq", [(s, (s + CORES * step) % seq_count) for s in range(seq_count)])


def call(kernel, name, in_specs, out_shapes, out_specs=None, scratch_shapes=(), cost=0):
    out_specs = [VMEM] * len(out_shapes) if out_specs is None else out_specs
    shapes = [
        pltpu.VMEM(shape.shape, shape.dtype) if spec is VMEM else shape for shape, spec in zip(out_shapes, out_specs)
    ]
    inner = pl.pallas_call(
        kernel,
        out_shape=shapes,
        in_specs=in_specs,
        out_specs=out_specs,
        scratch_shapes=scratch_shapes,
        cost_estimate=pl.CostEstimate(flops=cost, bytes_accessed=0, transcendentals=0) if cost else None,
        compiler_params=pltpu.CompilerParams(vmem_limit_bytes=24 << 20),
        name=name,
    )

    def run(*args):
        return inner(
            *[
                pltpu.with_memory_space_constraint(arg, pltpu.HBM if spec is SMEM else spec.memory_space)
                for arg, spec in zip(args, in_specs)
            ]
        )

    return run


def shaped(shape, dtype):
    return jax.ShapeDtypeStruct(shape, dtype)


def strips(width, columns):
    strip = min(width, columns)
    return [(start, strip) for start in range(0, width, strip)]


def halves(qkv_weight, out_weight):
    rows, columns = qkv_weight.shape
    head_columns = columns // 3
    own = head_columns // CORES
    out_rows, width = out_weight.shape
    side = width // CORES
    pieces = strips(side, 3 * own)

    def kernel(qkv_ref, out_ref, half_ref, packed_ref, sems):
        core = lax.rem(lax.axis_index("seq"), CORES)
        copies = []

        def copy(source, target):
            copies.append(pltpu.make_async_copy(source, target, sems.at[len(copies)]))
            copies[-1].start()

        for part in range(3):
            source = qkv_ref.at[:, pl.ds(pl.multiple_of(part * head_columns + core * own, LANES), own)]
            lanes = slice(part * own, (part + 1) * own)
            copy(source, half_ref.at[:, lanes])
            copy(source, packed_ref.at[:rows, lanes])
        for piece, (start, strip) in enumerate(pieces):
            first = rows + piece * out_rows
            copy(
                out_ref.at[:, pl.ds(pl.multiple_of(core * side + start, LANES), strip)],
                packed_ref.at[first : first + out_rows, :strip],
            )
        for each in copies:
            each.wait()

    return call(
        kernel,
        "halves",
        [HBM, HBM],
        [
            shaped((rows, 3 * own), qkv_weight.dtype),
            shaped((rows + len(pieces) * out_rows, 3 * own), qkv_weight.dtype),
        ],
        scratch_shapes=[pltpu.SemaphoreType.DMA((6 + len(pieces),))],
    )(qkv_weight, out_weight)


def side_by_side(blocks, x_count, rows, out_rows, side):
    pieces = strips(side, blocks[0].shape[1])

    def kernel(*refs):
        x_index = lax.rem(lax.axis_index("fsdp"), x_count)
        for step in range(x_count):
            place = lax.rem(x_index + x_count - step, x_count)
            for piece, (start, strip) in enumerate(pieces):
                first = rows + piece * out_rows
                refs[x_count][pl.ds(pl.multiple_of(place * out_rows, 16), out_rows), start : start + strip] = refs[step][
                    first : first + out_rows, :strip
                ]

    return call(kernel, "side_by_side", [VMEM] * x_count, [shaped((x_count * out_rows, side), blocks[0].dtype)])(
        *blocks
    )[0]


def pair_up(own, got, units, shift, x_count):
    rows, columns = own.shape
    each = rows // units

    def kernel(own_ref, got_ref, pair_ref):
        bit = lax.rem(lax.axis_index("fsdp") // (x_count * shift), 2)
        for unit in range(units):
            piece = slice(unit * each, (unit + 1) * each)
            pair_ref[pl.ds(pl.multiple_of((2 * unit + bit) * each, 16), each), :] = own_ref[piece, :]
            pair_ref[pl.ds(pl.multiple_of((2 * unit + 1 - bit) * each, 16), each), :] = got_ref[piece, :]

    return call(kernel, "pair_up", [VMEM, VMEM], [shaped((2 * rows, columns), own.dtype)])(own, got)[0]


def lane_pick(per_head):
    lane = lax.broadcasted_iota(jnp.int32, (1, LANES), 1)
    picked = per_head[0]
    for head in range(1, len(per_head)):
        picked = jnp.where(lane >= head * E, per_head[head], picked)
    return jnp.broadcast_to(picked, (picked.shape[0], LANES))


def attend_part(queries, keys, values, bias):
    lane = lax.broadcasted_iota(jnp.int32, (1, LANES), 1)
    maxima, sums, outs = [], [], []
    for head in range(LANES // E):
        inside = (lane >= head * E) & (lane < (head + 1) * E)
        head_queries = jnp.where(inside, queries, jnp.zeros_like(queries))
        scores = lax.dot_general(head_queries, keys, (((1,), (1,)), ((), ())), preferred_element_type=jnp.float32)
        scores = scores + bias
        row_max = jnp.max(scores, axis=1, keepdims=True)
        numerators = jnp.exp(scores - row_max).astype(values.dtype)
        summed = jnp.dot(numerators, values, preferred_element_type=jnp.float32)
        maxima.append(row_max)
        sums.append(summed[:, LANES:])
        outs.append(summed[:, :LANES])
    return lane_pick(maxima), lane_pick(sums), lane_pick(outs)


def merge(old, new):
    top = jnp.maximum(old[0], new[0])
    keep = jnp.exp(old[0] - top)
    add = jnp.exp(new[0] - top)
    return top, old[1] * keep + new[1] * add, old[2] * keep + new[2] * add


def key_bias(mask_ref, count_ref, tile, key_tile, slots):
    slot = lax.broadcasted_iota(jnp.int32, (1, slots), 1)
    live = jnp.where(mask_ref[tile, key_tile] > 0, count_ref[key_tile], 0)
    return jnp.where(slot < live, 0.0, NEG)


def project(z_count, x_count, shifts, blocks, latents_own, latents_other):
    count = len(blocks)
    columns = blocks[0].shape[1]
    own = columns // 3
    row_count, depth = latents_own.shape
    rows = depth // count
    dtype = latents_own.dtype
    scale = float(E) ** -0.5

    def kernel(own_ref, other_ref, *refs):
        block_refs = refs[:count]
        queries_ref, weight_ref, key_value_ref, latents_ref, sem = refs[count:]
        fetch = pltpu.make_async_copy(own_ref, latents_ref, sem)
        fetch.start()
        fsdp_index = lax.axis_index("fsdp")
        z_index = fsdp_index // x_count
        x_index = lax.rem(fsdp_index, x_count)
        for (dz, dx), block_ref in zip(shifts, block_refs):
            place = lax.rem(z_index + z_count - dz, z_count) * x_count + lax.rem(x_index + x_count - dx, x_count)
            weight_ref[pl.ds(pl.multiple_of(place * rows, 16), rows), :] = block_ref[:rows, :]
        for member, from_ref in ((1, other_ref), (0, latents_ref)):
            if member == 0:
                fetch.wait()
            projected = jnp.dot(from_ref[...], weight_ref[...], preferred_element_type=jnp.float32).astype(dtype)
            queries_ref[member] = projected[:, :own] * jnp.asarray(scale, dtype)
            key_value_ref[member * row_count : (member + 1) * row_count, :] = projected[:, own:]

    return call(
        kernel,
        "project",
        [HBM] + [VMEM] * (count + 1),
        [
            shaped((CORES, row_count, own), dtype),
            shaped((depth, columns), dtype),
            shaped((CORES * row_count, 2 * own), dtype),
        ],
        scratch_shapes=[pltpu.VMEM((row_count, depth), dtype), pltpu.SemaphoreType.DMA(())],
        cost=COST1,
    )(latents_own, latents_other, *blocks)


def attend(seq_count, sources, key_value, state, last, weight, queries, tile_mask, tile_counts):
    columns = weight.shape[1]
    own = columns // 3
    row_count = queries.shape[1]
    dtype = queries.dtype
    groups = own // LANES
    local_rows = 0 if key_value is None else CORES * row_count
    slots = local_rows + len(sources) * row_count
    given = [weight, queries] + [latents for latents, _, _ in sources]
    given += [array for array in (key_value, state) if array is not None]

    def kernel(mask_ref, count_ref, weight_ref, queries_ref, *refs):
        latents_refs, refs = refs[: len(sources)], list(refs[len(sources) :])
        key_value_ref = None if key_value is None else refs.pop(0)
        old_ref = None if state is None else refs.pop(0)
        values_ref, keys_ref = refs.pop(), refs.pop()
        seq_index = lax.axis_index("seq")
        core = lax.rem(seq_index, CORES)
        chip_tile = seq_index - core
        tiles = [chip_tile + core, chip_tile + 1 - core]
        key_tiles = list(tiles) if local_rows else []

        def place(start, keys, values):
            rows = slice(start, start + keys.shape[0])
            keys_ref[rows, :] = keys
            for group in range(groups):
                first = 2 * group * LANES
                values_ref[rows, first : first + LANES] = values[:, group * LANES : (group + 1) * LANES]
                values_ref[rows, first + LANES : first + 2 * LANES] = jnp.ones((keys.shape[0], LANES), dtype)

        if local_rows:
            place(0, key_value_ref[:, :own], key_value_ref[:, own:])
        for part, (_, y_step, swapped) in enumerate(sources):
            projected = jnp.dot(
                latents_refs[part][...], weight_ref[:, own:], preferred_element_type=jnp.float32
            ).astype(dtype)
            place(local_rows + part * row_count, projected[:, :own], projected[:, own:])
            from_same = lax.rem(seq_index + seq_count - CORES * y_step, seq_count)
            key_tiles.append(from_same + 1 - 2 * core if swapped else from_same)
        for member in range(CORES):
            bias = jnp.concatenate(
                [key_bias(mask_ref, count_ref, tiles[member], key_tile, row_count) for key_tile in key_tiles], axis=1
            )
            for group in range(groups):
                lanes = slice(group * LANES, (group + 1) * LANES)
                for start in range(0, row_count, ROWS):
                    chunk = slice(start, start + ROWS)
                    parts = attend_part(
                        queries_ref[member, chunk, lanes],
                        keys_ref[:, lanes],
                        values_ref[:, 2 * group * LANES : 2 * (group + 1) * LANES],
                        bias,
                    )
                    if old_ref is not None:
                        parts = merge([old_ref[member, which, chunk, lanes] for which in range(3)], parts)
                    if last:
                        position = start + lax.broadcasted_iota(jnp.int32, (ROWS, 1), 0)
                        attended = jnp.where(position < count_ref[tiles[member]], parts[2] / parts[1], 0.0)
                        refs[member][chunk, lanes] = attended.astype(dtype)
                    else:
                        for which, part in enumerate(parts):
                            refs[0][member, which, chunk, lanes] = part

    if last:
        out_shapes = [shaped((row_count, own), dtype)] * CORES
    else:
        out_shapes = [shaped((CORES, 3, row_count, own), jnp.float32)]
    return call(
        kernel,
        "attend_last" if last else "attend",
        [SMEM, SMEM] + [VMEM] * len(given),
        out_shapes,
        scratch_shapes=[pltpu.VMEM((slots, own), dtype), pltpu.VMEM((slots, 2 * own), dtype)],
        cost=COST,
    )(tile_mask, tile_counts, *given)


def project_out(attended_own, attended_partner, out_own, out_partner):
    row_count, own = attended_own.shape
    side = out_own.shape[1]
    dtype = attended_own.dtype

    def kernel(own_ref, partner_ref, out_own_ref, out_partner_ref, result_ref, staged_ref, sems):
        core = lax.rem(lax.axis_index("seq"), CORES)
        own_rows = pl.ds(pl.multiple_of(core * own, 16), own)
        partner_rows = pl.ds(pl.multiple_of((1 - core) * own, 16), own)
        copies = []
        for half, weight_ref in enumerate((out_own_ref, out_partner_ref)):
            total = jnp.dot(own_ref[...], weight_ref[own_rows, :], preferred_element_type=jnp.float32)
            total += jnp.dot(partner_ref[...], weight_ref[partner_rows, :], preferred_element_type=jnp.float32)
            staged_ref[half] = total.astype(dtype)
            start = pl.multiple_of((core if half == 0 else 1 - core) * side, LANES)
            copies.append(
                pltpu.make_async_copy(staged_ref.at[half], result_ref.at[:, pl.ds(start, side)], sems.at[half])
            )
            copies[-1].start()
        for copy in copies:
            copy.wait()

    return call(
        kernel,
        "project_out",
        [VMEM] * 4,
        [shaped((row_count, CORES * side), dtype)],
        [HBM],
        scratch_shapes=[pltpu.VMEM((CORES, row_count, side), dtype), pltpu.SemaphoreType.DMA((CORES,))],
    )(attended_own, attended_partner, out_own, out_partner)[0]


def after(array, *others):
    return lax.optimization_barrier((array, *others))[0]


def local(latents, qkv_weight, out_weight, tile_mask, tile_counts):
    seq_count = lax.axis_size("seq")
    fsdp_count = lax.axis_size("fsdp")
    z_count, x_count = grid_of(fsdp_count)
    chips = seq_count // CORES
    latents_own = latents[0]

    def hop(array, z_step, x_step):
        return lax.ppermute(array, "fsdp", rotation(z_count, x_count, z_step, x_step))

    def flip(array, shift):
        return lax.ppermute(array, "fsdp", [(f, f ^ (shift * x_count)) for f in range(fsdp_count)])

    along_y = [y_rotation(latents_own, seq_count, step) for step in range(1, chips)]
    latents_other = core_swap(latents_own, seq_count)
    half, packed = halves(qkv_weight, out_weight)

    came = {(0, 0): half}
    for x_step in range(1, x_count):
        came[0, x_step] = hop(after(packed, latents_other), 0, x_step)
    beside = [came[0, x_step] for x_step in range(1, x_count)]
    order = [step for step in range(2, z_count)] + [1]
    for z_step in order:
        came[z_step, 0] = hop(half, z_step, 0)
        for x_step in range(1, x_count):
            if z_step > 1:
                came[z_step, x_step] = hop(after(came[z_step, 0], came[0, 1]), 0, x_step)
            else:
                came[z_step, x_step] = hop(after(half, *beside, came[2, 0]), z_step, x_step)

    out_own = side_by_side([packed] + beside, x_count, half.shape[0], out_weight.shape[0], out_weight.shape[1] // CORES)
    units, shift = 1, z_count // 2
    while shift > 1:
        out_own = pair_up(out_own, flip(after(out_own, came[1, 0], came[2, 1]), shift), units, shift, x_count)
        units, shift = 2 * units, shift // 2
    out_got = flip(out_own, shift)

    queries, weight, key_value = project(
        z_count, x_count, list(came), list(came.values()), latents_own, latents_other
    )
    steps = [(step, swapped) for step in range(1, chips) for swapped in (False, True)]
    near, _, _ = lax.optimization_barrier((along_y, key_value, out_own))
    tokens = {(step, False): near[step - 1] for step in range(1, chips)}
    tokens.update({(step, True): core_swap(near[step - 1], seq_count) for step in range(1, chips)})
    state = None
    for first in range(-1, len(steps), 2):
        sources = [(tokens[step], *step) for step in steps[max(first, 0) : first + 2]]
        last = first + 2 > len(steps)
        result = attend(
            seq_count,
            sources,
            key_value if first < 0 else None,
            state,
            last,
            weight,
            queries,
            tile_mask,
            tile_counts,
        )
        if first < 0:
            out_own = pair_up(out_own, after(out_got, result[0]), units, shift, x_count)
            out_partner = core_swap(out_own, seq_count)
        state = None if last else result[0]
    attended_own, attended_other = result
    attended_partner = core_swap(attended_other, seq_count)
    return project_out(attended_own, attended_partner, out_own, out_partner)[None]


def solution(mesh):
    return jax.shard_map(
        local,
        mesh=mesh,
        in_specs=(P("fsdp", "seq", None), P("fsdp", None), P("fsdp", None), P(), P()),
        out_specs=P("fsdp", "seq", None),
        check_vma=False,
    )
```

time: 49.8 us -> 48.1 us (0.966)
  waiting for transfers between devices: 15.4 us -> 12.3 us
  starting transfers between devices: 20.4 us -> 22 us
    ppermute x0 -> x2, starting transfers between devices: none -> 5.62 us  [flip(): lax.ppermute(array, 'fsdp', [(f, f ^ shift * x_count) for f in range(fsdp...]
    ppermute x10 -> x7, starting transfers between devices: 16.9 us -> 12.8 us  [hop(): lax.ppermute(array, 'fsdp', rotation(z_count, x_count, z_step, x_step))]
    ppermute x10 -> x7, waiting for transfers between devices: 13.3 us -> 10.1 us  [hop(): lax.ppermute(array, 'fsdp', rotation(z_count, x_count, z_step, x_step))]
    ppermute x0 -> x2, waiting for transfers between devices: none -> 1.32 us  [flip(): lax.ppermute(array, 'fsdp', [(f, f ^ shift * x_count) for f in range(fsdp...]
    ppermute x1, waiting for transfers between devices: 0.71 us -> 0.01 us  [y_rotation(): lax.ppermute(array, 'seq', [(s, (s + CORES * step) % seq_count) for s in...]
    ppermute x4, starting transfers between devices: 0.57 us -> 1.15 us  [core_swap(): return lax.ppermute(array, 'seq', [(s, s ^ 1) for s in range(seq_count)])]
    pallas_call x5 -> x8, Pallas kernels: 13.6 us -> 13.4 us  [run(): inner(*[pltpu.with_memory_space_constraint(arg, pltpu.HBM if spec is SMEM...]
  transfers between devices with their start and end apart: 15 -> 14, of which waited for: 5 -> 5; matrix products, arithmetic and copies ran while one was open for 0% -> 0% of each run, Pallas kernels for 15% -> 25%
where the time goes in v4:
time: 48.1 us; the launch traced here: 47.9 us
  starting transfers between devices  22 us (46%)
  Pallas kernels  13.4 us (28%)
  waiting for transfers between devices  12.3 us (26%)
    pallas_call x8, Pallas kernels, run(): inner(*[pltpu.with_memory_space_constraint(arg, pltpu.HBM if spec is SMEM...  13.4 us
    ppermute x7, starting transfers between devices, hop(): lax.ppermute(array, 'fsdp', rotation(z_count, x_count, z_step, x_step))  12.8 us
    ppermute x7, waiting for transfers between devices, hop(): lax.ppermute(array, 'fsdp', rotation(z_count, x_count, z_step, x_step))  10.1 us
    ppermute x2, starting transfers between devices, flip(): lax.ppermute(array, 'fsdp', [(f, f ^ shift * x_count) for f in range(fsdp...  5.62 us
    ppermute x1, starting transfers between devices, y_rotation(): lax.ppermute(array, 'seq', [(s, (s + CORES * step) % seq_count) for s in...  2.52 us
    ppermute x2, waiting for transfers between devices, flip(): lax.ppermute(array, 'fsdp', [(f, f ^ shift * x_count) for f in range(fsdp...  1.32 us
    ppermute x4, starting transfers between devices, core_swap(): return lax.ppermute(array, 'seq', [(s, s ^ 1) for s in range(seq_count)])  1.15 us
  transfers between devices with their start and end apart: 14, of which 5 were waited for; matrix products, arithmetic and copies ran while one was open for 0% of the time, Pallas kernels for 25%

profile of v4, /device:TPU:0, one launch (start us, length us, event | category | flops | bytes accessed | tf_op | source)
XLA Modules:
  0.0 47.9 jit_solution(9691924245731026006)
XLA Ops:
  0.0 0.5 collective-permute-start
  0.5 2.5 %collective-permute-start.8 = (bf16[384,1536]{1,0:T(8,128)(2,1)}, bf16[384,1536]{1,0:T(8,128)(2,1)S(1)}, u32[]{:S(2)}, u32[]{:S(2)}) collective-permute-start(bf16[384,1536]{1,0:T(8,128)(2,1)} %bitcast.3), channel_id=1, source_target_pairs={{0,16},{8,24},{16,0},{24,8},{1,17},{9,25},{17,1},{25,9},{2,18},{10... | collective-permute-start | bytes 3538952 | tf_op jit(solution)/shard_map/ppermute | solution.py:41
  3.0 1.0 %halves.1 = (bf16[192,384]{1,0:T(8,128)(2,1)S(1)}, bf16[256,384]{1,0:T(8,128)(2,1)S(1)}) custom-call(bf16[192,768]{1,0:T(8,128)(2,1)} %qkv_ref.1, bf16[32,1536]{1,0:T(8,128)(2,1)} %out_ref.1), custom_call_target="tpu_custom_call" | custom-call | tf_op jit(solution)/shard_map/halves/pallas_call | solution.py:61
  4.0 0.0 collective-permute-done.other_ref
  4.0 2.0 %collective-permute-start.1 = (bf16[256,384]{1,0:T(8,128)(2,1)S(1)}, bf16[256,384]{1,0:T(8,128)(2,1)S(1)}, u32[]{:S(2)}, u32[]{:S(2)}) collective-permute-start(bf16[256,384]{1,0:T(8,128)(2,1)S(1)} %get-tuple-element.21.refs_0_), channel_id=1, source_target_pairs={{0,1},{1,0},{2,3},{3,2},{4,5},{5,4},{6,7},{7,6},{8,9},{9,8},{10,11... | collective-permute-start | bytes 589832 | tf_op jit(solution)/shard_map/ppermute | solution.py:354
  6.0 2.6 %collective-permute-start.2 = (bf16[192,384]{1,0:T(8,128)(2,1)S(1)}, bf16[192,384]{1,0:T(8,128)(2,1)S(1)}, u32[]{:S(2)}, u32[]{:S(2)}) collective-permute-start(bf16[192,384]{1,0:T(8,128)(2,1)S(1)} %get-tuple-element.24.refs_0_), channel_id=1, source_target_pairs={{0,4},{1,5},{2,6},{3,7},{4,0},{5,1},{6,2},{7,3},{8,12},{9,13},{10,... | collective-permute-start | bytes 442376 | tf_op jit(solution)/shard_map/ppermute | solution.py:354
  8.6 1.3 %collective-permute-start.4 = (bf16[192,384]{1,0:T(8,128)(2,1)S(1)}, bf16[192,384]{1,0:T(8,128)(2,1)S(1)}, u32[]{:S(2)}, u32[]{:S(2)}) collective-permute-start(bf16[192,384]{1,0:T(8,128)(2,1)S(1)} %get-tuple-element.24.refs_0_), channel_id=1, source_target_pairs={{0,6},{1,7},{2,0},{3,1},{4,2},{5,3},{6,4},{7,5},{8,14},{9,15},{10,... | collective-permute-start | bytes 442376 | tf_op jit(solution)/shard_map/ppermute | solution.py:354
  9.9 0.7 %collective-permute-start.6 = (bf16[192,384]{1,0:T(8,128)(2,1)S(1)}, bf16[192,384]{1,0:T(8,128)(2,1)S(1)}, u32[]{:S(2)}, u32[]{:S(2)}) collective-permute-start(bf16[192,384]{1,0:T(8,128)(2,1)S(1)} %get-tuple-element.24.refs_0_), channel_id=1, source_target_pairs={{0,2},{1,3},{2,4},{3,5},{4,6},{5,7},{6,0},{7,1},{8,10},{9,11},{10,... | collective-permute-start | bytes 442376 | tf_op jit(solution)/shard_map/ppermute | solution.py:354
  10.6 7.2 %collective-permute-done.2.refs_2_ = bf16[192,384]{1,0:T(8,128)(2,1)S(1)} collective-permute-done((bf16[192,384]{1,0:T(8,128)(2,1)S(1)}, bf16[192,384]{1,0:T(8,128)(2,1)S(1)}, u32[]{:S(2)}, u32[]{:S(2)}) %collective-permute-start.2) | collective-permute-done | bytes 147488 | tf_op jit(solution)/shard_map/ppermute | solution.py:354
  17.9 0.0 collective-permute-done.1.refs_1_
  17.9 0.0 collective-permute-start.3
  17.9 0.0 collective-permute-done.4.refs_4_
  17.9 2.0 %collective-permute-start.5 = (bf16[192,384]{1,0:T(8,128)(2,1)S(1)}, bf16[192,384]{1,0:T(8,128)(2,1)S(1)}, u32[]{:S(2)}, u32[]{:S(2)}) collective-permute-start(bf16[192,384]{1,0:T(8,128)(2,1)S(1)} %collective-permute-done.4.refs_4_), channel_id=1, source_target_pairs={{0,1},{1,0},{2,3},{3,2},{4,5},{5,4},{6,7},{7,6},{8,9},{9,8},{10,11... | collective-permute-start | bytes 442376 | tf_op jit(solution)/shard_map/ppermute | solution.py:354
  19.9 4.1 %collective-permute-start.7 = (bf16[192,384]{1,0:T(8,128)(2,1)S(1)}, bf16[192,384]{1,0:T(8,128)(2,1)S(1)}, u32[]{:S(2)}, u32[]{:S(2)}) collective-permute-start(bf16[192,384]{1,0:T(8,128)(2,1)S(1)} %get-tuple-element.24.refs_0_), channel_id=1, source_target_pairs={{0,3},{1,2},{2,5},{3,4},{4,7},{5,6},{6,1},{7,0},{8,11},{9,10},{10,... | collective-permute-start | bytes 442376 | tf_op jit(solution)/shard_map/ppermute | solution.py:354
  24.0 0.0 collective-permute-done.6.refs_6_
  24.0 0.0 collective-permute-done.3.refs_3_
  24.1 1.1 %collective-permute-start.9 = (bf16[64,768]{1,0:T(8,128)(2,1)S(1)}, bf16[64,768]{1,0:T(8,128)(2,1)S(1)}, u32[]{:S(2)}, u32[]{:S(2)}) collective-permute-start(bf16[64,768]{1,0:T(8,128)(2,1)S(1)} %side_by_side.1.own_ref), channel_id=1, source_target_pairs={{0,4},{1,5},{2,6},{3,7},{4,0},{5,1},{6,2},{7,3},{8,12},{9,13},{10,... | collective-permute-start | bytes 294920 | tf_op jit(solution)/shard_map/ppermute | solution.py:357
  25.1 0.0 collective-permute-done.5.refs_5_
  25.1 2.8 %collective-permute-done.7.refs_7_ = bf16[192,384]{1,0:T(8,128)(2,1)S(1)} collective-permute-done((bf16[192,384]{1,0:T(8,128)(2,1)S(1)}, bf16[192,384]{1,0:T(8,128)(2,1)S(1)}, u32[]{:S(2)}, u32[]{:S(2)}) %collective-permute-start.7) | collective-permute-done | bytes 147488 | tf_op jit(solution)/shard_map/ppermute | solution.py:354
  27.9 2.2 %project.1 = (bf16[2,384,128]{2,1,0:T(8,128)(2,1)S(1)}, bf16[1536,384]{1,0:T(8,128)(2,1)S(1)}, bf16[768,256]{1,0:T(8,128)(2,1)S(1)}) custom-call(bf16[384,1536]{1,0:T(8,128)(2,1)} %bitcast.4, bf16[384,1536]{1,0:T(8,128)(2,1)S(1)} %collective-permute-done.other_ref, bf16[192,384]{1,0:T(8,128)(2,1)S(1)} %get-tuple-element.24.refs_0_, ...), custom_call_target="tpu_custom_call" | custom-call | flops 1000000000 | tf_op jit(solution)/shard_map/project/pallas_call | solution.py:61
  30.1 0.9 %collective-permute-done.9.got_ref = bf16[64,768]{1,0:T(8,128)(2,1)S(1)} collective-permute-done((bf16[64,768]{1,0:T(8,128)(2,1)S(1)}, bf16[64,768]{1,0:T(8,128)(2,1)S(1)}, u32[]{:S(2)}, u32[]{:S(2)}) %collective-permute-start.9) | collective-permute-done | bytes 98336 | tf_op jit(solution)/shard_map/ppermute | solution.py:357
  31.1 0.0 collective-permute-done.8.refs_0_
  31.1 0.1 collective-permute-start.10
  31.1 4.5 %collective-permute-start.12 = (bf16[128,768]{1,0:T(8,128)(2,1)S(1)}, bf16[128,768]{1,0:T(8,128)(2,1)S(1)}, u32[]{:S(2)}, u32[]{:S(2)}) collective-permute-start(bf16[128,768]{1,0:T(8,128)(2,1)S(1)} %pair_up.2.own_ref), channel_id=1, source_target_pairs={{0,2},{1,3},{2,0},{3,1},{4,6},{5,7},{6,4},{7,5},{8,10},{9,11},{10,... | collective-permute-start | bytes 589832 | tf_op jit(solution)/shard_map/ppermute | solution.py:357
  35.7 5.1 %attend.1.refs_1_ = f32[2,3,384,128]{3,2,1,0:T(8,128)S(1)} custom-call(s32[4,4]{1,0:T(4,128)} %mask_ref.3, s32[4]{0:T(128)} %count_ref.3, bf16[1536,384]{1,0:T(8,128)(2,1)S(1)} %get-tuple-element.25.weight_ref, bf16[2,384,128]{2,1,0:T(8,128)(2,1)S(1)} %get-tuple-element.26.queries_ref, bf16[384,1536]{1,0:T(8,128)(2,1)S(1)} %collective-permute-done.8.refs_0_, ...), custom_call_target="tpu_custom_call" | custom-call | flops 1000000000 | tf_op jit(solution)/shard_map/attend/pallas_call | solution.py:61
  40.8 0.4 collective-permute-done.12.got_ref
  41.2 0.1 collective-permute-start.13
  41.3 0.0 collective-permute-done.10.refs_0_
  41.3 3.4 %attend_last.1 = (bf16[384,128]{1,0:T(8,128)(2,1)S(1)}, bf16[384,128]{1,0:T(8,128)(2,1)S(1)}) custom-call(s32[4,4]{1,0:T(4,128)} %mask_ref.3, s32[4]{0:T(128)} %count_ref.3, bf16[1536,384]{1,0:T(8,128)(2,1)S(1)} %get-tuple-element.25.weight_ref, bf16[2,384,128]{2,1,0:T(8,128)(2,1)S(1)} %get-tuple-element.26.queries_ref, ...), custom_call_target="tpu_custom_call" | custom-call | flops 1000000000 | tf_op jit(solution)/shard_map/attend_last/pallas_call | solution.py:61
  44.8 0.6 %collective-permute-start.11 = (bf16[384,128]{1,0:T(8,128)(2,1)S(1)}, bf16[384,128]{1,0:T(8,128)(2,1)S(1)}, u32[]{:S(2)}, u32[]{:S(2)}) collective-permute-start(bf16[384,128]{1,0:T(8,128)(2,1)S(1)} %get-tuple-element.31), channel_id=1, source_target_pairs={{0,8},{8,0},{16,24},{24,16},{1,9},{9,1},{17,25},{25,17},{2,10},{10... | collective-permute-start | bytes 294920 | tf_op jit(solution)/shard_map/ppermute | solution.py:37
  45.3 0.0 collective-permute-done.13.out_partner_ref
  45.3 0.9 %collective-permute-done.11.partner_ref = bf16[384,128]{1,0:T(8,128)(2,1)S(1)} collective-permute-done((bf16[384,128]{1,0:T(8,128)(2,1)S(1)}, bf16[384,128]{1,0:T(8,128)(2,1)S(1)}, u32[]{:S(2)}, u32[]{:S(2)}) %collective-permute-start.11) | collective-permute-done | bytes 98336 | tf_op jit(solution)/shard_map/ppermute | solution.py:37
  46.3 1.6 %project_out.1 = bf16[384,1536]{1,0:T(8,128)(2,1)} custom-call(bf16[384,128]{1,0:T(8,128)(2,1)S(1)} %get-tuple-element.30.own_ref, bf16[384,128]{1,0:T(8,128)(2,1)S(1)} %collective-permute-done.11.partner_ref, bf16[256,768]{1,0:T(8,128)(2,1)S(1)} %pair_up.3.out_own_ref, bf16[256,768]{1,0:T(8,128)(2,1)S(1)} %collective-permute-done.13.out_partner_ref), custom_call_target="tpu_custom_call" | custom-call | tf_op jit(solution)/shard_map/project_out/pallas_call | solution.py:61
  (3 shorter events, 0.1 us)
Async XLA Ops:
  0.0 4.0 %collective-permute-start = (bf16[384,1536]{1,0:T(8,128)(2,1)}, bf16[384,1536]{1,0:T(8,128)(2,1)S(1)}, u32[]{:S(2)}, u32[]{:S(2)}) collective-permute-start(bf16[384,1536]{1,0:T(8,128)(2,1)} %bitcast.2), channel_id=1, source_target_pairs={{0,8},{8,0},{16,24},{24,16},{1,9},{9,1},{17,25},{25,17},{2,10},{10... | collective-permute-start | bytes 3538952 | tf_op jit(solution)/shard_map/ppermute | solution.py:37
  0.5 30.6 %collective-permute-start.8 = (bf16[384,1536]{1,0:T(8,128)(2,1)}, bf16[384,1536]{1,0:T(8,128)(2,1)S(1)}, u32[]{:S(2)}, u32[]{:S(2)}) collective-permute-start(bf16[384,1536]{1,0:T(8,128)(2,1)} %bitcast.3), channel_id=1, source_target_pairs={{0,16},{8,24},{16,0},{24,8},{1,17},{9,25},{17,1},{25,9},{2,18},{10... | collective-permute-start | bytes 3538952 | tf_op jit(solution)/shard_map/ppermute | solution.py:41
  4.0 13.9 %collective-permute-start.1 = (bf16[256,384]{1,0:T(8,128)(2,1)S(1)}, bf16[256,384]{1,0:T(8,128)(2,1)S(1)}, u32[]{:S(2)}, u32[]{:S(2)}) collective-permute-start(bf16[256,384]{1,0:T(8,128)(2,1)S(1)} %get-tuple-element.21.refs_0_), channel_id=1, source_target_pairs={{0,1},{1,0},{2,3},{3,2},{4,5},{5,4},{6,7},{7,6},{8,9},{9,8},{10,11... | collective-permute-start | bytes 589832 | tf_op jit(solution)/shard_map/ppermute | solution.py:354
  6.0 11.9 %collective-permute-start.2 = (bf16[192,384]{1,0:T(8,128)(2,1)S(1)}, bf16[192,384]{1,0:T(8,128)(2,1)S(1)}, u32[]{:S(2)}, u32[]{:S(2)}) collective-permute-start(bf16[192,384]{1,0:T(8,128)(2,1)S(1)} %get-tuple-element.24.refs_0_), channel_id=1, source_target_pairs={{0,4},{1,5},{2,6},{3,7},{4,0},{5,1},{6,2},{7,3},{8,12},{9,13},{10,... | collective-permute-start | bytes 442376 | tf_op jit(solution)/shard_map/ppermute | solution.py:354
  8.6 9.3 %collective-permute-start.4 = (bf16[192,384]{1,0:T(8,128)(2,1)S(1)}, bf16[192,384]{1,0:T(8,128)(2,1)S(1)}, u32[]{:S(2)}, u32[]{:S(2)}) collective-permute-start(bf16[192,384]{1,0:T(8,128)(2,1)S(1)} %get-tuple-element.24.refs_0_), channel_id=1, source_target_pairs={{0,6},{1,7},{2,0},{3,1},{4,2},{5,3},{6,4},{7,5},{8,14},{9,15},{10,... | collective-permute-start | bytes 442376 | tf_op jit(solution)/shard_map/ppermute | solution.py:354
  9.9 14.1 %collective-permute-start.6 = (bf16[192,384]{1,0:T(8,128)(2,1)S(1)}, bf16[192,384]{1,0:T(8,128)(2,1)S(1)}, u32[]{:S(2)}, u32[]{:S(2)}) collective-permute-start(bf16[192,384]{1,0:T(8,128)(2,1)S(1)} %get-tuple-element.24.refs_0_), channel_id=1, source_target_pairs={{0,2},{1,3},{2,4},{3,5},{4,6},{5,7},{6,0},{7,1},{8,10},{9,11},{10,... | collective-permute-start | bytes 442376 | tf_op jit(solution)/shard_map/ppermute | solution.py:354
  17.9 6.2 %collective-permute-start.3 = (bf16[192,384]{1,0:T(8,128)(2,1)S(1)}, bf16[192,384]{1,0:T(8,128)(2,1)S(1)}, u32[]{:S(2)}, u32[]{:S(2)}) collective-permute-start(bf16[192,384]{1,0:T(8,128)(2,1)S(1)} %collective-permute-done.2.refs_2_), channel_id=1, source_target_pairs={{0,1},{1,0},{2,3},{3,2},{4,5},{5,4},{6,7},{7,6},{8,9},{9,8},{10,11... | collective-permute-start | bytes 442376 | tf_op jit(solution)/shard_map/ppermute | solution.py:354
  17.9 7.3 %collective-permute-start.5 = (bf16[192,384]{1,0:T(8,128)(2,1)S(1)}, bf16[192,384]{1,0:T(8,128)(2,1)S(1)}, u32[]{:S(2)}, u32[]{:S(2)}) collective-permute-start(bf16[192,384]{1,0:T(8,128)(2,1)S(1)} %collective-permute-done.4.refs_4_), channel_id=1, source_target_pairs={{0,1},{1,0},{2,3},{3,2},{4,5},{5,4},{6,7},{7,6},{8,9},{9,8},{10,11... | collective-permute-start | bytes 442376 | tf_op jit(solution)/shard_map/ppermute | solution.py:354
  19.9 8.0 %collective-permute-start.7 = (bf16[192,384]{1,0:T(8,128)(2,1)S(1)}, bf16[192,384]{1,0:T(8,128)(2,1)S(1)}, u32[]{:S(2)}, u32[]{:S(2)}) collective-permute-start(bf16[192,384]{1,0:T(8,128)(2,1)S(1)} %get-tuple-element.24.refs_0_), channel_id=1, source_target_pairs={{0,3},{1,2},{2,5},{3,4},{4,7},{5,6},{6,1},{7,0},{8,11},{9,10},{10,... | collective-permute-start | bytes 442376 | tf_op jit(solution)/shard_map/ppermute | solution.py:354
  24.1 7.0 %collective-permute-start.9 = (bf16[64,768]{1,0:T(8,128)(2,1)S(1)}, bf16[64,768]{1,0:T(8,128)(2,1)S(1)}, u32[]{:S(2)}, u32[]{:S(2)}) collective-permute-start(bf16[64,768]{1,0:T(8,128)(2,1)S(1)} %side_by_side.1.own_ref), channel_id=1, source_target_pairs={{0,4},{1,5},{2,6},{3,7},{4,0},{5,1},{6,2},{7,3},{8,12},{9,13},{10,... | collective-permute-start | bytes 294920 | tf_op jit(solution)/shard_map/ppermute | solution.py:357
  31.1 10.2 %collective-permute-start.10 = (bf16[384,1536]{1,0:T(8,128)(2,1)S(1)}, bf16[384,1536]{1,0:T(8,128)(2,1)S(1)}, u32[]{:S(2)}, u32[]{:S(2)}) collective-permute-start(bf16[384,1536]{1,0:T(8,128)(2,1)S(1)} %collective-permute-done.8.refs_0_), channel_id=1, source_target_pairs={{0,8},{8,0},{16,24},{24,16},{1,9},{9,1},{17,25},{25,17},{2,10},{10... | collective-permute-start | bytes 3538952 | tf_op jit(solution)/shard_map/ppermute | solution.py:37
  31.1 10.0 %collective-permute-start.12 = (bf16[128,768]{1,0:T(8,128)(2,1)S(1)}, bf16[128,768]{1,0:T(8,128)(2,1)S(1)}, u32[]{:S(2)}, u32[]{:S(2)}) collective-permute-start(bf16[128,768]{1,0:T(8,128)(2,1)S(1)} %pair_up.2.own_ref), channel_id=1, source_target_pairs={{0,2},{1,3},{2,0},{3,1},{4,6},{5,7},{6,4},{7,5},{8,10},{9,11},{10,... | collective-permute-start | bytes 589832 | tf_op jit(solution)/shard_map/ppermute | solution.py:357
  41.2 4.1 %collective-permute-start.13 = (bf16[256,768]{1,0:T(8,128)(2,1)S(1)}, bf16[256,768]{1,0:T(8,128)(2,1)S(1)}, u32[]{:S(2)}, u32[]{:S(2)}) collective-permute-start(bf16[256,768]{1,0:T(8,128)(2,1)S(1)} %pair_up.3.out_own_ref), channel_id=1, source_target_pairs={{0,8},{8,0},{16,24},{24,16},{1,9},{9,1},{17,25},{25,17},{2,10},{10... | collective-permute-start | bytes 1179656 | tf_op jit(solution)/shard_map/ppermute | solution.py:37
  44.8 1.5 %collective-permute-start.11 = (bf16[384,128]{1,0:T(8,128)(2,1)S(1)}, bf16[384,128]{1,0:T(8,128)(2,1)S(1)}, u32[]{:S(2)}, u32[]{:S(2)}) collective-permute-start(bf16[384,128]{1,0:T(8,128)(2,1)S(1)} %get-tuple-element.31), channel_id=1, source_target_pairs={{0,8},{8,0},{16,24},{24,16},{1,9},{9,1},{17,25},{25,17},{2,10},{10... | collective-permute-start | bytes 294920 | tf_op jit(solution)/shard_map/ppermute | solution.py:37

commit v5 on v4

--- a/solution.py
+++ b/solution.py
@@ -41,7 +41,7 @@
     return lax.ppermute(array, "seq", [(s, (s + CORES * step) % seq_count) for s in range(seq_count)])
 
 
-def call(kernel, name, in_specs, out_shapes, out_specs=None, scratch_shapes=(), cost=0):
+def call(kernel, name, in_specs, out_shapes, out_specs=None, scratch_shapes=(), cost=0, aliases={}):
     out_specs = [VMEM] * len(out_shapes) if out_specs is None else out_specs
     shapes = [
         pltpu.VMEM(shape.shape, shape.dtype) if spec is VMEM else shape for shape, spec in zip(out_shapes, out_specs)
@@ -52,6 +52,7 @@
         in_specs=in_specs,
         out_specs=out_specs,
         scratch_shapes=scratch_shapes,
+        input_output_aliases=aliases,
         cost_estimate=pl.CostEstimate(flops=cost, bytes_accessed=0, transcendentals=0) if cost else None,
         compiler_params=pltpu.CompilerParams(vmem_limit_bytes=24 << 20),
         name=name,
@@ -119,22 +120,25 @@
     )(qkv_weight, out_weight)
 
 
-def side_by_side(blocks, x_count, rows, out_rows, side):
-    pieces = strips(side, blocks[0].shape[1])
+def collect(blocks, x_count, z_count, rows, out_rows, side):
+    pieces = strips(side, blocks[0][0].shape[1])
+    flat = [(half, step) for half in range(len(blocks)) for step in range(x_count)]
 
     def kernel(*refs):
-        x_index = lax.rem(lax.axis_index("fsdp"), x_count)
-        for step in range(x_count):
-            place = lax.rem(x_index + x_count - step, x_count)
+        fsdp_index = lax.axis_index("fsdp")
+        x_index = lax.rem(fsdp_index, x_count)
+        bit = lax.rem(fsdp_index // (x_count * (z_count // 2)), 2)
+        for (half, step), ref in zip(flat, refs):
+            place = (1 - bit if half else bit) * x_count + lax.rem(x_index + x_count - step, x_count)
             for piece, (start, strip) in enumerate(pieces):
                 first = rows + piece * out_rows
-                refs[x_count][pl.ds(pl.multiple_of(place * out_rows, 16), out_rows), start : start + strip] = refs[step][
+                refs[-1][pl.ds(pl.multiple_of(place * out_rows, 16), out_rows), start : start + strip] = ref[
                     first : first + out_rows, :strip
                 ]
 
-    return call(kernel, "side_by_side", [VMEM] * x_count, [shaped((x_count * out_rows, side), blocks[0].dtype)])(
-        *blocks
-    )[0]
+    return call(
+        kernel, "collect", [VMEM] * len(flat), [shaped((len(flat) * out_rows, side), blocks[0][0].dtype)]
+    )(*[blocks[half][step] for half, step in flat])[0]
 
 
 def pair_up(own, got, units, shift, x_count):
@@ -161,19 +165,21 @@
 
 def attend_part(queries, keys, values, bias):
     lane = lax.broadcasted_iota(jnp.int32, (1, LANES), 1)
-    maxima, sums, outs = [], [], []
-    for head in range(LANES // E):
-        inside = (lane >= head * E) & (lane < (head + 1) * E)
-        head_queries = jnp.where(inside, queries, jnp.zeros_like(queries))
-        scores = lax.dot_general(head_queries, keys, (((1,), (1,)), ((), ())), preferred_element_type=jnp.float32)
-        scores = scores + bias
-        row_max = jnp.max(scores, axis=1, keepdims=True)
-        numerators = jnp.exp(scores - row_max).astype(values.dtype)
-        summed = jnp.dot(numerators, values, preferred_element_type=jnp.float32)
-        maxima.append(row_max)
-        sums.append(summed[:, LANES:])
-        outs.append(summed[:, :LANES])
-    return lane_pick(maxima), lane_pick(sums), lane_pick(outs)
+    rows = queries.shape[0]
+    heads = LANES // E
+    zero = jnp.zeros_like(queries)
+    stacked = jnp.concatenate(
+        [jnp.where((lane >= head * E) & (lane < (head + 1) * E), queries, zero) for head in range(heads)], axis=0
+    )
+    scores = lax.dot_general(stacked, keys, (((1,), (1,)), ((), ())), preferred_element_type=jnp.float32) + bias
+    row_max = jnp.max(scores, axis=1, keepdims=True)
+    numerators = jnp.exp(scores - row_max).astype(values.dtype)
+    summed = jnp.dot(numerators, values, preferred_element_type=jnp.float32)
+
+    def pick(array):
+        return lane_pick([array[head * rows : (head + 1) * rows] for head in range(heads)])
+
+    return pick(row_max), pick(summed[:, LANES:]), pick(summed[:, :LANES])
 
 
 def merge(old, new):
@@ -307,36 +313,34 @@
     )(tile_mask, tile_counts, *given)
 
 
-def project_out(attended_own, attended_partner, out_own, out_partner):
+def project_out(far, attended_own, attended_partner, weight, result):
     row_count, own = attended_own.shape
-    side = out_own.shape[1]
+    side = weight.shape[1]
     dtype = attended_own.dtype
-
-    def kernel(own_ref, partner_ref, out_own_ref, out_partner_ref, result_ref, staged_ref, sems):
+    given = [attended_own, attended_partner, weight]
+
+    def kernel(own_ref, partner_ref, weight_ref, *refs):
+        result_ref, staged_ref, sem = refs[-3:]
         core = lax.rem(lax.axis_index("seq"), CORES)
         own_rows = pl.ds(pl.multiple_of(core * own, 16), own)
         partner_rows = pl.ds(pl.multiple_of((1 - core) * own, 16), own)
-        copies = []
-        for half, weight_ref in enumerate((out_own_ref, out_partner_ref)):
-            total = jnp.dot(own_ref[...], weight_ref[own_rows, :], preferred_element_type=jnp.float32)
-            total += jnp.dot(partner_ref[...], weight_ref[partner_rows, :], preferred_element_type=jnp.float32)
-            staged_ref[half] = total.astype(dtype)
-            start = pl.multiple_of((core if half == 0 else 1 - core) * side, LANES)
-            copies.append(
-                pltpu.make_async_copy(staged_ref.at[half], result_ref.at[:, pl.ds(start, side)], sems.at[half])
-            )
-            copies[-1].start()
-        for copy in copies:
-            copy.wait()
+        total = jnp.dot(own_ref[...], weight_ref[own_rows, :], preferred_element_type=jnp.float32)
+        total += jnp.dot(partner_ref[...], weight_ref[partner_rows, :], preferred_element_type=jnp.float32)
+        staged_ref[...] = total.astype(dtype)
+        start = pl.multiple_of((1 - core if far else core) * side, LANES)
+        copy = pltpu.make_async_copy(staged_ref, result_ref.at[:, pl.ds(start, side)], sem)
+        copy.start()
+        copy.wait()
 
     return call(
         kernel,
         "project_out",
-        [VMEM] * 4,
+        [VMEM] * 3 + ([HBM] if far else []),
         [shaped((row_count, CORES * side), dtype)],
         [HBM],
-        scratch_shapes=[pltpu.VMEM((CORES, row_count, side), dtype), pltpu.SemaphoreType.DMA((CORES,))],
-    )(attended_own, attended_partner, out_own, out_partner)[0]
+        scratch_shapes=[pltpu.VMEM((row_count, side), dtype), pltpu.SemaphoreType.DMA(())],
+        aliases={3: 0} if far else {},
+    )(*given, *([result] if far else []))[0]
 
 
 def after(array, *others):
@@ -365,18 +369,26 @@
         came[0, x_step] = hop(after(packed, latents_other), 0, x_step)
     beside = [came[0, x_step] for x_step in range(1, x_count)]
     order = [step for step in range(2, z_count)] + [1]
+    turn = z_count // 2
     for z_step in order:
-        came[z_step, 0] = hop(half, z_step, 0)
-        for x_step in range(1, x_count):
-            if z_step > 1:
-                came[z_step, x_step] = hop(after(came[z_step, 0], came[0, 1]), 0, x_step)
-            else:
-                came[z_step, x_step] = hop(after(half, *beside, came[2, 0]), z_step, x_step)
-
-    out_own = side_by_side([packed] + beside, x_count, half.shape[0], out_weight.shape[0], out_weight.shape[1] // CORES)
-    units, shift = 1, z_count // 2
+        came[z_step, 0] = hop(packed if z_step == turn else half, z_step, 0)
+    for x_step in range(1, x_count):
+        for z_step in order[:-1]:
+            ahead = beside if z_step == turn else [came[1, 0]]
+            came[z_step, x_step] = hop(after(came[z_step, 0], *ahead), 0, x_step)
+        came[1, x_step] = hop(after(half, *beside, came[turn, 0]), 1, x_step)
+
+    out_own = collect(
+        [[packed] + beside, [came[turn, x_step] for x_step in range(x_count)]],
+        x_count,
+        z_count,
+        half.shape[0],
+        out_weight.shape[0],
+        out_weight.shape[1] // CORES,
+    )
+    units, shift = 2, turn // 2
     while shift > 1:
-        out_own = pair_up(out_own, flip(after(out_own, came[1, 0], came[2, 1]), shift), units, shift, x_count)
+        out_own = pair_up(out_own, flip(out_own, shift), units, shift, x_count)
         units, shift = 2 * units, shift // 2
     out_got = flip(out_own, shift)
 
@@ -402,13 +414,13 @@
             tile_mask,
             tile_counts,
         )
-        if first < 0:
-            out_own = pair_up(out_own, after(out_got, result[0]), units, shift, x_count)
-            out_partner = core_swap(out_own, seq_count)
         state = None if last else result[0]
     attended_own, attended_other = result
     attended_partner = core_swap(attended_other, seq_count)
-    return project_out(attended_own, attended_partner, out_own, out_partner)[None]
+    out_own = pair_up(out_own, after(out_got, attended_other), units, shift, x_count)
+    out_partner = core_swap(out_own, seq_count)
+    near_side = project_out(False, attended_own, attended_partner, out_own, None)
+    return project_out(True, attended_own, attended_partner, out_partner, near_side)[None]
 
 
 def solution(mesh):

time: 48.1 us -> 47.7 us (level)
  starting transfers between devices: 22 us -> 17.2 us
  waiting for transfers between devices: 12.3 us -> 17.1 us
    ppermute x7, waiting for transfers between devices: 10.1 us -> 15.7 us  [hop(): lax.ppermute(array, 'fsdp', rotation(z_count, x_count, z_step, x_step))]
    ppermute x2 -> x1, starting transfers between devices: 5.62 us -> 2.81 us  [flip(): lax.ppermute(array, 'fsdp', [(f, f ^ shift * x_count) for f in range(fsdp...]
    ppermute x7, starting transfers between devices: 12.8 us -> 10.8 us  [hop(): lax.ppermute(array, 'fsdp', rotation(z_count, x_count, z_step, x_step))]
    ppermute x2 -> x1, waiting for transfers between devices: 1.32 us -> 0.01 us  [flip(): lax.ppermute(array, 'fsdp', [(f, f ^ shift * x_count) for f in range(fsdp...]
  transfers between devices with their start and end apart: 14 -> 13, of which waited for: 5 -> 4; matrix products, arithmetic and copies ran while one was open for 0% -> 0% of each run, Pallas kernels for 25% -> 25%
where the time goes in v5:
time: 47.7 us; the launch traced here: 47.4 us
  starting transfers between devices  17.2 us (36%)
  waiting for transfers between devices  17.1 us (36%)
  Pallas kernels  13.1 us (27%)
    ppermute x7, waiting for transfers between devices, hop(): lax.ppermute(array, 'fsdp', rotation(z_count, x_count, z_step, x_step))  15.7 us
    pallas_call x8, Pallas kernels, run(): inner(*[pltpu.with_memory_space_constraint(arg, pltpu.HBM if spec is SMEM...  13.1 us
    ppermute x7, starting transfers between devices, hop(): lax.ppermute(array, 'fsdp', rotation(z_count, x_count, z_step, x_step))  10.8 us
    ppermute x1, starting transfers between devices, flip(): lax.ppermute(array, 'fsdp', [(f, f ^ shift * x_count) for f in range(fsdp...  2.81 us
    ppermute x1, starting transfers between devices, y_rotation(): lax.ppermute(array, 'seq', [(s, (s + CORES * step) % seq_count) for s in...  2.52 us
    ppermute x4, waiting for transfers between devices, core_swap(): return lax.ppermute(array, 'seq', [(s, s ^ 1) for s in range(seq_count)])  1.36 us
    ppermute x4, starting transfers between devices, core_swap(): return lax.ppermute(array, 'seq', [(s, s ^ 1) for s in range(seq_count)])  1.1 us
  transfers between devices with their start and end apart: 13, of which 4 were waited for; matrix products, arithmetic and copies ran while one was open for 0% of the time, Pallas kernels for 25%

profile of v5, /device:TPU:0, one launch (start us, length us, event | category | flops | bytes accessed | tf_op | source)
XLA Modules:
  0.0 47.4 jit_solution(2691118359761559904)
XLA Ops:
  0.0 0.5 collective-permute-start
  0.5 2.5 %collective-permute-start.8 = (bf16[384,1536]{1,0:T(8,128)(2,1)}, bf16[384,1536]{1,0:T(8,128)(2,1)S(1)}, u32[]{:S(2)}, u32[]{:S(2)}) collective-permute-start(bf16[384,1536]{1,0:T(8,128)(2,1)} %bitcast.3), channel_id=1, source_target_pairs={{0,16},{8,24},{16,0},{24,8},{1,17},{9,25},{17,1},{25,9},{2,18},{10... | collective-permute-start | bytes 3538952 | tf_op jit(solution)/shard_map/ppermute | solution.py:41
  3.0 1.0 %halves.1 = (bf16[192,384]{1,0:T(8,128)(2,1)S(1)}, bf16[256,384]{1,0:T(8,128)(2,1)S(1)}) custom-call(bf16[192,768]{1,0:T(8,128)(2,1)} %qkv_ref.1, bf16[32,1536]{1,0:T(8,128)(2,1)} %out_ref.1), custom_call_target="tpu_custom_call" | custom-call | tf_op jit(solution)/shard_map/halves/pallas_call | solution.py:62
  4.0 2.7 %collective-permute-start.2 = (bf16[256,384]{1,0:T(8,128)(2,1)S(1)}, bf16[256,384]{1,0:T(8,128)(2,1)S(1)}, u32[]{:S(2)}, u32[]{:S(2)}) collective-permute-start(bf16[256,384]{1,0:T(8,128)(2,1)S(1)} %get-tuple-element.20.refs_0_), channel_id=1, source_target_pairs={{0,4},{1,5},{2,6},{3,7},{4,0},{5,1},{6,2},{7,3},{8,12},{9,13},{10,... | collective-permute-start | bytes 589832 | tf_op jit(solution)/shard_map/ppermute | solution.py:358
  6.6 0.0 collective-permute-done.other_ref
  6.6 1.5 %collective-permute-start.1 = (bf16[256,384]{1,0:T(8,128)(2,1)S(1)}, bf16[256,384]{1,0:T(8,128)(2,1)S(1)}, u32[]{:S(2)}, u32[]{:S(2)}) collective-permute-start(bf16[256,384]{1,0:T(8,128)(2,1)S(1)} %get-tuple-element.20.refs_0_), channel_id=1, source_target_pairs={{0,1},{1,0},{2,3},{3,2},{4,5},{5,4},{6,7},{7,6},{8,9},{9,8},{10,11... | collective-permute-start | bytes 589832 | tf_op jit(solution)/shard_map/ppermute | solution.py:358
  8.1 1.5 %collective-permute-start.3 = (bf16[192,384]{1,0:T(8,128)(2,1)S(1)}, bf16[192,384]{1,0:T(8,128)(2,1)S(1)}, u32[]{:S(2)}, u32[]{:S(2)}) collective-permute-start(bf16[192,384]{1,0:T(8,128)(2,1)S(1)} %get-tuple-element.23.refs_0_), channel_id=1, source_target_pairs={{0,6},{1,7},{2,0},{3,1},{4,2},{5,3},{6,4},{7,5},{8,14},{9,15},{10,... | collective-permute-start | bytes 442376 | tf_op jit(solution)/shard_map/ppermute | solution.py:358
  9.6 0.6 %collective-permute-start.4 = (bf16[192,384]{1,0:T(8,128)(2,1)S(1)}, bf16[192,384]{1,0:T(8,128)(2,1)S(1)}, u32[]{:S(2)}, u32[]{:S(2)}) collective-permute-start(bf16[192,384]{1,0:T(8,128)(2,1)S(1)} %get-tuple-element.23.refs_0_), channel_id=1, source_target_pairs={{0,2},{1,3},{2,4},{3,5},{4,6},{5,7},{6,0},{7,1},{8,10},{9,11},{10,... | collective-permute-start | bytes 442376 | tf_op jit(solution)/shard_map/ppermute | solution.py:358
  10.2 9.9 %collective-permute-done.2.refs_2_ = bf16[256,384]{1,0:T(8,128)(2,1)S(1)} collective-permute-done((bf16[256,384]{1,0:T(8,128)(2,1)S(1)}, bf16[256,384]{1,0:T(8,128)(2,1)S(1)}, u32[]{:S(2)}, u32[]{:S(2)}) %collective-permute-start.2) | collective-permute-done | bytes 196640 | tf_op jit(solution)/shard_map/ppermute | solution.py:358
  20.1 0.0 collective-permute-done.1.refs_1_
  20.1 1.4 %collective-permute-start.5 = (bf16[256,384]{1,0:T(8,128)(2,1)S(1)}, bf16[256,384]{1,0:T(8,128)(2,1)S(1)}, u32[]{:S(2)}, u32[]{:S(2)}) collective-permute-start(bf16[256,384]{1,0:T(8,128)(2,1)S(1)} %collective-permute-done.2.refs_2_), channel_id=1, source_target_pairs={{0,1},{1,0},{2,3},{3,2},{4,5},{5,4},{6,7},{7,6},{8,9},{9,8},{10,11... | collective-permute-start | bytes 589832 | tf_op jit(solution)/shard_map/ppermute | solution.py:358
  21.5 0.0 collective-permute-done.3.refs_3_
  21.5 0.0 collective-permute-done.4.refs_4_
  21.6 0.6 %collective-permute-start.6 = (bf16[192,384]{1,0:T(8,128)(2,1)S(1)}, bf16[192,384]{1,0:T(8,128)(2,1)S(1)}, u32[]{:S(2)}, u32[]{:S(2)}) collective-permute-start(bf16[192,384]{1,0:T(8,128)(2,1)S(1)} %collective-permute-done.3.refs_3_), channel_id=1, source_target_pairs={{0,1},{1,0},{2,3},{3,2},{4,5},{5,4},{6,7},{7,6},{8,9},{9,8},{10,11... | collective-permute-start | bytes 442376 | tf_op jit(solution)/shard_map/ppermute | solution.py:358
  22.1 2.6 %collective-permute-start.7 = (bf16[192,384]{1,0:T(8,128)(2,1)S(1)}, bf16[192,384]{1,0:T(8,128)(2,1)S(1)}, u32[]{:S(2)}, u32[]{:S(2)}) collective-permute-start(bf16[192,384]{1,0:T(8,128)(2,1)S(1)} %get-tuple-element.23.refs_0_), channel_id=1, source_target_pairs={{0,3},{1,2},{2,5},{3,4},{4,7},{5,6},{6,1},{7,0},{8,11},{9,10},{10,... | collective-permute-start | bytes 442376 | tf_op jit(solution)/shard_map/ppermute | solution.py:358
  24.7 1.6 %collective-permute-done.5.refs_5_.refs_3_ = bf16[256,384]{1,0:T(8,128)(2,1)S(1)} collective-permute-done((bf16[256,384]{1,0:T(8,128)(2,1)S(1)}, bf16[256,384]{1,0:T(8,128)(2,1)S(1)}, u32[]{:S(2)}, u32[]{:S(2)}) %collective-permute-start.5) | collective-permute-done | bytes 196640 | tf_op jit(solution)/shard_map/ppermute | solution.py:358
  26.4 4.1 %collective-permute-done.6.refs_6_ = bf16[192,384]{1,0:T(8,128)(2,1)S(1)} collective-permute-done((bf16[192,384]{1,0:T(8,128)(2,1)S(1)}, bf16[192,384]{1,0:T(8,128)(2,1)S(1)}, u32[]{:S(2)}, u32[]{:S(2)}) %collective-permute-start.6) | collective-permute-done | bytes 147488 | tf_op jit(solution)/shard_map/ppermute | solution.py:358
  30.5 0.0 collective-permute-done.7.refs_7_
  30.5 2.2 %project.1 = (bf16[2,384,128]{2,1,0:T(8,128)(2,1)S(1)}, bf16[1536,384]{1,0:T(8,128)(2,1)S(1)}, bf16[768,256]{1,0:T(8,128)(2,1)S(1)}) custom-call(bf16[384,1536]{1,0:T(8,128)(2,1)} %bitcast.4, bf16[384,1536]{1,0:T(8,128)(2,1)S(1)} %collective-permute-done.other_ref, bf16[192,384]{1,0:T(8,128)(2,1)S(1)} %get-tuple-element.23.refs_0_, ...), custom_call_target="tpu_custom_call" | custom-call | flops 1000000000 | tf_op jit(solution)/shard_map/project/pallas_call | solution.py:62
  32.7 0.0 collective-permute-done.8.refs_0_
  32.7 0.1 collective-permute-start.9
  32.8 2.8 %collective-permute-start.11 = (bf16[128,768]{1,0:T(8,128)(2,1)S(1)}, bf16[128,768]{1,0:T(8,128)(2,1)S(1)}, u32[]{:S(2)}, u32[]{:S(2)}) collective-permute-start(bf16[128,768]{1,0:T(8,128)(2,1)S(1)} %collect.1.own_ref), channel_id=1, source_target_pairs={{0,2},{1,3},{2,0},{3,1},{4,6},{5,7},{6,4},{7,5},{8,10},{9,11},{10,... | collective-permute-start | bytes 589832 | tf_op jit(solution)/shard_map/ppermute | solution.py:361
  35.6 4.5 %attend.1.refs_1_ = f32[2,3,384,128]{3,2,1,0:T(8,128)S(1)} custom-call(s32[4,4]{1,0:T(4,128)} %mask_ref.3, s32[4]{0:T(128)} %count_ref.3, bf16[1536,384]{1,0:T(8,128)(2,1)S(1)} %get-tuple-element.24.weight_ref, bf16[2,384,128]{2,1,0:T(8,128)(2,1)S(1)} %get-tuple-element.25.queries_ref, bf16[384,1536]{1,0:T(8,128)(2,1)S(1)} %collective-permute-done.8.refs_0_, ...), custom_call_target="tpu_custom_call" | custom-call | flops 1000000000 | tf_op jit(solution)/shard_map/attend/pallas_call | solution.py:62
  40.1 0.0 collective-permute-done.9.refs_0_
  40.1 2.8 %attend_last.1 = (bf16[384,128]{1,0:T(8,128)(2,1)S(1)}, bf16[384,128]{1,0:T(8,128)(2,1)S(1)}) custom-call(s32[4,4]{1,0:T(4,128)} %mask_ref.3, s32[4]{0:T(128)} %count_ref.3, bf16[1536,384]{1,0:T(8,128)(2,1)S(1)} %get-tuple-element.24.weight_ref, bf16[2,384,128]{2,1,0:T(8,128)(2,1)S(1)} %get-tuple-element.25.queries_ref, ...), custom_call_target="tpu_custom_call" | custom-call | flops 1000000000 | tf_op jit(solution)/shard_map/attend_last/pallas_call | solution.py:62
  42.9 0.0 collective-permute-done.11.got_ref
  42.9 0.2 collective-permute-start.12
  43.2 0.3 collective-permute-start.10
  43.5 1.4 %collective-permute-done.10.partner_ref = bf16[384,128]{1,0:T(8,128)(2,1)S(1)} collective-permute-done((bf16[384,128]{1,0:T(8,128)(2,1)S(1)}, bf16[384,128]{1,0:T(8,128)(2,1)S(1)}, u32[]{:S(2)}, u32[]{:S(2)}) %collective-permute-start.10) | collective-permute-done | bytes 98336 | tf_op jit(solution)/shard_map/ppermute | solution.py:37
  44.9 1.3 %project_out.2.refs_0_ = bf16[384,1536]{1,0:T(8,128)(2,1)} custom-call(bf16[384,128]{1,0:T(8,128)(2,1)S(1)} %get-tuple-element.28.own_ref, bf16[384,128]{1,0:T(8,128)(2,1)S(1)} %collective-permute-done.10.partner_ref, bf16[256,768]{1,0:T(8,128)(2,1)S(1)} %pair_up.1.weight_ref), custom_call_target="tpu_custom_call" | custom-call | tf_op jit(solution)/shard_map/project_out/pallas_call | solution.py:62
  46.1 0.0 collective-permute-done.12.weight_ref
  46.1 1.3 %project_out.3 = bf16[384,1536]{1,0:T(8,128)(2,1)} custom-call(bf16[384,128]{1,0:T(8,128)(2,1)S(1)} %get-tuple-element.28.own_ref, bf16[384,128]{1,0:T(8,128)(2,1)S(1)} %collective-permute-done.10.partner_ref, bf16[256,768]{1,0:T(8,128)(2,1)S(1)} %collective-permute-done.12.weight_ref, ...), custom_call_target="tpu_custom_call", output_to_operand_aliasing={{}: (3, {})} | custom-call | tf_op jit(solution)/shard_map/project_out/pallas_call | solution.py:62
  (2 shorter events, 0.1 us)
Async XLA Ops:
  0.0 6.6 %collective-permute-start = (bf16[384,1536]{1,0:T(8,128)(2,1)}, bf16[384,1536]{1,0:T(8,128)(2,1)S(1)}, u32[]{:S(2)}, u32[]{:S(2)}) collective-permute-start(bf16[384,1536]{1,0:T(8,128)(2,1)} %bitcast.2), channel_id=1, source_target_pairs={{0,8},{8,0},{16,24},{24,16},{1,9},{9,1},{17,25},{25,17},{2,10},{10... | collective-permute-start | bytes 3538952 | tf_op jit(solution)/shard_map/ppermute | solution.py:37
  0.5 32.2 %collective-permute-start.8 = (bf16[384,1536]{1,0:T(8,128)(2,1)}, bf16[384,1536]{1,0:T(8,128)(2,1)S(1)}, u32[]{:S(2)}, u32[]{:S(2)}) collective-permute-start(bf16[384,1536]{1,0:T(8,128)(2,1)} %bitcast.3), channel_id=1, source_target_pairs={{0,16},{8,24},{16,0},{24,8},{1,17},{9,25},{17,1},{25,9},{2,18},{10... | collective-permute-start | bytes 3538952 | tf_op jit(solution)/shard_map/ppermute | solution.py:41
  4.0 16.1 %collective-permute-start.2 = (bf16[256,384]{1,0:T(8,128)(2,1)S(1)}, bf16[256,384]{1,0:T(8,128)(2,1)S(1)}, u32[]{:S(2)}, u32[]{:S(2)}) collective-permute-start(bf16[256,384]{1,0:T(8,128)(2,1)S(1)} %get-tuple-element.20.refs_0_), channel_id=1, source_target_pairs={{0,4},{1,5},{2,6},{3,7},{4,0},{5,1},{6,2},{7,3},{8,12},{9,13},{10,... | collective-permute-start | bytes 589832 | tf_op jit(solution)/shard_map/ppermute | solution.py:358
  6.6 13.5 %collective-permute-start.1 = (bf16[256,384]{1,0:T(8,128)(2,1)S(1)}, bf16[256,384]{1,0:T(8,128)(2,1)S(1)}, u32[]{:S(2)}, u32[]{:S(2)}) collective-permute-start(bf16[256,384]{1,0:T(8,128)(2,1)S(1)} %get-tuple-element.20.refs_0_), channel_id=1, source_target_pairs={{0,1},{1,0},{2,3},{3,2},{4,5},{5,4},{6,7},{7,6},{8,9},{9,8},{10,11... | collective-permute-start | bytes 589832 | tf_op jit(solution)/shard_map/ppermute | solution.py:358
  8.1 13.4 %collective-permute-start.3 = (bf16[192,384]{1,0:T(8,128)(2,1)S(1)}, bf16[192,384]{1,0:T(8,128)(2,1)S(1)}, u32[]{:S(2)}, u32[]{:S(2)}) collective-permute-start(bf16[192,384]{1,0:T(8,128)(2,1)S(1)} %get-tuple-element.23.refs_0_), channel_id=1, source_target_pairs={{0,6},{1,7},{2,0},{3,1},{4,2},{5,3},{6,4},{7,5},{8,14},{9,15},{10,... | collective-permute-start | bytes 442376 | tf_op jit(solution)/shard_map/ppermute | solution.py:358
  9.6 11.9 %collective-permute-start.4 = (bf16[192,384]{1,0:T(8,128)(2,1)S(1)}, bf16[192,384]{1,0:T(8,128)(2,1)S(1)}, u32[]{:S(2)}, u32[]{:S(2)}) collective-permute-start(bf16[192,384]{1,0:T(8,128)(2,1)S(1)} %get-tuple-element.23.refs_0_), channel_id=1, source_target_pairs={{0,2},{1,3},{2,4},{3,5},{4,6},{5,7},{6,0},{7,1},{8,10},{9,11},{10,... | collective-permute-start | bytes 442376 | tf_op jit(solution)/shard_map/ppermute | solution.py:358
  20.1 6.2 %collective-permute-start.5 = (bf16[256,384]{1,0:T(8,128)(2,1)S(1)}, bf16[256,384]{1,0:T(8,128)(2,1)S(1)}, u32[]{:S(2)}, u32[]{:S(2)}) collective-permute-start(bf16[256,384]{1,0:T(8,128)(2,1)S(1)} %collective-permute-done.2.refs_2_), channel_id=1, source_target_pairs={{0,1},{1,0},{2,3},{3,2},{4,5},{5,4},{6,7},{7,6},{8,9},{9,8},{10,11... | collective-permute-start | bytes 589832 | tf_op jit(solution)/shard_map/ppermute | solution.py:358
  21.6 9.0 %collective-permute-start.6 = (bf16[192,384]{1,0:T(8,128)(2,1)S(1)}, bf16[192,384]{1,0:T(8,128)(2,1)S(1)}, u32[]{:S(2)}, u32[]{:S(2)}) collective-permute-start(bf16[192,384]{1,0:T(8,128)(2,1)S(1)} %collective-permute-done.3.refs_3_), channel_id=1, source_target_pairs={{0,1},{1,0},{2,3},{3,2},{4,5},{5,4},{6,7},{7,6},{8,9},{9,8},{10,11... | collective-permute-start | bytes 442376 | tf_op jit(solution)/shard_map/ppermute | solution.py:358
  22.1 8.4 %collective-permute-start.7 = (bf16[192,384]{1,0:T(8,128)(2,1)S(1)}, bf16[192,384]{1,0:T(8,128)(2,1)S(1)}, u32[]{:S(2)}, u32[]{:S(2)}) collective-permute-start(bf16[192,384]{1,0:T(8,128)(2,1)S(1)} %get-tuple-element.23.refs_0_), channel_id=1, source_target_pairs={{0,3},{1,2},{2,5},{3,4},{4,7},{5,6},{6,1},{7,0},{8,11},{9,10},{10,... | collective-permute-start | bytes 442376 | tf_op jit(solution)/shard_map/ppermute | solution.py:358
  32.7 7.4 %collective-permute-start.9 = (bf16[384,1536]{1,0:T(8,128)(2,1)S(1)}, bf16[384,1536]{1,0:T(8,128)(2,1)S(1)}, u32[]{:S(2)}, u32[]{:S(2)}) collective-permute-start(bf16[384,1536]{1,0:T(8,128)(2,1)S(1)} %collective-permute-done.8.refs_0_), channel_id=1, source_target_pairs={{0,8},{8,0},{16,24},{24,16},{1,9},{9,1},{17,25},{25,17},{2,10},{10... | collective-permute-start | bytes 3538952 | tf_op jit(solution)/shard_map/ppermute | solution.py:37
  32.8 10.1 %collective-permute-start.11 = (bf16[128,768]{1,0:T(8,128)(2,1)S(1)}, bf16[128,768]{1,0:T(8,128)(2,1)S(1)}, u32[]{:S(2)}, u32[]{:S(2)}) collective-permute-start(bf16[128,768]{1,0:T(8,128)(2,1)S(1)} %collect.1.own_ref), channel_id=1, source_target_pairs={{0,2},{1,3},{2,0},{3,1},{4,6},{5,7},{6,4},{7,5},{8,10},{9,11},{10,... | collective-permute-start | bytes 589832 | tf_op jit(solution)/shard_map/ppermute | solution.py:361
  42.9 3.2 %collective-permute-start.12 = (bf16[256,768]{1,0:T(8,128)(2,1)S(1)}, bf16[256,768]{1,0:T(8,128)(2,1)S(1)}, u32[]{:S(2)}, u32[]{:S(2)}) collective-permute-start(bf16[256,768]{1,0:T(8,128)(2,1)S(1)} %pair_up.1.weight_ref), channel_id=1, source_target_pairs={{0,8},{8,0},{16,24},{24,16},{1,9},{9,1},{17,25},{25,17},{2,10},{10... | collective-permute-start | bytes 1179656 | tf_op jit(solution)/shard_map/ppermute | solution.py:37
  43.2 1.7 %collective-permute-start.10 = (bf16[384,128]{1,0:T(8,128)(2,1)S(1)}, bf16[384,128]{1,0:T(8,128)(2,1)S(1)}, u32[]{:S(2)}, u32[]{:S(2)}) collective-permute-start(bf16[384,128]{1,0:T(8,128)(2,1)S(1)} %get-tuple-element.29), channel_id=1, source_target_pairs={{0,8},{8,0},{16,24},{24,16},{1,9},{9,1},{17,25},{25,17},{2,10},{10... | collective-permute-start | bytes 294920 | tf_op jit(solution)/shard_map/ppermute | solution.py:37

commit v6 on v5

--- a/solution.py
+++ b/solution.py
@@ -313,34 +313,36 @@
     )(tile_mask, tile_counts, *given)
 
 
-def project_out(far, attended_own, attended_partner, weight, result):
+def project_out(attended_own, attended_partner, out_own, out_partner):
     row_count, own = attended_own.shape
-    side = weight.shape[1]
+    side = out_own.shape[1]
     dtype = attended_own.dtype
-    given = [attended_own, attended_partner, weight]
-
-    def kernel(own_ref, partner_ref, weight_ref, *refs):
-        result_ref, staged_ref, sem = refs[-3:]
+
+    def kernel(own_ref, partner_ref, out_own_ref, out_partner_ref, result_ref, staged_ref, sems):
         core = lax.rem(lax.axis_index("seq"), CORES)
         own_rows = pl.ds(pl.multiple_of(core * own, 16), own)
         partner_rows = pl.ds(pl.multiple_of((1 - core) * own, 16), own)
-        total = jnp.dot(own_ref[...], weight_ref[own_rows, :], preferred_element_type=jnp.float32)
-        total += jnp.dot(partner_ref[...], weight_ref[partner_rows, :], preferred_element_type=jnp.float32)
-        staged_ref[...] = total.astype(dtype)
-        start = pl.multiple_of((1 - core if far else core) * side, LANES)
-        copy = pltpu.make_async_copy(staged_ref, result_ref.at[:, pl.ds(start, side)], sem)
-        copy.start()
-        copy.wait()
+        copies = []
+        for half, weight_ref in enumerate((out_own_ref, out_partner_ref)):
+            total = jnp.dot(own_ref[...], weight_ref[own_rows, :], preferred_element_type=jnp.float32)
+            total += jnp.dot(partner_ref[...], weight_ref[partner_rows, :], preferred_element_type=jnp.float32)
+            staged_ref[half] = total.astype(dtype)
+            start = pl.multiple_of((core if half == 0 else 1 - core) * side, LANES)
+            copies.append(
+                pltpu.make_async_copy(staged_ref.at[half], result_ref.at[:, pl.ds(start, side)], sems.at[half])
+            )
+            copies[-1].start()
+        for copy in copies:
+            copy.wait()
 
     return call(
         kernel,
         "project_out",
-        [VMEM] * 3 + ([HBM] if far else []),
+        [VMEM] * 4,
         [shaped((row_count, CORES * side), dtype)],
         [HBM],
-        scratch_shapes=[pltpu.VMEM((row_count, side), dtype), pltpu.SemaphoreType.DMA(())],
-        aliases={3: 0} if far else {},
-    )(*given, *([result] if far else []))[0]
+        scratch_shapes=[pltpu.VMEM((CORES, row_count, side), dtype), pltpu.SemaphoreType.DMA((CORES,))],
+    )(attended_own, attended_partner, out_own, out_partner)[0]
 
 
 def after(array, *others):
@@ -368,15 +370,19 @@
     for x_step in range(1, x_count):
         came[0, x_step] = hop(after(packed, latents_other), 0, x_step)
     beside = [came[0, x_step] for x_step in range(1, x_count)]
-    order = [step for step in range(2, z_count)] + [1]
     turn = z_count // 2
-    for z_step in order:
+    for z_step in (turn, 1):
         came[z_step, 0] = hop(packed if z_step == turn else half, z_step, 0)
+    second = after(half, came[1, 0], *beside)
+    third = after(half, came[turn, 0])
     for x_step in range(1, x_count):
-        for z_step in order[:-1]:
-            ahead = beside if z_step == turn else [came[1, 0]]
-            came[z_step, x_step] = hop(after(came[z_step, 0], *ahead), 0, x_step)
-        came[1, x_step] = hop(after(half, *beside, came[turn, 0]), 1, x_step)
+        came[turn, x_step] = hop(came[turn, 0], 0, x_step)
+        came[1, x_step] = hop(second, 1, x_step)
+    for z_step in range(2, z_count):
+        if z_step != turn:
+            came[z_step, 0] = hop(second, z_step, 0)
+            for x_step in range(1, x_count):
+                came[z_step, x_step] = hop(third, z_step, x_step)
 
     out_own = collect(
         [[packed] + beside, [came[turn, x_step] for x_step in range(x_count)]],
@@ -392,21 +398,19 @@
         units, shift = 2 * units, shift // 2
     out_got = flip(out_own, shift)
 
+    near = after(along_y, out_own, *list(came.values())[1:])
+    far = [core_swap(array, seq_count) for array in near]
+    came[0, 0] = after(half, *near)
     queries, weight, key_value = project(
         z_count, x_count, list(came), list(came.values()), latents_own, latents_other
     )
-    steps = [(step, swapped) for step in range(1, chips) for swapped in (False, True)]
-    near, _, _ = lax.optimization_barrier((along_y, key_value, out_own))
-    tokens = {(step, False): near[step - 1] for step in range(1, chips)}
-    tokens.update({(step, True): core_swap(near[step - 1], seq_count) for step in range(1, chips)})
     state = None
-    for first in range(-1, len(steps), 2):
-        sources = [(tokens[step], *step) for step in steps[max(first, 0) : first + 2]]
-        last = first + 2 > len(steps)
+    for step in range(1, chips):
+        last = step == chips - 1
         result = attend(
             seq_count,
-            sources,
-            key_value if first < 0 else None,
+            [(near[step - 1], step, False), (far[step - 1], step, True)],
+            key_value if step == 1 else None,
             state,
             last,
             weight,
@@ -419,8 +423,7 @@
     attended_partner = core_swap(attended_other, seq_count)
     out_own = pair_up(out_own, after(out_got, attended_other), units, shift, x_count)
     out_partner = core_swap(out_own, seq_count)
-    near_side = project_out(False, attended_own, attended_partner, out_own, None)
-    return project_out(True, attended_own, attended_partner, out_partner, near_side)[None]
+    return project_out(attended_own, attended_partner, out_own, out_partner)[None]
 
 
 def solution(mesh):

time: 47.7 us -> 45 us (0.943)
  Pallas kernels: 13.1 us -> 9.87 us
  waiting for transfers between devices: 17.1 us -> 19 us
  starting transfers between devices: 17.2 us -> 15.8 us
    pallas_call x8 -> x6, Pallas kernels: 13.1 us -> 9.87 us  [run(): inner(*[pltpu.with_memory_space_constraint(arg, pltpu.HBM if spec is SMEM...]
    ppermute x7, waiting for transfers between devices: 15.7 us -> 17.7 us  [hop(): lax.ppermute(array, 'fsdp', rotation(z_count, x_count, z_step, x_step))]
    ppermute x1, starting transfers between devices: 2.81 us -> 1.71 us  [flip(): lax.ppermute(array, 'fsdp', [(f, f ^ shift * x_count) for f in range(fsdp...]
  transfers between devices with their start and end apart: 13 -> 13, of which waited for: 4 -> 5; matrix products, arithmetic and copies ran while one was open for 0% -> 0% of each run, Pallas kernels for 25% -> 18%
where the time goes in v6:
time: 45 us; the launch traced here: 44.8 us
  waiting for transfers between devices  19 us (42%)
  starting transfers between devices  15.8 us (35%)
  Pallas kernels  9.87 us (22%)
    ppermute x7, waiting for transfers between devices, hop(): lax.ppermute(array, 'fsdp', rotation(z_count, x_count, z_step, x_step))  17.7 us
    ppermute x7, starting transfers between devices, hop(): lax.ppermute(array, 'fsdp', rotation(z_count, x_count, z_step, x_step))  10.5 us
    pallas_call x6, Pallas kernels, run(): inner(*[pltpu.with_memory_space_constraint(arg, pltpu.HBM if spec is SMEM...  9.87 us
    ppermute x1, starting transfers between devices, y_rotation(): lax.ppermute(array, 'seq', [(s, (s + CORES * step) % seq_count) for s in...  2.52 us
    ppermute x1, starting transfers between devices, flip(): lax.ppermute(array, 'fsdp', [(f, f ^ shift * x_count) for f in range(fsdp...  1.71 us
    ppermute x4, waiting for transfers between devices, core_swap(): return lax.ppermute(array, 'seq', [(s, s ^ 1) for s in range(seq_count)])  1.36 us
    ppermute x4, starting transfers between devices, core_swap(): return lax.ppermute(array, 'seq', [(s, s ^ 1) for s in range(seq_count)])  1.03 us
  transfers between devices with their start and end apart: 13, of which 5 were waited for; matrix products, arithmetic and copies ran while one was open for 0% of the time, Pallas kernels for 18%

profile of v6, /device:TPU:0, one launch (start us, length us, event | category | flops | bytes accessed | tf_op | source)
XLA Modules:
  0.0 44.8 jit_solution(5283985299271948286)
XLA Ops:
  0.0 0.5 %collective-permute-start = (bf16[384,1536]{1,0:T(8,128)(2,1)}, bf16[384,1536]{1,0:T(8,128)(2,1)S(1)}, u32[]{:S(2)}, u32[]{:S(2)}) collective-permute-start(bf16[384,1536]{1,0:T(8,128)(2,1)} %bitcast.2), channel_id=1, source_target_pairs={{0,8},{8,0},{16,24},{24,16},{1,9},{9,1},{17,25},{25,17},{2,10},{10... | collective-permute-start | bytes 3538952 | tf_op jit(solution)/shard_map/ppermute | solution.py:37
  0.5 2.5 %collective-permute-start.1 = (bf16[384,1536]{1,0:T(8,128)(2,1)}, bf16[384,1536]{1,0:T(8,128)(2,1)S(1)}, u32[]{:S(2)}, u32[]{:S(2)}) collective-permute-start(bf16[384,1536]{1,0:T(8,128)(2,1)} %bitcast.3), channel_id=1, source_target_pairs={{0,16},{8,24},{16,0},{24,8},{1,17},{9,25},{17,1},{25,9},{2,18},{10... | collective-permute-start | bytes 3538952 | tf_op jit(solution)/shard_map/ppermute | solution.py:41
  3.0 1.0 %halves.1 = (bf16[192,384]{1,0:T(8,128)(2,1)S(1)}, bf16[256,384]{1,0:T(8,128)(2,1)S(1)}) custom-call(bf16[192,768]{1,0:T(8,128)(2,1)} %qkv_ref.1, bf16[32,1536]{1,0:T(8,128)(2,1)} %out_ref.1), custom_call_target="tpu_custom_call" | custom-call | tf_op jit(solution)/shard_map/halves/pallas_call | solution.py:62
  4.0 2.7 %collective-permute-start.3 = (bf16[256,384]{1,0:T(8,128)(2,1)S(1)}, bf16[256,384]{1,0:T(8,128)(2,1)S(1)}, u32[]{:S(2)}, u32[]{:S(2)}) collective-permute-start(bf16[256,384]{1,0:T(8,128)(2,1)S(1)} %get-tuple-element.20.refs_0_), channel_id=1, source_target_pairs={{0,4},{1,5},{2,6},{3,7},{4,0},{5,1},{6,2},{7,3},{8,12},{9,13},{10,... | collective-permute-start | bytes 589832 | tf_op jit(solution)/shard_map/ppermute | solution.py:360
  6.6 0.0 collective-permute-done.other_ref
  6.6 1.5 %collective-permute-start.2 = (bf16[256,384]{1,0:T(8,128)(2,1)S(1)}, bf16[256,384]{1,0:T(8,128)(2,1)S(1)}, u32[]{:S(2)}, u32[]{:S(2)}) collective-permute-start(bf16[256,384]{1,0:T(8,128)(2,1)S(1)} %get-tuple-element.20.refs_0_), channel_id=1, source_target_pairs={{0,1},{1,0},{2,3},{3,2},{4,5},{5,4},{6,7},{7,6},{8,9},{9,8},{10,11... | collective-permute-start | bytes 589832 | tf_op jit(solution)/shard_map/ppermute | solution.py:360
  8.1 1.6 %collective-permute-start.5 = (bf16[192,384]{1,0:T(8,128)(2,1)S(1)}, bf16[192,384]{1,0:T(8,128)(2,1)S(1)}, u32[]{:S(2)}, u32[]{:S(2)}) collective-permute-start(bf16[192,384]{1,0:T(8,128)(2,1)S(1)} %get-tuple-element.24.refs_0_), channel_id=1, source_target_pairs={{0,2},{1,3},{2,4},{3,5},{4,6},{5,7},{6,0},{7,1},{8,10},{9,11},{10,... | collective-permute-start | bytes 442376 | tf_op jit(solution)/shard_map/ppermute | solution.py:360
  9.7 9.7 %collective-permute-done.3.refs_2_ = bf16[256,384]{1,0:T(8,128)(2,1)S(1)} collective-permute-done((bf16[256,384]{1,0:T(8,128)(2,1)S(1)}, bf16[256,384]{1,0:T(8,128)(2,1)S(1)}, u32[]{:S(2)}, u32[]{:S(2)}) %collective-permute-start.3) | collective-permute-done | bytes 196640 | tf_op jit(solution)/shard_map/ppermute | solution.py:360
  19.4 1.5 %collective-permute-start.4 = (bf16[256,384]{1,0:T(8,128)(2,1)S(1)}, bf16[256,384]{1,0:T(8,128)(2,1)S(1)}, u32[]{:S(2)}, u32[]{:S(2)}) collective-permute-start(bf16[256,384]{1,0:T(8,128)(2,1)S(1)} %collective-permute-done.3.refs_2_), channel_id=1, source_target_pairs={{0,1},{1,0},{2,3},{3,2},{4,5},{5,4},{6,7},{7,6},{8,9},{9,8},{10,11... | collective-permute-start | bytes 589832 | tf_op jit(solution)/shard_map/ppermute | solution.py:360
  20.8 0.4 collective-permute-start.8
  21.2 0.0 collective-permute-done.5.refs_3_
  21.2 0.0 collective-permute-done.2.refs_1_
  21.2 0.6 %collective-permute-start.7 = (bf16[192,384]{1,0:T(8,128)(2,1)S(1)}, bf16[192,384]{1,0:T(8,128)(2,1)S(1)}, u32[]{:S(2)}, u32[]{:S(2)}) collective-permute-start(bf16[192,384]{1,0:T(8,128)(2,1)S(1)} %get-tuple-element.24.refs_0_), channel_id=1, source_target_pairs={{0,6},{1,7},{2,0},{3,1},{4,2},{5,3},{6,4},{7,5},{8,14},{9,15},{10,... | collective-permute-start | bytes 442376 | tf_op jit(solution)/shard_map/ppermute | solution.py:360
  21.8 2.3 %collective-permute-start.6 = (bf16[192,384]{1,0:T(8,128)(2,1)S(1)}, bf16[192,384]{1,0:T(8,128)(2,1)S(1)}, u32[]{:S(2)}, u32[]{:S(2)}) collective-permute-start(bf16[192,384]{1,0:T(8,128)(2,1)S(1)} %get-tuple-element.24.refs_0_), channel_id=1, source_target_pairs={{0,3},{1,2},{2,5},{3,4},{4,7},{5,6},{6,1},{7,0},{8,11},{9,10},{10,... | collective-permute-start | bytes 442376 | tf_op jit(solution)/shard_map/ppermute | solution.py:360
  24.2 6.8 %collective-permute-done.4.refs_3_.refs_4_ = bf16[256,384]{1,0:T(8,128)(2,1)S(1)} collective-permute-done((bf16[256,384]{1,0:T(8,128)(2,1)S(1)}, bf16[256,384]{1,0:T(8,128)(2,1)S(1)}, u32[]{:S(2)}, u32[]{:S(2)}) %collective-permute-start.4) | collective-permute-done | bytes 196640 | tf_op jit(solution)/shard_map/ppermute | solution.py:360
  31.0 0.0 collective-permute-done.8.refs_7_
  31.0 0.0 collective-permute-done.1.refs_0_
  31.0 1.1 %collective-permute-done.7.refs_6_ = bf16[192,384]{1,0:T(8,128)(2,1)S(1)} collective-permute-done((bf16[192,384]{1,0:T(8,128)(2,1)S(1)}, bf16[192,384]{1,0:T(8,128)(2,1)S(1)}, u32[]{:S(2)}, u32[]{:S(2)}) %collective-permute-start.7) | collective-permute-done | bytes 147488 | tf_op jit(solution)/shard_map/ppermute | solution.py:360
  32.1 0.2 collective-permute-done.6.refs_5_
  32.2 0.0 collective-permute-start.9
  32.3 1.7 %collective-permute-start.11 = (bf16[128,768]{1,0:T(8,128)(2,1)S(1)}, bf16[128,768]{1,0:T(8,128)(2,1)S(1)}, u32[]{:S(2)}, u32[]{:S(2)}) collective-permute-start(bf16[128,768]{1,0:T(8,128)(2,1)S(1)} %collect.1.own_ref), channel_id=1, source_target_pairs={{0,2},{1,3},{2,0},{3,1},{4,6},{5,7},{6,4},{7,5},{8,10},{9,11},{10,... | collective-permute-start | bytes 589832 | tf_op jit(solution)/shard_map/ppermute | solution.py:363
  34.0 2.2 %project.1 = (bf16[2,384,128]{2,1,0:T(8,128)(2,1)S(1)}, bf16[1536,384]{1,0:T(8,128)(2,1)S(1)}, bf16[768,256]{1,0:T(8,128)(2,1)S(1)}) custom-call(bf16[384,1536]{1,0:T(8,128)(2,1)} %bitcast.4, bf16[384,1536]{1,0:T(8,128)(2,1)S(1)} %collective-permute-done.other_ref, bf16[192,384]{1,0:T(8,128)(2,1)S(1)} %get-tuple-element.24.refs_0_, ...), custom_call_target="tpu_custom_call" | custom-call | flops 1000000000 | tf_op jit(solution)/shard_map/project/pallas_call | solution.py:62
  36.1 0.0 collective-permute-done.9.refs_1_
  36.1 5.0 %attend_last.1 = (bf16[384,128]{1,0:T(8,128)(2,1)S(1)}, bf16[384,128]{1,0:T(8,128)(2,1)S(1)}) custom-call(s32[4,4]{1,0:T(4,128)} %mask_ref.1, s32[4]{0:T(128)} %count_ref.1, bf16[1536,384]{1,0:T(8,128)(2,1)S(1)} %get-tuple-element.25.weight_ref, bf16[2,384,128]{2,1,0:T(8,128)(2,1)S(1)} %get-tuple-element.26.queries_ref, ...), custom_call_target="tpu_custom_call" | custom-call | flops 1000000000 | tf_op jit(solution)/shard_map/attend_last/pallas_call | solution.py:62
  41.2 0.0 collective-permute-done.11.got_ref
  41.2 0.3 collective-permute-start.12
  41.5 0.3 collective-permute-start.10
  41.8 1.4 %collective-permute-done.10.partner_ref = bf16[384,128]{1,0:T(8,128)(2,1)S(1)} collective-permute-done((bf16[384,128]{1,0:T(8,128)(2,1)S(1)}, bf16[384,128]{1,0:T(8,128)(2,1)S(1)}, u32[]{:S(2)}, u32[]{:S(2)}) %collective-permute-start.10) | collective-permute-done | bytes 98336 | tf_op jit(solution)/shard_map/ppermute | solution.py:37
  43.2 0.0 collective-permute-done.12.out_partner_ref
  43.2 1.6 %project_out.1 = bf16[384,1536]{1,0:T(8,128)(2,1)} custom-call(bf16[384,128]{1,0:T(8,128)(2,1)S(1)} %get-tuple-element.28.own_ref, bf16[384,128]{1,0:T(8,128)(2,1)S(1)} %collective-permute-done.10.partner_ref, bf16[256,768]{1,0:T(8,128)(2,1)S(1)} %pair_up.1.out_own_ref, bf16[256,768]{1,0:T(8,128)(2,1)S(1)} %collective-permute-done.12.out_partner_ref), custom_call_target="tpu_custom_call" | custom-call | tf_op jit(solution)/shard_map/project_out/pallas_call | solution.py:62
  (2 shorter events, 0.1 us)
Async XLA Ops:
  0.0 6.6 %collective-permute-start = (bf16[384,1536]{1,0:T(8,128)(2,1)}, bf16[384,1536]{1,0:T(8,128)(2,1)S(1)}, u32[]{:S(2)}, u32[]{:S(2)}) collective-permute-start(bf16[384,1536]{1,0:T(8,128)(2,1)} %bitcast.2), channel_id=1, source_target_pairs={{0,8},{8,0},{16,24},{24,16},{1,9},{9,1},{17,25},{25,17},{2,10},{10... | collective-permute-start | bytes 3538952 | tf_op jit(solution)/shard_map/ppermute | solution.py:37
  0.5 30.5 %collective-permute-start.1 = (bf16[384,1536]{1,0:T(8,128)(2,1)}, bf16[384,1536]{1,0:T(8,128)(2,1)S(1)}, u32[]{:S(2)}, u32[]{:S(2)}) collective-permute-start(bf16[384,1536]{1,0:T(8,128)(2,1)} %bitcast.3), channel_id=1, source_target_pairs={{0,16},{8,24},{16,0},{24,8},{1,17},{9,25},{17,1},{25,9},{2,18},{10... | collective-permute-start | bytes 3538952 | tf_op jit(solution)/shard_map/ppermute | solution.py:41
  4.0 15.4 %collective-permute-start.3 = (bf16[256,384]{1,0:T(8,128)(2,1)S(1)}, bf16[256,384]{1,0:T(8,128)(2,1)S(1)}, u32[]{:S(2)}, u32[]{:S(2)}) collective-permute-start(bf16[256,384]{1,0:T(8,128)(2,1)S(1)} %get-tuple-element.20.refs_0_), channel_id=1, source_target_pairs={{0,4},{1,5},{2,6},{3,7},{4,0},{5,1},{6,2},{7,3},{8,12},{9,13},{10,... | collective-permute-start | bytes 589832 | tf_op jit(solution)/shard_map/ppermute | solution.py:360
  6.6 14.6 %collective-permute-start.2 = (bf16[256,384]{1,0:T(8,128)(2,1)S(1)}, bf16[256,384]{1,0:T(8,128)(2,1)S(1)}, u32[]{:S(2)}, u32[]{:S(2)}) collective-permute-start(bf16[256,384]{1,0:T(8,128)(2,1)S(1)} %get-tuple-element.20.refs_0_), channel_id=1, source_target_pairs={{0,1},{1,0},{2,3},{3,2},{4,5},{5,4},{6,7},{7,6},{8,9},{9,8},{10,11... | collective-permute-start | bytes 589832 | tf_op jit(solution)/shard_map/ppermute | solution.py:360
  8.1 13.1 %collective-permute-start.5 = (bf16[192,384]{1,0:T(8,128)(2,1)S(1)}, bf16[192,384]{1,0:T(8,128)(2,1)S(1)}, u32[]{:S(2)}, u32[]{:S(2)}) collective-permute-start(bf16[192,384]{1,0:T(8,128)(2,1)S(1)} %get-tuple-element.24.refs_0_), channel_id=1, source_target_pairs={{0,2},{1,3},{2,4},{3,5},{4,6},{5,7},{6,0},{7,1},{8,10},{9,11},{10,... | collective-permute-start | bytes 442376 | tf_op jit(solution)/shard_map/ppermute | solution.py:360
  19.4 11.6 %collective-permute-start.4 = (bf16[256,384]{1,0:T(8,128)(2,1)S(1)}, bf16[256,384]{1,0:T(8,128)(2,1)S(1)}, u32[]{:S(2)}, u32[]{:S(2)}) collective-permute-start(bf16[256,384]{1,0:T(8,128)(2,1)S(1)} %collective-permute-done.3.refs_2_), channel_id=1, source_target_pairs={{0,1},{1,0},{2,3},{3,2},{4,5},{5,4},{6,7},{7,6},{8,9},{9,8},{10,11... | collective-permute-start | bytes 589832 | tf_op jit(solution)/shard_map/ppermute | solution.py:360
  20.8 10.1 %collective-permute-start.8 = (bf16[192,384]{1,0:T(8,128)(2,1)S(1)}, bf16[192,384]{1,0:T(8,128)(2,1)S(1)}, u32[]{:S(2)}, u32[]{:S(2)}) collective-permute-start(bf16[192,384]{1,0:T(8,128)(2,1)S(1)} %get-tuple-element.24.refs_0_), channel_id=1, source_target_pairs={{0,7},{1,6},{2,1},{3,0},{4,3},{5,2},{6,5},{7,4},{8,15},{9,14},{10,... | collective-permute-start | bytes 442376 | tf_op jit(solution)/shard_map/ppermute | solution.py:360
  21.2 10.9 %collective-permute-start.7 = (bf16[192,384]{1,0:T(8,128)(2,1)S(1)}, bf16[192,384]{1,0:T(8,128)(2,1)S(1)}, u32[]{:S(2)}, u32[]{:S(2)}) collective-permute-start(bf16[192,384]{1,0:T(8,128)(2,1)S(1)} %get-tuple-element.24.refs_0_), channel_id=1, source_target_pairs={{0,6},{1,7},{2,0},{3,1},{4,2},{5,3},{6,4},{7,5},{8,14},{9,15},{10,... | collective-permute-start | bytes 442376 | tf_op jit(solution)/shard_map/ppermute | solution.py:360
  21.8 10.4 %collective-permute-start.6 = (bf16[192,384]{1,0:T(8,128)(2,1)S(1)}, bf16[192,384]{1,0:T(8,128)(2,1)S(1)}, u32[]{:S(2)}, u32[]{:S(2)}) collective-permute-start(bf16[192,384]{1,0:T(8,128)(2,1)S(1)} %get-tuple-element.24.refs_0_), channel_id=1, source_target_pairs={{0,3},{1,2},{2,5},{3,4},{4,7},{5,6},{6,1},{7,0},{8,11},{9,10},{10,... | collective-permute-start | bytes 442376 | tf_op jit(solution)/shard_map/ppermute | solution.py:360
  32.2 3.9 %collective-permute-start.9 = (bf16[384,1536]{1,0:T(8,128)(2,1)S(1)}, bf16[384,1536]{1,0:T(8,128)(2,1)S(1)}, u32[]{:S(2)}, u32[]{:S(2)}) collective-permute-start(bf16[384,1536]{1,0:T(8,128)(2,1)S(1)} %collective-permute-done.1.refs_0_), channel_id=1, source_target_pairs={{0,8},{8,0},{16,24},{24,16},{1,9},{9,1},{17,25},{25,17},{2,10},{10... | collective-permute-start | bytes 3538952 | tf_op jit(solution)/shard_map/ppermute | solution.py:37
  32.3 8.9 %collective-permute-start.11 = (bf16[128,768]{1,0:T(8,128)(2,1)S(1)}, bf16[128,768]{1,0:T(8,128)(2,1)S(1)}, u32[]{:S(2)}, u32[]{:S(2)}) collective-permute-start(bf16[128,768]{1,0:T(8,128)(2,1)S(1)} %collect.1.own_ref), channel_id=1, source_target_pairs={{0,2},{1,3},{2,0},{3,1},{4,6},{5,7},{6,4},{7,5},{8,10},{9,11},{10,... | collective-permute-start | bytes 589832 | tf_op jit(solution)/shard_map/ppermute | solution.py:363
  41.2 1.9 %collective-permute-start.12 = (bf16[256,768]{1,0:T(8,128)(2,1)S(1)}, bf16[256,768]{1,0:T(8,128)(2,1)S(1)}, u32[]{:S(2)}, u32[]{:S(2)}) collective-permute-start(bf16[256,768]{1,0:T(8,128)(2,1)S(1)} %pair_up.1.out_own_ref), channel_id=1, source_target_pairs={{0,8},{8,0},{16,24},{24,16},{1,9},{9,1},{17,25},{25,17},{2,10},{10... | collective-permute-start | bytes 1179656 | tf_op jit(solution)/shard_map/ppermute | solution.py:37
  41.5 1.6 %collective-permute-start.10 = (bf16[384,128]{1,0:T(8,128)(2,1)S(1)}, bf16[384,128]{1,0:T(8,128)(2,1)S(1)}, u32[]{:S(2)}, u32[]{:S(2)}) collective-permute-start(bf16[384,128]{1,0:T(8,128)(2,1)S(1)} %get-tuple-element.29), channel_id=1, source_target_pairs={{0,8},{8,0},{16,24},{24,16},{1,9},{9,1},{17,25},{25,17},{2,10},{10... | collective-permute-start | bytes 294920 | tf_op jit(solution)/shard_map/ppermute | solution.py:37

commit v7 on v6

--- a/solution.py
+++ b/solution.py
@@ -374,15 +374,14 @@
     for z_step in (turn, 1):
         came[z_step, 0] = hop(packed if z_step == turn else half, z_step, 0)
     second = after(half, came[1, 0], *beside)
-    third = after(half, came[turn, 0])
     for x_step in range(1, x_count):
-        came[turn, x_step] = hop(came[turn, 0], 0, x_step)
+        came[turn, x_step] = hop(after(came[turn, 0], came[1, 0]), 0, x_step)
         came[1, x_step] = hop(second, 1, x_step)
     for z_step in range(2, z_count):
         if z_step != turn:
             came[z_step, 0] = hop(second, z_step, 0)
             for x_step in range(1, x_count):
-                came[z_step, x_step] = hop(third, z_step, x_step)
+                came[z_step, x_step] = hop(second, z_step, x_step)
 
     out_own = collect(
         [[packed] + beside, [came[turn, x_step] for x_step in range(x_count)]],

time: 45 us -> 47.5 us (1.056)
  waiting for transfers between devices: 19 us -> 22.5 us
  starting transfers between devices: 15.8 us -> 14.8 us
    ppermute x7, waiting for transfers between devices: 17.7 us -> 19.5 us  [hop(): lax.ppermute(array, 'fsdp', rotation(z_count, x_count, z_step, x_step))]
    ppermute x1, starting transfers between devices: 1.71 us -> 0.01 us  [flip(): lax.ppermute(array, 'fsdp', [(f, f ^ shift * x_count) for f in range(fsdp...]
    ppermute x1, waiting for transfers between devices: 0.01 us -> 1.03 us  [y_rotation(): lax.ppermute(array, 'seq', [(s, (s + CORES * step) % seq_count) for s in...]
    ppermute x7, starting transfers between devices: 10.5 us -> 11.2 us  [hop(): lax.ppermute(array, 'fsdp', rotation(z_count, x_count, z_step, x_step))]
    ppermute x4, waiting for transfers between devices: 1.36 us -> 2.03 us  [core_swap(): return lax.ppermute(array, 'seq', [(s, s ^ 1) for s in range(seq_count)])]
  transfers between devices with their start and end apart: 13 -> 13, of which waited for: 5 -> 7; matrix products, arithmetic and copies ran while one was open for 0% -> 0% of each run, Pallas kernels for 18% -> 17%
where the time goes in v7:
time: 47.5 us; the launch traced here: 47.2 us
  waiting for transfers between devices  22.5 us (47%)
  starting transfers between devices  14.8 us (31%)
  Pallas kernels  9.87 us (21%)
    ppermute x7, waiting for transfers between devices, hop(): lax.ppermute(array, 'fsdp', rotation(z_count, x_count, z_step, x_step))  19.5 us
    ppermute x7, starting transfers between devices, hop(): lax.ppermute(array, 'fsdp', rotation(z_count, x_count, z_step, x_step))  11.2 us
    pallas_call x6, Pallas kernels, run(): inner(*[pltpu.with_memory_space_constraint(arg, pltpu.HBM if spec is SMEM...  9.87 us
    ppermute x1, starting transfers between devices, y_rotation(): lax.ppermute(array, 'seq', [(s, (s + CORES * step) % seq_count) for s in...  2.52 us
    ppermute x4, waiting for transfers between devices, core_swap(): return lax.ppermute(array, 'seq', [(s, s ^ 1) for s in range(seq_count)])  2.03 us
    ppermute x1, waiting for transfers between devices, y_rotation(): lax.ppermute(array, 'seq', [(s, (s + CORES * step) % seq_count) for s in...  1.03 us
    ppermute x4, starting transfers between devices, core_swap(): return lax.ppermute(array, 'seq', [(s, s ^ 1) for s in range(seq_count)])  1.03 us
  transfers between devices with their start and end apart: 13, of which 7 were waited for; matrix products, arithmetic and copies ran while one was open for 0% of the time, Pallas kernels for 17%

profile of v7, /device:TPU:0, one launch (start us, length us, event | category | flops | bytes accessed | tf_op | source)
XLA Modules:
  0.0 47.2 jit_solution(13246172649678425462)
XLA Ops:
  0.0 0.5 collective-permute-start
  0.5 2.5 %collective-permute-start.1 = (bf16[384,1536]{1,0:T(8,128)(2,1)}, bf16[384,1536]{1,0:T(8,128)(2,1)S(1)}, u32[]{:S(2)}, u32[]{:S(2)}) collective-permute-start(bf16[384,1536]{1,0:T(8,128)(2,1)} %bitcast.3), channel_id=1, source_target_pairs={{0,16},{8,24},{16,0},{24,8},{1,17},{9,25},{17,1},{25,9},{2,18},{10... | collective-permute-start | bytes 3538952 | tf_op jit(solution)/shard_map/ppermute | solution.py:41
  3.0 1.0 %halves.1 = (bf16[192,384]{1,0:T(8,128)(2,1)S(1)}, bf16[256,384]{1,0:T(8,128)(2,1)S(1)}) custom-call(bf16[192,768]{1,0:T(8,128)(2,1)} %qkv_ref.1, bf16[32,1536]{1,0:T(8,128)(2,1)} %out_ref.1), custom_call_target="tpu_custom_call" | custom-call | tf_op jit(solution)/shard_map/halves/pallas_call | solution.py:62
  4.0 2.7 %collective-permute-start.3 = (bf16[256,384]{1,0:T(8,128)(2,1)S(1)}, bf16[256,384]{1,0:T(8,128)(2,1)S(1)}, u32[]{:S(2)}, u32[]{:S(2)}) collective-permute-start(bf16[256,384]{1,0:T(8,128)(2,1)S(1)} %get-tuple-element.20.refs_0_), channel_id=1, source_target_pairs={{0,4},{1,5},{2,6},{3,7},{4,0},{5,1},{6,2},{7,3},{8,12},{9,13},{10,... | collective-permute-start | bytes 589832 | tf_op jit(solution)/shard_map/ppermute | solution.py:360
  6.6 1.6 %collective-permute-start.4 = (bf16[192,384]{1,0:T(8,128)(2,1)S(1)}, bf16[192,384]{1,0:T(8,128)(2,1)S(1)}, u32[]{:S(2)}, u32[]{:S(2)}) collective-permute-start(bf16[192,384]{1,0:T(8,128)(2,1)S(1)} %get-tuple-element.24.refs_0_), channel_id=1, source_target_pairs={{0,2},{1,3},{2,4},{3,5},{4,6},{5,7},{6,0},{7,1},{8,10},{9,11},{10,... | collective-permute-start | bytes 442376 | tf_op jit(solution)/shard_map/ppermute | solution.py:360
  8.2 0.0 collective-permute-done.other_ref
  8.2 1.5 %collective-permute-start.2 = (bf16[256,384]{1,0:T(8,128)(2,1)S(1)}, bf16[256,384]{1,0:T(8,128)(2,1)S(1)}, u32[]{:S(2)}, u32[]{:S(2)}) collective-permute-start(bf16[256,384]{1,0:T(8,128)(2,1)S(1)} %get-tuple-element.20.refs_0_), channel_id=1, source_target_pairs={{0,1},{1,0},{2,3},{3,2},{4,5},{5,4},{6,7},{7,6},{8,9},{9,8},{10,11... | collective-permute-start | bytes 589832 | tf_op jit(solution)/shard_map/ppermute | solution.py:360
  9.7 6.6 %collective-permute-done.4.refs_3_ = bf16[192,384]{1,0:T(8,128)(2,1)S(1)} collective-permute-done((bf16[192,384]{1,0:T(8,128)(2,1)S(1)}, bf16[192,384]{1,0:T(8,128)(2,1)S(1)}, u32[]{:S(2)}, u32[]{:S(2)}) %collective-permute-start.4) | collective-permute-done | bytes 147488 | tf_op jit(solution)/shard_map/ppermute | solution.py:360
  16.3 3.1 %collective-permute-done.3.refs_2_ = bf16[256,384]{1,0:T(8,128)(2,1)S(1)} collective-permute-done((bf16[256,384]{1,0:T(8,128)(2,1)S(1)}, bf16[256,384]{1,0:T(8,128)(2,1)S(1)}, u32[]{:S(2)}, u32[]{:S(2)}) %collective-permute-start.3) | collective-permute-done | bytes 196640 | tf_op jit(solution)/shard_map/ppermute | solution.py:360
  19.4 1.5 %collective-permute-start.5 = (bf16[256,384]{1,0:T(8,128)(2,1)S(1)}, bf16[256,384]{1,0:T(8,128)(2,1)S(1)}, u32[]{:S(2)}, u32[]{:S(2)}) collective-permute-start(bf16[256,384]{1,0:T(8,128)(2,1)S(1)} %collective-permute-done.3.refs_2_), channel_id=1, source_target_pairs={{0,1},{1,0},{2,3},{3,2},{4,5},{5,4},{6,7},{7,6},{8,9},{9,8},{10,11... | collective-permute-start | bytes 589832 | tf_op jit(solution)/shard_map/ppermute | solution.py:360
  20.8 0.0 collective-permute-done.2.refs_1_
  20.9 0.4 collective-permute-start.8
  21.2 3.7 %collective-permute-start.7 = (bf16[192,384]{1,0:T(8,128)(2,1)S(1)}, bf16[192,384]{1,0:T(8,128)(2,1)S(1)}, u32[]{:S(2)}, u32[]{:S(2)}) collective-permute-start(bf16[192,384]{1,0:T(8,128)(2,1)S(1)} %get-tuple-element.24.refs_0_), channel_id=1, source_target_pairs={{0,6},{1,7},{2,0},{3,1},{4,2},{5,3},{6,4},{7,5},{8,14},{9,15},{10,... | collective-permute-start | bytes 442376 | tf_op jit(solution)/shard_map/ppermute | solution.py:360
  24.9 0.0 collective-permute-start.6
  24.9 3.9 %collective-permute-done.5.refs_3_.refs_4_ = bf16[256,384]{1,0:T(8,128)(2,1)S(1)} collective-permute-done((bf16[256,384]{1,0:T(8,128)(2,1)S(1)}, bf16[256,384]{1,0:T(8,128)(2,1)S(1)}, u32[]{:S(2)}, u32[]{:S(2)}) %collective-permute-start.5) | collective-permute-done | bytes 196640 | tf_op jit(solution)/shard_map/ppermute | solution.py:360
  28.8 1.0 %collective-permute-done.1.refs_0_ = bf16[384,1536]{1,0:T(8,128)(2,1)S(1)} collective-permute-done((bf16[384,1536]{1,0:T(8,128)(2,1)}, bf16[384,1536]{1,0:T(8,128)(2,1)S(1)}, u32[]{:S(2)}, u32[]{:S(2)}) %collective-permute-start.1) | collective-permute-done | bytes 1179680 | tf_op jit(solution)/shard_map/ppermute | solution.py:41
  29.8 0.0 collective-permute-done.8.refs_7_
  29.8 0.0 collective-permute-done.7.refs_6_
  29.8 5.9 %collective-permute-done.6.refs_5_ = bf16[192,384]{1,0:T(8,128)(2,1)S(1)} collective-permute-done((bf16[192,384]{1,0:T(8,128)(2,1)S(1)}, bf16[192,384]{1,0:T(8,128)(2,1)S(1)}, u32[]{:S(2)}, u32[]{:S(2)}) %collective-permute-start.6) | collective-permute-done | bytes 147488 | tf_op jit(solution)/shard_map/ppermute | solution.py:360
  35.8 0.0 collective-permute-start.9
  35.8 0.0 collective-permute-start.11
  35.8 2.2 %project.1 = (bf16[2,384,128]{2,1,0:T(8,128)(2,1)S(1)}, bf16[1536,384]{1,0:T(8,128)(2,1)S(1)}, bf16[768,256]{1,0:T(8,128)(2,1)S(1)}) custom-call(bf16[384,1536]{1,0:T(8,128)(2,1)} %bitcast.4, bf16[384,1536]{1,0:T(8,128)(2,1)S(1)} %collective-permute-done.other_ref, bf16[192,384]{1,0:T(8,128)(2,1)S(1)} %get-tuple-element.24.refs_0_, ...), custom_call_target="tpu_custom_call" | custom-call | flops 1000000000 | tf_op jit(solution)/shard_map/project/pallas_call | solution.py:62
  37.9 0.7 %collective-permute-done.9.refs_1_ = bf16[384,1536]{1,0:T(8,128)(2,1)S(1)} collective-permute-done((bf16[384,1536]{1,0:T(8,128)(2,1)S(1)}, bf16[384,1536]{1,0:T(8,128)(2,1)S(1)}, u32[]{:S(2)}, u32[]{:S(2)}) %collective-permute-start.9) | collective-permute-done | bytes 1179680 | tf_op jit(solution)/shard_map/ppermute | solution.py:37
  38.6 5.0 %attend_last.1 = (bf16[384,128]{1,0:T(8,128)(2,1)S(1)}, bf16[384,128]{1,0:T(8,128)(2,1)S(1)}) custom-call(s32[4,4]{1,0:T(4,128)} %mask_ref.1, s32[4]{0:T(128)} %count_ref.1, bf16[1536,384]{1,0:T(8,128)(2,1)S(1)} %get-tuple-element.25.weight_ref, bf16[2,384,128]{2,1,0:T(8,128)(2,1)S(1)} %get-tuple-element.26.queries_ref, ...), custom_call_target="tpu_custom_call" | custom-call | flops 1000000000 | tf_op jit(solution)/shard_map/attend_last/pallas_call | solution.py:62
  43.6 0.0 collective-permute-done.11.got_ref
  43.7 0.2 collective-permute-start.12
  43.9 0.4 collective-permute-start.10
  44.3 1.4 %collective-permute-done.10.partner_ref = bf16[384,128]{1,0:T(8,128)(2,1)S(1)} collective-permute-done((bf16[384,128]{1,0:T(8,128)(2,1)S(1)}, bf16[384,128]{1,0:T(8,128)(2,1)S(1)}, u32[]{:S(2)}, u32[]{:S(2)}) %collective-permute-start.10) | collective-permute-done | bytes 98336 | tf_op jit(solution)/shard_map/ppermute | solution.py:37
  45.6 0.0 collective-permute-done.12.out_partner_ref
  45.6 1.6 %project_out.1 = bf16[384,1536]{1,0:T(8,128)(2,1)} custom-call(bf16[384,128]{1,0:T(8,128)(2,1)S(1)} %get-tuple-element.28.own_ref, bf16[384,128]{1,0:T(8,128)(2,1)S(1)} %collective-permute-done.10.partner_ref, bf16[256,768]{1,0:T(8,128)(2,1)S(1)} %pair_up.1.out_own_ref, bf16[256,768]{1,0:T(8,128)(2,1)S(1)} %collective-permute-done.12.out_partner_ref), custom_call_target="tpu_custom_call" | custom-call | tf_op jit(solution)/shard_map/project_out/pallas_call | solution.py:62
  (2 shorter events, 0.1 us)
Async XLA Ops:
  0.0 8.2 %collective-permute-start = (bf16[384,1536]{1,0:T(8,128)(2,1)}, bf16[384,1536]{1,0:T(8,128)(2,1)S(1)}, u32[]{:S(2)}, u32[]{:S(2)}) collective-permute-start(bf16[384,1536]{1,0:T(8,128)(2,1)} %bitcast.2), channel_id=1, source_target_pairs={{0,8},{8,0},{16,24},{24,16},{1,9},{9,1},{17,25},{25,17},{2,10},{10... | collective-permute-start | bytes 3538952 | tf_op jit(solution)/shard_map/ppermute | solution.py:37
  0.5 29.4 %collective-permute-start.1 = (bf16[384,1536]{1,0:T(8,128)(2,1)}, bf16[384,1536]{1,0:T(8,128)(2,1)S(1)}, u32[]{:S(2)}, u32[]{:S(2)}) collective-permute-start(bf16[384,1536]{1,0:T(8,128)(2,1)} %bitcast.3), channel_id=1, source_target_pairs={{0,16},{8,24},{16,0},{24,8},{1,17},{9,25},{17,1},{25,9},{2,18},{10... | collective-permute-start | bytes 3538952 | tf_op jit(solution)/shard_map/ppermute | solution.py:41
  4.0 15.4 %collective-permute-start.3 = (bf16[256,384]{1,0:T(8,128)(2,1)S(1)}, bf16[256,384]{1,0:T(8,128)(2,1)S(1)}, u32[]{:S(2)}, u32[]{:S(2)}) collective-permute-start(bf16[256,384]{1,0:T(8,128)(2,1)S(1)} %get-tuple-element.20.refs_0_), channel_id=1, source_target_pairs={{0,4},{1,5},{2,6},{3,7},{4,0},{5,1},{6,2},{7,3},{8,12},{9,13},{10,... | collective-permute-start | bytes 589832 | tf_op jit(solution)/shard_map/ppermute | solution.py:360
  6.6 9.6 %collective-permute-start.4 = (bf16[192,384]{1,0:T(8,128)(2,1)S(1)}, bf16[192,384]{1,0:T(8,128)(2,1)S(1)}, u32[]{:S(2)}, u32[]{:S(2)}) collective-permute-start(bf16[192,384]{1,0:T(8,128)(2,1)S(1)} %get-tuple-element.24.refs_0_), channel_id=1, source_target_pairs={{0,2},{1,3},{2,4},{3,5},{4,6},{5,7},{6,0},{7,1},{8,10},{9,11},{10,... | collective-permute-start | bytes 442376 | tf_op jit(solution)/shard_map/ppermute | solution.py:360
  8.2 12.6 %collective-permute-start.2 = (bf16[256,384]{1,0:T(8,128)(2,1)S(1)}, bf16[256,384]{1,0:T(8,128)(2,1)S(1)}, u32[]{:S(2)}, u32[]{:S(2)}) collective-permute-start(bf16[256,384]{1,0:T(8,128)(2,1)S(1)} %get-tuple-element.20.refs_0_), channel_id=1, source_target_pairs={{0,1},{1,0},{2,3},{3,2},{4,5},{5,4},{6,7},{7,6},{8,9},{9,8},{10,11... | collective-permute-start | bytes 589832 | tf_op jit(solution)/shard_map/ppermute | solution.py:360
  19.4 9.4 %collective-permute-start.5 = (bf16[256,384]{1,0:T(8,128)(2,1)S(1)}, bf16[256,384]{1,0:T(8,128)(2,1)S(1)}, u32[]{:S(2)}, u32[]{:S(2)}) collective-permute-start(bf16[256,384]{1,0:T(8,128)(2,1)S(1)} %collective-permute-done.3.refs_2_), channel_id=1, source_target_pairs={{0,1},{1,0},{2,3},{3,2},{4,5},{5,4},{6,7},{7,6},{8,9},{9,8},{10,11... | collective-permute-start | bytes 589832 | tf_op jit(solution)/shard_map/ppermute | solution.py:360
  20.9 9.0 %collective-permute-start.8 = (bf16[192,384]{1,0:T(8,128)(2,1)S(1)}, bf16[192,384]{1,0:T(8,128)(2,1)S(1)}, u32[]{:S(2)}, u32[]{:S(2)}) collective-permute-start(bf16[192,384]{1,0:T(8,128)(2,1)S(1)} %get-tuple-element.24.refs_0_), channel_id=1, source_target_pairs={{0,7},{1,6},{2,1},{3,0},{4,3},{5,2},{6,5},{7,4},{8,15},{9,14},{10,... | collective-permute-start | bytes 442376 | tf_op jit(solution)/shard_map/ppermute | solution.py:360
  21.2 8.6 %collective-permute-start.7 = (bf16[192,384]{1,0:T(8,128)(2,1)S(1)}, bf16[192,384]{1,0:T(8,128)(2,1)S(1)}, u32[]{:S(2)}, u32[]{:S(2)}) collective-permute-start(bf16[192,384]{1,0:T(8,128)(2,1)S(1)} %get-tuple-element.24.refs_0_), channel_id=1, source_target_pairs={{0,6},{1,7},{2,0},{3,1},{4,2},{5,3},{6,4},{7,5},{8,14},{9,15},{10,... | collective-permute-start | bytes 442376 | tf_op jit(solution)/shard_map/ppermute | solution.py:360
  24.9 10.9 %collective-permute-start.6 = (bf16[192,384]{1,0:T(8,128)(2,1)S(1)}, bf16[192,384]{1,0:T(8,128)(2,1)S(1)}, u32[]{:S(2)}, u32[]{:S(2)}) collective-permute-start(bf16[192,384]{1,0:T(8,128)(2,1)S(1)} %get-tuple-element.24.refs_0_), channel_id=1, source_target_pairs={{0,3},{1,2},{2,5},{3,4},{4,7},{5,6},{6,1},{7,0},{8,11},{9,10},{10,... | collective-permute-start | bytes 442376 | tf_op jit(solution)/shard_map/ppermute | solution.py:360
  35.8 2.8 %collective-permute-start.9 = (bf16[384,1536]{1,0:T(8,128)(2,1)S(1)}, bf16[384,1536]{1,0:T(8,128)(2,1)S(1)}, u32[]{:S(2)}, u32[]{:S(2)}) collective-permute-start(bf16[384,1536]{1,0:T(8,128)(2,1)S(1)} %collective-permute-done.1.refs_0_), channel_id=1, source_target_pairs={{0,8},{8,0},{16,24},{24,16},{1,9},{9,1},{17,25},{25,17},{2,10},{10... | collective-permute-start | bytes 3538952 | tf_op jit(solution)/shard_map/ppermute | solution.py:37
  35.8 7.9 %collective-permute-start.11 = (bf16[128,768]{1,0:T(8,128)(2,1)S(1)}, bf16[128,768]{1,0:T(8,128)(2,1)S(1)}, u32[]{:S(2)}, u32[]{:S(2)}) collective-permute-start(bf16[128,768]{1,0:T(8,128)(2,1)S(1)} %collect.1.own_ref), channel_id=1, source_target_pairs={{0,2},{1,3},{2,0},{3,1},{4,6},{5,7},{6,4},{7,5},{8,10},{9,11},{10,... | collective-permute-start | bytes 589832 | tf_op jit(solution)/shard_map/ppermute | solution.py:363
  43.7 1.9 %collective-permute-start.12 = (bf16[256,768]{1,0:T(8,128)(2,1)S(1)}, bf16[256,768]{1,0:T(8,128)(2,1)S(1)}, u32[]{:S(2)}, u32[]{:S(2)}) collective-permute-start(bf16[256,768]{1,0:T(8,128)(2,1)S(1)} %pair_up.1.out_own_ref), channel_id=1, source_target_pairs={{0,8},{8,0},{16,24},{24,16},{1,9},{9,1},{17,25},{25,17},{2,10},{10... | collective-permute-start | bytes 1179656 | tf_op jit(solution)/shard_map/ppermute | solution.py:37
  43.9 1.7 %collective-permute-start.10 = (bf16[384,128]{1,0:T(8,128)(2,1)S(1)}, bf16[384,128]{1,0:T(8,128)(2,1)S(1)}, u32[]{:S(2)}, u32[]{:S(2)}) collective-permute-start(bf16[384,128]{1,0:T(8,128)(2,1)S(1)} %get-tuple-element.29), channel_id=1, source_target_pairs={{0,8},{8,0},{16,24},{24,16},{1,9},{9,1},{17,25},{25,17},{2,10},{10... | collective-permute-start | bytes 294920 | tf_op jit(solution)/shard_map/ppermute | solution.py:37

commit v8 on v6

--- a/solution.py
+++ b/solution.py
@@ -10,6 +10,8 @@
 CORES = 2
 NEG = -1e30
 ROWS = 192
+BLOCK = 256
+GRAIN = 64
 COST1 = 1_000_000_000
 COST = 1_000_000_000
 
@@ -187,12 +189,6 @@
     keep = jnp.exp(old[0] - top)
     add = jnp.exp(new[0] - top)
     return top, old[1] * keep + new[1] * add, old[2] * keep + new[2] * add
-
-
-def key_bias(mask_ref, count_ref, tile, key_tile, slots):
-    slot = lax.broadcasted_iota(jnp.int32, (1, slots), 1)
-    live = jnp.where(mask_ref[tile, key_tile] > 0, count_ref[key_tile], 0)
-    return jnp.where(slot < live, 0.0, NEG)
 
 
 def project(z_count, x_count, shifts, blocks, latents_own, latents_other):
@@ -256,48 +252,66 @@
         core = lax.rem(seq_index, CORES)
         chip_tile = seq_index - core
         tiles = [chip_tile + core, chip_tile + 1 - core]
-        key_tiles = list(tiles) if local_rows else []
-
-        def place(start, keys, values):
-            rows = slice(start, start + keys.shape[0])
+        ends = [jnp.int32(0)]
+        spans = []
+
+        def place(key_tile, keys, values):
+            rows = pl.ds(pl.multiple_of(ends[-1], GRAIN), keys.shape[0])
             keys_ref[rows, :] = keys
             for group in range(groups):
                 first = 2 * group * LANES
                 values_ref[rows, first : first + LANES] = values[:, group * LANES : (group + 1) * LANES]
-                values_ref[rows, first + LANES : first + 2 * LANES] = jnp.ones((keys.shape[0], LANES), dtype)
-
-        if local_rows:
-            place(0, key_value_ref[:, :own], key_value_ref[:, own:])
+            spans.append((key_tile, ends[-1]))
+            ends.append(ends[-1] + count_ref[key_tile])
+
+        for member in range(CORES if local_rows else 0):
+            rows = slice(member * row_count, (member + 1) * row_count)
+            place(tiles[member], key_value_ref[rows, :own], key_value_ref[rows, own:])
         for part, (_, y_step, swapped) in enumerate(sources):
             projected = jnp.dot(
                 latents_refs[part][...], weight_ref[:, own:], preferred_element_type=jnp.float32
             ).astype(dtype)
-            place(local_rows + part * row_count, projected[:, :own], projected[:, own:])
             from_same = lax.rem(seq_index + seq_count - CORES * y_step, seq_count)
-            key_tiles.append(from_same + 1 - 2 * core if swapped else from_same)
-        for member in range(CORES):
-            bias = jnp.concatenate(
-                [key_bias(mask_ref, count_ref, tiles[member], key_tile, row_count) for key_tile in key_tiles], axis=1
-            )
-            for group in range(groups):
-                lanes = slice(group * LANES, (group + 1) * LANES)
-                for start in range(0, row_count, ROWS):
-                    chunk = slice(start, start + ROWS)
-                    parts = attend_part(
-                        queries_ref[member, chunk, lanes],
-                        keys_ref[:, lanes],
-                        values_ref[:, 2 * group * LANES : 2 * (group + 1) * LANES],
-                        bias,
-                    )
-                    if old_ref is not None:
-                        parts = merge([old_ref[member, which, chunk, lanes] for which in range(3)], parts)
-                    if last:
-                        position = start + lax.broadcasted_iota(jnp.int32, (ROWS, 1), 0)
-                        attended = jnp.where(position < count_ref[tiles[member]], parts[2] / parts[1], 0.0)
-                        refs[member][chunk, lanes] = attended.astype(dtype)
-                    else:
-                        for which, part in enumerate(parts):
-                            refs[0][member, which, chunk, lanes] = part
+            place(from_same + 1 - 2 * core if swapped else from_same, projected[:, :own], projected[:, own:])
+        rest = pl.ds(pl.multiple_of(spans[-1][1] + row_count, GRAIN), BLOCK)
+        keys_ref[rest, :] = jnp.zeros((BLOCK, own), dtype)
+        values_ref[rest, :] = jnp.zeros((BLOCK, 2 * own), dtype)
+        for group in range(groups):
+            first = (2 * group + 1) * LANES
+            values_ref[:, first : first + LANES] = jnp.ones((slots + BLOCK, LANES), dtype)
+
+        def over(keys_taken):
+            slot = lax.broadcasted_iota(jnp.int32, (1, keys_taken), 1)
+            for member in range(CORES):
+                bias = jnp.full((1, keys_taken), NEG, jnp.float32)
+                for key_tile, start in spans:
+                    end = start + jnp.where(mask_ref[tiles[member], key_tile] > 0, count_ref[key_tile], 0)
+                    bias = jnp.where((slot >= start) & (slot < end), 0.0, bias)
+                for group in range(groups):
+                    lanes = slice(group * LANES, (group + 1) * LANES)
+                    for start in range(0, row_count, ROWS):
+                        chunk = slice(start, start + ROWS)
+                        parts = attend_part(
+                            queries_ref[member, chunk, lanes],
+                            keys_ref[:keys_taken, lanes],
+                            values_ref[:keys_taken, 2 * group * LANES : 2 * (group + 1) * LANES],
+                            bias,
+                        )
+                        if old_ref is not None:
+                            parts = merge([old_ref[member, which, chunk, lanes] for which in range(3)], parts)
+                        if last:
+                            position = start + lax.broadcasted_iota(jnp.int32, (ROWS, 1), 0)
+                            attended = jnp.where(position < count_ref[tiles[member]], parts[2] / parts[1], 0.0)
+                            refs[member][chunk, lanes] = attended.astype(dtype)
+                        else:
+                            for which, part in enumerate(parts):
+                                refs[0][member, which, chunk, lanes] = part
+
+        blocks = (ends[-1] + BLOCK - 1) // BLOCK
+        fewest, most = max(slots // (2 * BLOCK), 1), slots // BLOCK
+        for taken in range(fewest, most + 1):
+            fits = blocks <= taken if taken == fewest else blocks == taken
+            pl.when(fits)(lambda taken=taken: over(taken * BLOCK))
 
     if last:
         out_shapes = [shaped((row_count, own), dtype)] * CORES
@@ -308,7 +322,7 @@
         "attend_last" if last else "attend",
         [SMEM, SMEM] + [VMEM] * len(given),
         out_shapes,
-        scratch_shapes=[pltpu.VMEM((slots, own), dtype), pltpu.VMEM((slots, 2 * own), dtype)],
+        scratch_shapes=[pltpu.VMEM((slots + BLOCK, own), dtype), pltpu.VMEM((slots + BLOCK, 2 * own), dtype)],
         cost=COST,
     )(tile_mask, tile_counts, *given)
 

time: 45 us -> 44.7 us (level)
  no operation moved by 1% of the time
where the time goes in v8:
time: 44.7 us; the launch traced here: 44.8 us
  waiting for transfers between devices  19 us (43%)
  starting transfers between devices  15.8 us (35%)
  Pallas kernels  9.68 us (22%)
    ppermute x7, waiting for transfers between devices, hop(): lax.ppermute(array, 'fsdp', rotation(z_count, x_count, z_step, x_step))  17.7 us
    ppermute x7, starting transfers between devices, hop(): lax.ppermute(array, 'fsdp', rotation(z_count, x_count, z_step, x_step))  10.5 us
    pallas_call x6, Pallas kernels, run(): inner(*[pltpu.with_memory_space_constraint(arg, pltpu.HBM if spec is SMEM...  9.68 us
    ppermute x1, starting transfers between devices, y_rotation(): lax.ppermute(array, 'seq', [(s, (s + CORES * step) % seq_count) for s in...  2.52 us
    ppermute x1, starting transfers between devices, flip(): lax.ppermute(array, 'fsdp', [(f, f ^ shift * x_count) for f in range(fsdp...  1.71 us
    ppermute x4, waiting for transfers between devices, core_swap(): return lax.ppermute(array, 'seq', [(s, s ^ 1) for s in range(seq_count)])  1.36 us
    ppermute x4, starting transfers between devices, core_swap(): return lax.ppermute(array, 'seq', [(s, s ^ 1) for s in range(seq_count)])  1.03 us
  transfers between devices with their start and end apart: 13, of which 5 were waited for; matrix products, arithmetic and copies ran while one was open for 0% of the time, Pallas kernels for 18%

profile of v8, /device:TPU:0, one launch (start us, length us, event | category | flops | bytes accessed | tf_op | source)
XLA Modules:
  0.0 44.8 jit_solution(617001985111554024)
XLA Ops:
  0.0 0.5 %collective-permute-start = (bf16[384,1536]{1,0:T(8,128)(2,1)}, bf16[384,1536]{1,0:T(8,128)(2,1)S(1)}, u32[]{:S(2)}, u32[]{:S(2)}) collective-permute-start(bf16[384,1536]{1,0:T(8,128)(2,1)} %bitcast.2), channel_id=1, source_target_pairs={{0,8},{8,0},{16,24},{24,16},{1,9},{9,1},{17,25},{25,17},{2,10},{10... | collective-permute-start | bytes 3538952 | tf_op jit(solution)/shard_map/ppermute | solution.py:39
  0.5 2.5 %collective-permute-start.1 = (bf16[384,1536]{1,0:T(8,128)(2,1)}, bf16[384,1536]{1,0:T(8,128)(2,1)S(1)}, u32[]{:S(2)}, u32[]{:S(2)}) collective-permute-start(bf16[384,1536]{1,0:T(8,128)(2,1)} %bitcast.3), channel_id=1, source_target_pairs={{0,16},{8,24},{16,0},{24,8},{1,17},{9,25},{17,1},{25,9},{2,18},{10... | collective-permute-start | bytes 3538952 | tf_op jit(solution)/shard_map/ppermute | solution.py:43
  3.0 1.0 %halves.1 = (bf16[192,384]{1,0:T(8,128)(2,1)S(1)}, bf16[256,384]{1,0:T(8,128)(2,1)S(1)}) custom-call(bf16[192,768]{1,0:T(8,128)(2,1)} %qkv_ref.1, bf16[32,1536]{1,0:T(8,128)(2,1)} %out_ref.1), custom_call_target="tpu_custom_call" | custom-call | tf_op jit(solution)/shard_map/halves/pallas_call | solution.py:64
  4.0 2.7 %collective-permute-start.3 = (bf16[256,384]{1,0:T(8,128)(2,1)S(1)}, bf16[256,384]{1,0:T(8,128)(2,1)S(1)}, u32[]{:S(2)}, u32[]{:S(2)}) collective-permute-start(bf16[256,384]{1,0:T(8,128)(2,1)S(1)} %get-tuple-element.20.refs_0_), channel_id=1, source_target_pairs={{0,4},{1,5},{2,6},{3,7},{4,0},{5,1},{6,2},{7,3},{8,12},{9,13},{10,... | collective-permute-start | bytes 589832 | tf_op jit(solution)/shard_map/ppermute | solution.py:374
  6.6 0.0 collective-permute-done.other_ref
  6.6 1.5 %collective-permute-start.2 = (bf16[256,384]{1,0:T(8,128)(2,1)S(1)}, bf16[256,384]{1,0:T(8,128)(2,1)S(1)}, u32[]{:S(2)}, u32[]{:S(2)}) collective-permute-start(bf16[256,384]{1,0:T(8,128)(2,1)S(1)} %get-tuple-element.20.refs_0_), channel_id=1, source_target_pairs={{0,1},{1,0},{2,3},{3,2},{4,5},{5,4},{6,7},{7,6},{8,9},{9,8},{10,11... | collective-permute-start | bytes 589832 | tf_op jit(solution)/shard_map/ppermute | solution.py:374
  8.1 1.6 %collective-permute-start.5 = (bf16[192,384]{1,0:T(8,128)(2,1)S(1)}, bf16[192,384]{1,0:T(8,128)(2,1)S(1)}, u32[]{:S(2)}, u32[]{:S(2)}) collective-permute-start(bf16[192,384]{1,0:T(8,128)(2,1)S(1)} %get-tuple-element.24.refs_0_), channel_id=1, source_target_pairs={{0,2},{1,3},{2,4},{3,5},{4,6},{5,7},{6,0},{7,1},{8,10},{9,11},{10,... | collective-permute-start | bytes 442376 | tf_op jit(solution)/shard_map/ppermute | solution.py:374
  9.7 9.7 %collective-permute-done.3.refs_2_ = bf16[256,384]{1,0:T(8,128)(2,1)S(1)} collective-permute-done((bf16[256,384]{1,0:T(8,128)(2,1)S(1)}, bf16[256,384]{1,0:T(8,128)(2,1)S(1)}, u32[]{:S(2)}, u32[]{:S(2)}) %collective-permute-start.3) | collective-permute-done | bytes 196640 | tf_op jit(solution)/shard_map/ppermute | solution.py:374
  19.4 1.5 %collective-permute-start.4 = (bf16[256,384]{1,0:T(8,128)(2,1)S(1)}, bf16[256,384]{1,0:T(8,128)(2,1)S(1)}, u32[]{:S(2)}, u32[]{:S(2)}) collective-permute-start(bf16[256,384]{1,0:T(8,128)(2,1)S(1)} %collective-permute-done.3.refs_2_), channel_id=1, source_target_pairs={{0,1},{1,0},{2,3},{3,2},{4,5},{5,4},{6,7},{7,6},{8,9},{9,8},{10,11... | collective-permute-start | bytes 589832 | tf_op jit(solution)/shard_map/ppermute | solution.py:374
  20.8 0.4 collective-permute-start.8
  21.2 0.0 collective-permute-done.5.refs_3_
  21.2 0.0 collective-permute-done.2.refs_1_
  21.2 0.6 %collective-permute-start.7 = (bf16[192,384]{1,0:T(8,128)(2,1)S(1)}, bf16[192,384]{1,0:T(8,128)(2,1)S(1)}, u32[]{:S(2)}, u32[]{:S(2)}) collective-permute-start(bf16[192,384]{1,0:T(8,128)(2,1)S(1)} %get-tuple-element.24.refs_0_), channel_id=1, source_target_pairs={{0,6},{1,7},{2,0},{3,1},{4,2},{5,3},{6,4},{7,5},{8,14},{9,15},{10,... | collective-permute-start | bytes 442376 | tf_op jit(solution)/shard_map/ppermute | solution.py:374
  21.8 2.3 %collective-permute-start.6 = (bf16[192,384]{1,0:T(8,128)(2,1)S(1)}, bf16[192,384]{1,0:T(8,128)(2,1)S(1)}, u32[]{:S(2)}, u32[]{:S(2)}) collective-permute-start(bf16[192,384]{1,0:T(8,128)(2,1)S(1)} %get-tuple-element.24.refs_0_), channel_id=1, source_target_pairs={{0,3},{1,2},{2,5},{3,4},{4,7},{5,6},{6,1},{7,0},{8,11},{9,10},{10,... | collective-permute-start | bytes 442376 | tf_op jit(solution)/shard_map/ppermute | solution.py:374
  24.2 6.8 %collective-permute-done.4.refs_3_.refs_4_ = bf16[256,384]{1,0:T(8,128)(2,1)S(1)} collective-permute-done((bf16[256,384]{1,0:T(8,128)(2,1)S(1)}, bf16[256,384]{1,0:T(8,128)(2,1)S(1)}, u32[]{:S(2)}, u32[]{:S(2)}) %collective-permute-start.4) | collective-permute-done | bytes 196640 | tf_op jit(solution)/shard_map/ppermute | solution.py:374
  31.0 0.0 collective-permute-done.8.refs_7_
  31.0 0.0 collective-permute-done.1.refs_0_
  31.0 1.1 %collective-permute-done.7.refs_6_ = bf16[192,384]{1,0:T(8,128)(2,1)S(1)} collective-permute-done((bf16[192,384]{1,0:T(8,128)(2,1)S(1)}, bf16[192,384]{1,0:T(8,128)(2,1)S(1)}, u32[]{:S(2)}, u32[]{:S(2)}) %collective-permute-start.7) | collective-permute-done | bytes 147488 | tf_op jit(solution)/shard_map/ppermute | solution.py:374
  32.1 0.2 collective-permute-done.6.refs_5_
  32.2 0.0 collective-permute-start.9
  32.3 1.7 %collective-permute-start.11 = (bf16[128,768]{1,0:T(8,128)(2,1)S(1)}, bf16[128,768]{1,0:T(8,128)(2,1)S(1)}, u32[]{:S(2)}, u32[]{:S(2)}) collective-permute-start(bf16[128,768]{1,0:T(8,128)(2,1)S(1)} %collect.1.own_ref), channel_id=1, source_target_pairs={{0,2},{1,3},{2,0},{3,1},{4,6},{5,7},{6,4},{7,5},{8,10},{9,11},{10,... | collective-permute-start | bytes 589832 | tf_op jit(solution)/shard_map/ppermute | solution.py:377
  34.0 2.2 %project.1 = (bf16[2,384,128]{2,1,0:T(8,128)(2,1)S(1)}, bf16[1536,384]{1,0:T(8,128)(2,1)S(1)}, bf16[768,256]{1,0:T(8,128)(2,1)S(1)}) custom-call(bf16[384,1536]{1,0:T(8,128)(2,1)} %bitcast.4, bf16[384,1536]{1,0:T(8,128)(2,1)S(1)} %collective-permute-done.other_ref, bf16[192,384]{1,0:T(8,128)(2,1)S(1)} %get-tuple-element.24.refs_0_, ...), custom_call_target="tpu_custom_call" | custom-call | flops 1000000000 | tf_op jit(solution)/shard_map/project/pallas_call | solution.py:64
  36.1 0.0 collective-permute-done.9.refs_1_
  36.1 4.9 %attend_last.1 = (bf16[384,128]{1,0:T(8,128)(2,1)S(1)}, bf16[384,128]{1,0:T(8,128)(2,1)S(1)}) custom-call(s32[4,4]{1,0:T(4,128)} %mask_ref.1, s32[4]{0:T(128)} %count_ref.1, bf16[1536,384]{1,0:T(8,128)(2,1)S(1)} %get-tuple-element.25.weight_ref, bf16[2,384,128]{2,1,0:T(8,128)(2,1)S(1)} %get-tuple-element.26.queries_ref, ...), custom_call_target="tpu_custom_call" | custom-call | flops 1000000000 | tf_op jit(solution)/shard_map/attend_last/pallas_call | solution.py:64
  41.0 0.0 collective-permute-done.11.got_ref
  41.1 0.3 collective-permute-start.12
  41.4 0.3 collective-permute-start.10
  41.6 1.4 %collective-permute-done.10.partner_ref = bf16[384,128]{1,0:T(8,128)(2,1)S(1)} collective-permute-done((bf16[384,128]{1,0:T(8,128)(2,1)S(1)}, bf16[384,128]{1,0:T(8,128)(2,1)S(1)}, u32[]{:S(2)}, u32[]{:S(2)}) %collective-permute-start.10) | collective-permute-done | bytes 98336 | tf_op jit(solution)/shard_map/ppermute | solution.py:39
  43.0 0.0 collective-permute-done.12.out_partner_ref
  43.0 1.6 %project_out.1 = bf16[384,1536]{1,0:T(8,128)(2,1)} custom-call(bf16[384,128]{1,0:T(8,128)(2,1)S(1)} %get-tuple-element.28.own_ref, bf16[384,128]{1,0:T(8,128)(2,1)S(1)} %collective-permute-done.10.partner_ref, bf16[256,768]{1,0:T(8,128)(2,1)S(1)} %pair_up.1.out_own_ref, bf16[256,768]{1,0:T(8,128)(2,1)S(1)} %collective-permute-done.12.out_partner_ref), custom_call_target="tpu_custom_call" | custom-call | tf_op jit(solution)/shard_map/project_out/pallas_call | solution.py:64
  (2 shorter events, 0.1 us)
Async XLA Ops:
  0.0 6.6 %collective-permute-start = (bf16[384,1536]{1,0:T(8,128)(2,1)}, bf16[384,1536]{1,0:T(8,128)(2,1)S(1)}, u32[]{:S(2)}, u32[]{:S(2)}) collective-permute-start(bf16[384,1536]{1,0:T(8,128)(2,1)} %bitcast.2), channel_id=1, source_target_pairs={{0,8},{8,0},{16,24},{24,16},{1,9},{9,1},{17,25},{25,17},{2,10},{10... | collective-permute-start | bytes 3538952 | tf_op jit(solution)/shard_map/ppermute | solution.py:39
  0.5 30.5 %collective-permute-start.1 = (bf16[384,1536]{1,0:T(8,128)(2,1)}, bf16[384,1536]{1,0:T(8,128)(2,1)S(1)}, u32[]{:S(2)}, u32[]{:S(2)}) collective-permute-start(bf16[384,1536]{1,0:T(8,128)(2,1)} %bitcast.3), channel_id=1, source_target_pairs={{0,16},{8,24},{16,0},{24,8},{1,17},{9,25},{17,1},{25,9},{2,18},{10... | collective-permute-start | bytes 3538952 | tf_op jit(solution)/shard_map/ppermute | solution.py:43
  4.0 15.4 %collective-permute-start.3 = (bf16[256,384]{1,0:T(8,128)(2,1)S(1)}, bf16[256,384]{1,0:T(8,128)(2,1)S(1)}, u32[]{:S(2)}, u32[]{:S(2)}) collective-permute-start(bf16[256,384]{1,0:T(8,128)(2,1)S(1)} %get-tuple-element.20.refs_0_), channel_id=1, source_target_pairs={{0,4},{1,5},{2,6},{3,7},{4,0},{5,1},{6,2},{7,3},{8,12},{9,13},{10,... | collective-permute-start | bytes 589832 | tf_op jit(solution)/shard_map/ppermute | solution.py:374
  6.6 14.6 %collective-permute-start.2 = (bf16[256,384]{1,0:T(8,128)(2,1)S(1)}, bf16[256,384]{1,0:T(8,128)(2,1)S(1)}, u32[]{:S(2)}, u32[]{:S(2)}) collective-permute-start(bf16[256,384]{1,0:T(8,128)(2,1)S(1)} %get-tuple-element.20.refs_0_), channel_id=1, source_target_pairs={{0,1},{1,0},{2,3},{3,2},{4,5},{5,4},{6,7},{7,6},{8,9},{9,8},{10,11... | collective-permute-start | bytes 589832 | tf_op jit(solution)/shard_map/ppermute | solution.py:374
  8.1 13.1 %collective-permute-start.5 = (bf16[192,384]{1,0:T(8,128)(2,1)S(1)}, bf16[192,384]{1,0:T(8,128)(2,1)S(1)}, u32[]{:S(2)}, u32[]{:S(2)}) collective-permute-start(bf16[192,384]{1,0:T(8,128)(2,1)S(1)} %get-tuple-element.24.refs_0_), channel_id=1, source_target_pairs={{0,2},{1,3},{2,4},{3,5},{4,6},{5,7},{6,0},{7,1},{8,10},{9,11},{10,... | collective-permute-start | bytes 442376 | tf_op jit(solution)/shard_map/ppermute | solution.py:374
  19.4 11.6 %collective-permute-start.4 = (bf16[256,384]{1,0:T(8,128)(2,1)S(1)}, bf16[256,384]{1,0:T(8,128)(2,1)S(1)}, u32[]{:S(2)}, u32[]{:S(2)}) collective-permute-start(bf16[256,384]{1,0:T(8,128)(2,1)S(1)} %collective-permute-done.3.refs_2_), channel_id=1, source_target_pairs={{0,1},{1,0},{2,3},{3,2},{4,5},{5,4},{6,7},{7,6},{8,9},{9,8},{10,11... | collective-permute-start | bytes 589832 | tf_op jit(solution)/shard_map/ppermute | solution.py:374
  20.8 10.1 %collective-permute-start.8 = (bf16[192,384]{1,0:T(8,128)(2,1)S(1)}, bf16[192,384]{1,0:T(8,128)(2,1)S(1)}, u32[]{:S(2)}, u32[]{:S(2)}) collective-permute-start(bf16[192,384]{1,0:T(8,128)(2,1)S(1)} %get-tuple-element.24.refs_0_), channel_id=1, source_target_pairs={{0,7},{1,6},{2,1},{3,0},{4,3},{5,2},{6,5},{7,4},{8,15},{9,14},{10,... | collective-permute-start | bytes 442376 | tf_op jit(solution)/shard_map/ppermute | solution.py:374
  21.2 10.9 %collective-permute-start.7 = (bf16[192,384]{1,0:T(8,128)(2,1)S(1)}, bf16[192,384]{1,0:T(8,128)(2,1)S(1)}, u32[]{:S(2)}, u32[]{:S(2)}) collective-permute-start(bf16[192,384]{1,0:T(8,128)(2,1)S(1)} %get-tuple-element.24.refs_0_), channel_id=1, source_target_pairs={{0,6},{1,7},{2,0},{3,1},{4,2},{5,3},{6,4},{7,5},{8,14},{9,15},{10,... | collective-permute-start | bytes 442376 | tf_op jit(solution)/shard_map/ppermute | solution.py:374
  21.8 10.4 %collective-permute-start.6 = (bf16[192,384]{1,0:T(8,128)(2,1)S(1)}, bf16[192,384]{1,0:T(8,128)(2,1)S(1)}, u32[]{:S(2)}, u32[]{:S(2)}) collective-permute-start(bf16[192,384]{1,0:T(8,128)(2,1)S(1)} %get-tuple-element.24.refs_0_), channel_id=1, source_target_pairs={{0,3},{1,2},{2,5},{3,4},{4,7},{5,6},{6,1},{7,0},{8,11},{9,10},{10,... | collective-permute-start | bytes 442376 | tf_op jit(solution)/shard_map/ppermute | solution.py:374
  32.2 3.9 %collective-permute-start.9 = (bf16[384,1536]{1,0:T(8,128)(2,1)S(1)}, bf16[384,1536]{1,0:T(8,128)(2,1)S(1)}, u32[]{:S(2)}, u32[]{:S(2)}) collective-permute-start(bf16[384,1536]{1,0:T(8,128)(2,1)S(1)} %collective-permute-done.1.refs_0_), channel_id=1, source_target_pairs={{0,8},{8,0},{16,24},{24,16},{1,9},{9,1},{17,25},{25,17},{2,10},{10... | collective-permute-start | bytes 3538952 | tf_op jit(solution)/shard_map/ppermute | solution.py:39
  32.3 8.8 %collective-permute-start.11 = (bf16[128,768]{1,0:T(8,128)(2,1)S(1)}, bf16[128,768]{1,0:T(8,128)(2,1)S(1)}, u32[]{:S(2)}, u32[]{:S(2)}) collective-permute-start(bf16[128,768]{1,0:T(8,128)(2,1)S(1)} %collect.1.own_ref), channel_id=1, source_target_pairs={{0,2},{1,3},{2,0},{3,1},{4,6},{5,7},{6,4},{7,5},{8,10},{9,11},{10,... | collective-permute-start | bytes 589832 | tf_op jit(solution)/shard_map/ppermute | solution.py:377
  41.1 1.9 %collective-permute-start.12 = (bf16[256,768]{1,0:T(8,128)(2,1)S(1)}, bf16[256,768]{1,0:T(8,128)(2,1)S(1)}, u32[]{:S(2)}, u32[]{:S(2)}) collective-permute-start(bf16[256,768]{1,0:T(8,128)(2,1)S(1)} %pair_up.1.out_own_ref), channel_id=1, source_target_pairs={{0,8},{8,0},{16,24},{24,16},{1,9},{9,1},{17,25},{25,17},{2,10},{10... | collective-permute-start | bytes 1179656 | tf_op jit(solution)/shard_map/ppermute | solution.py:39
  41.4 1.6 %collective-permute-start.10 = (bf16[384,128]{1,0:T(8,128)(2,1)S(1)}, bf16[384,128]{1,0:T(8,128)(2,1)S(1)}, u32[]{:S(2)}, u32[]{:S(2)}) collective-permute-start(bf16[384,128]{1,0:T(8,128)(2,1)S(1)} %get-tuple-element.29), channel_id=1, source_target_pairs={{0,8},{8,0},{16,24},{24,16},{1,9},{9,1},{17,25},{25,17},{2,10},{10... | collective-permute-start | bytes 294920 | tf_op jit(solution)/shard_map/ppermute | solution.py:39

commit v9 on v8

--- a/solution.py
+++ b/solution.py
@@ -191,7 +191,76 @@
     return top, old[1] * keep + new[1] * add, old[2] * keep + new[2] * add
 
 
-def project(z_count, x_count, shifts, blocks, latents_own, latents_other):
+def project(z_count, x_count, shifts, blocks, latents_own, latents_other, early=None):
+    count = len(blocks)
+    columns = blocks[0].shape[1]
+    own = columns // 3
+    row_count, depth = latents_own.shape
+    rows = depth // (z_count * x_count)
+    band = x_count * rows
+    steps = sorted({dz for dz, _ in shifts})
+    dtype = latents_own.dtype
+    scale = float(E) ** -0.5
+
+    def assemble(block_refs, weight_ref):
+        fsdp_index = lax.axis_index("fsdp")
+        z_index = fsdp_index // x_count
+        x_index = lax.rem(fsdp_index, x_count)
+        for (dz, dx), block_ref in zip(shifts, block_refs):
+            place = lax.rem(z_index + z_count - dz, z_count) * x_count + lax.rem(x_index + x_count - dx, x_count)
+            weight_ref[pl.ds(pl.multiple_of(place * rows, 16), rows), :] = block_ref[:rows, :]
+        starts = [pl.multiple_of(lax.rem(z_index + z_count - dz, z_count) * band, LANES) for dz in steps]
+        return starts, jnp.concatenate([weight_ref[pl.ds(start, band), :] for start in starts], axis=0)
+
+    def partial(latents_ref, starts, weight):
+        latents = jnp.concatenate([latents_ref[:, pl.ds(start, band)] for start in starts], axis=1)
+        return jnp.dot(latents, weight, preferred_element_type=jnp.float32)
+
+    def first(own_ref, other_ref, *refs):
+        block_refs = refs[:count]
+        latents_ref, weight_ref, total_ref, sem = refs[count:]
+        fetch = pltpu.make_async_copy(own_ref, latents_ref, sem)
+        fetch.start()
+        starts, weight = assemble(block_refs, weight_ref)
+        total_ref[1] = partial(other_ref, starts, weight)
+        fetch.wait()
+        total_ref[0] = partial(latents_ref, starts, weight)
+
+    def rest(own_ref, other_ref, old_weight_ref, total_ref, *refs):
+        block_refs = refs[:count]
+        queries_ref, weight_ref, key_value_ref = refs[count:]
+        starts, weight = assemble(block_refs, weight_ref)
+        for member, from_ref in enumerate((own_ref, other_ref)):
+            projected = (total_ref[member] + partial(from_ref, starts, weight)).astype(dtype)
+            queries_ref[member] = projected[:, :own] * jnp.asarray(scale, dtype)
+            key_value_ref[member * row_count : (member + 1) * row_count, :] = projected[:, own:]
+
+    weight_shape = shaped((depth, columns), dtype)
+    if early is None:
+        return call(
+            first,
+            "project_first",
+            [HBM] + [VMEM] * (count + 1),
+            [shaped((row_count, depth), dtype), weight_shape, shaped((CORES, row_count, columns), jnp.float32)],
+            scratch_shapes=[pltpu.SemaphoreType.DMA(())],
+            cost=COST1,
+        )(latents_own, latents_other, *blocks)
+    own_tile, weight, total = early
+    return call(
+        rest,
+        "project",
+        [VMEM] * (count + 4),
+        [
+            shaped((CORES, row_count, own), dtype),
+            weight_shape,
+            shaped((CORES * row_count, 2 * own), dtype),
+        ],
+        cost=COST1,
+        aliases={2: 1},
+    )(own_tile, latents_other, weight, total, *blocks)
+
+
+def project_whole(z_count, x_count, shifts, blocks, latents_own, latents_other):
     count = len(blocks)
     columns = blocks[0].shape[1]
     own = columns // 3
@@ -398,6 +467,13 @@
             for x_step in range(1, x_count):
                 came[z_step, x_step] = hop(third, z_step, x_step)
 
+    axes = (z_count, x_count)
+    early = None
+    if x_count * half.shape[0] % LANES == 0:
+        sooner = [shift for shift in came if shift[0] in (0, turn)]
+        early = project(*axes, sooner, [came[shift] for shift in sooner], latents_own, latents_other)
+        packed = after(packed, early[2])
+
     out_own = collect(
         [[packed] + beside, [came[turn, x_step] for x_step in range(x_count)]],
         x_count,
@@ -414,10 +490,15 @@
 
     near = after(along_y, out_own, *list(came.values())[1:])
     far = [core_swap(array, seq_count) for array in near]
-    came[0, 0] = after(half, *near)
-    queries, weight, key_value = project(
-        z_count, x_count, list(came), list(came.values()), latents_own, latents_other
-    )
+    if early is not None:
+        later = [shift for shift in came if shift not in sooner]
+        came[later[-1]] = after(came[later[-1]], *near)
+        queries, weight, key_value = project(
+            *axes, later, [came[shift] for shift in later], latents_own, latents_other, early
+        )
+    else:
+        came[0, 0] = after(half, *near)
+        queries, weight, key_value = project_whole(*axes, list(came), list(came.values()), latents_own, latents_other)
     state = None
     for step in range(1, chips):
         last = step == chips - 1

time: 44.7 us -> 44.4 us (level)
  starting transfers between devices: 15.8 us -> 15.2 us
  Pallas kernels: 9.68 us -> 10.2 us
    ppermute x7, waiting for transfers between devices: 17.7 us -> 16.4 us  [hop(): lax.ppermute(array, 'fsdp', rotation(z_count, x_count, z_step, x_step))]
    ppermute x4, waiting for transfers between devices: 1.36 us -> 2.29 us  [core_swap(): return lax.ppermute(array, 'seq', [(s, s ^ 1) for s in range(seq_count)])]
    ppermute x1, starting transfers between devices: 1.71 us -> 1.03 us  [flip(): lax.ppermute(array, 'fsdp', [(f, f ^ shift * x_count) for f in range(fsdp...]
    pallas_call x6 -> x7, Pallas kernels: 9.68 us -> 10.2 us  [run(): inner(*[pltpu.with_memory_space_constraint(arg, pltpu.HBM if spec is SMEM...]
  transfers between devices with their start and end apart: 13 -> 13, of which waited for: 5 -> 4; matrix products, arithmetic and copies ran while one was open for 0% -> 0% of each run, Pallas kernels for 18% -> 19%
where the time goes in v9:
time: 44.4 us
  waiting for transfers between devices  18.7 us (42%)
  starting transfers between devices  15.2 us (34%)
  Pallas kernels  10.2 us (23%)
    ppermute x7, waiting for transfers between devices, hop(): lax.ppermute(array, 'fsdp', rotation(z_count, x_count, z_step, x_step))  16.4 us
    ppermute x7, starting transfers between devices, hop(): lax.ppermute(array, 'fsdp', rotation(z_count, x_count, z_step, x_step))  10.5 us
    pallas_call x7, Pallas kernels, run(): inner(*[pltpu.with_memory_space_constraint(arg, pltpu.HBM if spec is SMEM...  10.2 us
    ppermute x1, starting transfers between devices, y_rotation(): lax.ppermute(array, 'seq', [(s, (s + CORES * step) % seq_count) for s in...  2.52 us
    ppermute x4, waiting for transfers between devices, core_swap(): return lax.ppermute(array, 'seq', [(s, s ^ 1) for s in range(seq_count)])  2.29 us
    ppermute x4, starting transfers between devices, core_swap(): return lax.ppermute(array, 'seq', [(s, s ^ 1) for s in range(seq_count)])  1.1 us
    ppermute x1, starting transfers between devices, flip(): lax.ppermute(array, 'fsdp', [(f, f ^ shift * x_count) for f in range(fsdp...  1.03 us
  transfers between devices with their start and end apart: 13, of which 4 were waited for; matrix products, arithmetic and copies ran while one was open for 0% of the time, Pallas kernels for 19%

profile of v9, /device:TPU:0, one launch (start us, length us, event | category | flops | bytes accessed | tf_op | source)
XLA Modules:
  0.0 44.4 jit_solution(12345125483627536544)
XLA Ops:
  0.0 0.5 %collective-permute-start = (bf16[384,1536]{1,0:T(8,128)(2,1)}, bf16[384,1536]{1,0:T(8,128)(2,1)S(1)}, u32[]{:S(2)}, u32[]{:S(2)}) collective-permute-start(bf16[384,1536]{1,0:T(8,128)(2,1)} %bitcast.2), channel_id=1, source_target_pairs={{0,8},{8,0},{16,24},{24,16},{1,9},{9,1},{17,25},{25,17},{2,10},{10... | collective-permute-start | bytes 3538952 | tf_op jit(solution)/shard_map/ppermute | solution.py:39
  0.5 2.5 %collective-permute-start.8 = (bf16[384,1536]{1,0:T(8,128)(2,1)}, bf16[384,1536]{1,0:T(8,128)(2,1)S(1)}, u32[]{:S(2)}, u32[]{:S(2)}) collective-permute-start(bf16[384,1536]{1,0:T(8,128)(2,1)} %bitcast.3), channel_id=1, source_target_pairs={{0,16},{8,24},{16,0},{24,8},{1,17},{9,25},{17,1},{25,9},{2,18},{10... | collective-permute-start | bytes 3538952 | tf_op jit(solution)/shard_map/ppermute | solution.py:43
  3.0 1.0 %halves.1 = (bf16[192,384]{1,0:T(8,128)(2,1)S(1)}, bf16[256,384]{1,0:T(8,128)(2,1)S(1)}) custom-call(bf16[192,768]{1,0:T(8,128)(2,1)} %qkv_ref.1, bf16[32,1536]{1,0:T(8,128)(2,1)} %out_ref.1), custom_call_target="tpu_custom_call" | custom-call | tf_op jit(solution)/shard_map/halves/pallas_call | solution.py:64
  4.0 2.7 %collective-permute-start.2 = (bf16[256,384]{1,0:T(8,128)(2,1)S(1)}, bf16[256,384]{1,0:T(8,128)(2,1)S(1)}, u32[]{:S(2)}, u32[]{:S(2)}) collective-permute-start(bf16[256,384]{1,0:T(8,128)(2,1)S(1)} %get-tuple-element.30.refs_0_), channel_id=1, source_target_pairs={{0,4},{1,5},{2,6},{3,7},{4,0},{5,1},{6,2},{7,3},{8,12},{9,13},{10,... | collective-permute-start | bytes 589832 | tf_op jit(solution)/shard_map/ppermute | solution.py:443
  6.6 0.0 collective-permute-done.other_ref
  6.6 1.5 %collective-permute-start.1 = (bf16[256,384]{1,0:T(8,128)(2,1)S(1)}, bf16[256,384]{1,0:T(8,128)(2,1)S(1)}, u32[]{:S(2)}, u32[]{:S(2)}) collective-permute-start(bf16[256,384]{1,0:T(8,128)(2,1)S(1)} %get-tuple-element.30.refs_0_), channel_id=1, source_target_pairs={{0,1},{1,0},{2,3},{3,2},{4,5},{5,4},{6,7},{7,6},{8,9},{9,8},{10,11... | collective-permute-start | bytes 589832 | tf_op jit(solution)/shard_map/ppermute | solution.py:443
  8.1 1.6 %collective-permute-start.4 = (bf16[192,384]{1,0:T(8,128)(2,1)S(1)}, bf16[192,384]{1,0:T(8,128)(2,1)S(1)}, u32[]{:S(2)}, u32[]{:S(2)}) collective-permute-start(bf16[192,384]{1,0:T(8,128)(2,1)S(1)} %get-tuple-element.29.refs_0_), channel_id=1, source_target_pairs={{0,2},{1,3},{2,4},{3,5},{4,6},{5,7},{6,0},{7,1},{8,10},{9,11},{10,... | collective-permute-start | bytes 442376 | tf_op jit(solution)/shard_map/ppermute | solution.py:443
  9.7 9.7 %collective-permute-done.2.refs_2_ = bf16[256,384]{1,0:T(8,128)(2,1)S(1)} collective-permute-done((bf16[256,384]{1,0:T(8,128)(2,1)S(1)}, bf16[256,384]{1,0:T(8,128)(2,1)S(1)}, u32[]{:S(2)}, u32[]{:S(2)}) %collective-permute-start.2) | collective-permute-done | bytes 196640 | tf_op jit(solution)/shard_map/ppermute | solution.py:443
  19.4 1.5 %collective-permute-start.3 = (bf16[256,384]{1,0:T(8,128)(2,1)S(1)}, bf16[256,384]{1,0:T(8,128)(2,1)S(1)}, u32[]{:S(2)}, u32[]{:S(2)}) collective-permute-start(bf16[256,384]{1,0:T(8,128)(2,1)S(1)} %collective-permute-done.2.refs_2_), channel_id=1, source_target_pairs={{0,1},{1,0},{2,3},{3,2},{4,5},{5,4},{6,7},{7,6},{8,9},{9,8},{10,11... | collective-permute-start | bytes 589832 | tf_op jit(solution)/shard_map/ppermute | solution.py:443
  20.8 0.4 collective-permute-start.7
  21.2 0.0 collective-permute-done.4.refs_0_
  21.2 0.0 collective-permute-done.1.refs_1_
  21.2 0.6 %collective-permute-start.6 = (bf16[192,384]{1,0:T(8,128)(2,1)S(1)}, bf16[192,384]{1,0:T(8,128)(2,1)S(1)}, u32[]{:S(2)}, u32[]{:S(2)}) collective-permute-start(bf16[192,384]{1,0:T(8,128)(2,1)S(1)} %get-tuple-element.29.refs_0_), channel_id=1, source_target_pairs={{0,6},{1,7},{2,0},{3,1},{4,2},{5,3},{6,4},{7,5},{8,14},{9,15},{10,... | collective-permute-start | bytes 442376 | tf_op jit(solution)/shard_map/ppermute | solution.py:443
  21.8 2.3 %collective-permute-start.5 = (bf16[192,384]{1,0:T(8,128)(2,1)S(1)}, bf16[192,384]{1,0:T(8,128)(2,1)S(1)}, u32[]{:S(2)}, u32[]{:S(2)}) collective-permute-start(bf16[192,384]{1,0:T(8,128)(2,1)S(1)} %get-tuple-element.29.refs_0_), channel_id=1, source_target_pairs={{0,3},{1,2},{2,5},{3,4},{4,7},{5,6},{6,1},{7,0},{8,11},{9,10},{10,... | collective-permute-start | bytes 442376 | tf_op jit(solution)/shard_map/ppermute | solution.py:443
  24.2 6.8 %collective-permute-done.3.refs_3_ = bf16[256,384]{1,0:T(8,128)(2,1)S(1)} collective-permute-done((bf16[256,384]{1,0:T(8,128)(2,1)S(1)}, bf16[256,384]{1,0:T(8,128)(2,1)S(1)}, u32[]{:S(2)}, u32[]{:S(2)}) %collective-permute-start.3) | collective-permute-done | bytes 196640 | tf_op jit(solution)/shard_map/ppermute | solution.py:443
  30.9 1.8 %project_first.1 = (bf16[384,1536]{1,0:T(8,128)(2,1)S(1)}, bf16[1536,384]{1,0:T(8,128)(2,1)S(1)}, f32[2,384,384]{2,1,0:T(8,128)S(1)}) custom-call(bf16[384,1536]{1,0:T(8,128)(2,1)} %bitcast.4, bf16[384,1536]{1,0:T(8,128)(2,1)S(1)} %collective-permute-done.other_ref, bf16[192,384]{1,0:T(8,128)(2,1)S(1)} %get-tuple-element.29.refs_0_, ...), custom_call_target="tpu_custom_call" | custom-call | flops 1000000000 | tf_op jit(solution)/shard_map/project_first/pallas_call | solution.py:64
  32.8 0.0 collective-permute-done.7.refs_3_
  32.8 0.0 collective-permute-done.8.refs_0_
  32.8 0.0 collective-permute-done.6.refs_2_
  32.8 0.0 collective-permute-done.5.refs_1_
  32.8 0.1 collective-permute-start.9
  32.9 1.0 %collective-permute-start.11 = (bf16[128,768]{1,0:T(8,128)(2,1)S(1)}, bf16[128,768]{1,0:T(8,128)(2,1)S(1)}, u32[]{:S(2)}, u32[]{:S(2)}) collective-permute-start(bf16[128,768]{1,0:T(8,128)(2,1)S(1)} %collect.1.own_ref), channel_id=1, source_target_pairs={{0,2},{1,3},{2,0},{3,1},{4,6},{5,7},{6,4},{7,5},{8,10},{9,11},{10,... | collective-permute-start | bytes 589832 | tf_op jit(solution)/shard_map/ppermute | solution.py:446
  34.0 0.9 %project.1 = (bf16[2,384,128]{2,1,0:T(8,128)(2,1)S(1)}, bf16[1536,384]{1,0:T(8,128)(2,1)S(1)}, bf16[768,256]{1,0:T(8,128)(2,1)S(1)}) custom-call(bf16[384,1536]{1,0:T(8,128)(2,1)S(1)} %get-tuple-element.25.own_ref, bf16[384,1536]{1,0:T(8,128)(2,1)S(1)} %collective-permute-done.other_ref, ...), custom_call_target="tpu_custom_call", output_to_operand_aliasing={{1}: (2, {})} | custom-call | flops 1000000000 | tf_op jit(solution)/shard_map/project/pallas_call | solution.py:64
  34.8 0.9 %collective-permute-done.9.refs_1_ = bf16[384,1536]{1,0:T(8,128)(2,1)S(1)} collective-permute-done((bf16[384,1536]{1,0:T(8,128)(2,1)S(1)}, bf16[384,1536]{1,0:T(8,128)(2,1)S(1)}, u32[]{:S(2)}, u32[]{:S(2)}) %collective-permute-start.9) | collective-permute-done | bytes 1179680 | tf_op jit(solution)/shard_map/ppermute | solution.py:39
  35.8 4.8 %attend_last.1 = (bf16[384,128]{1,0:T(8,128)(2,1)S(1)}, bf16[384,128]{1,0:T(8,128)(2,1)S(1)}) custom-call(s32[4,4]{1,0:T(4,128)} %mask_ref.1, s32[4]{0:T(128)} %count_ref.1, bf16[1536,384]{1,0:T(8,128)(2,1)S(1)} %get-tuple-element.33.weight_ref, bf16[2,384,128]{2,1,0:T(8,128)(2,1)S(1)} %get-tuple-element.34.queries_ref, ...), custom_call_target="tpu_custom_call" | custom-call | flops 1000000000 | tf_op jit(solution)/shard_map/attend_last/pallas_call | solution.py:64
  40.6 0.0 collective-permute-done.11.got_ref
  40.7 0.2 collective-permute-start.12
  40.9 0.4 collective-permute-start.10
  41.3 1.4 %collective-permute-done.10.partner_ref = bf16[384,128]{1,0:T(8,128)(2,1)S(1)} collective-permute-done((bf16[384,128]{1,0:T(8,128)(2,1)S(1)}, bf16[384,128]{1,0:T(8,128)(2,1)S(1)}, u32[]{:S(2)}, u32[]{:S(2)}) %collective-permute-start.10) | collective-permute-done | bytes 98336 | tf_op jit(solution)/shard_map/ppermute | solution.py:39
  42.6 0.0 collective-permute-done.12.out_partner_ref
  42.6 1.6 %project_out.1 = bf16[384,1536]{1,0:T(8,128)(2,1)} custom-call(bf16[384,128]{1,0:T(8,128)(2,1)S(1)} %get-tuple-element.36.own_ref, bf16[384,128]{1,0:T(8,128)(2,1)S(1)} %collective-permute-done.10.partner_ref, bf16[256,768]{1,0:T(8,128)(2,1)S(1)} %pair_up.1.out_own_ref, bf16[256,768]{1,0:T(8,128)(2,1)S(1)} %collective-permute-done.12.out_partner_ref), custom_call_target="tpu_custom_call" | custom-call | tf_op jit(solution)/shard_map/project_out/pallas_call | solution.py:64
  (2 shorter events, 0.1 us)
Async XLA Ops:
  0.0 6.6 %collective-permute-start = (bf16[384,1536]{1,0:T(8,128)(2,1)}, bf16[384,1536]{1,0:T(8,128)(2,1)S(1)}, u32[]{:S(2)}, u32[]{:S(2)}) collective-permute-start(bf16[384,1536]{1,0:T(8,128)(2,1)} %bitcast.2), channel_id=1, source_target_pairs={{0,8},{8,0},{16,24},{24,16},{1,9},{9,1},{17,25},{25,17},{2,10},{10... | collective-permute-start | bytes 3538952 | tf_op jit(solution)/shard_map/ppermute | solution.py:39
  0.5 32.4 %collective-permute-start.8 = (bf16[384,1536]{1,0:T(8,128)(2,1)}, bf16[384,1536]{1,0:T(8,128)(2,1)S(1)}, u32[]{:S(2)}, u32[]{:S(2)}) collective-permute-start(bf16[384,1536]{1,0:T(8,128)(2,1)} %bitcast.3), channel_id=1, source_target_pairs={{0,16},{8,24},{16,0},{24,8},{1,17},{9,25},{17,1},{25,9},{2,18},{10... | collective-permute-start | bytes 3538952 | tf_op jit(solution)/shard_map/ppermute | solution.py:43
  4.0 15.4 %collective-permute-start.2 = (bf16[256,384]{1,0:T(8,128)(2,1)S(1)}, bf16[256,384]{1,0:T(8,128)(2,1)S(1)}, u32[]{:S(2)}, u32[]{:S(2)}) collective-permute-start(bf16[256,384]{1,0:T(8,128)(2,1)S(1)} %get-tuple-element.30.refs_0_), channel_id=1, source_target_pairs={{0,4},{1,5},{2,6},{3,7},{4,0},{5,1},{6,2},{7,3},{8,12},{9,13},{10,... | collective-permute-start | bytes 589832 | tf_op jit(solution)/shard_map/ppermute | solution.py:443
  6.6 14.6 %collective-permute-start.1 = (bf16[256,384]{1,0:T(8,128)(2,1)S(1)}, bf16[256,384]{1,0:T(8,128)(2,1)S(1)}, u32[]{:S(2)}, u32[]{:S(2)}) collective-permute-start(bf16[256,384]{1,0:T(8,128)(2,1)S(1)} %get-tuple-element.30.refs_0_), channel_id=1, source_target_pairs={{0,1},{1,0},{2,3},{3,2},{4,5},{5,4},{6,7},{7,6},{8,9},{9,8},{10,11... | collective-permute-start | bytes 589832 | tf_op jit(solution)/shard_map/ppermute | solution.py:443
  8.1 13.1 %collective-permute-start.4 = (bf16[192,384]{1,0:T(8,128)(2,1)S(1)}, bf16[192,384]{1,0:T(8,128)(2,1)S(1)}, u32[]{:S(2)}, u32[]{:S(2)}) collective-permute-start(bf16[192,384]{1,0:T(8,128)(2,1)S(1)} %get-tuple-element.29.refs_0_), channel_id=1, source_target_pairs={{0,2},{1,3},{2,4},{3,5},{4,6},{5,7},{6,0},{7,1},{8,10},{9,11},{10,... | collective-permute-start | bytes 442376 | tf_op jit(solution)/shard_map/ppermute | solution.py:443
  19.4 11.6 %collective-permute-start.3 = (bf16[256,384]{1,0:T(8,128)(2,1)S(1)}, bf16[256,384]{1,0:T(8,128)(2,1)S(1)}, u32[]{:S(2)}, u32[]{:S(2)}) collective-permute-start(bf16[256,384]{1,0:T(8,128)(2,1)S(1)} %collective-permute-done.2.refs_2_), channel_id=1, source_target_pairs={{0,1},{1,0},{2,3},{3,2},{4,5},{5,4},{6,7},{7,6},{8,9},{9,8},{10,11... | collective-permute-start | bytes 589832 | tf_op jit(solution)/shard_map/ppermute | solution.py:443
  20.8 12.0 %collective-permute-start.7 = (bf16[192,384]{1,0:T(8,128)(2,1)S(1)}, bf16[192,384]{1,0:T(8,128)(2,1)S(1)}, u32[]{:S(2)}, u32[]{:S(2)}) collective-permute-start(bf16[192,384]{1,0:T(8,128)(2,1)S(1)} %get-tuple-element.29.refs_0_), channel_id=1, source_target_pairs={{0,7},{1,6},{2,1},{3,0},{4,3},{5,2},{6,5},{7,4},{8,15},{9,14},{10,... | collective-permute-start | bytes 442376 | tf_op jit(solution)/shard_map/ppermute | solution.py:443
  21.2 11.6 %collective-permute-start.6 = (bf16[192,384]{1,0:T(8,128)(2,1)S(1)}, bf16[192,384]{1,0:T(8,128)(2,1)S(1)}, u32[]{:S(2)}, u32[]{:S(2)}) collective-permute-start(bf16[192,384]{1,0:T(8,128)(2,1)S(1)} %get-tuple-element.29.refs_0_), channel_id=1, source_target_pairs={{0,6},{1,7},{2,0},{3,1},{4,2},{5,3},{6,4},{7,5},{8,14},{9,15},{10,... | collective-permute-start | bytes 442376 | tf_op jit(solution)/shard_map/ppermute | solution.py:443
  21.8 11.0 %collective-permute-start.5 = (bf16[192,384]{1,0:T(8,128)(2,1)S(1)}, bf16[192,384]{1,0:T(8,128)(2,1)S(1)}, u32[]{:S(2)}, u32[]{:S(2)}) collective-permute-start(bf16[192,384]{1,0:T(8,128)(2,1)S(1)} %get-tuple-element.29.refs_0_), channel_id=1, source_target_pairs={{0,3},{1,2},{2,5},{3,4},{4,7},{5,6},{6,1},{7,0},{8,11},{9,10},{10,... | collective-permute-start | bytes 442376 | tf_op jit(solution)/shard_map/ppermute | solution.py:443
  32.8 2.9 %collective-permute-start.9 = (bf16[384,1536]{1,0:T(8,128)(2,1)S(1)}, bf16[384,1536]{1,0:T(8,128)(2,1)S(1)}, u32[]{:S(2)}, u32[]{:S(2)}) collective-permute-start(bf16[384,1536]{1,0:T(8,128)(2,1)S(1)} %collective-permute-done.8.refs_0_), channel_id=1, source_target_pairs={{0,8},{8,0},{16,24},{24,16},{1,9},{9,1},{17,25},{25,17},{2,10},{10... | collective-permute-start | bytes 3538952 | tf_op jit(solution)/shard_map/ppermute | solution.py:39
  32.9 7.7 %collective-permute-start.11 = (bf16[128,768]{1,0:T(8,128)(2,1)S(1)}, bf16[128,768]{1,0:T(8,128)(2,1)S(1)}, u32[]{:S(2)}, u32[]{:S(2)}) collective-permute-start(bf16[128,768]{1,0:T(8,128)(2,1)S(1)} %collect.1.own_ref), channel_id=1, source_target_pairs={{0,2},{1,3},{2,0},{3,1},{4,6},{5,7},{6,4},{7,5},{8,10},{9,11},{10,... | collective-permute-start | bytes 589832 | tf_op jit(solution)/shard_map/ppermute | solution.py:446
  40.7 1.9 %collective-permute-start.12 = (bf16[256,768]{1,0:T(8,128)(2,1)S(1)}, bf16[256,768]{1,0:T(8,128)(2,1)S(1)}, u32[]{:S(2)}, u32[]{:S(2)}) collective-permute-start(bf16[256,768]{1,0:T(8,128)(2,1)S(1)} %pair_up.1.out_own_ref), channel_id=1, source_target_pairs={{0,8},{8,0},{16,24},{24,16},{1,9},{9,1},{17,25},{25,17},{2,10},{10... | collective-permute-start | bytes 1179656 | tf_op jit(solution)/shard_map/ppermute | solution.py:39
  40.9 1.7 %collective-permute-start.10 = (bf16[384,128]{1,0:T(8,128)(2,1)S(1)}, bf16[384,128]{1,0:T(8,128)(2,1)S(1)}, u32[]{:S(2)}, u32[]{:S(2)}) collective-permute-start(bf16[384,128]{1,0:T(8,128)(2,1)S(1)} %get-tuple-element.37), channel_id=1, source_target_pairs={{0,8},{8,0},{16,24},{24,16},{1,9},{9,1},{17,25},{25,17},{2,10},{10... | collective-permute-start | bytes 294920 | tf_op jit(solution)/shard_map/ppermute | solution.py:39

commit v10 on v9

--- a/solution.py
+++ b/solution.py
@@ -191,7 +191,7 @@
     return top, old[1] * keep + new[1] * add, old[2] * keep + new[2] * add
 
 
-def project(z_count, x_count, shifts, blocks, latents_own, latents_other, early=None):
+def project(z_count, x_count, shifts, blocks, latents_own, latents_other, near=None, early=None):
     count = len(blocks)
     columns = blocks[0].shape[1]
     own = columns // 3
@@ -226,7 +226,7 @@
         fetch.wait()
         total_ref[0] = partial(latents_ref, starts, weight)
 
-    def rest(own_ref, other_ref, old_weight_ref, total_ref, *refs):
+    def rest(own_ref, other_ref, old_weight_ref, total_ref, near_ref, *refs):
         block_refs = refs[:count]
         queries_ref, weight_ref, key_value_ref = refs[count:]
         starts, weight = assemble(block_refs, weight_ref)
@@ -234,6 +234,9 @@
             projected = (total_ref[member] + partial(from_ref, starts, weight)).astype(dtype)
             queries_ref[member] = projected[:, :own] * jnp.asarray(scale, dtype)
             key_value_ref[member * row_count : (member + 1) * row_count, :] = projected[:, own:]
+        key_value_ref[CORES * row_count :, :] = jnp.dot(
+            near_ref[...], weight_ref[:, own:], preferred_element_type=jnp.float32
+        ).astype(dtype)
 
     weight_shape = shaped((depth, columns), dtype)
     if early is None:
@@ -249,18 +252,18 @@
     return call(
         rest,
         "project",
-        [VMEM] * (count + 4),
+        [VMEM] * (count + 5),
         [
             shaped((CORES, row_count, own), dtype),
             weight_shape,
-            shaped((CORES * row_count, 2 * own), dtype),
+            shaped(((CORES + 1) * row_count, 2 * own), dtype),
         ],
         cost=COST1,
         aliases={2: 1},
-    )(own_tile, latents_other, weight, total, *blocks)
-
-
-def project_whole(z_count, x_count, shifts, blocks, latents_own, latents_other):
+    )(own_tile, latents_other, weight, total, near, *blocks)
+
+
+def project_whole(z_count, x_count, shifts, blocks, latents_own, latents_other, near):
     count = len(blocks)
     columns = blocks[0].shape[1]
     own = columns // 3
@@ -269,7 +272,7 @@
     dtype = latents_own.dtype
     scale = float(E) ** -0.5
 
-    def kernel(own_ref, other_ref, *refs):
+    def kernel(own_ref, other_ref, near_ref, *refs):
         block_refs = refs[:count]
         queries_ref, weight_ref, key_value_ref, latents_ref, sem = refs[count:]
         fetch = pltpu.make_async_copy(own_ref, latents_ref, sem)
@@ -286,19 +289,22 @@
             projected = jnp.dot(from_ref[...], weight_ref[...], preferred_element_type=jnp.float32).astype(dtype)
             queries_ref[member] = projected[:, :own] * jnp.asarray(scale, dtype)
             key_value_ref[member * row_count : (member + 1) * row_count, :] = projected[:, own:]
+        key_value_ref[CORES * row_count :, :] = jnp.dot(
+            near_ref[...], weight_ref[:, own:], preferred_element_type=jnp.float32
+        ).astype(dtype)
 
     return call(
         kernel,
         "project",
-        [HBM] + [VMEM] * (count + 1),
+        [HBM] + [VMEM] * (count + 2),
         [
             shaped((CORES, row_count, own), dtype),
             shaped((depth, columns), dtype),
-            shaped((CORES * row_count, 2 * own), dtype),
+            shaped(((CORES + 1) * row_count, 2 * own), dtype),
         ],
         scratch_shapes=[pltpu.VMEM((row_count, depth), dtype), pltpu.SemaphoreType.DMA(())],
         cost=COST1,
-    )(latents_own, latents_other, *blocks)
+    )(latents_own, latents_other, near, *blocks)
 
 
 def attend(seq_count, sources, key_value, state, last, weight, queries, tile_mask, tile_counts):
@@ -307,7 +313,7 @@
     row_count = queries.shape[1]
     dtype = queries.dtype
     groups = own // LANES
-    local_rows = 0 if key_value is None else CORES * row_count
+    local_rows = 0 if key_value is None else key_value.shape[0]
     slots = local_rows + len(sources) * row_count
     given = [weight, queries] + [latents for latents, _, _ in sources]
     given += [array for array in (key_value, state) if array is not None]
@@ -333,15 +339,18 @@
             spans.append((key_tile, ends[-1]))
             ends.append(ends[-1] + count_ref[key_tile])
 
-        for member in range(CORES if local_rows else 0):
-            rows = slice(member * row_count, (member + 1) * row_count)
-            place(tiles[member], key_value_ref[rows, :own], key_value_ref[rows, own:])
+        def tile_of(y_step, swapped):
+            from_same = lax.rem(seq_index + seq_count - CORES * y_step, seq_count)
+            return from_same + 1 - 2 * core if swapped else from_same
+
+        for index, key_tile in enumerate([*tiles, tile_of(1, False)] if local_rows else []):
+            rows = slice(index * row_count, (index + 1) * row_count)
+            place(key_tile, key_value_ref[rows, :own], key_value_ref[rows, own:])
         for part, (_, y_step, swapped) in enumerate(sources):
             projected = jnp.dot(
                 latents_refs[part][...], weight_ref[:, own:], preferred_element_type=jnp.float32
             ).astype(dtype)
-            from_same = lax.rem(seq_index + seq_count - CORES * y_step, seq_count)
-            place(from_same + 1 - 2 * core if swapped else from_same, projected[:, :own], projected[:, own:])
+            place(tile_of(y_step, swapped), projected[:, :own], projected[:, own:])
         rest = pl.ds(pl.multiple_of(spans[-1][1] + row_count, GRAIN), BLOCK)
         keys_ref[rest, :] = jnp.zeros((BLOCK, own), dtype)
         values_ref[rest, :] = jnp.zeros((BLOCK, 2 * own), dtype)
@@ -494,17 +503,19 @@
         later = [shift for shift in came if shift not in sooner]
         came[later[-1]] = after(came[later[-1]], *near)
         queries, weight, key_value = project(
-            *axes, later, [came[shift] for shift in later], latents_own, latents_other, early
+            *axes, later, [came[shift] for shift in later], latents_own, latents_other, near[0], early
         )
     else:
         came[0, 0] = after(half, *near)
-        queries, weight, key_value = project_whole(*axes, list(came), list(came.values()), latents_own, latents_other)
+        queries, weight, key_value = project_whole(
+            *axes, list(came), list(came.values()), latents_own, latents_other, near[0]
+        )
     state = None
     for step in range(1, chips):
         last = step == chips - 1
         result = attend(
             seq_count,
-            [(near[step - 1], step, False), (far[step - 1], step, True)],
+            [(near[step - 1], step, False)] * (step > 1) + [(far[step - 1], step, True)],
             key_value if step == 1 else None,
             state,
             last,

time: 44.4 us -> 44.3 us (level)
  no operation moved by 1% of the time
where the time goes in v10:
time: 44.3 us; the launch traced here: 44.1 us
  waiting for transfers between devices  18.4 us (42%)
  starting transfers between devices  15.2 us (34%)
  Pallas kernels  10.2 us (23%)
    ppermute x7, waiting for transfers between devices, hop(): lax.ppermute(array, 'fsdp', rotation(z_count, x_count, z_step, x_step))  16.4 us
    ppermute x7, starting transfers between devices, hop(): lax.ppermute(array, 'fsdp', rotation(z_count, x_count, z_step, x_step))  10.5 us
    pallas_call x7, Pallas kernels, run(): inner(*[pltpu.with_memory_space_constraint(arg, pltpu.HBM if spec is SMEM...  10.2 us
    ppermute x1, starting transfers between devices, y_rotation(): lax.ppermute(array, 'seq', [(s, (s + CORES * step) % seq_count) for s in...  2.52 us
    ppermute x4, waiting for transfers between devices, core_swap(): return lax.ppermute(array, 'seq', [(s, s ^ 1) for s in range(seq_count)])  1.96 us
    ppermute x4, starting transfers between devices, core_swap(): return lax.ppermute(array, 'seq', [(s, s ^ 1) for s in range(seq_count)])  1.1 us
    ppermute x1, starting transfers between devices, flip(): lax.ppermute(array, 'fsdp', [(f, f ^ shift * x_count) for f in range(fsdp...  1.03 us
  transfers between devices with their start and end apart: 13, of which 4 were waited for; matrix products, arithmetic and copies ran while one was open for 0% of the time, Pallas kernels for 19%

profile of v10, /device:TPU:0, one launch (start us, length us, event | category | flops | bytes accessed | tf_op | source)
XLA Modules:
  0.0 44.1 jit_solution(7221620749463321502)
XLA Ops:
  0.0 0.5 %collective-permute-start = (bf16[384,1536]{1,0:T(8,128)(2,1)}, bf16[384,1536]{1,0:T(8,128)(2,1)S(1)}, u32[]{:S(2)}, u32[]{:S(2)}) collective-permute-start(bf16[384,1536]{1,0:T(8,128)(2,1)} %bitcast.2), channel_id=1, source_target_pairs={{0,8},{8,0},{16,24},{24,16},{1,9},{9,1},{17,25},{25,17},{2,10},{10... | collective-permute-start | bytes 3538952 | tf_op jit(solution)/shard_map/ppermute | solution.py:39
  0.5 2.5 %collective-permute-start.4 = (bf16[384,1536]{1,0:T(8,128)(2,1)}, bf16[384,1536]{1,0:T(8,128)(2,1)S(1)}, u32[]{:S(2)}, u32[]{:S(2)}) collective-permute-start(bf16[384,1536]{1,0:T(8,128)(2,1)} %bitcast.3), channel_id=1, source_target_pairs={{0,16},{8,24},{16,0},{24,8},{1,17},{9,25},{17,1},{25,9},{2,18},{10... | collective-permute-start | bytes 3538952 | tf_op jit(solution)/shard_map/ppermute | solution.py:43
  3.0 1.0 %halves.1 = (bf16[192,384]{1,0:T(8,128)(2,1)S(1)}, bf16[256,384]{1,0:T(8,128)(2,1)S(1)}) custom-call(bf16[192,768]{1,0:T(8,128)(2,1)} %qkv_ref.1, bf16[32,1536]{1,0:T(8,128)(2,1)} %out_ref.1), custom_call_target="tpu_custom_call" | custom-call | tf_op jit(solution)/shard_map/halves/pallas_call | solution.py:64
  4.0 2.7 %collective-permute-start.2 = (bf16[256,384]{1,0:T(8,128)(2,1)S(1)}, bf16[256,384]{1,0:T(8,128)(2,1)S(1)}, u32[]{:S(2)}, u32[]{:S(2)}) collective-permute-start(bf16[256,384]{1,0:T(8,128)(2,1)S(1)} %get-tuple-element.28.refs_0_), channel_id=1, source_target_pairs={{0,4},{1,5},{2,6},{3,7},{4,0},{5,1},{6,2},{7,3},{8,12},{9,13},{10,... | collective-permute-start | bytes 589832 | tf_op jit(solution)/shard_map/ppermute | solution.py:452
  6.6 0.0 collective-permute-done.other_ref
  6.6 1.5 %collective-permute-start.1 = (bf16[256,384]{1,0:T(8,128)(2,1)S(1)}, bf16[256,384]{1,0:T(8,128)(2,1)S(1)}, u32[]{:S(2)}, u32[]{:S(2)}) collective-permute-start(bf16[256,384]{1,0:T(8,128)(2,1)S(1)} %get-tuple-element.28.refs_0_), channel_id=1, source_target_pairs={{0,1},{1,0},{2,3},{3,2},{4,5},{5,4},{6,7},{7,6},{8,9},{9,8},{10,11... | collective-permute-start | bytes 589832 | tf_op jit(solution)/shard_map/ppermute | solution.py:452
  8.1 1.6 %collective-permute-start.5 = (bf16[192,384]{1,0:T(8,128)(2,1)S(1)}, bf16[192,384]{1,0:T(8,128)(2,1)S(1)}, u32[]{:S(2)}, u32[]{:S(2)}) collective-permute-start(bf16[192,384]{1,0:T(8,128)(2,1)S(1)} %get-tuple-element.30.refs_0_), channel_id=1, source_target_pairs={{0,2},{1,3},{2,4},{3,5},{4,6},{5,7},{6,0},{7,1},{8,10},{9,11},{10,... | collective-permute-start | bytes 442376 | tf_op jit(solution)/shard_map/ppermute | solution.py:452
  9.7 9.7 %collective-permute-done.2.refs_2_ = bf16[256,384]{1,0:T(8,128)(2,1)S(1)} collective-permute-done((bf16[256,384]{1,0:T(8,128)(2,1)S(1)}, bf16[256,384]{1,0:T(8,128)(2,1)S(1)}, u32[]{:S(2)}, u32[]{:S(2)}) %collective-permute-start.2) | collective-permute-done | bytes 196640 | tf_op jit(solution)/shard_map/ppermute | solution.py:452
  19.4 1.5 %collective-permute-start.3 = (bf16[256,384]{1,0:T(8,128)(2,1)S(1)}, bf16[256,384]{1,0:T(8,128)(2,1)S(1)}, u32[]{:S(2)}, u32[]{:S(2)}) collective-permute-start(bf16[256,384]{1,0:T(8,128)(2,1)S(1)} %collective-permute-done.2.refs_2_), channel_id=1, source_target_pairs={{0,1},{1,0},{2,3},{3,2},{4,5},{5,4},{6,7},{7,6},{8,9},{9,8},{10,11... | collective-permute-start | bytes 589832 | tf_op jit(solution)/shard_map/ppermute | solution.py:452
  20.8 0.4 collective-permute-start.8
  21.2 0.0 collective-permute-done.5.refs_0_
  21.2 0.0 collective-permute-done.1.refs_1_
  21.2 0.6 %collective-permute-start.7 = (bf16[192,384]{1,0:T(8,128)(2,1)S(1)}, bf16[192,384]{1,0:T(8,128)(2,1)S(1)}, u32[]{:S(2)}, u32[]{:S(2)}) collective-permute-start(bf16[192,384]{1,0:T(8,128)(2,1)S(1)} %get-tuple-element.30.refs_0_), channel_id=1, source_target_pairs={{0,6},{1,7},{2,0},{3,1},{4,2},{5,3},{6,4},{7,5},{8,14},{9,15},{10,... | collective-permute-start | bytes 442376 | tf_op jit(solution)/shard_map/ppermute | solution.py:452
  21.8 2.3 %collective-permute-start.6 = (bf16[192,384]{1,0:T(8,128)(2,1)S(1)}, bf16[192,384]{1,0:T(8,128)(2,1)S(1)}, u32[]{:S(2)}, u32[]{:S(2)}) collective-permute-start(bf16[192,384]{1,0:T(8,128)(2,1)S(1)} %get-tuple-element.30.refs_0_), channel_id=1, source_target_pairs={{0,3},{1,2},{2,5},{3,4},{4,7},{5,6},{6,1},{7,0},{8,11},{9,10},{10,... | collective-permute-start | bytes 442376 | tf_op jit(solution)/shard_map/ppermute | solution.py:452
  24.2 6.8 %collective-permute-done.3.refs_3_ = bf16[256,384]{1,0:T(8,128)(2,1)S(1)} collective-permute-done((bf16[256,384]{1,0:T(8,128)(2,1)S(1)}, bf16[256,384]{1,0:T(8,128)(2,1)S(1)}, u32[]{:S(2)}, u32[]{:S(2)}) %collective-permute-start.3) | collective-permute-done | bytes 196640 | tf_op jit(solution)/shard_map/ppermute | solution.py:452
  30.9 1.8 %project_first.1 = (bf16[384,1536]{1,0:T(8,128)(2,1)S(1)}, bf16[1536,384]{1,0:T(8,128)(2,1)S(1)}, f32[2,384,384]{2,1,0:T(8,128)S(1)}) custom-call(bf16[384,1536]{1,0:T(8,128)(2,1)} %bitcast.4, bf16[384,1536]{1,0:T(8,128)(2,1)S(1)} %collective-permute-done.other_ref, bf16[192,384]{1,0:T(8,128)(2,1)S(1)} %get-tuple-element.30.refs_0_, ...), custom_call_target="tpu_custom_call" | custom-call | flops 1000000000 | tf_op jit(solution)/shard_map/project_first/pallas_call | solution.py:64
  32.8 0.0 collective-permute-done.8.refs_3_
  32.8 0.0 collective-permute-done.4.near_ref
  32.8 0.0 collective-permute-done.7.refs_2_
  32.8 0.0 collective-permute-done.6.refs_1_
  32.8 0.1 collective-permute-start.9
  32.9 1.0 %collective-permute-start.11 = (bf16[128,768]{1,0:T(8,128)(2,1)S(1)}, bf16[128,768]{1,0:T(8,128)(2,1)S(1)}, u32[]{:S(2)}, u32[]{:S(2)}) collective-permute-start(bf16[128,768]{1,0:T(8,128)(2,1)S(1)} %collect.1.own_ref), channel_id=1, source_target_pairs={{0,2},{1,3},{2,0},{3,1},{4,6},{5,7},{6,4},{7,5},{8,10},{9,11},{10,... | collective-permute-start | bytes 589832 | tf_op jit(solution)/shard_map/ppermute | solution.py:455
  34.0 1.2 %project.1 = (bf16[2,384,128]{2,1,0:T(8,128)(2,1)S(1)}, bf16[1536,384]{1,0:T(8,128)(2,1)S(1)}, bf16[1152,256]{1,0:T(8,128)(2,1)S(1)}) custom-call(bf16[384,1536]{1,0:T(8,128)(2,1)S(1)} %get-tuple-element.25.own_ref, bf16[384,1536]{1,0:T(8,128)(2,1)S(1)} %collective-permute-done.other_ref, ...), custom_call_target="tpu_custom_call", output_to_operand_aliasing={{1}: (2, {})} | custom-call | flops 1000000000 | tf_op jit(solution)/shard_map/project/pallas_call | solution.py:64
  35.2 0.6 %collective-permute-done.9.refs_0_ = bf16[384,1536]{1,0:T(8,128)(2,1)S(1)} collective-permute-done((bf16[384,1536]{1,0:T(8,128)(2,1)S(1)}, bf16[384,1536]{1,0:T(8,128)(2,1)S(1)}, u32[]{:S(2)}, u32[]{:S(2)}) %collective-permute-start.9) | collective-permute-done | bytes 1179680 | tf_op jit(solution)/shard_map/ppermute | solution.py:39
  35.8 4.5 %attend_last.1 = (bf16[384,128]{1,0:T(8,128)(2,1)S(1)}, bf16[384,128]{1,0:T(8,128)(2,1)S(1)}) custom-call(s32[4,4]{1,0:T(4,128)} %mask_ref.1, s32[4]{0:T(128)} %count_ref.1, bf16[1536,384]{1,0:T(8,128)(2,1)S(1)} %get-tuple-element.33.weight_ref, bf16[2,384,128]{2,1,0:T(8,128)(2,1)S(1)} %get-tuple-element.34.queries_ref, ...), custom_call_target="tpu_custom_call" | custom-call | flops 1000000000 | tf_op jit(solution)/shard_map/attend_last/pallas_call | solution.py:64
  40.3 0.0 collective-permute-done.11.got_ref
  40.4 0.2 collective-permute-start.12
  40.6 0.4 collective-permute-start.10
  40.9 1.4 %collective-permute-done.10.partner_ref = bf16[384,128]{1,0:T(8,128)(2,1)S(1)} collective-permute-done((bf16[384,128]{1,0:T(8,128)(2,1)S(1)}, bf16[384,128]{1,0:T(8,128)(2,1)S(1)}, u32[]{:S(2)}, u32[]{:S(2)}) %collective-permute-start.10) | collective-permute-done | bytes 98336 | tf_op jit(solution)/shard_map/ppermute | solution.py:39
  42.3 0.0 collective-permute-done.12.out_partner_ref
  42.3 1.6 %project_out.1 = bf16[384,1536]{1,0:T(8,128)(2,1)} custom-call(bf16[384,128]{1,0:T(8,128)(2,1)S(1)} %get-tuple-element.36.own_ref, bf16[384,128]{1,0:T(8,128)(2,1)S(1)} %collective-permute-done.10.partner_ref, bf16[256,768]{1,0:T(8,128)(2,1)S(1)} %pair_up.1.out_own_ref, bf16[256,768]{1,0:T(8,128)(2,1)S(1)} %collective-permute-done.12.out_partner_ref), custom_call_target="tpu_custom_call" | custom-call | tf_op jit(solution)/shard_map/project_out/pallas_call | solution.py:64
  (2 shorter events, 0.1 us)
Async XLA Ops:
  0.0 6.6 %collective-permute-start = (bf16[384,1536]{1,0:T(8,128)(2,1)}, bf16[384,1536]{1,0:T(8,128)(2,1)S(1)}, u32[]{:S(2)}, u32[]{:S(2)}) collective-permute-start(bf16[384,1536]{1,0:T(8,128)(2,1)} %bitcast.2), channel_id=1, source_target_pairs={{0,8},{8,0},{16,24},{24,16},{1,9},{9,1},{17,25},{25,17},{2,10},{10... | collective-permute-start | bytes 3538952 | tf_op jit(solution)/shard_map/ppermute | solution.py:39
  0.5 32.4 %collective-permute-start.4 = (bf16[384,1536]{1,0:T(8,128)(2,1)}, bf16[384,1536]{1,0:T(8,128)(2,1)S(1)}, u32[]{:S(2)}, u32[]{:S(2)}) collective-permute-start(bf16[384,1536]{1,0:T(8,128)(2,1)} %bitcast.3), channel_id=1, source_target_pairs={{0,16},{8,24},{16,0},{24,8},{1,17},{9,25},{17,1},{25,9},{2,18},{10... | collective-permute-start | bytes 3538952 | tf_op jit(solution)/shard_map/ppermute | solution.py:43
  4.0 15.4 %collective-permute-start.2 = (bf16[256,384]{1,0:T(8,128)(2,1)S(1)}, bf16[256,384]{1,0:T(8,128)(2,1)S(1)}, u32[]{:S(2)}, u32[]{:S(2)}) collective-permute-start(bf16[256,384]{1,0:T(8,128)(2,1)S(1)} %get-tuple-element.28.refs_0_), channel_id=1, source_target_pairs={{0,4},{1,5},{2,6},{3,7},{4,0},{5,1},{6,2},{7,3},{8,12},{9,13},{10,... | collective-permute-start | bytes 589832 | tf_op jit(solution)/shard_map/ppermute | solution.py:452
  6.6 14.6 %collective-permute-start.1 = (bf16[256,384]{1,0:T(8,128)(2,1)S(1)}, bf16[256,384]{1,0:T(8,128)(2,1)S(1)}, u32[]{:S(2)}, u32[]{:S(2)}) collective-permute-start(bf16[256,384]{1,0:T(8,128)(2,1)S(1)} %get-tuple-element.28.refs_0_), channel_id=1, source_target_pairs={{0,1},{1,0},{2,3},{3,2},{4,5},{5,4},{6,7},{7,6},{8,9},{9,8},{10,11... | collective-permute-start | bytes 589832 | tf_op jit(solution)/shard_map/ppermute | solution.py:452
  8.1 13.1 %collective-permute-start.5 = (bf16[192,384]{1,0:T(8,128)(2,1)S(1)}, bf16[192,384]{1,0:T(8,128)(2,1)S(1)}, u32[]{:S(2)}, u32[]{:S(2)}) collective-permute-start(bf16[192,384]{1,0:T(8,128)(2,1)S(1)} %get-tuple-element.30.refs_0_), channel_id=1, source_target_pairs={{0,2},{1,3},{2,4},{3,5},{4,6},{5,7},{6,0},{7,1},{8,10},{9,11},{10,... | collective-permute-start | bytes 442376 | tf_op jit(solution)/shard_map/ppermute | solution.py:452
  19.4 11.6 %collective-permute-start.3 = (bf16[256,384]{1,0:T(8,128)(2,1)S(1)}, bf16[256,384]{1,0:T(8,128)(2,1)S(1)}, u32[]{:S(2)}, u32[]{:S(2)}) collective-permute-start(bf16[256,384]{1,0:T(8,128)(2,1)S(1)} %collective-permute-done.2.refs_2_), channel_id=1, source_target_pairs={{0,1},{1,0},{2,3},{3,2},{4,5},{5,4},{6,7},{7,6},{8,9},{9,8},{10,11... | collective-permute-start | bytes 589832 | tf_op jit(solution)/shard_map/ppermute | solution.py:452
  20.8 12.0 %collective-permute-start.8 = (bf16[192,384]{1,0:T(8,128)(2,1)S(1)}, bf16[192,384]{1,0:T(8,128)(2,1)S(1)}, u32[]{:S(2)}, u32[]{:S(2)}) collective-permute-start(bf16[192,384]{1,0:T(8,128)(2,1)S(1)} %get-tuple-element.30.refs_0_), channel_id=1, source_target_pairs={{0,7},{1,6},{2,1},{3,0},{4,3},{5,2},{6,5},{7,4},{8,15},{9,14},{10,... | collective-permute-start | bytes 442376 | tf_op jit(solution)/shard_map/ppermute | solution.py:452
  21.2 11.6 %collective-permute-start.7 = (bf16[192,384]{1,0:T(8,128)(2,1)S(1)}, bf16[192,384]{1,0:T(8,128)(2,1)S(1)}, u32[]{:S(2)}, u32[]{:S(2)}) collective-permute-start(bf16[192,384]{1,0:T(8,128)(2,1)S(1)} %get-tuple-element.30.refs_0_), channel_id=1, source_target_pairs={{0,6},{1,7},{2,0},{3,1},{4,2},{5,3},{6,4},{7,5},{8,14},{9,15},{10,... | collective-permute-start | bytes 442376 | tf_op jit(solution)/shard_map/ppermute | solution.py:452
  21.8 11.0 %collective-permute-start.6 = (bf16[192,384]{1,0:T(8,128)(2,1)S(1)}, bf16[192,384]{1,0:T(8,128)(2,1)S(1)}, u32[]{:S(2)}, u32[]{:S(2)}) collective-permute-start(bf16[192,384]{1,0:T(8,128)(2,1)S(1)} %get-tuple-element.30.refs_0_), channel_id=1, source_target_pairs={{0,3},{1,2},{2,5},{3,4},{4,7},{5,6},{6,1},{7,0},{8,11},{9,10},{10,... | collective-permute-start | bytes 442376 | tf_op jit(solution)/shard_map/ppermute | solution.py:452
  32.8 2.9 %collective-permute-start.9 = (bf16[384,1536]{1,0:T(8,128)(2,1)S(1)}, bf16[384,1536]{1,0:T(8,128)(2,1)S(1)}, u32[]{:S(2)}, u32[]{:S(2)}) collective-permute-start(bf16[384,1536]{1,0:T(8,128)(2,1)S(1)} %collective-permute-done.4.near_ref), channel_id=1, source_target_pairs={{0,8},{8,0},{16,24},{24,16},{1,9},{9,1},{17,25},{25,17},{2,10},{10... | collective-permute-start | bytes 3538952 | tf_op jit(solution)/shard_map/ppermute | solution.py:39
  32.9 7.4 %collective-permute-start.11 = (bf16[128,768]{1,0:T(8,128)(2,1)S(1)}, bf16[128,768]{1,0:T(8,128)(2,1)S(1)}, u32[]{:S(2)}, u32[]{:S(2)}) collective-permute-start(bf16[128,768]{1,0:T(8,128)(2,1)S(1)} %collect.1.own_ref), channel_id=1, source_target_pairs={{0,2},{1,3},{2,0},{3,1},{4,6},{5,7},{6,4},{7,5},{8,10},{9,11},{10,... | collective-permute-start | bytes 589832 | tf_op jit(solution)/shard_map/ppermute | solution.py:455
  40.4 1.9 %collective-permute-start.12 = (bf16[256,768]{1,0:T(8,128)(2,1)S(1)}, bf16[256,768]{1,0:T(8,128)(2,1)S(1)}, u32[]{:S(2)}, u32[]{:S(2)}) collective-permute-start(bf16[256,768]{1,0:T(8,128)(2,1)S(1)} %pair_up.1.out_own_ref), channel_id=1, source_target_pairs={{0,8},{8,0},{16,24},{24,16},{1,9},{9,1},{17,25},{25,17},{2,10},{10... | collective-permute-start | bytes 1179656 | tf_op jit(solution)/shard_map/ppermute | solution.py:39
  40.6 1.7 %collective-permute-start.10 = (bf16[384,128]{1,0:T(8,128)(2,1)S(1)}, bf16[384,128]{1,0:T(8,128)(2,1)S(1)}, u32[]{:S(2)}, u32[]{:S(2)}) collective-permute-start(bf16[384,128]{1,0:T(8,128)(2,1)S(1)} %get-tuple-element.37), channel_id=1, source_target_pairs={{0,8},{8,0},{16,24},{24,16},{1,9},{9,1},{17,25},{25,17},{2,10},{10... | collective-permute-start | bytes 294920 | tf_op jit(solution)/shard_map/ppermute | solution.py:39

commit v11 on v10

--- a/solution.py
+++ b/solution.py
@@ -408,6 +408,7 @@
 def project_out(attended_own, attended_partner, out_own, out_partner):
     row_count, own = attended_own.shape
     side = out_own.shape[1]
+    strip = side // 3 if side % (3 * BLOCK) == 0 else side
     dtype = attended_own.dtype
 
     def kernel(own_ref, partner_ref, out_own_ref, out_partner_ref, result_ref, staged_ref, sems):
@@ -416,14 +417,18 @@
         partner_rows = pl.ds(pl.multiple_of((1 - core) * own, 16), own)
         copies = []
         for half, weight_ref in enumerate((out_own_ref, out_partner_ref)):
-            total = jnp.dot(own_ref[...], weight_ref[own_rows, :], preferred_element_type=jnp.float32)
-            total += jnp.dot(partner_ref[...], weight_ref[partner_rows, :], preferred_element_type=jnp.float32)
-            staged_ref[half] = total.astype(dtype)
-            start = pl.multiple_of((core if half == 0 else 1 - core) * side, LANES)
-            copies.append(
-                pltpu.make_async_copy(staged_ref.at[half], result_ref.at[:, pl.ds(start, side)], sems.at[half])
-            )
-            copies[-1].start()
+            for first in range(0, side, strip):
+                columns = slice(first, first + strip)
+                total = jnp.dot(own_ref[...], weight_ref[own_rows, columns], preferred_element_type=jnp.float32)
+                total += jnp.dot(partner_ref[...], weight_ref[partner_rows, columns], preferred_element_type=jnp.float32)
+                staged_ref[half, :, columns] = total.astype(dtype)
+                start = pl.multiple_of((core if half == 0 else 1 - core) * side + first, LANES)
+                copies.append(
+                    pltpu.make_async_copy(
+                        staged_ref.at[half, :, columns], result_ref.at[:, pl.ds(start, strip)], sems.at[len(copies)]
+                    )
+                )
+                copies[-1].start()
         for copy in copies:
             copy.wait()
 
@@ -433,7 +438,7 @@
         [VMEM] * 4,
         [shaped((row_count, CORES * side), dtype)],
         [HBM],
-        scratch_shapes=[pltpu.VMEM((CORES, row_count, side), dtype), pltpu.SemaphoreType.DMA((CORES,))],
+        scratch_shapes=[pltpu.VMEM((CORES, row_count, side), dtype), pltpu.SemaphoreType.DMA((CORES * side // strip,))],
     )(attended_own, attended_partner, out_own, out_partner)[0]
 
 

time: 44.3 us -> 44.2 us (level)
  Pallas kernels: 10.2 us -> 9.54 us
  waiting for transfers between devices: 18.4 us -> 19 us
    pallas_call x7, Pallas kernels: 10.2 us -> 9.54 us  [run(): inner(*[pltpu.with_memory_space_constraint(arg, pltpu.HBM if spec is SMEM...]
    ppermute x1, waiting for transfers between devices: 0.01 us -> 0.58 us  [flip(): lax.ppermute(array, 'fsdp', [(f, f ^ shift * x_count) for f in range(fsdp...]
  transfers between devices with their start and end apart: 13 -> 13, of which waited for: 4 -> 5; matrix products, arithmetic and copies ran while one was open for 0% -> 0% of each run, Pallas kernels for 19% -> 18%
where the time goes in v11:
time: 44.2 us; the launch traced here: 44 us
  waiting for transfers between devices  19 us (43%)
  starting transfers between devices  15.2 us (34%)
  Pallas kernels  9.54 us (22%)
    ppermute x7, waiting for transfers between devices, hop(): lax.ppermute(array, 'fsdp', rotation(z_count, x_count, z_step, x_step))  16.4 us
    ppermute x7, starting transfers between devices, hop(): lax.ppermute(array, 'fsdp', rotation(z_count, x_count, z_step, x_step))  10.5 us
    pallas_call x7, Pallas kernels, run(): inner(*[pltpu.with_memory_space_constraint(arg, pltpu.HBM if spec is SMEM...  9.54 us
    ppermute x1, starting transfers between devices, y_rotation(): lax.ppermute(array, 'seq', [(s, (s + CORES * step) % seq_count) for s in...  2.52 us
    ppermute x4, waiting for transfers between devices, core_swap(): return lax.ppermute(array, 'seq', [(s, s ^ 1) for s in range(seq_count)])  1.96 us
    ppermute x4, starting transfers between devices, core_swap(): return lax.ppermute(array, 'seq', [(s, s ^ 1) for s in range(seq_count)])  1.09 us
    ppermute x1, starting transfers between devices, flip(): lax.ppermute(array, 'fsdp', [(f, f ^ shift * x_count) for f in range(fsdp...  1.03 us
  transfers between devices with their start and end apart: 13, of which 5 were waited for; matrix products, arithmetic and copies ran while one was open for 0% of the time, Pallas kernels for 18%

profile of v11, /device:TPU:0, one launch (start us, length us, event | category | flops | bytes accessed | tf_op | source)
XLA Modules:
  0.0 44.0 jit_solution(3725827184570810509)
XLA Ops:
  0.0 0.5 %collective-permute-start = (bf16[384,1536]{1,0:T(8,128)(2,1)}, bf16[384,1536]{1,0:T(8,128)(2,1)S(1)}, u32[]{:S(2)}, u32[]{:S(2)}) collective-permute-start(bf16[384,1536]{1,0:T(8,128)(2,1)} %bitcast.2), channel_id=1, source_target_pairs={{0,8},{8,0},{16,24},{24,16},{1,9},{9,1},{17,25},{25,17},{2,10},{10... | collective-permute-start | bytes 3538952 | tf_op jit(solution)/shard_map/ppermute | solution.py:39
  0.5 2.5 %collective-permute-start.4 = (bf16[384,1536]{1,0:T(8,128)(2,1)}, bf16[384,1536]{1,0:T(8,128)(2,1)S(1)}, u32[]{:S(2)}, u32[]{:S(2)}) collective-permute-start(bf16[384,1536]{1,0:T(8,128)(2,1)} %bitcast.3), channel_id=1, source_target_pairs={{0,16},{8,24},{16,0},{24,8},{1,17},{9,25},{17,1},{25,9},{2,18},{10... | collective-permute-start | bytes 3538952 | tf_op jit(solution)/shard_map/ppermute | solution.py:43
  3.0 1.0 %halves.1 = (bf16[192,384]{1,0:T(8,128)(2,1)S(1)}, bf16[256,384]{1,0:T(8,128)(2,1)S(1)}) custom-call(bf16[192,768]{1,0:T(8,128)(2,1)} %qkv_ref.1, bf16[32,1536]{1,0:T(8,128)(2,1)} %out_ref.1), custom_call_target="tpu_custom_call" | custom-call | tf_op jit(solution)/shard_map/halves/pallas_call | solution.py:64
  4.0 2.7 %collective-permute-start.2 = (bf16[256,384]{1,0:T(8,128)(2,1)S(1)}, bf16[256,384]{1,0:T(8,128)(2,1)S(1)}, u32[]{:S(2)}, u32[]{:S(2)}) collective-permute-start(bf16[256,384]{1,0:T(8,128)(2,1)S(1)} %get-tuple-element.28.refs_0_), channel_id=1, source_target_pairs={{0,4},{1,5},{2,6},{3,7},{4,0},{5,1},{6,2},{7,3},{8,12},{9,13},{10,... | collective-permute-start | bytes 589832 | tf_op jit(solution)/shard_map/ppermute | solution.py:457
  6.6 0.0 collective-permute-done.other_ref
  6.6 1.5 %collective-permute-start.1 = (bf16[256,384]{1,0:T(8,128)(2,1)S(1)}, bf16[256,384]{1,0:T(8,128)(2,1)S(1)}, u32[]{:S(2)}, u32[]{:S(2)}) collective-permute-start(bf16[256,384]{1,0:T(8,128)(2,1)S(1)} %get-tuple-element.28.refs_0_), channel_id=1, source_target_pairs={{0,1},{1,0},{2,3},{3,2},{4,5},{5,4},{6,7},{7,6},{8,9},{9,8},{10,11... | collective-permute-start | bytes 589832 | tf_op jit(solution)/shard_map/ppermute | solution.py:457
  8.1 1.6 %collective-permute-start.5 = (bf16[192,384]{1,0:T(8,128)(2,1)S(1)}, bf16[192,384]{1,0:T(8,128)(2,1)S(1)}, u32[]{:S(2)}, u32[]{:S(2)}) collective-permute-start(bf16[192,384]{1,0:T(8,128)(2,1)S(1)} %get-tuple-element.30.refs_0_), channel_id=1, source_target_pairs={{0,2},{1,3},{2,4},{3,5},{4,6},{5,7},{6,0},{7,1},{8,10},{9,11},{10,... | collective-permute-start | bytes 442376 | tf_op jit(solution)/shard_map/ppermute | solution.py:457
  9.7 9.7 %collective-permute-done.2.refs_2_ = bf16[256,384]{1,0:T(8,128)(2,1)S(1)} collective-permute-done((bf16[256,384]{1,0:T(8,128)(2,1)S(1)}, bf16[256,384]{1,0:T(8,128)(2,1)S(1)}, u32[]{:S(2)}, u32[]{:S(2)}) %collective-permute-start.2) | collective-permute-done | bytes 196640 | tf_op jit(solution)/shard_map/ppermute | solution.py:457
  19.4 1.5 %collective-permute-start.3 = (bf16[256,384]{1,0:T(8,128)(2,1)S(1)}, bf16[256,384]{1,0:T(8,128)(2,1)S(1)}, u32[]{:S(2)}, u32[]{:S(2)}) collective-permute-start(bf16[256,384]{1,0:T(8,128)(2,1)S(1)} %collective-permute-done.2.refs_2_), channel_id=1, source_target_pairs={{0,1},{1,0},{2,3},{3,2},{4,5},{5,4},{6,7},{7,6},{8,9},{9,8},{10,11... | collective-permute-start | bytes 589832 | tf_op jit(solution)/shard_map/ppermute | solution.py:457
  20.8 0.4 collective-permute-start.8
  21.2 0.0 collective-permute-done.5.refs_0_
  21.2 0.0 collective-permute-done.1.refs_1_
  21.2 0.6 %collective-permute-start.7 = (bf16[192,384]{1,0:T(8,128)(2,1)S(1)}, bf16[192,384]{1,0:T(8,128)(2,1)S(1)}, u32[]{:S(2)}, u32[]{:S(2)}) collective-permute-start(bf16[192,384]{1,0:T(8,128)(2,1)S(1)} %get-tuple-element.30.refs_0_), channel_id=1, source_target_pairs={{0,6},{1,7},{2,0},{3,1},{4,2},{5,3},{6,4},{7,5},{8,14},{9,15},{10,... | collective-permute-start | bytes 442376 | tf_op jit(solution)/shard_map/ppermute | solution.py:457
  21.8 2.3 %collective-permute-start.6 = (bf16[192,384]{1,0:T(8,128)(2,1)S(1)}, bf16[192,384]{1,0:T(8,128)(2,1)S(1)}, u32[]{:S(2)}, u32[]{:S(2)}) collective-permute-start(bf16[192,384]{1,0:T(8,128)(2,1)S(1)} %get-tuple-element.30.refs_0_), channel_id=1, source_target_pairs={{0,3},{1,2},{2,5},{3,4},{4,7},{5,6},{6,1},{7,0},{8,11},{9,10},{10,... | collective-permute-start | bytes 442376 | tf_op jit(solution)/shard_map/ppermute | solution.py:457
  24.2 6.8 %collective-permute-done.3.refs_3_ = bf16[256,384]{1,0:T(8,128)(2,1)S(1)} collective-permute-done((bf16[256,384]{1,0:T(8,128)(2,1)S(1)}, bf16[256,384]{1,0:T(8,128)(2,1)S(1)}, u32[]{:S(2)}, u32[]{:S(2)}) %collective-permute-start.3) | collective-permute-done | bytes 196640 | tf_op jit(solution)/shard_map/ppermute | solution.py:457
  30.9 1.8 %project_first.1 = (bf16[384,1536]{1,0:T(8,128)(2,1)S(1)}, bf16[1536,384]{1,0:T(8,128)(2,1)S(1)}, f32[2,384,384]{2,1,0:T(8,128)S(1)}) custom-call(bf16[384,1536]{1,0:T(8,128)(2,1)} %bitcast.4, bf16[384,1536]{1,0:T(8,128)(2,1)S(1)} %collective-permute-done.other_ref, bf16[192,384]{1,0:T(8,128)(2,1)S(1)} %get-tuple-element.30.refs_0_, ...), custom_call_target="tpu_custom_call" | custom-call | flops 1000000000 | tf_op jit(solution)/shard_map/project_first/pallas_call | solution.py:64
  32.8 0.0 collective-permute-done.8.refs_3_
  32.8 0.0 collective-permute-done.4.near_ref
  32.8 0.0 collective-permute-done.7.refs_2_
  32.8 0.0 collective-permute-done.6.refs_1_
  32.8 0.1 collective-permute-start.9
  32.9 1.0 %collective-permute-start.11 = (bf16[128,768]{1,0:T(8,128)(2,1)S(1)}, bf16[128,768]{1,0:T(8,128)(2,1)S(1)}, u32[]{:S(2)}, u32[]{:S(2)}) collective-permute-start(bf16[128,768]{1,0:T(8,128)(2,1)S(1)} %collect.1.own_ref), channel_id=1, source_target_pairs={{0,2},{1,3},{2,0},{3,1},{4,6},{5,7},{6,4},{7,5},{8,10},{9,11},{10,... | collective-permute-start | bytes 589832 | tf_op jit(solution)/shard_map/ppermute | solution.py:460
  34.0 1.2 %project.1 = (bf16[2,384,128]{2,1,0:T(8,128)(2,1)S(1)}, bf16[1536,384]{1,0:T(8,128)(2,1)S(1)}, bf16[1152,256]{1,0:T(8,128)(2,1)S(1)}) custom-call(bf16[384,1536]{1,0:T(8,128)(2,1)S(1)} %get-tuple-element.25.own_ref, bf16[384,1536]{1,0:T(8,128)(2,1)S(1)} %collective-permute-done.other_ref, ...), custom_call_target="tpu_custom_call", output_to_operand_aliasing={{1}: (2, {})} | custom-call | flops 1000000000 | tf_op jit(solution)/shard_map/project/pallas_call | solution.py:64
  35.2 0.6 %collective-permute-done.9.refs_0_ = bf16[384,1536]{1,0:T(8,128)(2,1)S(1)} collective-permute-done((bf16[384,1536]{1,0:T(8,128)(2,1)S(1)}, bf16[384,1536]{1,0:T(8,128)(2,1)S(1)}, u32[]{:S(2)}, u32[]{:S(2)}) %collective-permute-start.9) | collective-permute-done | bytes 1179680 | tf_op jit(solution)/shard_map/ppermute | solution.py:39
  35.8 3.9 %attend_last.1 = (bf16[384,128]{1,0:T(8,128)(2,1)S(1)}, bf16[384,128]{1,0:T(8,128)(2,1)S(1)}) custom-call(s32[4,4]{1,0:T(4,128)} %mask_ref.1, s32[4]{0:T(128)} %count_ref.1, bf16[1536,384]{1,0:T(8,128)(2,1)S(1)} %get-tuple-element.33.weight_ref, bf16[2,384,128]{2,1,0:T(8,128)(2,1)S(1)} %get-tuple-element.34.queries_ref, ...), custom_call_target="tpu_custom_call" | custom-call | flops 1000000000 | tf_op jit(solution)/shard_map/attend_last/pallas_call | solution.py:64
  39.7 0.6 %collective-permute-done.11.got_ref = bf16[128,768]{1,0:T(8,128)(2,1)S(1)} collective-permute-done((bf16[128,768]{1,0:T(8,128)(2,1)S(1)}, bf16[128,768]{1,0:T(8,128)(2,1)S(1)}, u32[]{:S(2)}, u32[]{:S(2)}) %collective-permute-start.11) | collective-permute-done | bytes 196640 | tf_op jit(solution)/shard_map/ppermute | solution.py:460
  40.3 0.1 collective-permute-start.12
  40.4 0.5 %collective-permute-start.10 = (bf16[384,128]{1,0:T(8,128)(2,1)S(1)}, bf16[384,128]{1,0:T(8,128)(2,1)S(1)}, u32[]{:S(2)}, u32[]{:S(2)}) collective-permute-start(bf16[384,128]{1,0:T(8,128)(2,1)S(1)} %get-tuple-element.37), channel_id=1, source_target_pairs={{0,8},{8,0},{16,24},{24,16},{1,9},{9,1},{17,25},{25,17},{2,10},{10... | collective-permute-start | bytes 294920 | tf_op jit(solution)/shard_map/ppermute | solution.py:39
  40.9 1.4 %collective-permute-done.10.partner_ref = bf16[384,128]{1,0:T(8,128)(2,1)S(1)} collective-permute-done((bf16[384,128]{1,0:T(8,128)(2,1)S(1)}, bf16[384,128]{1,0:T(8,128)(2,1)S(1)}, u32[]{:S(2)}, u32[]{:S(2)}) %collective-permute-start.10) | collective-permute-done | bytes 98336 | tf_op jit(solution)/shard_map/ppermute | solution.py:39
  42.2 0.0 collective-permute-done.12.out_partner_ref
  42.2 1.6 %project_out.1 = bf16[384,1536]{1,0:T(8,128)(2,1)} custom-call(bf16[384,128]{1,0:T(8,128)(2,1)S(1)} %get-tuple-element.36.own_ref, bf16[384,128]{1,0:T(8,128)(2,1)S(1)} %collective-permute-done.10.partner_ref, bf16[256,768]{1,0:T(8,128)(2,1)S(1)} %pair_up.1.out_own_ref, bf16[256,768]{1,0:T(8,128)(2,1)S(1)} %collective-permute-done.12.out_partner_ref), custom_call_target="tpu_custom_call" | custom-call | tf_op jit(solution)/shard_map/project_out/pallas_call | solution.py:64
  (2 shorter events, 0.1 us)
Async XLA Ops:
  0.0 6.6 %collective-permute-start = (bf16[384,1536]{1,0:T(8,128)(2,1)}, bf16[384,1536]{1,0:T(8,128)(2,1)S(1)}, u32[]{:S(2)}, u32[]{:S(2)}) collective-permute-start(bf16[384,1536]{1,0:T(8,128)(2,1)} %bitcast.2), channel_id=1, source_target_pairs={{0,8},{8,0},{16,24},{24,16},{1,9},{9,1},{17,25},{25,17},{2,10},{10... | collective-permute-start | bytes 3538952 | tf_op jit(solution)/shard_map/ppermute | solution.py:39
  0.5 32.4 %collective-permute-start.4 = (bf16[384,1536]{1,0:T(8,128)(2,1)}, bf16[384,1536]{1,0:T(8,128)(2,1)S(1)}, u32[]{:S(2)}, u32[]{:S(2)}) collective-permute-start(bf16[384,1536]{1,0:T(8,128)(2,1)} %bitcast.3), channel_id=1, source_target_pairs={{0,16},{8,24},{16,0},{24,8},{1,17},{9,25},{17,1},{25,9},{2,18},{10... | collective-permute-start | bytes 3538952 | tf_op jit(solution)/shard_map/ppermute | solution.py:43
  4.0 15.4 %collective-permute-start.2 = (bf16[256,384]{1,0:T(8,128)(2,1)S(1)}, bf16[256,384]{1,0:T(8,128)(2,1)S(1)}, u32[]{:S(2)}, u32[]{:S(2)}) collective-permute-start(bf16[256,384]{1,0:T(8,128)(2,1)S(1)} %get-tuple-element.28.refs_0_), channel_id=1, source_target_pairs={{0,4},{1,5},{2,6},{3,7},{4,0},{5,1},{6,2},{7,3},{8,12},{9,13},{10,... | collective-permute-start | bytes 589832 | tf_op jit(solution)/shard_map/ppermute | solution.py:457
  6.6 14.6 %collective-permute-start.1 = (bf16[256,384]{1,0:T(8,128)(2,1)S(1)}, bf16[256,384]{1,0:T(8,128)(2,1)S(1)}, u32[]{:S(2)}, u32[]{:S(2)}) collective-permute-start(bf16[256,384]{1,0:T(8,128)(2,1)S(1)} %get-tuple-element.28.refs_0_), channel_id=1, source_target_pairs={{0,1},{1,0},{2,3},{3,2},{4,5},{5,4},{6,7},{7,6},{8,9},{9,8},{10,11... | collective-permute-start | bytes 589832 | tf_op jit(solution)/shard_map/ppermute | solution.py:457
  8.1 13.1 %collective-permute-start.5 = (bf16[192,384]{1,0:T(8,128)(2,1)S(1)}, bf16[192,384]{1,0:T(8,128)(2,1)S(1)}, u32[]{:S(2)}, u32[]{:S(2)}) collective-permute-start(bf16[192,384]{1,0:T(8,128)(2,1)S(1)} %get-tuple-element.30.refs_0_), channel_id=1, source_target_pairs={{0,2},{1,3},{2,4},{3,5},{4,6},{5,7},{6,0},{7,1},{8,10},{9,11},{10,... | collective-permute-start | bytes 442376 | tf_op jit(solution)/shard_map/ppermute | solution.py:457
  19.4 11.6 %collective-permute-start.3 = (bf16[256,384]{1,0:T(8,128)(2,1)S(1)}, bf16[256,384]{1,0:T(8,128)(2,1)S(1)}, u32[]{:S(2)}, u32[]{:S(2)}) collective-permute-start(bf16[256,384]{1,0:T(8,128)(2,1)S(1)} %collective-permute-done.2.refs_2_), channel_id=1, source_target_pairs={{0,1},{1,0},{2,3},{3,2},{4,5},{5,4},{6,7},{7,6},{8,9},{9,8},{10,11... | collective-permute-start | bytes 589832 | tf_op jit(solution)/shard_map/ppermute | solution.py:457
  20.8 12.0 %collective-permute-start.8 = (bf16[192,384]{1,0:T(8,128)(2,1)S(1)}, bf16[192,384]{1,0:T(8,128)(2,1)S(1)}, u32[]{:S(2)}, u32[]{:S(2)}) collective-permute-start(bf16[192,384]{1,0:T(8,128)(2,1)S(1)} %get-tuple-element.30.refs_0_), channel_id=1, source_target_pairs={{0,7},{1,6},{2,1},{3,0},{4,3},{5,2},{6,5},{7,4},{8,15},{9,14},{10,... | collective-permute-start | bytes 442376 | tf_op jit(solution)/shard_map/ppermute | solution.py:457
  21.2 11.6 %collective-permute-start.7 = (bf16[192,384]{1,0:T(8,128)(2,1)S(1)}, bf16[192,384]{1,0:T(8,128)(2,1)S(1)}, u32[]{:S(2)}, u32[]{:S(2)}) collective-permute-start(bf16[192,384]{1,0:T(8,128)(2,1)S(1)} %get-tuple-element.30.refs_0_), channel_id=1, source_target_pairs={{0,6},{1,7},{2,0},{3,1},{4,2},{5,3},{6,4},{7,5},{8,14},{9,15},{10,... | collective-permute-start | bytes 442376 | tf_op jit(solution)/shard_map/ppermute | solution.py:457
  21.8 11.0 %collective-permute-start.6 = (bf16[192,384]{1,0:T(8,128)(2,1)S(1)}, bf16[192,384]{1,0:T(8,128)(2,1)S(1)}, u32[]{:S(2)}, u32[]{:S(2)}) collective-permute-start(bf16[192,384]{1,0:T(8,128)(2,1)S(1)} %get-tuple-element.30.refs_0_), channel_id=1, source_target_pairs={{0,3},{1,2},{2,5},{3,4},{4,7},{5,6},{6,1},{7,0},{8,11},{9,10},{10,... | collective-permute-start | bytes 442376 | tf_op jit(solution)/shard_map/ppermute | solution.py:457
  32.8 2.9 %collective-permute-start.9 = (bf16[384,1536]{1,0:T(8,128)(2,1)S(1)}, bf16[384,1536]{1,0:T(8,128)(2,1)S(1)}, u32[]{:S(2)}, u32[]{:S(2)}) collective-permute-start(bf16[384,1536]{1,0:T(8,128)(2,1)S(1)} %collective-permute-done.4.near_ref), channel_id=1, source_target_pairs={{0,8},{8,0},{16,24},{24,16},{1,9},{9,1},{17,25},{25,17},{2,10},{10... | collective-permute-start | bytes 3538952 | tf_op jit(solution)/shard_map/ppermute | solution.py:39
  32.9 7.3 %collective-permute-start.11 = (bf16[128,768]{1,0:T(8,128)(2,1)S(1)}, bf16[128,768]{1,0:T(8,128)(2,1)S(1)}, u32[]{:S(2)}, u32[]{:S(2)}) collective-permute-start(bf16[128,768]{1,0:T(8,128)(2,1)S(1)} %collect.1.own_ref), channel_id=1, source_target_pairs={{0,2},{1,3},{2,0},{3,1},{4,6},{5,7},{6,4},{7,5},{8,10},{9,11},{10,... | collective-permute-start | bytes 589832 | tf_op jit(solution)/shard_map/ppermute | solution.py:460
  40.3 1.9 %collective-permute-start.12 = (bf16[256,768]{1,0:T(8,128)(2,1)S(1)}, bf16[256,768]{1,0:T(8,128)(2,1)S(1)}, u32[]{:S(2)}, u32[]{:S(2)}) collective-permute-start(bf16[256,768]{1,0:T(8,128)(2,1)S(1)} %pair_up.1.out_own_ref), channel_id=1, source_target_pairs={{0,8},{8,0},{16,24},{24,16},{1,9},{9,1},{17,25},{25,17},{2,10},{10... | collective-permute-start | bytes 1179656 | tf_op jit(solution)/shard_map/ppermute | solution.py:39
  40.4 1.9 %collective-permute-start.10 = (bf16[384,128]{1,0:T(8,128)(2,1)S(1)}, bf16[384,128]{1,0:T(8,128)(2,1)S(1)}, u32[]{:S(2)}, u32[]{:S(2)}) collective-permute-start(bf16[384,128]{1,0:T(8,128)(2,1)S(1)} %get-tuple-element.37), channel_id=1, source_target_pairs={{0,8},{8,0},{16,24},{24,16},{1,9},{9,1},{17,25},{25,17},{2,10},{10... | collective-permute-start | bytes 294920 | tf_op jit(solution)/shard_map/ppermute | solution.py:39

commit v12 on v11

--- a/solution.py
+++ b/solution.py
@@ -359,6 +359,7 @@
             values_ref[:, first : first + LANES] = jnp.ones((slots + BLOCK, LANES), dtype)
 
         def over(keys_taken):
+            later = []
             slot = lax.broadcasted_iota(jnp.int32, (1, keys_taken), 1)
             for member in range(CORES):
                 bias = jnp.full((1, keys_taken), NEG, jnp.float32)
@@ -369,21 +370,31 @@
                     lanes = slice(group * LANES, (group + 1) * LANES)
                     for start in range(0, row_count, ROWS):
                         chunk = slice(start, start + ROWS)
-                        parts = attend_part(
-                            queries_ref[member, chunk, lanes],
-                            keys_ref[:keys_taken, lanes],
-                            values_ref[:keys_taken, 2 * group * LANES : 2 * (group + 1) * LANES],
-                            bias,
-                        )
-                        if old_ref is not None:
-                            parts = merge([old_ref[member, which, chunk, lanes] for which in range(3)], parts)
-                        if last:
-                            position = start + lax.broadcasted_iota(jnp.int32, (ROWS, 1), 0)
-                            attended = jnp.where(position < count_ref[tiles[member]], parts[2] / parts[1], 0.0)
-                            refs[member][chunk, lanes] = attended.astype(dtype)
+
+                        def rows_of(member=member, group=group, lanes=lanes, start=start, chunk=chunk, bias=bias):
+                            parts = attend_part(
+                                queries_ref[member, chunk, lanes],
+                                keys_ref[:keys_taken, lanes],
+                                values_ref[:keys_taken, 2 * group * LANES : 2 * (group + 1) * LANES],
+                                bias,
+                            )
+                            if old_ref is not None:
+                                parts = merge([old_ref[member, which, chunk, lanes] for which in range(3)], parts)
+                            if last:
+                                position = start + lax.broadcasted_iota(jnp.int32, (ROWS, 1), 0)
+                                attended = jnp.where(position < count_ref[tiles[member]], parts[2] / parts[1], 0.0)
+                                refs[member][chunk, lanes] = attended.astype(dtype)
+                            else:
+                                for which, part in enumerate(parts):
+                                    refs[0][member, which, chunk, lanes] = part
+
+                        if last and start:
+                            refs[member][chunk, lanes] = jnp.zeros((ROWS, LANES), dtype)
+                            later.append((count_ref[tiles[member]] > start, rows_of))
                         else:
-                            for which, part in enumerate(parts):
-                                refs[0][member, which, chunk, lanes] = part
+                            rows_of()
+            for live, rows_of in later:
+                pl.when(live)(rows_of)
 
         blocks = (ends[-1] + BLOCK - 1) // BLOCK
         fewest, most = max(slots // (2 * BLOCK), 1), slots // BLOCK

time: 44.2 us -> 44.2 us (level)
  transfers between devices with their start and end apart: 13 -> 13, of which waited for: 5 -> 5; matrix products, arithmetic and copies ran while one was open for 0% -> 0% of each run, Pallas kernels for 18% -> 19%
where the time goes in v12:
time: 44.2 us; the launch traced here: 44 us
  waiting for transfers between devices  18.7 us (42%)
  starting transfers between devices  15.2 us (34%)
  Pallas kernels  9.8 us (22%)
    ppermute x7, waiting for transfers between devices, hop(): lax.ppermute(array, 'fsdp', rotation(z_count, x_count, z_step, x_step))  16.4 us
    ppermute x7, starting transfers between devices, hop(): lax.ppermute(array, 'fsdp', rotation(z_count, x_count, z_step, x_step))  10.5 us
    pallas_call x7, Pallas kernels, run(): inner(*[pltpu.with_memory_space_constraint(arg, pltpu.HBM if spec is SMEM...  9.8 us
    ppermute x1, starting transfers between devices, y_rotation(): lax.ppermute(array, 'seq', [(s, (s + CORES * step) % seq_count) for s in...  2.52 us
    ppermute x4, waiting for transfers between devices, core_swap(): return lax.ppermute(array, 'seq', [(s, s ^ 1) for s in range(seq_count)])  1.94 us
    ppermute x4, starting transfers between devices, core_swap(): return lax.ppermute(array, 'seq', [(s, s ^ 1) for s in range(seq_count)])  1.09 us
    ppermute x1, starting transfers between devices, flip(): lax.ppermute(array, 'fsdp', [(f, f ^ shift * x_count) for f in range(fsdp...  1.05 us
  transfers between devices with their start and end apart: 13, of which 5 were waited for; matrix products, arithmetic and copies ran while one was open for 0% of the time, Pallas kernels for 19%

profile of v12, /device:TPU:0, one launch (start us, length us, event | category | flops | bytes accessed | tf_op | source)
XLA Modules:
  0.0 44.0 jit_solution(312157376728166588)
XLA Ops:
  0.0 0.5 %collective-permute-start = (bf16[384,1536]{1,0:T(8,128)(2,1)}, bf16[384,1536]{1,0:T(8,128)(2,1)S(1)}, u32[]{:S(2)}, u32[]{:S(2)}) collective-permute-start(bf16[384,1536]{1,0:T(8,128)(2,1)} %bitcast.2), channel_id=1, source_target_pairs={{0,8},{8,0},{16,24},{24,16},{1,9},{9,1},{17,25},{25,17},{2,10},{10... | collective-permute-start | bytes 3538952 | tf_op jit(solution)/shard_map/ppermute | solution.py:39
  0.5 2.5 %collective-permute-start.4 = (bf16[384,1536]{1,0:T(8,128)(2,1)}, bf16[384,1536]{1,0:T(8,128)(2,1)S(1)}, u32[]{:S(2)}, u32[]{:S(2)}) collective-permute-start(bf16[384,1536]{1,0:T(8,128)(2,1)} %bitcast.3), channel_id=1, source_target_pairs={{0,16},{8,24},{16,0},{24,8},{1,17},{9,25},{17,1},{25,9},{2,18},{10... | collective-permute-start | bytes 3538952 | tf_op jit(solution)/shard_map/ppermute | solution.py:43
  3.0 1.1 %halves.1 = (bf16[192,384]{1,0:T(8,128)(2,1)S(1)}, bf16[256,384]{1,0:T(8,128)(2,1)S(1)}) custom-call(bf16[192,768]{1,0:T(8,128)(2,1)} %qkv_ref.1, bf16[32,1536]{1,0:T(8,128)(2,1)} %out_ref.1), custom_call_target="tpu_custom_call" | custom-call | tf_op jit(solution)/shard_map/halves/pallas_call | solution.py:64
  4.0 2.7 %collective-permute-start.2 = (bf16[256,384]{1,0:T(8,128)(2,1)S(1)}, bf16[256,384]{1,0:T(8,128)(2,1)S(1)}, u32[]{:S(2)}, u32[]{:S(2)}) collective-permute-start(bf16[256,384]{1,0:T(8,128)(2,1)S(1)} %get-tuple-element.28.refs_0_), channel_id=1, source_target_pairs={{0,4},{1,5},{2,6},{3,7},{4,0},{5,1},{6,2},{7,3},{8,12},{9,13},{10,... | collective-permute-start | bytes 589832 | tf_op jit(solution)/shard_map/ppermute | solution.py:468
  6.7 0.0 collective-permute-done.other_ref
  6.7 1.5 %collective-permute-start.1 = (bf16[256,384]{1,0:T(8,128)(2,1)S(1)}, bf16[256,384]{1,0:T(8,128)(2,1)S(1)}, u32[]{:S(2)}, u32[]{:S(2)}) collective-permute-start(bf16[256,384]{1,0:T(8,128)(2,1)S(1)} %get-tuple-element.28.refs_0_), channel_id=1, source_target_pairs={{0,1},{1,0},{2,3},{3,2},{4,5},{5,4},{6,7},{7,6},{8,9},{9,8},{10,11... | collective-permute-start | bytes 589832 | tf_op jit(solution)/shard_map/ppermute | solution.py:468
  8.2 1.6 %collective-permute-start.5 = (bf16[192,384]{1,0:T(8,128)(2,1)S(1)}, bf16[192,384]{1,0:T(8,128)(2,1)S(1)}, u32[]{:S(2)}, u32[]{:S(2)}) collective-permute-start(bf16[192,384]{1,0:T(8,128)(2,1)S(1)} %get-tuple-element.30.refs_0_), channel_id=1, source_target_pairs={{0,2},{1,3},{2,4},{3,5},{4,6},{5,7},{6,0},{7,1},{8,10},{9,11},{10,... | collective-permute-start | bytes 442376 | tf_op jit(solution)/shard_map/ppermute | solution.py:468
  9.8 9.6 %collective-permute-done.2.refs_2_ = bf16[256,384]{1,0:T(8,128)(2,1)S(1)} collective-permute-done((bf16[256,384]{1,0:T(8,128)(2,1)S(1)}, bf16[256,384]{1,0:T(8,128)(2,1)S(1)}, u32[]{:S(2)}, u32[]{:S(2)}) %collective-permute-start.2) | collective-permute-done | bytes 196640 | tf_op jit(solution)/shard_map/ppermute | solution.py:468
  19.4 1.5 %collective-permute-start.3 = (bf16[256,384]{1,0:T(8,128)(2,1)S(1)}, bf16[256,384]{1,0:T(8,128)(2,1)S(1)}, u32[]{:S(2)}, u32[]{:S(2)}) collective-permute-start(bf16[256,384]{1,0:T(8,128)(2,1)S(1)} %collective-permute-done.2.refs_2_), channel_id=1, source_target_pairs={{0,1},{1,0},{2,3},{3,2},{4,5},{5,4},{6,7},{7,6},{8,9},{9,8},{10,11... | collective-permute-start | bytes 589832 | tf_op jit(solution)/shard_map/ppermute | solution.py:468
  20.9 0.4 collective-permute-start.8
  21.3 0.0 collective-permute-done.5.refs_0_
  21.3 0.0 collective-permute-done.1.refs_1_
  21.3 0.6 %collective-permute-start.7 = (bf16[192,384]{1,0:T(8,128)(2,1)S(1)}, bf16[192,384]{1,0:T(8,128)(2,1)S(1)}, u32[]{:S(2)}, u32[]{:S(2)}) collective-permute-start(bf16[192,384]{1,0:T(8,128)(2,1)S(1)} %get-tuple-element.30.refs_0_), channel_id=1, source_target_pairs={{0,6},{1,7},{2,0},{3,1},{4,2},{5,3},{6,4},{7,5},{8,14},{9,15},{10,... | collective-permute-start | bytes 442376 | tf_op jit(solution)/shard_map/ppermute | solution.py:468
  21.9 2.3 %collective-permute-start.6 = (bf16[192,384]{1,0:T(8,128)(2,1)S(1)}, bf16[192,384]{1,0:T(8,128)(2,1)S(1)}, u32[]{:S(2)}, u32[]{:S(2)}) collective-permute-start(bf16[192,384]{1,0:T(8,128)(2,1)S(1)} %get-tuple-element.30.refs_0_), channel_id=1, source_target_pairs={{0,3},{1,2},{2,5},{3,4},{4,7},{5,6},{6,1},{7,0},{8,11},{9,10},{10,... | collective-permute-start | bytes 442376 | tf_op jit(solution)/shard_map/ppermute | solution.py:468
  24.2 6.8 %collective-permute-done.3.refs_3_ = bf16[256,384]{1,0:T(8,128)(2,1)S(1)} collective-permute-done((bf16[256,384]{1,0:T(8,128)(2,1)S(1)}, bf16[256,384]{1,0:T(8,128)(2,1)S(1)}, u32[]{:S(2)}, u32[]{:S(2)}) %collective-permute-start.3) | collective-permute-done | bytes 196640 | tf_op jit(solution)/shard_map/ppermute | solution.py:468
  31.0 1.8 %project_first.1 = (bf16[384,1536]{1,0:T(8,128)(2,1)S(1)}, bf16[1536,384]{1,0:T(8,128)(2,1)S(1)}, f32[2,384,384]{2,1,0:T(8,128)S(1)}) custom-call(bf16[384,1536]{1,0:T(8,128)(2,1)} %bitcast.4, bf16[384,1536]{1,0:T(8,128)(2,1)S(1)} %collective-permute-done.other_ref, bf16[192,384]{1,0:T(8,128)(2,1)S(1)} %get-tuple-element.30.refs_0_, ...), custom_call_target="tpu_custom_call" | custom-call | flops 1000000000 | tf_op jit(solution)/shard_map/project_first/pallas_call | solution.py:64
  32.8 0.0 collective-permute-done.8.refs_3_
  32.9 0.0 collective-permute-done.4.near_ref
  32.9 0.0 collective-permute-done.7.refs_2_
  32.9 0.0 collective-permute-done.6.refs_1_
  32.9 0.1 collective-permute-start.9
  33.0 1.1 %collective-permute-start.11 = (bf16[128,768]{1,0:T(8,128)(2,1)S(1)}, bf16[128,768]{1,0:T(8,128)(2,1)S(1)}, u32[]{:S(2)}, u32[]{:S(2)}) collective-permute-start(bf16[128,768]{1,0:T(8,128)(2,1)S(1)} %collect.1.own_ref), channel_id=1, source_target_pairs={{0,2},{1,3},{2,0},{3,1},{4,6},{5,7},{6,4},{7,5},{8,10},{9,11},{10,... | collective-permute-start | bytes 589832 | tf_op jit(solution)/shard_map/ppermute | solution.py:471
  34.0 1.2 %project.1 = (bf16[2,384,128]{2,1,0:T(8,128)(2,1)S(1)}, bf16[1536,384]{1,0:T(8,128)(2,1)S(1)}, bf16[1152,256]{1,0:T(8,128)(2,1)S(1)}) custom-call(bf16[384,1536]{1,0:T(8,128)(2,1)S(1)} %get-tuple-element.25.own_ref, bf16[384,1536]{1,0:T(8,128)(2,1)S(1)} %collective-permute-done.other_ref, ...), custom_call_target="tpu_custom_call", output_to_operand_aliasing={{1}: (2, {})} | custom-call | flops 1000000000 | tf_op jit(solution)/shard_map/project/pallas_call | solution.py:64
  35.2 0.6 %collective-permute-done.9.refs_0_ = bf16[384,1536]{1,0:T(8,128)(2,1)S(1)} collective-permute-done((bf16[384,1536]{1,0:T(8,128)(2,1)S(1)}, bf16[384,1536]{1,0:T(8,128)(2,1)S(1)}, u32[]{:S(2)}, u32[]{:S(2)}) %collective-permute-start.9) | collective-permute-done | bytes 1179680 | tf_op jit(solution)/shard_map/ppermute | solution.py:39
  35.8 4.1 %attend_last.1 = (bf16[384,128]{1,0:T(8,128)(2,1)S(1)}, bf16[384,128]{1,0:T(8,128)(2,1)S(1)}) custom-call(s32[4,4]{1,0:T(4,128)} %mask_ref.1, s32[4]{0:T(128)} %count_ref.1, bf16[1536,384]{1,0:T(8,128)(2,1)S(1)} %get-tuple-element.33.weight_ref, bf16[2,384,128]{2,1,0:T(8,128)(2,1)S(1)} %get-tuple-element.34.queries_ref, ...), custom_call_target="tpu_custom_call" | custom-call | flops 1000000000 | tf_op jit(solution)/shard_map/attend_last/pallas_call | solution.py:64
  39.9 0.4 collective-permute-done.11.got_ref
  40.3 0.1 collective-permute-start.12
  40.4 0.5 %collective-permute-start.10 = (bf16[384,128]{1,0:T(8,128)(2,1)S(1)}, bf16[384,128]{1,0:T(8,128)(2,1)S(1)}, u32[]{:S(2)}, u32[]{:S(2)}) collective-permute-start(bf16[384,128]{1,0:T(8,128)(2,1)S(1)} %get-tuple-element.37), channel_id=1, source_target_pairs={{0,8},{8,0},{16,24},{24,16},{1,9},{9,1},{17,25},{25,17},{2,10},{10... | collective-permute-start | bytes 294920 | tf_op jit(solution)/shard_map/ppermute | solution.py:39
  40.9 1.4 %collective-permute-done.10.partner_ref = bf16[384,128]{1,0:T(8,128)(2,1)S(1)} collective-permute-done((bf16[384,128]{1,0:T(8,128)(2,1)S(1)}, bf16[384,128]{1,0:T(8,128)(2,1)S(1)}, u32[]{:S(2)}, u32[]{:S(2)}) %collective-permute-start.10) | collective-permute-done | bytes 98336 | tf_op jit(solution)/shard_map/ppermute | solution.py:39
  42.3 0.0 collective-permute-done.12.out_partner_ref
  42.3 1.6 %project_out.1 = bf16[384,1536]{1,0:T(8,128)(2,1)} custom-call(bf16[384,128]{1,0:T(8,128)(2,1)S(1)} %get-tuple-element.36.own_ref, bf16[384,128]{1,0:T(8,128)(2,1)S(1)} %collective-permute-done.10.partner_ref, bf16[256,768]{1,0:T(8,128)(2,1)S(1)} %pair_up.1.out_own_ref, bf16[256,768]{1,0:T(8,128)(2,1)S(1)} %collective-permute-done.12.out_partner_ref), custom_call_target="tpu_custom_call" | custom-call | tf_op jit(solution)/shard_map/project_out/pallas_call | solution.py:64
  (2 shorter events, 0.1 us)
Async XLA Ops:
  0.0 6.7 %collective-permute-start = (bf16[384,1536]{1,0:T(8,128)(2,1)}, bf16[384,1536]{1,0:T(8,128)(2,1)S(1)}, u32[]{:S(2)}, u32[]{:S(2)}) collective-permute-start(bf16[384,1536]{1,0:T(8,128)(2,1)} %bitcast.2), channel_id=1, source_target_pairs={{0,8},{8,0},{16,24},{24,16},{1,9},{9,1},{17,25},{25,17},{2,10},{10... | collective-permute-start | bytes 3538952 | tf_op jit(solution)/shard_map/ppermute | solution.py:39
  0.5 32.4 %collective-permute-start.4 = (bf16[384,1536]{1,0:T(8,128)(2,1)}, bf16[384,1536]{1,0:T(8,128)(2,1)S(1)}, u32[]{:S(2)}, u32[]{:S(2)}) collective-permute-start(bf16[384,1536]{1,0:T(8,128)(2,1)} %bitcast.3), channel_id=1, source_target_pairs={{0,16},{8,24},{16,0},{24,8},{1,17},{9,25},{17,1},{25,9},{2,18},{10... | collective-permute-start | bytes 3538952 | tf_op jit(solution)/shard_map/ppermute | solution.py:43
  4.0 15.4 %collective-permute-start.2 = (bf16[256,384]{1,0:T(8,128)(2,1)S(1)}, bf16[256,384]{1,0:T(8,128)(2,1)S(1)}, u32[]{:S(2)}, u32[]{:S(2)}) collective-permute-start(bf16[256,384]{1,0:T(8,128)(2,1)S(1)} %get-tuple-element.28.refs_0_), channel_id=1, source_target_pairs={{0,4},{1,5},{2,6},{3,7},{4,0},{5,1},{6,2},{7,3},{8,12},{9,13},{10,... | collective-permute-start | bytes 589832 | tf_op jit(solution)/shard_map/ppermute | solution.py:468
  6.7 14.6 %collective-permute-start.1 = (bf16[256,384]{1,0:T(8,128)(2,1)S(1)}, bf16[256,384]{1,0:T(8,128)(2,1)S(1)}, u32[]{:S(2)}, u32[]{:S(2)}) collective-permute-start(bf16[256,384]{1,0:T(8,128)(2,1)S(1)} %get-tuple-element.28.refs_0_), channel_id=1, source_target_pairs={{0,1},{1,0},{2,3},{3,2},{4,5},{5,4},{6,7},{7,6},{8,9},{9,8},{10,11... | collective-permute-start | bytes 589832 | tf_op jit(solution)/shard_map/ppermute | solution.py:468
  8.2 13.1 %collective-permute-start.5 = (bf16[192,384]{1,0:T(8,128)(2,1)S(1)}, bf16[192,384]{1,0:T(8,128)(2,1)S(1)}, u32[]{:S(2)}, u32[]{:S(2)}) collective-permute-start(bf16[192,384]{1,0:T(8,128)(2,1)S(1)} %get-tuple-element.30.refs_0_), channel_id=1, source_target_pairs={{0,2},{1,3},{2,4},{3,5},{4,6},{5,7},{6,0},{7,1},{8,10},{9,11},{10,... | collective-permute-start | bytes 442376 | tf_op jit(solution)/shard_map/ppermute | solution.py:468
  19.4 11.6 %collective-permute-start.3 = (bf16[256,384]{1,0:T(8,128)(2,1)S(1)}, bf16[256,384]{1,0:T(8,128)(2,1)S(1)}, u32[]{:S(2)}, u32[]{:S(2)}) collective-permute-start(bf16[256,384]{1,0:T(8,128)(2,1)S(1)} %collective-permute-done.2.refs_2_), channel_id=1, source_target_pairs={{0,1},{1,0},{2,3},{3,2},{4,5},{5,4},{6,7},{7,6},{8,9},{9,8},{10,11... | collective-permute-start | bytes 589832 | tf_op jit(solution)/shard_map/ppermute | solution.py:468
  20.9 11.9 %collective-permute-start.8 = (bf16[192,384]{1,0:T(8,128)(2,1)S(1)}, bf16[192,384]{1,0:T(8,128)(2,1)S(1)}, u32[]{:S(2)}, u32[]{:S(2)}) collective-permute-start(bf16[192,384]{1,0:T(8,128)(2,1)S(1)} %get-tuple-element.30.refs_0_), channel_id=1, source_target_pairs={{0,7},{1,6},{2,1},{3,0},{4,3},{5,2},{6,5},{7,4},{8,15},{9,14},{10,... | collective-permute-start | bytes 442376 | tf_op jit(solution)/shard_map/ppermute | solution.py:468
  21.3 11.6 %collective-permute-start.7 = (bf16[192,384]{1,0:T(8,128)(2,1)S(1)}, bf16[192,384]{1,0:T(8,128)(2,1)S(1)}, u32[]{:S(2)}, u32[]{:S(2)}) collective-permute-start(bf16[192,384]{1,0:T(8,128)(2,1)S(1)} %get-tuple-element.30.refs_0_), channel_id=1, source_target_pairs={{0,6},{1,7},{2,0},{3,1},{4,2},{5,3},{6,4},{7,5},{8,14},{9,15},{10,... | collective-permute-start | bytes 442376 | tf_op jit(solution)/shard_map/ppermute | solution.py:468
  21.9 11.0 %collective-permute-start.6 = (bf16[192,384]{1,0:T(8,128)(2,1)S(1)}, bf16[192,384]{1,0:T(8,128)(2,1)S(1)}, u32[]{:S(2)}, u32[]{:S(2)}) collective-permute-start(bf16[192,384]{1,0:T(8,128)(2,1)S(1)} %get-tuple-element.30.refs_0_), channel_id=1, source_target_pairs={{0,3},{1,2},{2,5},{3,4},{4,7},{5,6},{6,1},{7,0},{8,11},{9,10},{10,... | collective-permute-start | bytes 442376 | tf_op jit(solution)/shard_map/ppermute | solution.py:468
  32.9 2.9 %collective-permute-start.9 = (bf16[384,1536]{1,0:T(8,128)(2,1)S(1)}, bf16[384,1536]{1,0:T(8,128)(2,1)S(1)}, u32[]{:S(2)}, u32[]{:S(2)}) collective-permute-start(bf16[384,1536]{1,0:T(8,128)(2,1)S(1)} %collective-permute-done.4.near_ref), channel_id=1, source_target_pairs={{0,8},{8,0},{16,24},{24,16},{1,9},{9,1},{17,25},{25,17},{2,10},{10... | collective-permute-start | bytes 3538952 | tf_op jit(solution)/shard_map/ppermute | solution.py:39
  33.0 7.3 %collective-permute-start.11 = (bf16[128,768]{1,0:T(8,128)(2,1)S(1)}, bf16[128,768]{1,0:T(8,128)(2,1)S(1)}, u32[]{:S(2)}, u32[]{:S(2)}) collective-permute-start(bf16[128,768]{1,0:T(8,128)(2,1)S(1)} %collect.1.own_ref), channel_id=1, source_target_pairs={{0,2},{1,3},{2,0},{3,1},{4,6},{5,7},{6,4},{7,5},{8,10},{9,11},{10,... | collective-permute-start | bytes 589832 | tf_op jit(solution)/shard_map/ppermute | solution.py:471
  40.3 1.9 %collective-permute-start.12 = (bf16[256,768]{1,0:T(8,128)(2,1)S(1)}, bf16[256,768]{1,0:T(8,128)(2,1)S(1)}, u32[]{:S(2)}, u32[]{:S(2)}) collective-permute-start(bf16[256,768]{1,0:T(8,128)(2,1)S(1)} %pair_up.1.out_own_ref), channel_id=1, source_target_pairs={{0,8},{8,0},{16,24},{24,16},{1,9},{9,1},{17,25},{25,17},{2,10},{10... | collective-permute-start | bytes 1179656 | tf_op jit(solution)/shard_map/ppermute | solution.py:39
  40.4 1.9 %collective-permute-start.10 = (bf16[384,128]{1,0:T(8,128)(2,1)S(1)}, bf16[384,128]{1,0:T(8,128)(2,1)S(1)}, u32[]{:S(2)}, u32[]{:S(2)}) collective-permute-start(bf16[384,128]{1,0:T(8,128)(2,1)S(1)} %get-tuple-element.37), channel_id=1, source_target_pairs={{0,8},{8,0},{16,24},{24,16},{1,9},{9,1},{17,25},{25,17},{2,10},{10... | collective-permute-start | bytes 294920 | tf_op jit(solution)/shard_map/ppermute | solution.py:39
